TPU v7x, 128 devices: a whole 4x4x4 slice. The times are simulated.
128 devices in a mesh: blk: 64 (over z_hi, x, y, core), feat: 2 (over z_lo).
Axes of the slice: x: 4, y: 4, z: 4 (z_hi: 2, z_lo: 2; z = z_hi * 2 + z_lo), core: 2. Of those that a mesh axis runs over, the one named last changes fastest.
Arguments:
- points: bfloat16 [65536, 64], P('blk', 'feat'), may hold values from -1.5 to 1.5
- vectors: bfloat16 [65536, 64], P('blk', 'feat'), may hold values from -5.5 to 5.5
- lengthscale: float32 [64], replicated, may hold values from 0.5 to 2
- outscale: float32 [1], replicated, may hold values from 0.1 to 0.4
- noise: float32 [1], replicated, may hold values from 0.05 to 0.5
Outputs:
- product: float32 [65536, 64], P('blk', 'feat')
All inputs are finite; a program needn't handle non-finite values.
Results may differ from a plain program's by a relative error of at most 0.0026.
Values may be sent and summed in bfloat16 or wider, within the bound.
No kernel may reach another device: no remote copies, remote signals or barrier semaphores. Data moves between devices by JAX's collectives and lax.ppermute only.
A program may use at most 64 MiB of HBM per device.

v0:
```python
import math

import jax
import jax.numpy as jnp
from jax import lax
from jax.sharding import PartitionSpec as P


def rows_first(arrays, axis, dims):
    turned = [jnp.moveaxis(a, dim, 0) for a, dim in zip(arrays, dims)]
    widths = [t[0].size for t in turned]
    both = jnp.concatenate([t.reshape(-1, w) for t, w in zip(turned, widths)], axis=1)
    out = lax.all_gather(both, axis, axis=0, tiled=True)
    blocks = jnp.split(out, [sum(widths[:k]) for k in range(1, len(widths))], axis=1)
    return tuple(
        (
            jnp.moveaxis(b.reshape(-1, *t.shape[1:]), 0, dim)
            for b, t, dim in zip(blocks, turned, dims)
        )
    )


def sent_together(arrays, axis, dim, along):
    both = jnp.concatenate(arrays, axis=along)
    out, at, done = (lax.all_gather(both, axis, axis=dim, tiled=True), 0, [])
    for a in arrays:
        done.append(lax.slice_in_dim(out, at, at + a.shape[along], axis=along))
        at += a.shape[along]
    return tuple(done)


def squares(values):
    wide = values.astype(jnp.float32)
    return jnp.sum(wide * wide, axis=1)


def kernel_tile(rows_left, norms_left, rows_right, norms_right, amplitude):
    inner = lax.dot_general(
        rows_left, rows_right, (((1,), (1,)), ((), ())), preferred_element_type=jnp.float32
    )
    distance = jnp.maximum(norms_left[:, None] + norms_right[None, :] - 2.0 * inner, 0.0)
    return (amplitude * jnp.exp(-0.5 * distance)).astype(jnp.bfloat16)


def per_device(points, vectors, lengthscale, outscale, noise):
    feature_width = points.shape[1]
    feat_index = lax.axis_index("feat")
    length_slice = lax.dynamic_slice_in_dim(lengthscale, feat_index * feature_width, feature_width)
    scaled = (points.astype(jnp.float32) / length_slice).astype(jnp.bfloat16)
    whole_points, whole_vectors = rows_first((scaled, vectors), "feat", (1, 1))
    block_rows = points.shape[0]
    row_share = block_rows // lax.axis_size("feat")
    amplitude = outscale[0]
    vector_count = whole_vectors.shape[1]
    whole_norms = squares(whole_points)
    share_points = lax.dynamic_slice_in_dim(whole_points, feat_index * row_share, row_share, 0)
    share_vectors = lax.dynamic_slice_in_dim(whole_vectors, feat_index * row_share, row_share, 0)
    guest_points, guest_vectors = sent_together((share_points, share_vectors), "blk", 0, 1)
    guest_total = guest_points.shape[0]
    step_rows = math.gcd(guest_total, 2048)
    step_count = guest_total // step_rows
    point_groups = guest_points.reshape(step_count, step_rows, guest_points.shape[1])
    vector_groups = guest_vectors.reshape(step_count, step_rows, guest_vectors.shape[1])

    def advance(partial_value, paired):
        group_points, group_vectors = paired
        kernel_block = kernel_tile(
            whole_points, whole_norms, group_points, squares(group_points), amplitude
        )
        return (
            partial_value
            + jnp.dot(kernel_block, group_vectors, preferred_element_type=jnp.float32),
            None,
        )

    start_sum = jnp.zeros((block_rows, vector_count), jnp.float32)
    direct, unused = lax.scan(advance, start_sum, (point_groups, vector_groups))
    result = lax.psum_scatter(direct, "feat", scatter_dimension=1, tiled=True)
    return result + noise[0] * vectors.astype(jnp.float32)


def solution(mesh):
    placed = (P("blk", "feat"), P("blk", "feat"), P(), P(), P())
    return jax.shard_map(
        per_device, mesh=mesh, in_specs=placed, out_specs=P("blk", "feat"), check_vma=False
    )
```

profile of v0, /device:TPU:0, one launch (start us, length us, event | category | flops | bytes accessed | tf_op | source)
XLA Modules:
  0.0 257.4 jit_solution(6274694604724855071)
XLA Ops:
  9.0 6.2 %all_gather.6 = bf16[64,2048]{1,0:T(8,128)(2,1)S(1)} all-gather(bf16[32,2048]{1,0:T(8,128)(2,1)S(1)} %pad_maximum_fusion), channel_id=1, replica_groups=mesh['blk'=64,'feat'=2] {'feat'}, dimensions={0}, use_global_device_ids=true | all-gather | bytes 393216 | tf_op jit(solution)/shard_map/all_gather | solution.py:13
  16.2 92.0 %all-gather.2.cloned.1.call-done = bf16[32768,128]{0,1:T(8,128)(2,1)} async-done(((bf16[512,128]{0,1:T(8,128)(2,1)}), bf16[32768,128]{0,1:T(8,128)(2,1)}) %all-gather.2.cloned.1.call-update) | async-done | bytes 8388624 | tf_op jit(solution)/shard_map/all_gather | solution.py:25
  108.3 5.8 %fusion.19 = (bf16[32768,64]{0,1:T(8,128)(2,1)}, bf16[32768,64]{0,1:T(8,128)(2,1)}) fusion(bf16[32768,128]{0,1:T(8,128)(2,1)} %all-gather.2.cloned.1.call-done), kind=kLoop, calls=%fused_computation.26 | loop fusion | bytes 16777216 | tf_op jit(solution)/shard_map/slice | solution.py:27
  114.0 8.4 %copy.11 = bf16[32768,64]{1,0:T(8,128)(2,1)} copy(bf16[32768,64]{0,1:T(8,128)(2,1)} %get-tuple-element.89) | data formatting | bytes 8388608
  122.4 8.4 %copy.12 = bf16[32768,64]{1,0:T(8,128)(2,1)} copy(bf16[32768,64]{0,1:T(8,128)(2,1)} %get-tuple-element.88) | data formatting | bytes 8388608
  130.8 104.6 %while.11 = (s32[]{:T(128)}, f32[1024,64]{0,1:T(8,128)S(1)}, f32[]{:T(128)}, f32[1024]{0:T(1024)S(1)}, bf16[16,2048,64]{2,1,0:T(8,128)(2,1)}, /*index=5*/bf16[10...) while((s32[]{:T(128)}, f32[1024,64]{0,1:T(8,128)S(1)}, f32[]{:T(128)}, ...), condition=%wide.region_3.4_spmd.clone, body=%wide.region_1.3_spmd.clone.sunk | while | flops 552073216 | bytes 1988203 | solution.py:77
  130.8 1.4 multiply_reduce_fusion.3
  132.3 5.1 %fusion.28 = f32[1024,64]{0,1:T(8,128)S(1)} fusion(bf16[1024,64]{1,0:T(8,128)(2,1)S(1)} %get-tuple-element.161, f32[2048]{0:T(1024)S(1)} %multiply_reduce_fusion.3, f32[1024]{0:T(1024)S(1)} %get-tuple-element.159, f32[]{:T(128)} %get-tuple-element.158, bf16[16,2048,64]{2,1,0:T(8,128)(2,1)} %get-tuple-element.162, s32[]{:T(128)} %get-tuple-element.147, ...), kind=kOutput, calls=%fused_computation.7.clone.1 | convolution fusion | flops 551682048 | bytes 1717761 | tf_op jit(solution)/shard_map/while/body/eval_jaxpr/dot_general | solution.py:72
  137.4 1.4 multiply_reduce_fusion.3
  138.8 5.1 %fusion.28 = f32[1024,64]{0,1:T(8,128)S(1)} fusion(bf16[1024,64]{1,0:T(8,128)(2,1)S(1)} %get-tuple-element.161, f32[2048]{0:T(1024)S(1)} %multiply_reduce_fusion.3, f32[1024]{0:T(1024)S(1)} %get-tuple-element.159, f32[]{:T(128)} %get-tuple-element.158, bf16[16,2048,64]{2,1,0:T(8,128)(2,1)} %get-tuple-element.162, s32[]{:T(128)} %get-tuple-element.147, ...), kind=kOutput, calls=%fused_computation.7.clone.1 | convolution fusion | flops 551682048 | bytes 1717761 | tf_op jit(solution)/shard_map/while/body/eval_jaxpr/dot_general | solution.py:72
  143.9 1.4 multiply_reduce_fusion.3
  145.3 5.1 %fusion.28 = f32[1024,64]{0,1:T(8,128)S(1)} fusion(bf16[1024,64]{1,0:T(8,128)(2,1)S(1)} %get-tuple-element.161, f32[2048]{0:T(1024)S(1)} %multiply_reduce_fusion.3, f32[1024]{0:T(1024)S(1)} %get-tuple-element.159, f32[]{:T(128)} %get-tuple-element.158, bf16[16,2048,64]{2,1,0:T(8,128)(2,1)} %get-tuple-element.162, s32[]{:T(128)} %get-tuple-element.147, ...), kind=kOutput, calls=%fused_computation.7.clone.1 | convolution fusion | flops 551682048 | bytes 1717761 | tf_op jit(solution)/shard_map/while/body/eval_jaxpr/dot_general | solution.py:72
  150.5 1.4 multiply_reduce_fusion.3
  151.9 5.1 %fusion.28 = f32[1024,64]{0,1:T(8,128)S(1)} fusion(bf16[1024,64]{1,0:T(8,128)(2,1)S(1)} %get-tuple-element.161, f32[2048]{0:T(1024)S(1)} %multiply_reduce_fusion.3, f32[1024]{0:T(1024)S(1)} %get-tuple-element.159, f32[]{:T(128)} %get-tuple-element.158, bf16[16,2048,64]{2,1,0:T(8,128)(2,1)} %get-tuple-element.162, s32[]{:T(128)} %get-tuple-element.147, ...), kind=kOutput, calls=%fused_computation.7.clone.1 | convolution fusion | flops 551682048 | bytes 1717761 | tf_op jit(solution)/shard_map/while/body/eval_jaxpr/dot_general | solution.py:72
  157.0 1.4 multiply_reduce_fusion.3
  158.4 5.1 %fusion.28 = f32[1024,64]{0,1:T(8,128)S(1)} fusion(bf16[1024,64]{1,0:T(8,128)(2,1)S(1)} %get-tuple-element.161, f32[2048]{0:T(1024)S(1)} %multiply_reduce_fusion.3, f32[1024]{0:T(1024)S(1)} %get-tuple-element.159, f32[]{:T(128)} %get-tuple-element.158, bf16[16,2048,64]{2,1,0:T(8,128)(2,1)} %get-tuple-element.162, s32[]{:T(128)} %get-tuple-element.147, ...), kind=kOutput, calls=%fused_computation.7.clone.1 | convolution fusion | flops 551682048 | bytes 1717761 | tf_op jit(solution)/shard_map/while/body/eval_jaxpr/dot_general | solution.py:72
  165.0 5.1 %fusion.28 = f32[1024,64]{0,1:T(8,128)S(1)} fusion(bf16[1024,64]{1,0:T(8,128)(2,1)S(1)} %get-tuple-element.161, f32[2048]{0:T(1024)S(1)} %multiply_reduce_fusion.3, f32[1024]{0:T(1024)S(1)} %get-tuple-element.159, f32[]{:T(128)} %get-tuple-element.158, bf16[16,2048,64]{2,1,0:T(8,128)(2,1)} %get-tuple-element.162, s32[]{:T(128)} %get-tuple-element.147, ...), kind=kOutput, calls=%fused_computation.7.clone.1 | convolution fusion | flops 551682048 | bytes 1717761 | tf_op jit(solution)/shard_map/while/body/eval_jaxpr/dot_general | solution.py:72
  170.1 1.4 multiply_reduce_fusion.3
  171.5 5.1 %fusion.28 = f32[1024,64]{0,1:T(8,128)S(1)} fusion(bf16[1024,64]{1,0:T(8,128)(2,1)S(1)} %get-tuple-element.161, f32[2048]{0:T(1024)S(1)} %multiply_reduce_fusion.3, f32[1024]{0:T(1024)S(1)} %get-tuple-element.159, f32[]{:T(128)} %get-tuple-element.158, bf16[16,2048,64]{2,1,0:T(8,128)(2,1)} %get-tuple-element.162, s32[]{:T(128)} %get-tuple-element.147, ...), kind=kOutput, calls=%fused_computation.7.clone.1 | convolution fusion | flops 551682048 | bytes 1717761 | tf_op jit(solution)/shard_map/while/body/eval_jaxpr/dot_general | solution.py:72
  176.6 1.4 multiply_reduce_fusion.3
  178.0 5.1 %fusion.28 = f32[1024,64]{0,1:T(8,128)S(1)} fusion(bf16[1024,64]{1,0:T(8,128)(2,1)S(1)} %get-tuple-element.161, f32[2048]{0:T(1024)S(1)} %multiply_reduce_fusion.3, f32[1024]{0:T(1024)S(1)} %get-tuple-element.159, f32[]{:T(128)} %get-tuple-element.158, bf16[16,2048,64]{2,1,0:T(8,128)(2,1)} %get-tuple-element.162, s32[]{:T(128)} %get-tuple-element.147, ...), kind=kOutput, calls=%fused_computation.7.clone.1 | convolution fusion | flops 551682048 | bytes 1717761 | tf_op jit(solution)/shard_map/while/body/eval_jaxpr/dot_general | solution.py:72
  184.6 5.1 %fusion.28 = f32[1024,64]{0,1:T(8,128)S(1)} fusion(bf16[1024,64]{1,0:T(8,128)(2,1)S(1)} %get-tuple-element.161, f32[2048]{0:T(1024)S(1)} %multiply_reduce_fusion.3, f32[1024]{0:T(1024)S(1)} %get-tuple-element.159, f32[]{:T(128)} %get-tuple-element.158, bf16[16,2048,64]{2,1,0:T(8,128)(2,1)} %get-tuple-element.162, s32[]{:T(128)} %get-tuple-element.147, ...), kind=kOutput, calls=%fused_computation.7.clone.1 | convolution fusion | flops 551682048 | bytes 1717761 | tf_op jit(solution)/shard_map/while/body/eval_jaxpr/dot_general | solution.py:72
  189.7 1.4 multiply_reduce_fusion.3
  191.1 5.1 %fusion.28 = f32[1024,64]{0,1:T(8,128)S(1)} fusion(bf16[1024,64]{1,0:T(8,128)(2,1)S(1)} %get-tuple-element.161, f32[2048]{0:T(1024)S(1)} %multiply_reduce_fusion.3, f32[1024]{0:T(1024)S(1)} %get-tuple-element.159, f32[]{:T(128)} %get-tuple-element.158, bf16[16,2048,64]{2,1,0:T(8,128)(2,1)} %get-tuple-element.162, s32[]{:T(128)} %get-tuple-element.147, ...), kind=kOutput, calls=%fused_computation.7.clone.1 | convolution fusion | flops 551682048 | bytes 1717761 | tf_op jit(solution)/shard_map/while/body/eval_jaxpr/dot_general | solution.py:72
  197.7 5.1 %fusion.28 = f32[1024,64]{0,1:T(8,128)S(1)} fusion(bf16[1024,64]{1,0:T(8,128)(2,1)S(1)} %get-tuple-element.161, f32[2048]{0:T(1024)S(1)} %multiply_reduce_fusion.3, f32[1024]{0:T(1024)S(1)} %get-tuple-element.159, f32[]{:T(128)} %get-tuple-element.158, bf16[16,2048,64]{2,1,0:T(8,128)(2,1)} %get-tuple-element.162, s32[]{:T(128)} %get-tuple-element.147, ...), kind=kOutput, calls=%fused_computation.7.clone.1 | convolution fusion | flops 551682048 | bytes 1717761 | tf_op jit(solution)/shard_map/while/body/eval_jaxpr/dot_general | solution.py:72
  204.2 5.1 %fusion.28 = f32[1024,64]{0,1:T(8,128)S(1)} fusion(bf16[1024,64]{1,0:T(8,128)(2,1)S(1)} %get-tuple-element.161, f32[2048]{0:T(1024)S(1)} %multiply_reduce_fusion.3, f32[1024]{0:T(1024)S(1)} %get-tuple-element.159, f32[]{:T(128)} %get-tuple-element.158, bf16[16,2048,64]{2,1,0:T(8,128)(2,1)} %get-tuple-element.162, s32[]{:T(128)} %get-tuple-element.147, ...), kind=kOutput, calls=%fused_computation.7.clone.1 | convolution fusion | flops 551682048 | bytes 1717761 | tf_op jit(solution)/shard_map/while/body/eval_jaxpr/dot_general | solution.py:72
  210.7 5.1 %fusion.28 = f32[1024,64]{0,1:T(8,128)S(1)} fusion(bf16[1024,64]{1,0:T(8,128)(2,1)S(1)} %get-tuple-element.161, f32[2048]{0:T(1024)S(1)} %multiply_reduce_fusion.3, f32[1024]{0:T(1024)S(1)} %get-tuple-element.159, f32[]{:T(128)} %get-tuple-element.158, bf16[16,2048,64]{2,1,0:T(8,128)(2,1)} %get-tuple-element.162, s32[]{:T(128)} %get-tuple-element.147, ...), kind=kOutput, calls=%fused_computation.7.clone.1 | convolution fusion | flops 551682048 | bytes 1717761 | tf_op jit(solution)/shard_map/while/body/eval_jaxpr/dot_general | solution.py:72
  217.3 5.1 %fusion.28 = f32[1024,64]{0,1:T(8,128)S(1)} fusion(bf16[1024,64]{1,0:T(8,128)(2,1)S(1)} %get-tuple-element.161, f32[2048]{0:T(1024)S(1)} %multiply_reduce_fusion.3, f32[1024]{0:T(1024)S(1)} %get-tuple-element.159, f32[]{:T(128)} %get-tuple-element.158, bf16[16,2048,64]{2,1,0:T(8,128)(2,1)} %get-tuple-element.162, s32[]{:T(128)} %get-tuple-element.147, ...), kind=kOutput, calls=%fused_computation.7.clone.1 | convolution fusion | flops 551682048 | bytes 1717761 | tf_op jit(solution)/shard_map/while/body/eval_jaxpr/dot_general | solution.py:72
  223.8 5.1 %fusion.28 = f32[1024,64]{0,1:T(8,128)S(1)} fusion(bf16[1024,64]{1,0:T(8,128)(2,1)S(1)} %get-tuple-element.161, f32[2048]{0:T(1024)S(1)} %multiply_reduce_fusion.3, f32[1024]{0:T(1024)S(1)} %get-tuple-element.159, f32[]{:T(128)} %get-tuple-element.158, bf16[16,2048,64]{2,1,0:T(8,128)(2,1)} %get-tuple-element.162, s32[]{:T(128)} %get-tuple-element.147, ...), kind=kOutput, calls=%fused_computation.7.clone.1 | convolution fusion | flops 551682048 | bytes 1717761 | tf_op jit(solution)/shard_map/while/body/eval_jaxpr/dot_general | solution.py:72
  230.4 5.1 %fusion.28 = f32[1024,64]{0,1:T(8,128)S(1)} fusion(bf16[1024,64]{1,0:T(8,128)(2,1)S(1)} %get-tuple-element.161, f32[2048]{0:T(1024)S(1)} %multiply_reduce_fusion.3, f32[1024]{0:T(1024)S(1)} %get-tuple-element.159, f32[]{:T(128)} %get-tuple-element.158, bf16[16,2048,64]{2,1,0:T(8,128)(2,1)} %get-tuple-element.162, s32[]{:T(128)} %get-tuple-element.147, ...), kind=kOutput, calls=%fused_computation.7.clone.1 | convolution fusion | flops 551682048 | bytes 1717761 | tf_op jit(solution)/shard_map/while/body/eval_jaxpr/dot_general | solution.py:72
  236.8 12.1 %reduce-scatter.2.cloned.1.call-done = f32[1024,32]{0,1:T(8,128)} async-done(((f32[1024,64]{0,1:T(8,128)}), f32[1024,32]{0,1:T(8,128)}) %reduce-scatter.2.cloned.1.call-update) | async-done | bytes 131088 | tf_op jit(solution)/shard_map/reduce_scatter | solution.py:78
  249.0 1.6 multiply_add_fusion
  (25 shorter events, 15.3 us)
Async XLA Ops:
  6.5 101.8 %all-gather.2.cloned.1.call-start = ((), (), s32[]{:S(2)}) async-start(), calls=%async_computation.1 | async-start | bytes 8519680 | tf_op jit(solution)/shard_map/all_gather | solution.py:25
  16.0 233.0 %reduce-scatter.2.cloned.1.call-start = ((), (), s32[]{:S(2)}) async-start(), calls=%async_computation.2 | async-start | bytes 393216 | tf_op jit(solution)/shard_map/reduce_scatter | solution.py:78
  130.8 118.2 %copy-start.1 = (bf16[1024,32]{0,1:T(8,128)(2,1)S(1)}, bf16[1024,32]{0,1:T(8,128)(2,1)}, u32[]{:S(2)}) copy-start(bf16[1024,32]{0,1:T(8,128)(2,1)} %param.8) | copy-start | bytes 196612
  235.5 0.7 copy-start
Sparse Core Ops, SparseCore 0:
  16.1 92.1 all-gather.1
  236.3 12.6 reduce-scatter.1
where the time goes:
time: 260 us; the launch traced here: 257 us
  waiting for transfers between devices  104 us (40%)
  matrix products  81.9 us (32%)
  other arithmetic  26.3 us (10%)
  local copies, waits for them, and re-layouts  24.2 us (9%)
  between operations  14.1 us (5%)
  blocking collectives  6.15 us (2%)
    all_gather x1, waiting for transfers between devices, sent_together(): out, at, done = (lax.all_gather(both, axis, axis=dim, tiled=True), 0, [])  92 us
    dot_general x16, matrix products, advance(): jnp.dot(kernel_block, group_vectors, preferred_element_type=jnp.float32)  81.9 us
    reduce_sum x17, other arithmetic, squares(): return jnp.sum(wide * wide, axis=1)  22.3 us
    unnamed x7, local copies, waits for them, and re-layouts  17.7 us
    reduce_scatter x1, waiting for transfers between devices, per_device(): result = lax.psum_scatter(direct, 'feat', scatter_dimension=1, tiled=True)  12.1 us
    all_gather x1, blocking collectives, rows_first(): out = lax.all_gather(both, axis, axis=0, tiled=True)  6.15 us
    slice x1, local copies, waits for them, and re-layouts, sent_together(): done.append(lax.slice_in_dim(out, at, at + a.shape[along], axis=along))  5.75 us
  transfers between devices with their start and end apart: 2, of which 2 were waited for; matrix products, arithmetic and copies ran while one was open for 0% of the time, Pallas kernels for 0%

commit v1 on v0

v1 whole, which is shorter than its diff:
```python
import jax
import jax.numpy as jnp
from jax import lax
from jax.experimental import pallas as pl
from jax.experimental.pallas import tpu as pltpu
from jax.sharding import Mesh, PartitionSpec as P

SIZES = (2, 4, 4, 2, 2)
NAMES = ("zh", "x", "y", "c", "zl")
BLK = ("zh", "x", "y", "c")
COLS = ("zh", "y", "c")
TM = 256
TN = 1024
F32 = jnp.float32
BF16 = jnp.bfloat16


def three_parts(wide):
    hi = wide.astype(BF16).astype(F32)
    mid = (wide - hi).astype(BF16).astype(F32)
    return hi, mid, wide - hi - mid


def with_norms(packed, offset, first, other):
    lane = lax.broadcasted_iota(jnp.int32, packed.shape, 1)
    wide = jnp.where(lane < 64, packed.astype(F32), 0.0)
    half = offset - 0.5 * jnp.sum(wide * wide, axis=1, keepdims=True)
    hi, mid, low = three_parts(half)
    ones = (lane >= other) & (lane < other + 3)
    wide = jnp.where(ones, 1.0, wide)
    wide = jnp.where(lane == first, hi, wide)
    wide = jnp.where(lane == first + 1, mid, wide)
    wide = jnp.where(lane == first + 2, low, wide)
    return wide.astype(BF16)


def kernel_body(amp_ref, rows_ref, cols_ref, out_ref, right_ref, vectors_ref):
    step = pl.program_id(0)
    total = cols_ref.shape[0]

    @pl.when(step == 0)
    def _():
        for at in range(0, total, TN):
            chunk = cols_ref[at : at + TN, :]
            right_ref[at : at + TN, :] = with_norms(chunk, 0.0, 64, 67)
            vectors_ref[:, at : at + TN] = chunk.astype(F32).T[64:, :].astype(BF16)

    rows = rows_ref[0].astype(F32)
    rows = jnp.where((step // 2) % 2 == 1, pltpu.roll(rows, 64, 1), rows)
    left = with_norms(rows, amp_ref[1], 67, 64)
    top = jnp.full((1, 1), amp_ref[0], F32).astype(BF16)
    total_sum = jnp.zeros((64, TM), F32)
    for at in range(0, total, TN):
        exponent = lax.dot_general(
            right_ref[at : at + TN, :], left, (((1,), (1,)), ((), ())), preferred_element_type=F32
        )
        block = jnp.minimum(jnp.exp(exponent).astype(BF16), top)
        total_sum += jnp.dot(vectors_ref[:, at : at + TN], block, preferred_element_type=F32)
    out_ref[0, 0] = total_sum[:32]
    out_ref[0, 1] = total_sum[32:]


def kernel_product(amp, rows, cols):
    groups, half, _ = rows.shape
    per = half // TM
    total = cols.shape[0]
    return pl.pallas_call(
        kernel_body,
        grid=(groups * 2 * per,),
        out_shape=jax.ShapeDtypeStruct((groups, 2, 32, 2 * half), F32),
        in_specs=[
            pl.BlockSpec(memory_space=pltpu.SMEM),
            pl.BlockSpec((1, TM, 128), lambda i: (i // (2 * per), i % per, 0)),
            pl.BlockSpec((total, 128), lambda i: (0, 0)),
        ],
        out_specs=pl.BlockSpec((1, 2, 32, TM), lambda i: (i // (2 * per), 0, 0, i % (2 * per))),
        scratch_shapes=[pltpu.VMEM((total, 128), BF16), pltpu.VMEM((64, total), BF16)],
        compiler_params=pltpu.CompilerParams(vmem_limit_bytes=48 << 20),
        name="rbf_product",
    )(amp, rows, cols)


def per_device(points, vectors, lengthscale, outscale, noise):
    zl = lax.axis_index("zl")
    length_slice = lax.dynamic_slice_in_dim(lengthscale, zl * 32, 32)
    scaled = (points.astype(F32) / length_slice).astype(BF16)
    mine = jnp.concatenate([scaled.T, vectors.T], axis=0)
    both = lax.all_gather(mine, "zl", axis=0, tiled=False)
    whole_points = both[:, :32].reshape(64, 1024)
    whole_vectors = both[:, 32:].reshape(64, 1024)
    rows = jnp.concatenate([whole_points[:, :512].T, whole_points[:, 512:].T], axis=1)
    share = jnp.concatenate([whole_points, whole_vectors], axis=0)
    share = lax.dynamic_slice_in_dim(share, zl * 512, 512, 1).T
    all_rows = lax.all_gather(rows, "x", axis=0, tiled=False)
    all_cols = lax.all_gather(share, COLS, axis=0, tiled=True)
    amp = jnp.concatenate([outscale, jnp.log(outscale)])
    partial = kernel_product(amp, all_rows, all_cols)
    result = lax.psum_scatter(partial.reshape(8, 32, 1024), ("x", "zl"), scatter_dimension=0, tiled=False)
    return result.T + noise[0] * vectors.astype(F32)


def solution(mesh):
    fine = Mesh(mesh.devices.reshape(SIZES), NAMES)
    placed = (P(BLK, "zl"), P(BLK, "zl"), P(), P(), P())
    return jax.shard_map(
        per_device, mesh=fine, in_specs=placed, out_specs=P(BLK, "zl"), check_vma=False
    )
```

time: 260 us -> 157 us (0.60)
  matrix products: 81.9 us -> 0 us
  Pallas kernels: 0 us -> 40.8 us
  waiting for transfers between devices: 104 us -> 74 us
  other arithmetic: 26.3 us -> 4.22 us
  local copies, waits for them, and re-layouts: 24.2 us -> 2.96 us
  blocking collectives: 6.15 us -> 19.5 us
    dot_general x16 -> x0, matrix products: 81.9 us -> none  [advance(): jnp.dot(kernel_block, group_vectors, preferred_element_type=jnp.float32)]
    all_gather x1, waiting for transfers between devices: 92 us -> 36.3 us  [per_device(): all_cols = lax.all_gather(share, COLS, axis=0, tiled=True)]
    pallas_call x0 -> x1, Pallas kernels: none -> 40.8 us  [kernel_product(): pl.pallas_call(kernel_body, grid=(groups * 2 * per,), out_shape=jax.Shape...]
    reduce_scatter x1, waiting for transfers between devices: 12.1 us -> 37.6 us  [per_device(): lax.psum_scatter(partial.reshape(8, 32, 1024), ('x', 'zl'), scatter_dimen...]
    reduce_sum x17 -> x0, other arithmetic: 22.3 us -> none  [squares(): return jnp.sum(wide * wide, axis=1)]
    unnamed x7 -> x4, local copies, waits for them, and re-layouts: 17.7 us -> 1.59 us
    all_gather x1 -> x2, blocking collectives: 6.15 us -> 19.5 us  [the longest x1 13.4 us: per_device(): all_rows = lax.all_gather(rows, 'x', axis=0, tiled=False)]
    slice x1, local copies, waits for them, and re-layouts: 5.75 us -> 0.02 us  [per_device(): whole_vectors = both[:, 32:].reshape(64, 1024)]
where the time goes in v1:
time: 157 us; the launch traced here: 156 us
  waiting for transfers between devices  74 us (47%)
  Pallas kernels  40.8 us (26%)
  blocking collectives  19.5 us (12%)
  between operations  14.8 us (9%)
  other arithmetic  4.22 us (3%)
  local copies, waits for them, and re-layouts  2.96 us (2%)
    pallas_call x1, Pallas kernels, kernel_product(): pl.pallas_call(kernel_body, grid=(groups * 2 * per,), out_shape=jax.Shape...  40.8 us
    reduce_scatter x1, waiting for transfers between devices, per_device(): lax.psum_scatter(partial.reshape(8, 32, 1024), ('x', 'zl'), scatter_dimen...  37.6 us
    all_gather x1, waiting for transfers between devices, per_device(): all_cols = lax.all_gather(share, COLS, axis=0, tiled=True)  36.3 us
    all_gather x1, blocking collectives, per_device(): all_rows = lax.all_gather(rows, 'x', axis=0, tiled=False)  13.4 us
    all_gather x1, blocking collectives, per_device(): both = lax.all_gather(mine, 'zl', axis=0, tiled=False)  6.15 us
  transfers between devices with their start and end apart: 2, of which 2 were waited for; matrix products, arithmetic and copies ran while one was open for 0% of the time, Pallas kernels for 0%

profile of v1, /device:TPU:0, one launch (start us, length us, event | category | flops | bytes accessed | tf_op | source)
XLA Modules:
  0.0 156.4 jit_solution(14363111571890722303)
XLA Ops:
  6.5 0.0 all-gather.4.cloned.1.call-start
  6.5 0.7 dynamic_slice.6
  7.3 0.9 fusion.2
  8.2 0.9 pad_maximum_fusion
  9.0 6.2 %all-gather = bf16[128,1024]{1,0:T(8,128)(2,1)S(1)} all-gather(bf16[64,1024]{1,0:T(8,128)(2,1)S(1)} %pad_maximum_fusion), channel_id=2, replica_groups=mesh['zh'=2,'x'=4,'y'=4,'c'=2,'zl'=2] {'zl'}, dimensions={0}, use_global_device_ids=true | all-gather | bytes 393216 | tf_op jit(solution)/shard_map/all_gather | solution.py:88
  15.2 0.2 copy.9
  15.4 0.2 copy.10
  15.6 0.8 fusion.1
  16.4 0.0 all-gather.4.cloned.1.call-update
  16.4 0.0 reduce-scatter.2.cloned.1.call-start
  16.5 13.4 %all-gather.1 = bf16[2048,128]{0,1:T(8,128)(2,1)S(1)} all-gather(bf16[512,128]{0,1:T(8,128)(2,1)S(1)} %pad_maximum_fusion.1), channel_id=3, replica_groups=mesh['zh'=2,'x'=4,'y'=4,'c'=2,'zl'=2] {'x'}, dimensions={0}, use_global_device_ids=true | all-gather | bytes 655360 | tf_op jit(solution)/shard_map/all_gather | solution.py:94
  29.8 0.3 copy.8
  30.8 0.1 pad_maximum_fusion.2.amp_ref
  30.9 36.3 %all-gather.4.cloned.1.call-done.cols_ref = bf16[8192,128]{1,0:T(8,128)(2,1)} async-done(((bf16[512,128]{1,0:T(8,128)(2,1)}), bf16[8192,128]{1,0:T(8,128)(2,1)}) %all-gather.4.cloned.1.call-update) | async-done | bytes 2097168 | tf_op jit(solution)/shard_map/all_gather | solution.py:95
  67.2 0.0 copy-start
  67.2 1.6 %copy-done = bf16[8192,128]{1,0:T(8,128)(2,1)S(1)} copy-done((bf16[8192,128]{1,0:T(8,128)(2,1)S(1)}, bf16[8192,128]{1,0:T(8,128)(2,1)}, u32[]{:S(2)}) %copy-start) | copy-done | bytes 2097176
  68.8 0.0 copy-start.1
  68.8 40.8 %rbf_product.1 = f32[4,2,32,1024]{3,2,1,0:T(8,128)} custom-call(f32[2]{0:T(128)S(1)} %pad_maximum_fusion.2.amp_ref, bf16[4,512,128]{2,1,0:T(8,128)(2,1)S(1)} %bitcast.20, bf16[8192,128]{1,0:T(8,128)(2,1)S(1)} %copy-done), custom_call_target="tpu_custom_call" | custom-call | tf_op jit(solution)/shard_map/rbf_product/pallas_call | solution.py:67
  109.6 0.0 reduce-scatter.2.cloned.1.call-update
  110.3 37.6 %reduce-scatter.2.cloned.1.call-done = f32[1,32,1024]{2,1,0:T(8,128)} async-done(((f32[8,32,1024]{2,1,0:T(8,128)}), f32[1,32,1024]{2,1,0:T(8,128)}) %reduce-scatter.2.cloned.1.call-update) | async-done | bytes 131088 | tf_op jit(solution)/shard_map/reduce_scatter | solution.py:98
  147.9 0.0 copy-done.1
  147.9 1.6 %bitcast_add_fusion = f32[1024,32]{0,1:T(8,128)} fusion(f32[1,32,1024]{2,1,0:T(8,128)} %reduce-scatter.2.cloned.1.call-done, bf16[1024,32]{0,1:T(8,128)(2,1)S(1)} %copy-done.1, f32[]{:T(128)} %bitcast.19), kind=kLoop, calls=%fused_computation.6 | loop fusion | flops 98304 | bytes 327684 | tf_op jit(solution)/shard_map/add | solution.py:99
  (3 shorter events, 0.0 us)
Async XLA Ops:
  6.5 60.7 %all-gather.4.cloned.1.call-start = ((), (), s32[]{:S(2)}) async-start(), calls=%async_computation.1 | async-start | bytes 2228224 | tf_op jit(solution)/shard_map/all_gather | solution.py:95
  16.4 131.6 %reduce-scatter.2.cloned.1.call-start = ((), (), s32[]{:S(2)}) async-start(), calls=%async_computation.2 | async-start | bytes 1179648 | tf_op jit(solution)/shard_map/reduce_scatter | solution.py:98
  67.2 1.6 %copy-start = (bf16[8192,128]{1,0:T(8,128)(2,1)S(1)}, bf16[8192,128]{1,0:T(8,128)(2,1)}, u32[]{:S(2)}) copy-start(bf16[8192,128]{1,0:T(8,128)(2,1)} %all-gather.4.cloned.1.call-done.cols_ref) | copy-start | bytes 6291460
  68.8 79.1 %copy-start.1 = (bf16[1024,32]{0,1:T(8,128)(2,1)S(1)}, bf16[1024,32]{0,1:T(8,128)(2,1)}, u32[]{:S(2)}) copy-start(bf16[1024,32]{0,1:T(8,128)(2,1)} %param.6) | copy-start | bytes 196612
Sparse Core Ops, SparseCore 0:
  16.5 50.6 all-gather.3
  109.8 38.1 reduce-scatter.1

commit v2 on v1

v2 whole, which is shorter than its diff:
```python
import jax
import jax.numpy as jnp
from jax import lax
from jax.experimental import pallas as pl
from jax.experimental.pallas import tpu as pltpu
from jax.sharding import Mesh, PartitionSpec as P

SIZES = (2, 4, 4, 2, 2)
NAMES = ("zh", "x", "y", "c", "zl")
BLK = ("zh", "x", "y", "c")
TM = 512
TN = 1024
F32 = jnp.float32
BF16 = jnp.bfloat16
PARAMS = pltpu.CompilerParams(vmem_limit_bytes=48 << 20)


def three_parts(wide):
    hi = wide.astype(BF16).astype(F32)
    mid = (wide - hi).astype(BF16).astype(F32)
    return hi, mid, wide - hi - mid


def with_norms(wide, offset, first, other):
    lane = lax.broadcasted_iota(jnp.int32, wide.shape, 1)
    wide = jnp.where(lane < 64, wide, 0.0)
    half = offset - 0.5 * jnp.sum(wide * wide, axis=1, keepdims=True)
    hi, mid, low = three_parts(half)
    ones = (lane >= other) & (lane < other + 3)
    wide = jnp.where(ones, 1.0, wide)
    wide = jnp.where(lane == first, hi, wide)
    wide = jnp.where(lane == first + 1, mid, wide)
    wide = jnp.where(lane == first + 2, low, wide)
    return wide.astype(BF16)


def ready_rows(amp, blocks):
    count = len(blocks)

    def body(amp_ref, *refs):
        out_ref = refs[count]
        for k in range(count):
            wide = refs[k][...].astype(F32)
            out_ref[k, :512] = with_norms(wide, amp_ref[1], 67, 64)
            out_ref[k, 512:] = with_norms(pltpu.roll(wide, 64, 1), amp_ref[1], 67, 64)

    return pl.pallas_call(
        body,
        out_shape=jax.ShapeDtypeStruct((count, 1024, 128), BF16),
        in_specs=[pl.BlockSpec(memory_space=pltpu.SMEM)]
        + [pl.BlockSpec(memory_space=pltpu.VMEM)] * count,
        out_specs=pl.BlockSpec(memory_space=pltpu.VMEM),
        compiler_params=PARAMS,
        name="ready_rows",
    )(amp, *blocks)


def ready_cols(blocks):
    count = len(blocks)
    total = sum(b.shape[0] for b in blocks)

    def body(*refs):
        right_ref, vectors_ref = refs[count:]
        at = 0
        for ref in refs[:count]:
            for sub in range(0, ref.shape[0], 512):
                wide = ref[sub : sub + 512, :].astype(F32)
                right_ref[at : at + 512, :] = with_norms(wide, 0.0, 64, 67)
                vectors_ref[:, at : at + 512] = wide.T[64:, :].astype(BF16)
                at += 512

    return pl.pallas_call(
        body,
        out_shape=(
            jax.ShapeDtypeStruct((total, 128), BF16),
            jax.ShapeDtypeStruct((64, total), BF16),
        ),
        in_specs=[pl.BlockSpec(memory_space=pltpu.VMEM)] * count,
        out_specs=(pl.BlockSpec(memory_space=pltpu.VMEM),) * 2,
        compiler_params=PARAMS,
        name="ready_cols",
    )(*blocks)


def tile_sum(amp_ref, left, right_ref, vectors_ref):
    top = jnp.full((1, 1), amp_ref[0], F32).astype(BF16)
    total = right_ref.shape[0]
    result = jnp.zeros((64, left.shape[0]), F32)
    for at in range(0, total, TN):
        exponent = lax.dot_general(
            right_ref[at : at + TN, :], left, (((1,), (1,)), ((), ())), preferred_element_type=F32
        )
        block = jnp.minimum(jnp.exp(exponent).astype(BF16), top)
        result += jnp.dot(vectors_ref[:, at : at + TN], block, preferred_element_type=F32)
    return result


def cost(rows, cols):
    return pl.CostEstimate(flops=rows * cols * 512, transcendentals=rows * cols, bytes_accessed=cols * 384)


def add_tiles(amp, left, right, vectors, before):
    total = right.shape[0]
    per = 1024 // TM
    old = [] if before is None else [before]

    def body(amp_ref, left_ref, right_ref, vectors_ref, *refs):
        value = tile_sum(amp_ref, left_ref[0], right_ref, vectors_ref)
        if old:
            value += refs[0][0]
        refs[-1][0] = value

    acc_spec = pl.BlockSpec((1, 64, TM), lambda i: (i // per, 0, i % per))
    return pl.pallas_call(
        body,
        grid=(4 * per,),
        out_shape=jax.ShapeDtypeStruct((4, 64, 1024), F32),
        in_specs=[
            pl.BlockSpec(memory_space=pltpu.SMEM),
            pl.BlockSpec((1, TM, 128), lambda i: (i // per, i % per, 0)),
            pl.BlockSpec((total, 128), lambda i: (0, 0)),
            pl.BlockSpec((64, total), lambda i: (0, 0)),
        ]
        + [acc_spec] * len(old),
        out_specs=acc_spec,
        compiler_params=PARAMS,
        cost_estimate=cost(4096, total),
        name="add_tiles",
    )(amp, left, right, vectors, *old)


def last_tiles(amp, left, right, vectors, before, group, kept):
    total = right.shape[0]

    def body(amp_ref, left_ref, right_ref, vectors_ref, before_ref, mine_ref, theirs_ref):
        value = tile_sum(amp_ref, left_ref[0], right_ref, vectors_ref) + before_ref[0]
        mine_ref[...] = value[:32].astype(kept)
        theirs_ref[...] = value[32:].astype(BF16)

    out_spec = pl.BlockSpec((32, TM), lambda i: (0, i))
    return pl.pallas_call(
        body,
        grid=(1024 // TM,),
        out_shape=(jax.ShapeDtypeStruct((32, 1024), kept), jax.ShapeDtypeStruct((32, 1024), BF16)),
        in_specs=[
            pl.BlockSpec(memory_space=pltpu.SMEM),
            pl.BlockSpec((1, TM, 128), lambda i: (group, i, 0)),
            pl.BlockSpec((total, 128), lambda i: (0, 0)),
            pl.BlockSpec((64, total), lambda i: (0, 0)),
            pl.BlockSpec((1, 64, TM), lambda i: (group, 0, i)),
        ],
        out_specs=(out_spec, out_spec),
        compiler_params=PARAMS,
        cost_estimate=cost(1024, total),
        name="last_tiles",
    )(amp, left, right, vectors, before)


def shift(value, axis, by):
    size = SIZES[NAMES.index(axis)]
    return lax.ppermute(value, axis, [(i, (i + by) % size) for i in range(size)])


def shift_swap(value, by):
    pairs = [(2 * i + j, 2 * ((i + by) % 4) + 1 - j) for i in range(4) for j in range(2)]
    return lax.ppermute(value, ("x", "zl"), pairs)


def per_device(points, vectors, lengthscale, outscale, noise):
    zl = lax.axis_index("zl")
    length_slice = lax.dynamic_slice_in_dim(lengthscale, zl * 32, 32)
    scaled = (points.astype(F32) / length_slice).astype(BF16).T
    flipped = vectors.T
    amp = jnp.concatenate([outscale, jnp.log(outscale)])

    given = jnp.concatenate(
        [scaled[:, :512], scaled[:, 512:], lax.dynamic_slice_in_dim(flipped, (1 - zl) * 512, 512, 1)], axis=0
    )
    got = shift(given, "zl", 1)
    low = jnp.concatenate([scaled[:, :512], got[:32]], axis=0)
    high = jnp.concatenate([scaled[:, 512:], got[32:64]], axis=0)
    rows = jnp.concatenate([low, high], axis=0).T
    share = jnp.concatenate(
        [
            jnp.where(zl == 0, low, high),
            lax.dynamic_slice_in_dim(flipped, zl * 512, 512, 1),
            got[64:],
        ],
        axis=0,
    ).T

    across = shift(share, "zh", 1)
    beside = shift(share, "c", 1)
    rows_in = [shift(rows, "x", by) for by in (1, -1, 2)]
    near = [shift(share, "y", by) for by in (1, -1, 2)]
    far = [across] + [shift(across, "y", by) for by in (1, -1, 2)]
    near = jnp.concatenate(near, axis=0)
    near_beside = shift(near, "c", 1)
    far = jnp.concatenate(far, axis=0)
    far_beside = shift(far, "c", 1)

    left = ready_rows(amp, [rows] + rows_in)
    acc = add_tiles(amp, left, *ready_cols([share, beside]), None)
    acc = add_tiles(amp, left, *ready_cols([near, near_beside]), acc)
    last = ready_cols([far, far_beside])

    arrived = []
    for group, by in ((3, 2), (1, -1), (2, 1)):
        mine, theirs = last_tiles(amp, left, *last, acc, group, BF16)
        arrived.append(shift(mine, "x", by))
        arrived.append(shift_swap(theirs, by))
    mine, theirs = last_tiles(amp, left, *last, acc, 0, F32)
    arrived.append(shift(theirs, "zl", 1))
    for part in arrived:
        mine = mine + part.astype(F32)
    return mine.T + noise[0] * vectors.astype(F32)


def solution(mesh):
    fine = Mesh(mesh.devices.reshape(SIZES), NAMES)
    placed = (P(BLK, "zl"), P(BLK, "zl"), P(), P(), P())
    return jax.shard_map(
        per_device, mesh=fine, in_specs=placed, out_specs=P(BLK, "zl"), check_vma=False
    )
```

time: 157 us -> 96.5 us (0.61)
  waiting for transfers between devices: 74 us -> 13.9 us
  starting transfers between devices: 0.04 us -> 33.9 us
  blocking collectives: 19.5 us -> 0 us
  between operations: 14.8 us -> 1.6 us
  other arithmetic: 4.22 us -> 1.5 us
  Pallas kernels: 40.8 us -> 42.5 us
    reduce_scatter x1 -> x0, waiting for transfers between devices: 37.6 us -> none  [per_device(): lax.psum_scatter(partial.reshape(8, 32, 1024), ('x', 'zl'), scatter_dimen...]
    all_gather x1 -> x0, waiting for transfers between devices: 36.3 us -> none  [per_device(): all_cols = lax.all_gather(share, COLS, axis=0, tiled=True)]
    ppermute x0 -> x21, starting transfers between devices: none -> 33.9 us  [the longest x18 28 us: shift(): lax.ppermute(value, axis, [(i, (i + by) % size) for i in range(size)])]
    all_gather x2 -> x0, blocking collectives: 19.5 us -> none  [the longest x1 13.4 us: per_device(): all_rows = lax.all_gather(rows, 'x', axis=0, tiled=False)]
    ppermute x0 -> x21, waiting for transfers between devices: none -> 13.9 us  [the longest x18 10.8 us: shift(): lax.ppermute(value, axis, [(i, (i + by) % size) for i in range(size)])]
    pallas_call x1 -> x10, Pallas kernels: 40.8 us -> 42.5 us  [the longest x2 19.2 us: add_tiles(): pl.pallas_call(body, grid=(4 * per,), out_shape=jax.ShapeDtypeStruct((4,...]
  transfers between devices with their start and end apart: 2 -> 21, of which waited for: 2 -> 8; matrix products, arithmetic and copies ran while one was open for 0% -> 1% of each run, Pallas kernels for 0% -> 28%
where the time goes in v2:
time: 96.5 us; the launch traced here: 96.3 us
  Pallas kernels  42.5 us (44%)
  starting transfers between devices  33.9 us (35%)
  waiting for transfers between devices  13.9 us (14%)
  local copies, waits for them, and re-layouts  2.86 us (3%)
  between operations  1.6 us (2%)
  other arithmetic  1.5 us (2%)
    ppermute x18, starting transfers between devices, shift(): lax.ppermute(value, axis, [(i, (i + by) % size) for i in range(size)])  28 us
    pallas_call x2, Pallas kernels, add_tiles(): pl.pallas_call(body, grid=(4 * per,), out_shape=jax.ShapeDtypeStruct((4,...  19.2 us
    pallas_call x4, Pallas kernels, last_tiles(): pl.pallas_call(body, grid=(1024 // TM,), out_shape=(jax.ShapeDtypeStruct(...  18.8 us
    ppermute x18, waiting for transfers between devices, shift(): lax.ppermute(value, axis, [(i, (i + by) % size) for i in range(size)])  10.8 us
    ppermute x3, starting transfers between devices, shift_swap(): return lax.ppermute(value, ('x', 'zl'), pairs)  5.92 us
    ppermute x3, waiting for transfers between devices, shift_swap(): return lax.ppermute(value, ('x', 'zl'), pairs)  3.16 us
    pallas_call x3, Pallas kernels, ready_cols(): pl.pallas_call(body, out_shape=(jax.ShapeDtypeStruct((total, 128), BF16),...  2.71 us
  transfers between devices with their start and end apart: 21, of which 8 were waited for; matrix products, arithmetic and copies ran while one was open for 1% of the time, Pallas kernels for 28%

profile of v2, /device:TPU:0, one launch (start us, length us, event | category | flops | bytes accessed | tf_op | source)
XLA Modules:
  0.0 96.3 jit_solution(2116162259584755508)
XLA Ops:
  0.0 0.8 constant_dynamic-slice_fusion
  0.9 0.7 copy-done.1
  2.7 2.1 %collective-permute-start = (bf16[96,512]{0,1:T(8,128)(2,1)S(1)}, bf16[96,512]{0,1:T(8,128)(2,1)S(1)}, u32[]{:S(2)}, u32[]{:S(2)}) collective-permute-start(bf16[96,512]{0,1:T(8,128)(2,1)S(1)} %pad_maximum_fusion), channel_id=1, source_target_pairs={{0,1},{1,0},{2,3},{3,2},{4,5},{5,4},{6,7},{7,6},{8,9},{9,8},{10,11... | collective-permute-start | bytes 294920 | tf_op jit(solution)/shard_map/ppermute | solution.py:161
  5.6 2.7 %collective-permute-done = bf16[96,512]{0,1:T(8,128)(2,1)S(1)} collective-permute-done((bf16[96,512]{0,1:T(8,128)(2,1)S(1)}, bf16[96,512]{0,1:T(8,128)(2,1)S(1)}, u32[]{:S(2)}, u32[]{:S(2)}) %collective-permute-start) | collective-permute-done | bytes 98336 | tf_op jit(solution)/shard_map/ppermute | solution.py:161
  8.8 1.6 %collective-permute-start.9 = (bf16[512,128]{1,0:T(8,128)(2,1)S(1)}, bf16[512,128]{1,0:T(8,128)(2,1)S(1)}, u32[]{:S(2)}, u32[]{:S(2)}) collective-permute-start(bf16[512,128]{1,0:T(8,128)(2,1)S(1)} %maximum_bitcast_fusion.1.refs_0_), channel_id=1, source_target_pairs={{0,4},{4,8},{8,12},{12,0},{1,5},{5,9},{9,13},{13,1},{2,6},{6,10},{... | collective-permute-start | bytes 393224 | tf_op jit(solution)/shard_map/ppermute | solution.py:161
  10.5 1.7 %collective-permute-start.10 = (bf16[512,128]{1,0:T(8,128)(2,1)S(1)}, bf16[512,128]{1,0:T(8,128)(2,1)S(1)}, u32[]{:S(2)}, u32[]{:S(2)}) collective-permute-start(bf16[512,128]{1,0:T(8,128)(2,1)S(1)} %maximum_bitcast_fusion.1.refs_0_), channel_id=1, source_target_pairs={{0,12},{4,0},{8,4},{12,8},{1,13},{5,1},{9,5},{13,9},{2,14},{6,2},{... | collective-permute-start | bytes 393224 | tf_op jit(solution)/shard_map/ppermute | solution.py:161
  12.2 2.0 %collective-permute-start.11 = (bf16[512,128]{1,0:T(8,128)(2,1)S(1)}, bf16[512,128]{1,0:T(8,128)(2,1)S(1)}, u32[]{:S(2)}, u32[]{:S(2)}) collective-permute-start(bf16[512,128]{1,0:T(8,128)(2,1)S(1)} %maximum_bitcast_fusion.1.refs_0_), channel_id=1, source_target_pairs={{0,8},{4,12},{8,0},{12,4},{1,9},{5,13},{9,1},{13,5},{2,10},{6,14},... | collective-permute-start | bytes 393224 | tf_op jit(solution)/shard_map/ppermute | solution.py:161
  14.4 1.6 %collective-permute-start.1 = (bf16[512,128]{1,0:T(8,128)(2,1)S(1)}, bf16[512,128]{1,0:T(8,128)(2,1)S(1)}, u32[]{:S(2)}, u32[]{:S(2)}) collective-permute-start(bf16[512,128]{1,0:T(8,128)(2,1)S(1)} %maximum_bitcast_fusion.refs_0_), channel_id=1, source_target_pairs={{0,16},{16,32},{32,48},{48,0},{1,17},{17,33},{33,49},{49,1},{2,18}... | collective-permute-start | bytes 393224 | tf_op jit(solution)/shard_map/ppermute | solution.py:161
  16.0 1.8 %collective-permute-start.2 = (bf16[512,128]{1,0:T(8,128)(2,1)S(1)}, bf16[512,128]{1,0:T(8,128)(2,1)S(1)}, u32[]{:S(2)}, u32[]{:S(2)}) collective-permute-start(bf16[512,128]{1,0:T(8,128)(2,1)S(1)} %maximum_bitcast_fusion.refs_0_), channel_id=1, source_target_pairs={{0,48},{16,0},{32,16},{48,32},{1,49},{17,1},{33,17},{49,33},{2,50}... | collective-permute-start | bytes 393224 | tf_op jit(solution)/shard_map/ppermute | solution.py:161
  17.8 2.1 %collective-permute-start.3 = (bf16[512,128]{1,0:T(8,128)(2,1)S(1)}, bf16[512,128]{1,0:T(8,128)(2,1)S(1)}, u32[]{:S(2)}, u32[]{:S(2)}) collective-permute-start(bf16[512,128]{1,0:T(8,128)(2,1)S(1)} %maximum_bitcast_fusion.refs_0_), channel_id=1, source_target_pairs={{0,32},{16,48},{32,0},{48,16},{1,33},{17,49},{33,1},{49,17},{2,34}... | collective-permute-start | bytes 393224 | tf_op jit(solution)/shard_map/ppermute | solution.py:161
  19.9 3.7 %collective-permute-start.4 = (bf16[512,128]{1,0:T(8,128)(2,1)S(1)}, bf16[512,128]{1,0:T(8,128)(2,1)S(1)}, u32[]{:S(2)}, u32[]{:S(2)}) collective-permute-start(bf16[512,128]{1,0:T(8,128)(2,1)S(1)} %maximum_bitcast_fusion.1.refs_0_), channel_id=1, source_target_pairs={{0,64},{64,0},{1,65},{65,1},{2,66},{66,2},{3,67},{67,3},{4,68},{68... | collective-permute-start | bytes 393224 | tf_op jit(solution)/shard_map/ppermute | solution.py:161
  24.1 2.4 %collective-permute-done.4 = bf16[512,128]{1,0:T(8,128)(2,1)S(1)} collective-permute-done((bf16[512,128]{1,0:T(8,128)(2,1)S(1)}, bf16[512,128]{1,0:T(8,128)(2,1)S(1)}, u32[]{:S(2)}, u32[]{:S(2)}) %collective-permute-start.4) | collective-permute-done | bytes 131104 | tf_op jit(solution)/shard_map/ppermute | solution.py:161
  26.5 2.0 %collective-permute-start.5 = (bf16[512,128]{1,0:T(8,128)(2,1)S(1)}, bf16[512,128]{1,0:T(8,128)(2,1)S(1)}, u32[]{:S(2)}, u32[]{:S(2)}) collective-permute-start(bf16[512,128]{1,0:T(8,128)(2,1)S(1)} %collective-permute-done.4), channel_id=1, source_target_pairs={{0,4},{4,8},{8,12},{12,0},{1,5},{5,9},{9,13},{13,1},{2,6},{6,10},{... | collective-permute-start | bytes 393224 | tf_op jit(solution)/shard_map/ppermute | solution.py:161
  28.5 1.8 %ready_rows.1.left_ref = bf16[4,1024,128]{2,1,0:T(8,128)(2,1)S(1)} custom-call(f32[2]{0:T(128)S(1)} %pad_maximum_fusion.1.amp_ref, bf16[512,128]{1,0:T(8,128)(2,1)S(1)} %maximum_bitcast_fusion.refs_0_, bf16[512,128]{1,0:T(8,128)(2,1)S(1)} %collective-permute-done.1.refs_1_, bf16[512,128]{1,0:T(8,128)(2,1)S(1)} %collective-permute-done.2.refs_2_, ...), custom_call_target="tpu_custom_call" | custom-call | tf_op jit(solution)/shard_map/ready_rows/pallas_call | solution.py:47
  30.3 5.8 %add_tiles.2.refs_0_ = f32[4,64,1024]{2,1,0:T(8,128)S(1)} custom-call(f32[2]{0:T(128)S(1)} %pad_maximum_fusion.1.amp_ref, bf16[4,1024,128]{2,1,0:T(8,128)(2,1)S(1)} %ready_rows.1.left_ref, bf16[1024,128]{1,0:T(8,128)(2,1)S(1)} %get-tuple-element.23.right_ref, bf16[64,1024]{1,0:T(8,128)(2,1)S(1)} %get-tuple-element.24.vectors_ref), custom_call_target="tpu_custom_call" | custom-call | flops 2147483648 | bytes 393216 | tf_op jit(solution)/shard_map/add_tiles/pallas_call | solution.py:114
  36.1 3.3 %collective-permute-start.6 = (bf16[512,128]{1,0:T(8,128)(2,1)S(1)}, bf16[512,128]{1,0:T(8,128)(2,1)S(1)}, u32[]{:S(2)}, u32[]{:S(2)}) collective-permute-start(bf16[512,128]{1,0:T(8,128)(2,1)S(1)} %collective-permute-done.4), channel_id=1, source_target_pairs={{0,12},{4,0},{8,4},{12,8},{1,13},{5,1},{9,5},{13,9},{2,14},{6,2},{... | collective-permute-start | bytes 393224 | tf_op jit(solution)/shard_map/ppermute | solution.py:161
  39.4 1.5 %collective-permute-start.7 = (bf16[512,128]{1,0:T(8,128)(2,1)S(1)}, bf16[512,128]{1,0:T(8,128)(2,1)S(1)}, u32[]{:S(2)}, u32[]{:S(2)}) collective-permute-start(bf16[512,128]{1,0:T(8,128)(2,1)S(1)} %collective-permute-done.4), channel_id=1, source_target_pairs={{0,8},{4,12},{8,0},{12,4},{1,9},{5,13},{9,1},{13,5},{2,10},{6,14},... | collective-permute-start | bytes 393224 | tf_op jit(solution)/shard_map/ppermute | solution.py:161
  41.0 1.9 %collective-permute-done.6 = bf16[512,128]{1,0:T(8,128)(2,1)S(1)} collective-permute-done((bf16[512,128]{1,0:T(8,128)(2,1)S(1)}, bf16[512,128]{1,0:T(8,128)(2,1)S(1)}, u32[]{:S(2)}, u32[]{:S(2)}) %collective-permute-start.6) | collective-permute-done | bytes 131104 | tf_op jit(solution)/shard_map/ppermute | solution.py:161
  42.8 3.1 %collective-permute-done.7 = bf16[512,128]{1,0:T(8,128)(2,1)S(1)} collective-permute-done((bf16[512,128]{1,0:T(8,128)(2,1)S(1)}, bf16[512,128]{1,0:T(8,128)(2,1)S(1)}, u32[]{:S(2)}, u32[]{:S(2)}) %collective-permute-start.7) | collective-permute-done | bytes 131104 | tf_op jit(solution)/shard_map/ppermute | solution.py:161
  46.3 1.0 %ready_cols.4 = (bf16[3072,128]{1,0:T(8,128)(2,1)S(1)}, bf16[64,3072]{1,0:T(8,128)(2,1)S(1)}) custom-call(bf16[1536,128]{1,0:T(8,128)(2,1)S(1)} %constant_dynamic-update-slice_fusion.4.refs_0_, bf16[1536,128]{1,0:T(8,128)(2,1)S(1)} %collective-permute-done.12.refs_1_), custom_call_target="tpu_custom_call" | custom-call | tf_op jit(solution)/shard_map/ready_cols/pallas_call | solution.py:72
  47.3 13.4 %add_tiles.3.before_ref = f32[4,64,1024]{2,1,0:T(8,128)S(1)} custom-call(f32[2]{0:T(128)S(1)} %pad_maximum_fusion.1.amp_ref, bf16[4,1024,128]{2,1,0:T(8,128)(2,1)S(1)} %ready_rows.1.left_ref, bf16[3072,128]{1,0:T(8,128)(2,1)S(1)} %get-tuple-element.21.right_ref, bf16[64,3072]{1,0:T(8,128)(2,1)S(1)} %get-tuple-element.22.vectors_ref, ...), custom_call_target="tpu_custom_call" | custom-call | flops 6442450944 | bytes 1179648 | tf_op jit(solution)/shard_map/add_tiles/pallas_call | solution.py:114
  60.7 1.3 %ready_cols.3 = (bf16[4096,128]{1,0:T(8,128)(2,1)S(1)}, bf16[64,4096]{1,0:T(8,128)(2,1)S(1)}) custom-call(bf16[2048,128]{1,0:T(8,128)(2,1)S(1)} %constant_dynamic-update-slice_fusion.refs_0_, bf16[2048,128]{1,0:T(8,128)(2,1)S(1)} %collective-permute-done.8.refs_1_), custom_call_target="tpu_custom_call" | custom-call | tf_op jit(solution)/shard_map/ready_cols/pallas_call | solution.py:72
  62.1 4.7 %last_tiles.5 = (bf16[32,1024]{1,0:T(8,128)(2,1)S(1)}, bf16[32,1024]{1,0:T(8,128)(2,1)S(1)}) custom-call(f32[2]{0:T(128)S(1)} %pad_maximum_fusion.1.amp_ref, bf16[4,1024,128]{2,1,0:T(8,128)(2,1)S(1)} %ready_rows.1.left_ref, bf16[4096,128]{1,0:T(8,128)(2,1)S(1)} %get-tuple-element.19.right_ref, bf16[64,4096]{1,0:T(8,128)(2,1)S(1)} %get-tuple-element.20.vectors_ref, ...), custom_call_target="tpu_custom_call" | custom-call | flops 2147483648 | bytes 1572864 | tf_op jit(solution)/shard_map/last_tiles/pallas_call | solution.py:141
  66.8 4.7 %last_tiles.6 = (bf16[32,1024]{1,0:T(8,128)(2,1)S(1)}, bf16[32,1024]{1,0:T(8,128)(2,1)S(1)}) custom-call(f32[2]{0:T(128)S(1)} %pad_maximum_fusion.1.amp_ref, bf16[4,1024,128]{2,1,0:T(8,128)(2,1)S(1)} %ready_rows.1.left_ref, bf16[4096,128]{1,0:T(8,128)(2,1)S(1)} %get-tuple-element.19.right_ref, bf16[64,4096]{1,0:T(8,128)(2,1)S(1)} %get-tuple-element.20.vectors_ref, ...), custom_call_target="tpu_custom_call" | custom-call | flops 2147483648 | bytes 1572864 | tf_op jit(solution)/shard_map/last_tiles/pallas_call | solution.py:141
  71.5 4.7 %last_tiles.7 = (bf16[32,1024]{1,0:T(8,128)(2,1)S(1)}, bf16[32,1024]{1,0:T(8,128)(2,1)S(1)}) custom-call(f32[2]{0:T(128)S(1)} %pad_maximum_fusion.1.amp_ref, bf16[4,1024,128]{2,1,0:T(8,128)(2,1)S(1)} %ready_rows.1.left_ref, bf16[4096,128]{1,0:T(8,128)(2,1)S(1)} %get-tuple-element.19.right_ref, bf16[64,4096]{1,0:T(8,128)(2,1)S(1)} %get-tuple-element.20.vectors_ref, ...), custom_call_target="tpu_custom_call" | custom-call | flops 2147483648 | bytes 1572864 | tf_op jit(solution)/shard_map/last_tiles/pallas_call | solution.py:141
  76.8 4.0 %collective-permute-start.15 = (bf16[32,1024]{1,0:T(8,128)(2,1)S(1)}, bf16[32,1024]{1,0:T(8,128)(2,1)S(1)}, u32[]{:S(2)}, u32[]{:S(2)}) collective-permute-start(bf16[32,1024]{1,0:T(8,128)(2,1)S(1)} %get-tuple-element.27), channel_id=1, source_target_pairs={{0,33},{1,32},{16,49},{17,48},{32,1},{33,0},{48,17},{49,16},{2,35}... | collective-permute-start | bytes 196616 | tf_op jit(solution)/shard_map/ppermute | solution.py:166
  80.8 4.7 %last_tiles.4 = (f32[32,1024]{1,0:T(8,128)S(1)}, bf16[32,1024]{1,0:T(8,128)(2,1)S(1)}) custom-call(f32[2]{0:T(128)S(1)} %pad_maximum_fusion.1.amp_ref, bf16[4,1024,128]{2,1,0:T(8,128)(2,1)S(1)} %ready_rows.1.left_ref, bf16[4096,128]{1,0:T(8,128)(2,1)S(1)} %get-tuple-element.19.right_ref, bf16[64,4096]{1,0:T(8,128)(2,1)S(1)} %get-tuple-element.20.vectors_ref, ...), custom_call_target="tpu_custom_call" | custom-call | flops 2147483648 | bytes 1572864 | tf_op jit(solution)/shard_map/last_tiles/pallas_call | solution.py:141
  85.5 1.2 %collective-permute-start.16 = (bf16[32,1024]{1,0:T(8,128)(2,1)S(1)}, bf16[32,1024]{1,0:T(8,128)(2,1)S(1)}, u32[]{:S(2)}, u32[]{:S(2)}) collective-permute-start(bf16[32,1024]{1,0:T(8,128)(2,1)S(1)} %get-tuple-element.28), channel_id=1, source_target_pairs={{0,48},{16,0},{32,16},{48,32},{1,49},{17,1},{33,17},{49,33},{2,50}... | collective-permute-start | bytes 196616 | tf_op jit(solution)/shard_map/ppermute | solution.py:161
  86.7 1.9 %collective-permute-start.18 = (bf16[32,1024]{1,0:T(8,128)(2,1)S(1)}, bf16[32,1024]{1,0:T(8,128)(2,1)S(1)}, u32[]{:S(2)}, u32[]{:S(2)}) collective-permute-start(bf16[32,1024]{1,0:T(8,128)(2,1)S(1)} %get-tuple-element.30), channel_id=1, source_target_pairs={{0,16},{16,32},{32,48},{48,0},{1,17},{17,33},{33,49},{49,1},{2,18}... | collective-permute-start | bytes 196616 | tf_op jit(solution)/shard_map/ppermute | solution.py:161
  88.7 1.9 %collective-permute-start.19 = (bf16[32,1024]{1,0:T(8,128)(2,1)S(1)}, bf16[32,1024]{1,0:T(8,128)(2,1)S(1)}, u32[]{:S(2)}, u32[]{:S(2)}) collective-permute-start(bf16[32,1024]{1,0:T(8,128)(2,1)S(1)} %get-tuple-element.31), channel_id=1, source_target_pairs={{0,17},{1,16},{16,33},{17,32},{32,49},{33,48},{48,1},{49,0},{2,19}... | collective-permute-start | bytes 196616 | tf_op jit(solution)/shard_map/ppermute | solution.py:166
  92.2 2.9 %collective-permute-done.19 = bf16[32,1024]{1,0:T(8,128)(2,1)S(1)} collective-permute-done((bf16[32,1024]{1,0:T(8,128)(2,1)S(1)}, bf16[32,1024]{1,0:T(8,128)(2,1)S(1)}, u32[]{:S(2)}, u32[]{:S(2)}) %collective-permute-start.19) | collective-permute-done | bytes 65568 | tf_op jit(solution)/shard_map/ppermute | solution.py:166
  95.5 0.7 bitcast_add_fusion
  (47 shorter events, 4.9 us)
Async XLA Ops:
  0.8 0.8 copy-start.1
  1.8 0.7 copy-start.2
  2.7 5.6 %collective-permute-start = (bf16[96,512]{0,1:T(8,128)(2,1)S(1)}, bf16[96,512]{0,1:T(8,128)(2,1)S(1)}, u32[]{:S(2)}, u32[]{:S(2)}) collective-permute-start(bf16[96,512]{0,1:T(8,128)(2,1)S(1)} %pad_maximum_fusion), channel_id=1, source_target_pairs={{0,1},{1,0},{2,3},{3,2},{4,5},{5,4},{6,7},{7,6},{8,9},{9,8},{10,11... | collective-permute-start | bytes 294920 | tf_op jit(solution)/shard_map/ppermute | solution.py:161
  8.8 7.2 %collective-permute-start.9 = (bf16[512,128]{1,0:T(8,128)(2,1)S(1)}, bf16[512,128]{1,0:T(8,128)(2,1)S(1)}, u32[]{:S(2)}, u32[]{:S(2)}) collective-permute-start(bf16[512,128]{1,0:T(8,128)(2,1)S(1)} %maximum_bitcast_fusion.1.refs_0_), channel_id=1, source_target_pairs={{0,4},{4,8},{8,12},{12,0},{1,5},{5,9},{9,13},{13,1},{2,6},{6,10},{... | collective-permute-start | bytes 393224 | tf_op jit(solution)/shard_map/ppermute | solution.py:161
  10.5 13.2 %collective-permute-start.13 = (bf16[512,128]{1,0:T(8,128)(2,1)S(1)}, bf16[512,128]{1,0:T(8,128)(2,1)S(1)}, u32[]{:S(2)}, u32[]{:S(2)}) collective-permute-start(bf16[512,128]{1,0:T(8,128)(2,1)S(1)} %maximum_bitcast_fusion.1.refs_0_), channel_id=1, source_target_pairs={{0,2},{2,0},{1,3},{3,1},{4,6},{6,4},{5,7},{7,5},{8,10},{10,8},{9,1... | collective-permute-start | bytes 393224 | tf_op jit(solution)/shard_map/ppermute | solution.py:161
  10.5 7.3 %collective-permute-start.10 = (bf16[512,128]{1,0:T(8,128)(2,1)S(1)}, bf16[512,128]{1,0:T(8,128)(2,1)S(1)}, u32[]{:S(2)}, u32[]{:S(2)}) collective-permute-start(bf16[512,128]{1,0:T(8,128)(2,1)S(1)} %maximum_bitcast_fusion.1.refs_0_), channel_id=1, source_target_pairs={{0,12},{4,0},{8,4},{12,8},{1,13},{5,1},{9,5},{13,9},{2,14},{6,2},{... | collective-permute-start | bytes 393224 | tf_op jit(solution)/shard_map/ppermute | solution.py:161
  12.2 7.7 %collective-permute-start.11 = (bf16[512,128]{1,0:T(8,128)(2,1)S(1)}, bf16[512,128]{1,0:T(8,128)(2,1)S(1)}, u32[]{:S(2)}, u32[]{:S(2)}) collective-permute-start(bf16[512,128]{1,0:T(8,128)(2,1)S(1)} %maximum_bitcast_fusion.1.refs_0_), channel_id=1, source_target_pairs={{0,8},{4,12},{8,0},{12,4},{1,9},{5,13},{9,1},{13,5},{2,10},{6,14},... | collective-permute-start | bytes 393224 | tf_op jit(solution)/shard_map/ppermute | solution.py:161
  14.4 14.1 %collective-permute-start.1 = (bf16[512,128]{1,0:T(8,128)(2,1)S(1)}, bf16[512,128]{1,0:T(8,128)(2,1)S(1)}, u32[]{:S(2)}, u32[]{:S(2)}) collective-permute-start(bf16[512,128]{1,0:T(8,128)(2,1)S(1)} %maximum_bitcast_fusion.refs_0_), channel_id=1, source_target_pairs={{0,16},{16,32},{32,48},{48,0},{1,17},{17,33},{33,49},{49,1},{2,18}... | collective-permute-start | bytes 393224 | tf_op jit(solution)/shard_map/ppermute | solution.py:161
  16.0 12.6 %collective-permute-start.2 = (bf16[512,128]{1,0:T(8,128)(2,1)S(1)}, bf16[512,128]{1,0:T(8,128)(2,1)S(1)}, u32[]{:S(2)}, u32[]{:S(2)}) collective-permute-start(bf16[512,128]{1,0:T(8,128)(2,1)S(1)} %maximum_bitcast_fusion.refs_0_), channel_id=1, source_target_pairs={{0,48},{16,0},{32,16},{48,32},{1,49},{17,1},{33,17},{49,33},{2,50}... | collective-permute-start | bytes 393224 | tf_op jit(solution)/shard_map/ppermute | solution.py:161
  17.8 10.7 %collective-permute-start.3 = (bf16[512,128]{1,0:T(8,128)(2,1)S(1)}, bf16[512,128]{1,0:T(8,128)(2,1)S(1)}, u32[]{:S(2)}, u32[]{:S(2)}) collective-permute-start(bf16[512,128]{1,0:T(8,128)(2,1)S(1)} %maximum_bitcast_fusion.refs_0_), channel_id=1, source_target_pairs={{0,32},{16,48},{32,0},{48,16},{1,33},{17,49},{33,1},{49,17},{2,34}... | collective-permute-start | bytes 393224 | tf_op jit(solution)/shard_map/ppermute | solution.py:161
  19.9 6.6 %collective-permute-start.4 = (bf16[512,128]{1,0:T(8,128)(2,1)S(1)}, bf16[512,128]{1,0:T(8,128)(2,1)S(1)}, u32[]{:S(2)}, u32[]{:S(2)}) collective-permute-start(bf16[512,128]{1,0:T(8,128)(2,1)S(1)} %maximum_bitcast_fusion.1.refs_0_), channel_id=1, source_target_pairs={{0,64},{64,0},{1,65},{65,1},{2,66},{66,2},{3,67},{67,3},{4,68},{68... | collective-permute-start | bytes 393224 | tf_op jit(solution)/shard_map/ppermute | solution.py:161
  23.7 22.6 %collective-permute-start.12 = (bf16[1536,128]{1,0:T(8,128)(2,1)S(1)}, bf16[1536,128]{1,0:T(8,128)(2,1)S(1)}, u32[]{:S(2)}, u32[]{:S(2)}) collective-permute-start(bf16[1536,128]{1,0:T(8,128)(2,1)S(1)} %constant_dynamic-update-slice_fusion.4.refs_0_), channel_id=1, source_target_pairs={{0,2},{2,0},{1,3},{3,1},{4,6},{6,4},{5,7},{7,5},{8,10},{10,8},{9,1... | collective-permute-start | bytes 1179656 | tf_op jit(solution)/shard_map/ppermute | solution.py:161
  26.5 14.4 %collective-permute-start.5 = (bf16[512,128]{1,0:T(8,128)(2,1)S(1)}, bf16[512,128]{1,0:T(8,128)(2,1)S(1)}, u32[]{:S(2)}, u32[]{:S(2)}) collective-permute-start(bf16[512,128]{1,0:T(8,128)(2,1)S(1)} %collective-permute-done.4), channel_id=1, source_target_pairs={{0,4},{4,8},{8,12},{12,0},{1,5},{5,9},{9,13},{13,1},{2,6},{6,10},{... | collective-permute-start | bytes 393224 | tf_op jit(solution)/shard_map/ppermute | solution.py:161
  36.1 6.8 %collective-permute-start.6 = (bf16[512,128]{1,0:T(8,128)(2,1)S(1)}, bf16[512,128]{1,0:T(8,128)(2,1)S(1)}, u32[]{:S(2)}, u32[]{:S(2)}) collective-permute-start(bf16[512,128]{1,0:T(8,128)(2,1)S(1)} %collective-permute-done.4), channel_id=1, source_target_pairs={{0,12},{4,0},{8,4},{12,8},{1,13},{5,1},{9,5},{13,9},{2,14},{6,2},{... | collective-permute-start | bytes 393224 | tf_op jit(solution)/shard_map/ppermute | solution.py:161
  39.4 6.6 %collective-permute-start.7 = (bf16[512,128]{1,0:T(8,128)(2,1)S(1)}, bf16[512,128]{1,0:T(8,128)(2,1)S(1)}, u32[]{:S(2)}, u32[]{:S(2)}) collective-permute-start(bf16[512,128]{1,0:T(8,128)(2,1)S(1)} %collective-permute-done.4), channel_id=1, source_target_pairs={{0,8},{4,12},{8,0},{12,4},{1,9},{5,13},{9,1},{13,5},{2,10},{6,14},... | collective-permute-start | bytes 393224 | tf_op jit(solution)/shard_map/ppermute | solution.py:161
  46.0 14.8 %collective-permute-start.8 = (bf16[2048,128]{1,0:T(8,128)(2,1)S(1)}, bf16[2048,128]{1,0:T(8,128)(2,1)S(1)}, u32[]{:S(2)}, u32[]{:S(2)}) collective-permute-start(bf16[2048,128]{1,0:T(8,128)(2,1)S(1)} %constant_dynamic-update-slice_fusion.refs_0_), channel_id=1, source_target_pairs={{0,2},{2,0},{1,3},{3,1},{4,6},{6,4},{5,7},{7,5},{8,10},{10,8},{9,1... | collective-permute-start | bytes 1572872 | tf_op jit(solution)/shard_map/ppermute | solution.py:161
  76.2 12.5 %collective-permute-start.14 = (bf16[32,1024]{1,0:T(8,128)(2,1)S(1)}, bf16[32,1024]{1,0:T(8,128)(2,1)S(1)}, u32[]{:S(2)}, u32[]{:S(2)}) collective-permute-start(bf16[32,1024]{1,0:T(8,128)(2,1)S(1)} %get-tuple-element.26), channel_id=1, source_target_pairs={{0,32},{16,48},{32,0},{48,16},{1,33},{17,49},{33,1},{49,17},{2,34}... | collective-permute-start | bytes 196616 | tf_op jit(solution)/shard_map/ppermute | solution.py:161
  76.8 18.7 %copy-start = (bf16[1024,32]{0,1:T(8,128)(2,1)S(1)}, bf16[1024,32]{0,1:T(8,128)(2,1)}, u32[]{:S(2)}) copy-start(bf16[1024,32]{0,1:T(8,128)(2,1)} %param.6) | copy-start | bytes 196612
  76.8 13.8 %collective-permute-start.15 = (bf16[32,1024]{1,0:T(8,128)(2,1)S(1)}, bf16[32,1024]{1,0:T(8,128)(2,1)S(1)}, u32[]{:S(2)}, u32[]{:S(2)}) collective-permute-start(bf16[32,1024]{1,0:T(8,128)(2,1)S(1)} %get-tuple-element.27), channel_id=1, source_target_pairs={{0,33},{1,32},{16,49},{17,48},{32,1},{33,0},{48,17},{49,16},{2,35}... | collective-permute-start | bytes 196616 | tf_op jit(solution)/shard_map/ppermute | solution.py:166
  85.5 6.1 %collective-permute-start.16 = (bf16[32,1024]{1,0:T(8,128)(2,1)S(1)}, bf16[32,1024]{1,0:T(8,128)(2,1)S(1)}, u32[]{:S(2)}, u32[]{:S(2)}) collective-permute-start(bf16[32,1024]{1,0:T(8,128)(2,1)S(1)} %get-tuple-element.28), channel_id=1, source_target_pairs={{0,48},{16,0},{32,16},{48,32},{1,49},{17,1},{33,17},{49,33},{2,50}... | collective-permute-start | bytes 196616 | tf_op jit(solution)/shard_map/ppermute | solution.py:161
  86.7 5.2 %collective-permute-start.17 = (bf16[32,1024]{1,0:T(8,128)(2,1)S(1)}, bf16[32,1024]{1,0:T(8,128)(2,1)S(1)}, u32[]{:S(2)}, u32[]{:S(2)}) collective-permute-start(bf16[32,1024]{1,0:T(8,128)(2,1)S(1)} %get-tuple-element.29), channel_id=1, source_target_pairs={{0,49},{1,48},{16,1},{17,0},{32,17},{33,16},{48,33},{49,32},{2,51}... | collective-permute-start | bytes 196616 | tf_op jit(solution)/shard_map/ppermute | solution.py:166
  86.7 5.5 %collective-permute-start.18 = (bf16[32,1024]{1,0:T(8,128)(2,1)S(1)}, bf16[32,1024]{1,0:T(8,128)(2,1)S(1)}, u32[]{:S(2)}, u32[]{:S(2)}) collective-permute-start(bf16[32,1024]{1,0:T(8,128)(2,1)S(1)} %get-tuple-element.30), channel_id=1, source_target_pairs={{0,16},{16,32},{32,48},{48,0},{1,17},{17,33},{33,49},{49,1},{2,18}... | collective-permute-start | bytes 196616 | tf_op jit(solution)/shard_map/ppermute | solution.py:161
  88.7 6.5 %collective-permute-start.19 = (bf16[32,1024]{1,0:T(8,128)(2,1)S(1)}, bf16[32,1024]{1,0:T(8,128)(2,1)S(1)}, u32[]{:S(2)}, u32[]{:S(2)}) collective-permute-start(bf16[32,1024]{1,0:T(8,128)(2,1)S(1)} %get-tuple-element.31), channel_id=1, source_target_pairs={{0,17},{1,16},{16,33},{17,32},{32,49},{33,48},{48,1},{49,0},{2,19}... | collective-permute-start | bytes 196616 | tf_op jit(solution)/shard_map/ppermute | solution.py:166
  90.6 5.0 %collective-permute-start.20 = (bf16[32,1024]{1,0:T(8,128)(2,1)S(1)}, bf16[32,1024]{1,0:T(8,128)(2,1)S(1)}, u32[]{:S(2)}, u32[]{:S(2)}) collective-permute-start(bf16[32,1024]{1,0:T(8,128)(2,1)S(1)} %get-tuple-element.32), channel_id=1, source_target_pairs={{0,1},{1,0},{2,3},{3,2},{4,5},{5,4},{6,7},{7,6},{8,9},{9,8},{10,11... | collective-permute-start | bytes 196616 | tf_op jit(solution)/shard_map/ppermute | solution.py:161

commit v3 on v2

--- a/solution.py
+++ b/solution.py
@@ -82,30 +82,34 @@
     )(*blocks)
 
 
-def tile_sum(amp_ref, left, right_ref, vectors_ref):
+def tile_sum(amp_ref, left, pairs):
     top = jnp.full((1, 1), amp_ref[0], F32).astype(BF16)
-    total = right_ref.shape[0]
     result = jnp.zeros((64, left.shape[0]), F32)
-    for at in range(0, total, TN):
-        exponent = lax.dot_general(
-            right_ref[at : at + TN, :], left, (((1,), (1,)), ((), ())), preferred_element_type=F32
-        )
-        block = jnp.minimum(jnp.exp(exponent).astype(BF16), top)
-        result += jnp.dot(vectors_ref[:, at : at + TN], block, preferred_element_type=F32)
+    for right_ref, vectors_ref in pairs:
+        for at in range(0, right_ref.shape[0], TN):
+            exponent = lax.dot_general(
+                right_ref[at : at + TN, :], left, (((1,), (1,)), ((), ())), preferred_element_type=F32
+            )
+            block = jnp.minimum(jnp.exp(exponent).astype(BF16), top)
+            result += jnp.dot(vectors_ref[:, at : at + TN], block, preferred_element_type=F32)
     return result
 
 
+SCALE = 512
+
+
 def cost(rows, cols):
-    return pl.CostEstimate(flops=rows * cols * 512, transcendentals=rows * cols, bytes_accessed=cols * 384)
+    return pl.CostEstimate(flops=rows * cols * SCALE, transcendentals=0, bytes_accessed=cols * 384)
 
 
 def add_tiles(amp, left, right, vectors, before):
+    count = left.shape[0]
     total = right.shape[0]
     per = 1024 // TM
     old = [] if before is None else [before]
 
     def body(amp_ref, left_ref, right_ref, vectors_ref, *refs):
-        value = tile_sum(amp_ref, left_ref[0], right_ref, vectors_ref)
+        value = tile_sum(amp_ref, left_ref[0], [(right_ref, vectors_ref)])
         if old:
             value += refs[0][0]
         refs[-1][0] = value
@@ -113,8 +117,8 @@
     acc_spec = pl.BlockSpec((1, 64, TM), lambda i: (i // per, 0, i % per))
     return pl.pallas_call(
         body,
-        grid=(4 * per,),
-        out_shape=jax.ShapeDtypeStruct((4, 64, 1024), F32),
+        grid=(count * per,),
+        out_shape=jax.ShapeDtypeStruct((count, 64, 1024), F32),
         in_specs=[
             pl.BlockSpec(memory_space=pltpu.SMEM),
             pl.BlockSpec((1, TM, 128), lambda i: (i // per, i % per, 0)),
@@ -124,46 +128,102 @@
         + [acc_spec] * len(old),
         out_specs=acc_spec,
         compiler_params=PARAMS,
-        cost_estimate=cost(4096, total),
+        cost_estimate=cost(1024 * count, total),
         name="add_tiles",
     )(amp, left, right, vectors, *old)
 
 
-def last_tiles(amp, left, right, vectors, before, group, kept):
+def last_tiles(amp, left, right, vectors, before):
+    count = left.shape[0]
     total = right.shape[0]
-
-    def body(amp_ref, left_ref, right_ref, vectors_ref, before_ref, mine_ref, theirs_ref):
-        value = tile_sum(amp_ref, left_ref[0], right_ref, vectors_ref) + before_ref[0]
-        mine_ref[...] = value[:32].astype(kept)
-        theirs_ref[...] = value[32:].astype(BF16)
-
-    out_spec = pl.BlockSpec((32, TM), lambda i: (0, i))
-    return pl.pallas_call(
-        body,
-        grid=(1024 // TM,),
-        out_shape=(jax.ShapeDtypeStruct((32, 1024), kept), jax.ShapeDtypeStruct((32, 1024), BF16)),
-        in_specs=[
-            pl.BlockSpec(memory_space=pltpu.SMEM),
-            pl.BlockSpec((1, TM, 128), lambda i: (group, i, 0)),
+    per = 1024 // TM
+
+    def body(amp_ref, left_ref, right_ref, vectors_ref, before_ref, *out_refs):
+        value = tile_sum(amp_ref, left_ref[0], [(right_ref, vectors_ref)]) + before_ref[0]
+        for k in range(count):
+
+            @pl.when(pl.program_id(0) // per == k)
+            def _():
+                out_refs[k][...] = value.astype(BF16)
+
+    def place(k):
+        return pl.BlockSpec((64, TM), lambda i: (0, jnp.clip(i - k * per, 0, per - 1)))
+
+    return pl.pallas_call(
+        body,
+        grid=(count * per,),
+        out_shape=[jax.ShapeDtypeStruct((64, 1024), BF16)] * count,
+        in_specs=[
+            pl.BlockSpec(memory_space=pltpu.SMEM),
+            pl.BlockSpec((1, TM, 128), lambda i: (i // per, i % per, 0)),
             pl.BlockSpec((total, 128), lambda i: (0, 0)),
             pl.BlockSpec((64, total), lambda i: (0, 0)),
-            pl.BlockSpec((1, 64, TM), lambda i: (group, 0, i)),
+            pl.BlockSpec((1, 64, TM), lambda i: (i // per, 0, i % per)),
         ],
-        out_specs=(out_spec, out_spec),
-        compiler_params=PARAMS,
-        cost_estimate=cost(1024, total),
+        out_specs=[place(k) for k in range(count)],
+        compiler_params=PARAMS,
+        cost_estimate=cost(1024 * count, total),
         name="last_tiles",
     )(amp, left, right, vectors, before)
+
+
+def own_tiles(amp, left, ready):
+    flat = [part for pair in ready for part in pair]
+
+    def body(amp_ref, left_ref, *refs):
+        pairs = [(refs[2 * k], refs[2 * k + 1]) for k in range(len(ready))]
+        refs[-1][...] = tile_sum(amp_ref, left_ref[0], pairs)
+
+    return pl.pallas_call(
+        body,
+        grid=(1024 // TM,),
+        out_shape=jax.ShapeDtypeStruct((64, 1024), F32),
+        in_specs=[
+            pl.BlockSpec(memory_space=pltpu.SMEM),
+            pl.BlockSpec((1, TM, 128), lambda i: (0, i, 0)),
+        ]
+        + [pl.BlockSpec(part.shape, lambda i: (0, 0)) for part in flat],
+        out_specs=pl.BlockSpec((64, TM), lambda i: (0, i)),
+        compiler_params=PARAMS,
+        cost_estimate=cost(1024, sum(right.shape[0] for right, _ in ready)),
+        name="own_tiles",
+    )(amp, left, *flat)
+
+
+def own_last(amp, left, right, vectors, before, arrived):
+    count = len(arrived)
+    total = right.shape[0]
+
+    def body(amp_ref, left_ref, right_ref, vectors_ref, before_ref, *refs):
+        mine_ref, theirs_ref = refs[count:]
+        value = tile_sum(amp_ref, left_ref[0], [(right_ref, vectors_ref)]) + before_ref[...]
+        for ref in refs[:count]:
+            value += ref[...].astype(F32)
+        mine_ref[...] = value[:32]
+        theirs_ref[...] = value[32:].astype(BF16)
+
+    out_spec = pl.BlockSpec((32, TM), lambda i: (0, i))
+    return pl.pallas_call(
+        body,
+        grid=(1024 // TM,),
+        out_shape=(jax.ShapeDtypeStruct((32, 1024), F32), jax.ShapeDtypeStruct((32, 1024), BF16)),
+        in_specs=[
+            pl.BlockSpec(memory_space=pltpu.SMEM),
+            pl.BlockSpec((1, TM, 128), lambda i: (0, i, 0)),
+            pl.BlockSpec((total, 128), lambda i: (0, 0)),
+            pl.BlockSpec((64, total), lambda i: (0, 0)),
+        ]
+        + [pl.BlockSpec((64, TM), lambda i: (0, i))] * (count + 1),
+        out_specs=(out_spec, out_spec),
+        compiler_params=PARAMS,
+        cost_estimate=cost(1024, total),
+        name="own_last",
+    )(amp, left, right, vectors, before, *arrived)
 
 
 def shift(value, axis, by):
     size = SIZES[NAMES.index(axis)]
     return lax.ppermute(value, axis, [(i, (i + by) % size) for i in range(size)])
-
-
-def shift_swap(value, by):
-    pairs = [(2 * i + j, 2 * ((i + by) % 4) + 1 - j) for i in range(4) for j in range(2)]
-    return lax.ppermute(value, ("x", "zl"), pairs)
 
 
 def per_device(points, vectors, lengthscale, outscale, noise):
@@ -189,30 +249,30 @@
         axis=0,
     ).T
 
-    across = shift(share, "zh", 1)
     beside = shift(share, "c", 1)
+    near = [shift(share, "y", by) for by in (1, -1, 2)]
     rows_in = [shift(rows, "x", by) for by in (1, -1, 2)]
-    near = [shift(share, "y", by) for by in (1, -1, 2)]
-    far = [across] + [shift(across, "y", by) for by in (1, -1, 2)]
+    near[2], rows_in[0] = lax.optimization_barrier((near[2], rows_in[0]))
     near = jnp.concatenate(near, axis=0)
     near_beside = shift(near, "c", 1)
-    far = jnp.concatenate(far, axis=0)
+    far = shift(jnp.concatenate([share, near], axis=0), "zh", 1)
+    own_left = ready_rows(amp, [rows])
+    left = ready_rows(amp, rows_in)
+    ready = [ready_cols([share, beside])]
+    acc = add_tiles(amp, left, *ready[0], None)
+    ready.append(ready_cols([near, near_beside]))
+    acc = add_tiles(amp, left, *ready[1], acc)
+    far, acc = lax.optimization_barrier((far, acc))
     far_beside = shift(far, "c", 1)
-
-    left = ready_rows(amp, [rows] + rows_in)
-    acc = add_tiles(amp, left, *ready_cols([share, beside]), None)
-    acc = add_tiles(amp, left, *ready_cols([near, near_beside]), acc)
-    last = ready_cols([far, far_beside])
-
-    arrived = []
-    for group, by in ((3, 2), (1, -1), (2, 1)):
-        mine, theirs = last_tiles(amp, left, *last, acc, group, BF16)
-        arrived.append(shift(mine, "x", by))
-        arrived.append(shift_swap(theirs, by))
-    mine, theirs = last_tiles(amp, left, *last, acc, 0, F32)
-    arrived.append(shift(theirs, "zl", 1))
-    for part in arrived:
-        mine = mine + part.astype(F32)
+    ready.append(ready_cols([far]))
+    acc = add_tiles(amp, left, *ready[2], acc)
+    ready.append(ready_cols([far_beside]))
+
+    sent = last_tiles(amp, left, *ready[3], acc)
+    arrived = [shift(part, "x", by) for part, by in zip(sent, (-1, 1, 2))]
+    own = own_tiles(amp, own_left, [ready[0], ready[1], ready[2]])
+    mine, theirs = own_last(amp, own_left, *ready[3], own, arrived)
+    mine = mine + shift(theirs, "zl", 1).astype(F32)
     return mine.T + noise[0] * vectors.astype(F32)
 
 

time: 96.5 us -> 84.5 us (0.88)
  starting transfers between devices: 33.9 us -> 24.5 us
  waiting for transfers between devices: 13.9 us -> 9.61 us
  Pallas kernels: 42.5 us -> 44.1 us
    ppermute x3 -> x0, starting transfers between devices: 5.92 us -> none  [shift_swap(): return lax.ppermute(value, ('x', 'zl'), pairs)]
    ppermute x18 -> x15, starting transfers between devices: 28 us -> 24.5 us  [shift(): lax.ppermute(value, axis, [(i, (i + by) % size) for i in range(size)])]
    ppermute x3 -> x0, waiting for transfers between devices: 3.16 us -> none  [shift_swap(): return lax.ppermute(value, ('x', 'zl'), pairs)]
    ppermute x18 -> x15, waiting for transfers between devices: 10.8 us -> 9.61 us  [shift(): lax.ppermute(value, axis, [(i, (i + by) % size) for i in range(size)])]
    pallas_call x6, Pallas kernels: 38 us -> 39 us  [the longest x3 22 us: add_tiles(): pl.pallas_call(body, grid=(count * per,), out_shape=jax.ShapeDtypeStruct(...]
    pallas_call x1 -> x2, Pallas kernels: 1.76 us -> 2.37 us  [ready_rows(): pl.pallas_call(body, out_shape=jax.ShapeDtypeStruct((count, 1024, 128), B...]
    pallas_call x3 -> x4, Pallas kernels: 2.71 us -> 2.78 us  [ready_cols(): pl.pallas_call(body, out_shape=(jax.ShapeDtypeStruct((total, 128), BF16),...]
  transfers between devices with their start and end apart: 21 -> 15, of which waited for: 8 -> 6; matrix products, arithmetic and copies ran while one was open for 1% -> 0% of each run, Pallas kernels for 28% -> 39%
where the time goes in v3:
time: 84.5 us; the launch traced here: 84.1 us
  Pallas kernels  44.1 us (52%)
  starting transfers between devices  24.5 us (29%)
  waiting for transfers between devices  9.61 us (11%)
  local copies, waits for them, and re-layouts  2.8 us (3%)
  between operations  1.62 us (2%)
  other arithmetic  1.47 us (2%)
    ppermute x15, starting transfers between devices, shift(): lax.ppermute(value, axis, [(i, (i + by) % size) for i in range(size)])  24.5 us
    pallas_call x3, Pallas kernels, add_tiles(): pl.pallas_call(body, grid=(count * per,), out_shape=jax.ShapeDtypeStruct(...  22 us
    ppermute x15, waiting for transfers between devices, shift(): lax.ppermute(value, axis, [(i, (i + by) % size) for i in range(size)])  9.61 us
    pallas_call x1, Pallas kernels, last_tiles(): pl.pallas_call(body, grid=(count * per,), out_shape=[jax.ShapeDtypeStruct...  7.58 us
    pallas_call x1, Pallas kernels, own_tiles(): pl.pallas_call(body, grid=(1024 // TM,), out_shape=jax.ShapeDtypeStruct((...  6.62 us
    pallas_call x1, Pallas kernels, own_last(): pl.pallas_call(body, grid=(1024 // TM,), out_shape=(jax.ShapeDtypeStruct(...  2.82 us
    pallas_call x4, Pallas kernels, ready_cols(): pl.pallas_call(body, out_shape=(jax.ShapeDtypeStruct((total, 128), BF16),...  2.78 us
    pallas_call x2, Pallas kernels, ready_rows(): pl.pallas_call(body, out_shape=jax.ShapeDtypeStruct((count, 1024, 128), B...  2.37 us
  transfers between devices with their start and end apart: 15, of which 6 were waited for; matrix products, arithmetic and copies ran while one was open for 0% of the time, Pallas kernels for 39%

profile of v3, /device:TPU:0, one launch (start us, length us, event | category | flops | bytes accessed | tf_op | source)
XLA Modules:
  0.0 84.1 jit_solution(13647465850263367556)
XLA Ops:
  0.0 0.8 constant_dynamic-slice_fusion
  0.9 0.7 copy-done.1
  1.8 0.6 copy-done.2
  2.7 2.1 %collective-permute-start = (bf16[96,512]{0,1:T(8,128)(2,1)S(1)}, bf16[96,512]{0,1:T(8,128)(2,1)S(1)}, u32[]{:S(2)}, u32[]{:S(2)}) collective-permute-start(bf16[96,512]{0,1:T(8,128)(2,1)S(1)} %pad_maximum_fusion.1), channel_id=1, source_target_pairs={{0,1},{1,0},{2,3},{3,2},{4,5},{5,4},{6,7},{7,6},{8,9},{9,8},{10,11... | collective-permute-start | bytes 294920 | tf_op jit(solution)/shard_map/ppermute | solution.py:226
  4.9 3.4 %collective-permute-done = bf16[96,512]{0,1:T(8,128)(2,1)S(1)} collective-permute-done((bf16[96,512]{0,1:T(8,128)(2,1)S(1)}, bf16[96,512]{0,1:T(8,128)(2,1)S(1)}, u32[]{:S(2)}, u32[]{:S(2)}) %collective-permute-start) | collective-permute-done | bytes 98336 | tf_op jit(solution)/shard_map/ppermute | solution.py:226
  8.9 3.3 %collective-permute-start.3 = (bf16[512,128]{1,0:T(8,128)(2,1)S(1)}, bf16[512,128]{1,0:T(8,128)(2,1)S(1)}, u32[]{:S(2)}, u32[]{:S(2)}) collective-permute-start(bf16[512,128]{1,0:T(8,128)(2,1)S(1)} %maximum_bitcast_fusion.1.refs_0_), channel_id=1, source_target_pairs={{0,8},{4,12},{8,0},{12,4},{1,9},{5,13},{9,1},{13,5},{2,10},{6,14},... | collective-permute-start | bytes 393224 | tf_op jit(solution)/shard_map/ppermute | solution.py:226
  12.2 1.5 %collective-permute-start.4 = (bf16[512,128]{1,0:T(8,128)(2,1)S(1)}, bf16[512,128]{1,0:T(8,128)(2,1)S(1)}, u32[]{:S(2)}, u32[]{:S(2)}) collective-permute-start(bf16[512,128]{1,0:T(8,128)(2,1)S(1)} %maximum_bitcast_fusion.refs_0_), channel_id=1, source_target_pairs={{0,16},{16,32},{32,48},{48,0},{1,17},{17,33},{33,49},{49,1},{2,18}... | collective-permute-start | bytes 393224 | tf_op jit(solution)/shard_map/ppermute | solution.py:226
  13.7 0.7 collective-permute-start.1
  14.4 2.6 %collective-permute-start.2 = (bf16[512,128]{1,0:T(8,128)(2,1)S(1)}, bf16[512,128]{1,0:T(8,128)(2,1)S(1)}, u32[]{:S(2)}, u32[]{:S(2)}) collective-permute-start(bf16[512,128]{1,0:T(8,128)(2,1)S(1)} %maximum_bitcast_fusion.1.refs_0_), channel_id=1, source_target_pairs={{0,12},{4,0},{8,4},{12,8},{1,13},{5,1},{9,5},{13,9},{2,14},{6,2},{... | collective-permute-start | bytes 393224 | tf_op jit(solution)/shard_map/ppermute | solution.py:226
  17.7 0.7 collective-permute-done.4.refs_0_
  18.4 1.5 %collective-permute-done.1 = bf16[512,128]{1,0:T(8,128)(2,1)S(1)} collective-permute-done((bf16[512,128]{1,0:T(8,128)(2,1)S(1)}, bf16[512,128]{1,0:T(8,128)(2,1)S(1)}, u32[]{:S(2)}, u32[]{:S(2)}) %collective-permute-start.1) | collective-permute-done | bytes 131104 | tf_op jit(solution)/shard_map/ppermute | solution.py:226
  20.6 1.7 %collective-permute-start.6 = (bf16[512,128]{1,0:T(8,128)(2,1)S(1)}, bf16[512,128]{1,0:T(8,128)(2,1)S(1)}, u32[]{:S(2)}, u32[]{:S(2)}) collective-permute-start(bf16[512,128]{1,0:T(8,128)(2,1)S(1)} %maximum_bitcast_fusion.refs_0_), channel_id=1, source_target_pairs={{0,48},{16,0},{32,16},{48,32},{1,49},{17,1},{33,17},{49,33},{2,50}... | collective-permute-start | bytes 393224 | tf_op jit(solution)/shard_map/ppermute | solution.py:226
  22.4 1.8 %collective-permute-start.7 = (bf16[512,128]{1,0:T(8,128)(2,1)S(1)}, bf16[512,128]{1,0:T(8,128)(2,1)S(1)}, u32[]{:S(2)}, u32[]{:S(2)}) collective-permute-start(bf16[512,128]{1,0:T(8,128)(2,1)S(1)} %maximum_bitcast_fusion.refs_0_), channel_id=1, source_target_pairs={{0,32},{16,48},{32,0},{48,16},{1,33},{17,49},{33,1},{49,17},{2,34}... | collective-permute-start | bytes 393224 | tf_op jit(solution)/shard_map/ppermute | solution.py:226
  24.2 3.8 %collective-permute-start.5 = (bf16[2048,128]{1,0:T(8,128)(2,1)S(1)}, bf16[2048,128]{1,0:T(8,128)(2,1)S(1)}, u32[]{:S(2)}, u32[]{:S(2)}) collective-permute-start(bf16[2048,128]{1,0:T(8,128)(2,1)S(1)} %pad_maximum_fusion), channel_id=1, source_target_pairs={{0,64},{64,0},{1,65},{65,1},{2,66},{66,2},{3,67},{67,3},{4,68},{68... | collective-permute-start | bytes 1572872 | tf_op jit(solution)/shard_map/ppermute | solution.py:226
  28.4 0.7 collective-permute-done.7.refs_2_
  29.1 1.5 %ready_rows.3.left_ref = bf16[3,1024,128]{2,1,0:T(8,128)(2,1)S(1)} custom-call(f32[2]{0:T(128)S(1)} %pad_maximum_fusion.2.amp_ref, bf16[512,128]{1,0:T(8,128)(2,1)S(1)} %collective-permute-done.4.refs_0_, bf16[512,128]{1,0:T(8,128)(2,1)S(1)} %collective-permute-done.6.refs_1_, bf16[512,128]{1,0:T(8,128)(2,1)S(1)} %collective-permute-done.7.refs_2_), custom_call_target="tpu_custom_call" | custom-call | tf_op jit(solution)/shard_map/ready_rows/pallas_call | solution.py:47
  30.6 4.5 %add_tiles.3.refs_0_ = f32[3,64,1024]{2,1,0:T(8,128)S(1)} custom-call(f32[2]{0:T(128)S(1)} %pad_maximum_fusion.2.amp_ref, bf16[3,1024,128]{2,1,0:T(8,128)(2,1)S(1)} %ready_rows.3.left_ref, bf16[1024,128]{1,0:T(8,128)(2,1)S(1)} %get-tuple-element.26.right_ref.refs_0_, bf16[64,1024]{1,0:T(8,128)(2,1)S(1)} %get-tuple-element.27.vectors_ref.refs_1_), custom_call_target="tpu_custom_call" | custom-call | flops 1610612736 | bytes 393216 | tf_op jit(solution)/shard_map/add_tiles/pallas_call | solution.py:118
  35.1 1.0 %ready_cols.4 = (bf16[3072,128]{1,0:T(8,128)(2,1)S(1)}, bf16[64,3072]{1,0:T(8,128)(2,1)S(1)}) custom-call(bf16[1536,128]{1,0:T(8,128)(2,1)S(1)} %constant_dynamic-update-slice_fusion.refs_0_, bf16[1536,128]{1,0:T(8,128)(2,1)S(1)} %collective-permute-done.8.refs_1_), custom_call_target="tpu_custom_call" | custom-call | tf_op jit(solution)/shard_map/ready_cols/pallas_call | solution.py:72
  36.1 10.3 %add_tiles.4.refs_0_ = f32[3,64,1024]{2,1,0:T(8,128)S(1)} custom-call(f32[2]{0:T(128)S(1)} %pad_maximum_fusion.2.amp_ref, bf16[3,1024,128]{2,1,0:T(8,128)(2,1)S(1)} %ready_rows.3.left_ref, bf16[3072,128]{1,0:T(8,128)(2,1)S(1)} %get-tuple-element.24.right_ref.refs_2_, bf16[64,3072]{1,0:T(8,128)(2,1)S(1)} %get-tuple-element.25.vectors_ref.refs_3_, ...), custom_call_target="tpu_custom_call" | custom-call | flops 4831838208 | bytes 1179648 | tf_op jit(solution)/shard_map/add_tiles/pallas_call | solution.py:118
  46.6 0.9 %ready_rows.2.left_ref = bf16[1,1024,128]{2,1,0:T(8,128)(2,1)S(1)} custom-call(f32[2]{0:T(128)S(1)} %pad_maximum_fusion.2.amp_ref, bf16[512,128]{1,0:T(8,128)(2,1)S(1)} %maximum_bitcast_fusion.refs_0_), custom_call_target="tpu_custom_call" | custom-call | tf_op jit(solution)/shard_map/ready_rows/pallas_call | solution.py:47
  47.5 0.7 ready_cols.7
  48.2 7.3 %add_tiles.5.before_ref = f32[3,64,1024]{2,1,0:T(8,128)S(1)} custom-call(f32[2]{0:T(128)S(1)} %pad_maximum_fusion.2.amp_ref, bf16[3,1024,128]{2,1,0:T(8,128)(2,1)S(1)} %ready_rows.3.left_ref, bf16[2048,128]{1,0:T(8,128)(2,1)S(1)} %get-tuple-element.31.refs_4_.right_ref, bf16[64,2048]{1,0:T(8,128)(2,1)S(1)} %get-tuple-element.32.refs_5_.vectors_ref, ...), custom_call_target="tpu_custom_call" | custom-call | flops 3221225472 | bytes 786432 | tf_op jit(solution)/shard_map/add_tiles/pallas_call | solution.py:118
  55.5 0.7 ready_cols.6
  56.2 7.6 %last_tiles.1 = (bf16[64,1024]{1,0:T(8,128)(2,1)S(1)}, bf16[64,1024]{1,0:T(8,128)(2,1)S(1)}, bf16[64,1024]{1,0:T(8,128)(2,1)S(1)}) custom-call(f32[2]{0:T(128)S(1)} %pad_maximum_fusion.2.amp_ref, bf16[3,1024,128]{2,1,0:T(8,128)(2,1)S(1)} %ready_rows.3.left_ref, bf16[2048,128]{1,0:T(8,128)(2,1)S(1)} %get-tuple-element.29.right_ref, ...), custom_call_target="tpu_custom_call" | custom-call | flops 3221225472 | bytes 786432 | tf_op jit(solution)/shard_map/last_tiles/pallas_call | solution.py:152
  63.8 2.8 %collective-permute-start.11 = (bf16[64,1024]{1,0:T(8,128)(2,1)S(1)}, bf16[64,1024]{1,0:T(8,128)(2,1)S(1)}, u32[]{:S(2)}, u32[]{:S(2)}) collective-permute-start(bf16[64,1024]{1,0:T(8,128)(2,1)S(1)} %get-tuple-element.34), channel_id=1, source_target_pairs={{0,48},{16,0},{32,16},{48,32},{1,49},{17,1},{33,17},{49,33},{2,50}... | collective-permute-start | bytes 393224 | tf_op jit(solution)/shard_map/ppermute | solution.py:226
  66.7 1.5 %collective-permute-start.13 = (bf16[64,1024]{1,0:T(8,128)(2,1)S(1)}, bf16[64,1024]{1,0:T(8,128)(2,1)S(1)}, u32[]{:S(2)}, u32[]{:S(2)}) collective-permute-start(bf16[64,1024]{1,0:T(8,128)(2,1)S(1)} %get-tuple-element.36), channel_id=1, source_target_pairs={{0,32},{16,48},{32,0},{48,16},{1,33},{17,49},{33,1},{49,17},{2,34}... | collective-permute-start | bytes 393224 | tf_op jit(solution)/shard_map/ppermute | solution.py:226
  68.2 6.6 %own_tiles.1.before_ref = f32[64,1024]{1,0:T(8,128)S(1)} custom-call(f32[2]{0:T(128)S(1)} %pad_maximum_fusion.2.amp_ref, bf16[1,1024,128]{2,1,0:T(8,128)(2,1)S(1)} %ready_rows.2.left_ref, bf16[1024,128]{1,0:T(8,128)(2,1)S(1)} %get-tuple-element.26.right_ref.refs_0_, bf16[64,1024]{1,0:T(8,128)(2,1)S(1)} %get-tuple-element.27.vectors_ref.refs_1_, ...), custom_call_target="tpu_custom_call" | custom-call | flops 3221225472 | bytes 2359296 | tf_op jit(solution)/shard_map/own_tiles/pallas_call | solution.py:177
  74.8 1.4 %collective-permute-done.12.refs_1_ = bf16[64,1024]{1,0:T(8,128)(2,1)S(1)} collective-permute-done((bf16[64,1024]{1,0:T(8,128)(2,1)S(1)}, bf16[64,1024]{1,0:T(8,128)(2,1)S(1)}, u32[]{:S(2)}, u32[]{:S(2)}) %collective-permute-start.12) | collective-permute-done | bytes 131104 | tf_op jit(solution)/shard_map/ppermute | solution.py:226
  76.3 2.8 %own_last.1 = (f32[32,1024]{1,0:T(8,128)S(1)}, bf16[32,1024]{1,0:T(8,128)(2,1)S(1)}) custom-call(f32[2]{0:T(128)S(1)} %pad_maximum_fusion.2.amp_ref, bf16[1,1024,128]{2,1,0:T(8,128)(2,1)S(1)} %ready_rows.2.left_ref, bf16[2048,128]{1,0:T(8,128)(2,1)S(1)} %get-tuple-element.29.right_ref, bf16[64,2048]{1,0:T(8,128)(2,1)S(1)} %get-tuple-element.30.vectors_ref, ...), custom_call_target="tpu_custom_call" | custom-call | flops 1073741824 | bytes 786432 | tf_op jit(solution)/shard_map/own_last/pallas_call | solution.py:206
  79.1 1.8 %collective-permute-start.14 = (bf16[32,1024]{1,0:T(8,128)(2,1)S(1)}, bf16[32,1024]{1,0:T(8,128)(2,1)S(1)}, u32[]{:S(2)}, u32[]{:S(2)}) collective-permute-start(bf16[32,1024]{1,0:T(8,128)(2,1)S(1)} %get-tuple-element.38), channel_id=1, source_target_pairs={{0,1},{1,0},{2,3},{3,2},{4,5},{5,4},{6,7},{7,6},{8,9},{9,8},{10,11... | collective-permute-start | bytes 196616 | tf_op jit(solution)/shard_map/ppermute | solution.py:226
  81.6 1.9 %collective-permute-done.14 = bf16[32,1024]{1,0:T(8,128)(2,1)S(1)} collective-permute-done((bf16[32,1024]{1,0:T(8,128)(2,1)S(1)}, bf16[32,1024]{1,0:T(8,128)(2,1)S(1)}, u32[]{:S(2)}, u32[]{:S(2)}) %collective-permute-start.14) | collective-permute-done | bytes 65568 | tf_op jit(solution)/shard_map/ppermute | solution.py:226
  83.5 0.7 bitcast_add_fusion
  (34 shorter events, 2.7 us)
Async XLA Ops:
  0.8 0.8 copy-start.1
  1.8 0.7 copy-start.2
  2.7 5.6 %collective-permute-start = (bf16[96,512]{0,1:T(8,128)(2,1)S(1)}, bf16[96,512]{0,1:T(8,128)(2,1)S(1)}, u32[]{:S(2)}, u32[]{:S(2)}) collective-permute-start(bf16[96,512]{0,1:T(8,128)(2,1)S(1)} %pad_maximum_fusion.1), channel_id=1, source_target_pairs={{0,1},{1,0},{2,3},{3,2},{4,5},{5,4},{6,7},{7,6},{8,9},{9,8},{10,11... | collective-permute-start | bytes 294920 | tf_op jit(solution)/shard_map/ppermute | solution.py:226
  8.9 8.7 %collective-permute-start.3 = (bf16[512,128]{1,0:T(8,128)(2,1)S(1)}, bf16[512,128]{1,0:T(8,128)(2,1)S(1)}, u32[]{:S(2)}, u32[]{:S(2)}) collective-permute-start(bf16[512,128]{1,0:T(8,128)(2,1)S(1)} %maximum_bitcast_fusion.1.refs_0_), channel_id=1, source_target_pairs={{0,8},{4,12},{8,0},{12,4},{1,9},{5,13},{9,1},{13,5},{2,10},{6,14},... | collective-permute-start | bytes 393224 | tf_op jit(solution)/shard_map/ppermute | solution.py:226
  12.2 6.2 %collective-permute-start.4 = (bf16[512,128]{1,0:T(8,128)(2,1)S(1)}, bf16[512,128]{1,0:T(8,128)(2,1)S(1)}, u32[]{:S(2)}, u32[]{:S(2)}) collective-permute-start(bf16[512,128]{1,0:T(8,128)(2,1)S(1)} %maximum_bitcast_fusion.refs_0_), channel_id=1, source_target_pairs={{0,16},{16,32},{32,48},{48,0},{1,17},{17,33},{33,49},{49,1},{2,18}... | collective-permute-start | bytes 393224 | tf_op jit(solution)/shard_map/ppermute | solution.py:226
  13.7 6.2 %collective-permute-start.1 = (bf16[512,128]{1,0:T(8,128)(2,1)S(1)}, bf16[512,128]{1,0:T(8,128)(2,1)S(1)}, u32[]{:S(2)}, u32[]{:S(2)}) collective-permute-start(bf16[512,128]{1,0:T(8,128)(2,1)S(1)} %maximum_bitcast_fusion.1.refs_0_), channel_id=1, source_target_pairs={{0,4},{4,8},{8,12},{12,0},{1,5},{5,9},{9,13},{13,1},{2,6},{6,10},{... | collective-permute-start | bytes 393224 | tf_op jit(solution)/shard_map/ppermute | solution.py:226
  14.4 5.5 %collective-permute-start.2 = (bf16[512,128]{1,0:T(8,128)(2,1)S(1)}, bf16[512,128]{1,0:T(8,128)(2,1)S(1)}, u32[]{:S(2)}, u32[]{:S(2)}) collective-permute-start(bf16[512,128]{1,0:T(8,128)(2,1)S(1)} %maximum_bitcast_fusion.1.refs_0_), channel_id=1, source_target_pairs={{0,12},{4,0},{8,4},{12,8},{1,13},{5,1},{9,5},{13,9},{2,14},{6,2},{... | collective-permute-start | bytes 393224 | tf_op jit(solution)/shard_map/ppermute | solution.py:226
  20.0 15.1 %collective-permute-start.8 = (bf16[1536,128]{1,0:T(8,128)(2,1)S(1)}, bf16[1536,128]{1,0:T(8,128)(2,1)S(1)}, u32[]{:S(2)}, u32[]{:S(2)}) collective-permute-start(bf16[1536,128]{1,0:T(8,128)(2,1)S(1)} %constant_dynamic-update-slice_fusion.refs_0_), channel_id=1, source_target_pairs={{0,2},{2,0},{1,3},{3,1},{4,6},{6,4},{5,7},{7,5},{8,10},{10,8},{9,1... | collective-permute-start | bytes 1179656 | tf_op jit(solution)/shard_map/ppermute | solution.py:226
  20.1 7.9 %collective-permute-start.9 = (bf16[512,128]{1,0:T(8,128)(2,1)S(1)}, bf16[512,128]{1,0:T(8,128)(2,1)S(1)}, u32[]{:S(2)}, u32[]{:S(2)}) collective-permute-start(bf16[512,128]{1,0:T(8,128)(2,1)S(1)} %maximum_bitcast_fusion.1.refs_0_), channel_id=1, source_target_pairs={{0,2},{2,0},{1,3},{3,1},{4,6},{6,4},{5,7},{7,5},{8,10},{10,8},{9,1... | collective-permute-start | bytes 393224 | tf_op jit(solution)/shard_map/ppermute | solution.py:226
  20.6 7.8 %collective-permute-start.6 = (bf16[512,128]{1,0:T(8,128)(2,1)S(1)}, bf16[512,128]{1,0:T(8,128)(2,1)S(1)}, u32[]{:S(2)}, u32[]{:S(2)}) collective-permute-start(bf16[512,128]{1,0:T(8,128)(2,1)S(1)} %maximum_bitcast_fusion.refs_0_), channel_id=1, source_target_pairs={{0,48},{16,0},{32,16},{48,32},{1,49},{17,1},{33,17},{49,33},{2,50}... | collective-permute-start | bytes 393224 | tf_op jit(solution)/shard_map/ppermute | solution.py:226
  22.4 6.7 %collective-permute-start.7 = (bf16[512,128]{1,0:T(8,128)(2,1)S(1)}, bf16[512,128]{1,0:T(8,128)(2,1)S(1)}, u32[]{:S(2)}, u32[]{:S(2)}) collective-permute-start(bf16[512,128]{1,0:T(8,128)(2,1)S(1)} %maximum_bitcast_fusion.refs_0_), channel_id=1, source_target_pairs={{0,32},{16,48},{32,0},{48,16},{1,33},{17,49},{33,1},{49,17},{2,34}... | collective-permute-start | bytes 393224 | tf_op jit(solution)/shard_map/ppermute | solution.py:226
  24.2 22.1 %collective-permute-start.5 = (bf16[2048,128]{1,0:T(8,128)(2,1)S(1)}, bf16[2048,128]{1,0:T(8,128)(2,1)S(1)}, u32[]{:S(2)}, u32[]{:S(2)}) collective-permute-start(bf16[2048,128]{1,0:T(8,128)(2,1)S(1)} %pad_maximum_fusion), channel_id=1, source_target_pairs={{0,64},{64,0},{1,65},{65,1},{2,66},{66,2},{3,67},{67,3},{4,68},{68... | collective-permute-start | bytes 1572872 | tf_op jit(solution)/shard_map/ppermute | solution.py:226
  46.3 9.2 %collective-permute-start.10 = (bf16[2048,128]{1,0:T(8,128)(2,1)S(1)}, bf16[2048,128]{1,0:T(8,128)(2,1)S(1)}, u32[]{:S(2)}, u32[]{:S(2)}) collective-permute-start(bf16[2048,128]{1,0:T(8,128)(2,1)S(1)} %collective-permute-done.5.refs_0_), channel_id=1, source_target_pairs={{0,2},{2,0},{1,3},{3,1},{4,6},{6,4},{5,7},{7,5},{8,10},{10,8},{9,1... | collective-permute-start | bytes 1572872 | tf_op jit(solution)/shard_map/ppermute | solution.py:226
  63.8 11.0 %collective-permute-start.11 = (bf16[64,1024]{1,0:T(8,128)(2,1)S(1)}, bf16[64,1024]{1,0:T(8,128)(2,1)S(1)}, u32[]{:S(2)}, u32[]{:S(2)}) collective-permute-start(bf16[64,1024]{1,0:T(8,128)(2,1)S(1)} %get-tuple-element.34), channel_id=1, source_target_pairs={{0,48},{16,0},{32,16},{48,32},{1,49},{17,1},{33,17},{49,33},{2,50}... | collective-permute-start | bytes 393224 | tf_op jit(solution)/shard_map/ppermute | solution.py:226
  66.7 9.6 %collective-permute-start.12 = (bf16[64,1024]{1,0:T(8,128)(2,1)S(1)}, bf16[64,1024]{1,0:T(8,128)(2,1)S(1)}, u32[]{:S(2)}, u32[]{:S(2)}) collective-permute-start(bf16[64,1024]{1,0:T(8,128)(2,1)S(1)} %get-tuple-element.35), channel_id=1, source_target_pairs={{0,16},{16,32},{32,48},{48,0},{1,17},{17,33},{33,49},{49,1},{2,18}... | collective-permute-start | bytes 393224 | tf_op jit(solution)/shard_map/ppermute | solution.py:226
  66.7 9.6 %collective-permute-start.13 = (bf16[64,1024]{1,0:T(8,128)(2,1)S(1)}, bf16[64,1024]{1,0:T(8,128)(2,1)S(1)}, u32[]{:S(2)}, u32[]{:S(2)}) collective-permute-start(bf16[64,1024]{1,0:T(8,128)(2,1)S(1)} %get-tuple-element.36), channel_id=1, source_target_pairs={{0,32},{16,48},{32,0},{48,16},{1,33},{17,49},{33,1},{49,17},{2,34}... | collective-permute-start | bytes 393224 | tf_op jit(solution)/shard_map/ppermute | solution.py:226
  74.8 8.6 %copy-start = (bf16[1024,32]{0,1:T(8,128)(2,1)S(1)}, bf16[1024,32]{0,1:T(8,128)(2,1)}, u32[]{:S(2)}) copy-start(bf16[1024,32]{0,1:T(8,128)(2,1)} %param.6) | copy-start | bytes 196612
  79.1 4.3 %collective-permute-start.14 = (bf16[32,1024]{1,0:T(8,128)(2,1)S(1)}, bf16[32,1024]{1,0:T(8,128)(2,1)S(1)}, u32[]{:S(2)}, u32[]{:S(2)}) collective-permute-start(bf16[32,1024]{1,0:T(8,128)(2,1)S(1)} %get-tuple-element.38), channel_id=1, source_target_pairs={{0,1},{1,0},{2,3},{3,2},{4,5},{5,4},{6,7},{7,6},{8,9},{9,8},{10,11... | collective-permute-start | bytes 196616 | tf_op jit(solution)/shard_map/ppermute | solution.py:226

commit v4 on v3

v4 whole, which is shorter than its diff:
```python
import jax
import jax.numpy as jnp
from jax import lax
from jax.experimental import pallas as pl
from jax.experimental.pallas import tpu as pltpu
from jax.sharding import Mesh, PartitionSpec as P

SIZES = (2, 4, 4, 2, 2)
NAMES = ("zh", "x", "y", "c", "zl")
BLK = ("zh", "x", "y", "c")
TM = 512
TN = 1024
F32 = jnp.float32
BF16 = jnp.bfloat16
PARAMS = pltpu.CompilerParams(vmem_limit_bytes=48 << 20)


def three_parts(wide):
    hi = wide.astype(BF16).astype(F32)
    mid = (wide - hi).astype(BF16).astype(F32)
    return hi, mid, wide - hi - mid


def with_norms(wide, offset, first, other):
    lane = lax.broadcasted_iota(jnp.int32, wide.shape, 1)
    wide = jnp.where(lane < 64, wide, 0.0)
    half = offset - 0.5 * jnp.sum(wide * wide, axis=1, keepdims=True)
    hi, mid, low = three_parts(half)
    ones = (lane >= other) & (lane < other + 3)
    wide = jnp.where(ones, 1.0, wide)
    wide = jnp.where(lane == first, hi, wide)
    wide = jnp.where(lane == first + 1, mid, wide)
    wide = jnp.where(lane == first + 2, low, wide)
    return wide.astype(BF16)


def ready_rows(amp, blocks):
    count = len(blocks)

    def body(amp_ref, *refs):
        out_ref = refs[count]
        for k in range(count):
            wide = refs[k][...].astype(F32)
            out_ref[k, :512] = with_norms(wide, amp_ref[1], 67, 64)
            out_ref[k, 512:] = with_norms(pltpu.roll(wide, 64, 1), amp_ref[1], 67, 64)

    return pl.pallas_call(
        body,
        out_shape=jax.ShapeDtypeStruct((count, 1024, 128), BF16),
        in_specs=[pl.BlockSpec(memory_space=pltpu.SMEM)]
        + [pl.BlockSpec(memory_space=pltpu.VMEM)] * count,
        out_specs=pl.BlockSpec(memory_space=pltpu.VMEM),
        compiler_params=PARAMS,
        name="ready_rows",
    )(amp, *blocks)


def first_pack(zl, points, vectors, lengthscale):
    def body(zl_ref, points_ref, vectors_ref, length_ref, out_ref):
        at = zl_ref[0]
        lane = lax.broadcasted_iota(jnp.int32, (32, 64), 1)
        row = lax.broadcasted_iota(jnp.int32, (32, 64), 0)
        column = jnp.sum(jnp.where(lane == row + 32 * at, length_ref[...], 0.0), axis=1, keepdims=True)
        scaled = (points_ref[...].astype(F32) / column).astype(BF16)
        out_ref[:32] = scaled[:, :512]
        out_ref[32:64] = scaled[:, 512:]
        given = vectors_ref[...].astype(F32)
        out_ref[64:] = jnp.where(at == 0, given[:, 512:], given[:, :512]).astype(BF16)

    return pl.pallas_call(
        body,
        out_shape=jax.ShapeDtypeStruct((96, 512), BF16),
        in_specs=[
            pl.BlockSpec(memory_space=pltpu.SMEM),
            pl.BlockSpec((32, 1024), lambda i: (0, 0)),
            pl.BlockSpec((32, 1024), lambda i: (0, 0)),
            pl.BlockSpec((1, 64), lambda i: (0, 0)),
        ],
        grid=(1,),
        out_specs=pl.BlockSpec((96, 512), lambda i: (0, 0)),
        compiler_params=PARAMS,
        name="first_pack",
    )(zl, points, vectors, lengthscale.reshape(1, 64))


def second_pack(zl, given, got, vectors):
    def body(zl_ref, given_ref, got_ref, vectors_ref, rows_ref, share_ref):
        first = zl_ref[0] == 0
        mine = given_ref[...].astype(F32)
        theirs = got_ref[...].astype(F32)
        both = vectors_ref[...].astype(F32)
        whole = jnp.concatenate([mine[:32], theirs[:32], mine[32:64], theirs[32:64]], axis=0)
        rows_ref[...] = whole.T.astype(BF16)
        picked = jnp.concatenate(
            [
                jnp.where(first, whole[:64], whole[64:]),
                jnp.where(first, both[:, :512], both[:, 512:]),
                theirs[64:],
            ],
            axis=0,
        )
        share_ref[...] = picked.T.astype(BF16)

    packed = jax.ShapeDtypeStruct((512, 128), BF16)
    return pl.pallas_call(
        body,
        out_shape=(packed, packed),
        in_specs=[pl.BlockSpec(memory_space=pltpu.SMEM)] + [pl.BlockSpec(memory_space=pltpu.VMEM)] * 3,
        out_specs=(pl.BlockSpec(memory_space=pltpu.VMEM),) * 2,
        compiler_params=PARAMS,
        name="second_pack",
    )(zl, given, got, vectors)


def one_block(amp_ref, left, right, vectors, top):
    exponent = lax.dot_general(right, left, (((1,), (1,)), ((), ())), preferred_element_type=F32)
    block = jnp.minimum(jnp.exp(exponent).astype(BF16), top)
    return jnp.dot(vectors, block, preferred_element_type=F32)


def amplitude(amp_ref):
    return jnp.full((1, 1), amp_ref[0], F32).astype(BF16)


def tile_sum(amp_ref, left, pairs):
    top = amplitude(amp_ref)
    result = jnp.zeros((64, left.shape[0]), F32)
    for right_ref, vectors_ref in pairs:
        for at in range(0, right_ref.shape[0], TN):
            result += one_block(
                amp_ref, left, right_ref[at : at + TN, :], vectors_ref[:, at : at + TN], top
            )
    return result


def raw_sum(amp_ref, left, raw_refs, right_ref, vectors_ref):
    top = amplitude(amp_ref)
    result = jnp.zeros((64, left.shape[0]), F32)
    at = 0
    for ref in raw_refs:
        for sub in range(0, ref.shape[0], 512):
            wide = ref[sub : sub + 512, :].astype(F32)
            right_ref[at : at + 512, :] = with_norms(wide, 0.0, 64, 67)
            vectors_ref[:, at : at + 512] = wide.T[64:, :].astype(BF16)
            at += 512
            if at % TN == 0:
                back = at - TN
                result += one_block(
                    amp_ref, left, right_ref[back:at, :], vectors_ref[:, back:at], top
                )
    return result


SCALE = 512


def cost(rows, cols):
    return pl.CostEstimate(flops=rows * cols * SCALE, transcendentals=0, bytes_accessed=cols * 384)


def add_tiles(amp, left, raws, before, narrow):
    count = left.shape[0]
    total = sum(raw.shape[0] for raw in raws)
    per = 1024 // TM
    old = [] if before is None else [before]
    sums = count if narrow else 1

    def body(amp_ref, left_ref, *refs):
        raw_refs = refs[: len(raws)]
        before_refs = refs[len(raws) : len(raws) + len(old)]
        sum_refs = refs[len(raws) + len(old) : len(raws) + len(old) + sums]
        right_ref, vectors_ref = refs[-2:]
        step = pl.program_id(0)

        def put(value):
            if before_refs:
                value += before_refs[0][0]
            if not narrow:
                sum_refs[0][0] = value
                return
            for k in range(count):

                @pl.when(step // per == k)
                def _():
                    sum_refs[k][...] = value.astype(BF16)

        @pl.when(step == 0)
        def _():
            put(raw_sum(amp_ref, left_ref[0], raw_refs, right_ref, vectors_ref))

        @pl.when(step > 0)
        def _():
            put(tile_sum(amp_ref, left_ref[0], [(right_ref, vectors_ref)]))

    def place(k):
        return pl.BlockSpec((64, TM), lambda i: (0, jnp.clip(i - k * per, 0, per - 1)))

    acc_spec = pl.BlockSpec((1, 64, TM), lambda i: (i // per, 0, i % per))
    if narrow:
        sum_shapes = [jax.ShapeDtypeStruct((64, 1024), BF16)] * count
        sum_specs = [place(k) for k in range(count)]
    else:
        sum_shapes = [jax.ShapeDtypeStruct((count, 64, 1024), F32)]
        sum_specs = [acc_spec]
    out = pl.pallas_call(
        body,
        grid=(count * per,),
        out_shape=sum_shapes
        + [jax.ShapeDtypeStruct((total, 128), BF16), jax.ShapeDtypeStruct((64, total), BF16)],
        in_specs=[
            pl.BlockSpec(memory_space=pltpu.SMEM),
            pl.BlockSpec((1, TM, 128), lambda i: (i // per, i % per, 0)),
        ]
        + [pl.BlockSpec(raw.shape, lambda i: (0, 0)) for raw in raws]
        + [acc_spec] * len(old),
        out_specs=sum_specs
        + [pl.BlockSpec((total, 128), lambda i: (0, 0)), pl.BlockSpec((64, total), lambda i: (0, 0))],
        compiler_params=PARAMS,
        cost_estimate=cost(1024 * count, total),
        name="add_tiles",
    )(amp, left, *raws, *old)
    return out[:sums], tuple(out[sums:])


def own_tiles(amp, left, ready):
    flat = [part for pair in ready for part in pair]

    def body(amp_ref, left_ref, *refs):
        pairs = [(refs[2 * k], refs[2 * k + 1]) for k in range(len(ready))]
        refs[-1][...] = tile_sum(amp_ref, left_ref[0], pairs)

    return pl.pallas_call(
        body,
        grid=(1024 // TM,),
        out_shape=jax.ShapeDtypeStruct((64, 1024), F32),
        in_specs=[
            pl.BlockSpec(memory_space=pltpu.SMEM),
            pl.BlockSpec((1, TM, 128), lambda i: (0, i, 0)),
        ]
        + [pl.BlockSpec(part.shape, lambda i: (0, 0)) for part in flat],
        out_specs=pl.BlockSpec((64, TM), lambda i: (0, i)),
        compiler_params=PARAMS,
        cost_estimate=cost(1024, sum(right.shape[0] for right, _ in ready)),
        name="own_tiles",
    )(amp, left, *flat)


def own_last(amp, left, right, vectors, before, arrived):
    count = len(arrived)
    total = right.shape[0]

    def body(amp_ref, left_ref, right_ref, vectors_ref, before_ref, *refs):
        mine_ref, theirs_ref = refs[count:]
        value = tile_sum(amp_ref, left_ref[0], [(right_ref, vectors_ref)]) + before_ref[...]
        for ref in refs[:count]:
            value += ref[...].astype(F32)
        mine_ref[...] = value[:32]
        theirs_ref[...] = value[32:]

    out_spec = pl.BlockSpec((32, TM), lambda i: (0, i))
    return pl.pallas_call(
        body,
        grid=(1024 // TM,),
        out_shape=(jax.ShapeDtypeStruct((32, 1024), F32), jax.ShapeDtypeStruct((32, 1024), F32)),
        in_specs=[
            pl.BlockSpec(memory_space=pltpu.SMEM),
            pl.BlockSpec((1, TM, 128), lambda i: (0, i, 0)),
            pl.BlockSpec((total, 128), lambda i: (0, 0)),
            pl.BlockSpec((64, total), lambda i: (0, 0)),
        ]
        + [pl.BlockSpec((64, TM), lambda i: (0, i))] * (count + 1),
        out_specs=(out_spec, out_spec),
        compiler_params=PARAMS,
        cost_estimate=cost(1024, total),
        name="own_last",
    )(amp, left, right, vectors, before, *arrived)


def shift(value, axis, by):
    size = SIZES[NAMES.index(axis)]
    return lax.ppermute(value, axis, [(i, (i + by) % size) for i in range(size)])


def per_device(points, vectors, lengthscale, outscale, noise):
    zl = lax.axis_index("zl").astype(jnp.int32).reshape(1)
    amp = jnp.concatenate([outscale, jnp.log(outscale)])

    given = first_pack(zl, points.T, vectors.T, lengthscale)
    got = shift(given, "zl", 1)
    rows, share = second_pack(zl, given, got, vectors.T)

    near = [shift(share, "y", by) for by in (1, -1, 2)]
    rows_in = [shift(rows, "x", by) for by in (1, -1, 2)]
    beside = shift(share, "c", 1)
    near[2], rows_in[0] = lax.optimization_barrier((near[2], rows_in[0]))
    near = jnp.concatenate(near, axis=0)
    near_beside = shift(near, "c", 1)
    far = shift(jnp.concatenate([share, near], axis=0), "zh", 1)

    own_left = ready_rows(amp, [rows])
    left = ready_rows(amp, rows_in)
    (acc,), ready0 = add_tiles(amp, left, [share, beside], None, False)
    (acc,), ready1 = add_tiles(amp, left, [near, near_beside], acc, False)
    far, acc = lax.optimization_barrier((far, acc))
    far_beside = shift(far, "c", 1)
    (acc,), ready2 = add_tiles(amp, left, [far], acc, False)
    sent, ready3 = add_tiles(amp, left, [far_beside], acc, True)
    arrived = [shift(part, "x", by) for part, by in zip(sent, (-1, 1, 2))]
    own = own_tiles(amp, own_left, [ready0, ready1, ready2])
    mine, theirs = own_last(amp, own_left, *ready3, own, arrived)
    mine = mine + shift(theirs, "zl", 1)
    return mine.T + noise[0] * vectors.astype(F32)


def solution(mesh):
    fine = Mesh(mesh.devices.reshape(SIZES), NAMES)
    placed = (P(BLK, "zl"), P(BLK, "zl"), P(), P(), P())
    return jax.shard_map(
        per_device, mesh=fine, in_specs=placed, out_specs=P(BLK, "zl"), check_vma=False
    )
```

time: 84.5 us -> 83.2 us (0.985)
    pallas_call x8 -> x6, Pallas kernels: 32.3 us -> 31.7 us  [the longest x4 31.5 us: add_tiles(): pl.pallas_call(body, grid=(count * per,), out_shape=sum_shapes + [jax.Sha...]
  transfers between devices with their start and end apart: 15 -> 15, of which waited for: 6 -> 7; matrix products, arithmetic and copies ran while one was open for 0% -> 0% of each run, Pallas kernels for 39% -> 39%
where the time goes in v4:
time: 83.2 us; the launch traced here: 82.8 us
  Pallas kernels  43.5 us (52%)
  starting transfers between devices  24.2 us (29%)
  waiting for transfers between devices  10.4 us (12%)
  local copies, waits for them, and re-layouts  2.38 us (3%)
  between operations  1.53 us (2%)
    pallas_call x4, Pallas kernels, add_tiles(): pl.pallas_call(body, grid=(count * per,), out_shape=sum_shapes + [jax.Sha...  31.5 us
    ppermute x15, starting transfers between devices, shift(): lax.ppermute(value, axis, [(i, (i + by) % size) for i in range(size)])  24.2 us
    ppermute x15, waiting for transfers between devices, shift(): lax.ppermute(value, axis, [(i, (i + by) % size) for i in range(size)])  10.4 us
    pallas_call x1, Pallas kernels, own_tiles(): pl.pallas_call(body, grid=(1024 // TM,), out_shape=jax.ShapeDtypeStruct((...  6.6 us
    pallas_call x1, Pallas kernels, own_last(): pl.pallas_call(body, grid=(1024 // TM,), out_shape=(jax.ShapeDtypeStruct(...  2.81 us
    pallas_call x2, Pallas kernels, ready_rows(): pl.pallas_call(body, out_shape=jax.ShapeDtypeStruct((count, 1024, 128), B...  2.37 us
    unnamed x10, local copies, waits for them, and re-layouts  2.37 us
  transfers between devices with their start and end apart: 15, of which 7 were waited for; matrix products, arithmetic and copies ran while one was open for 0% of the time, Pallas kernels for 39%

profile of v4, /device:TPU:0, one launch (start us, length us, event | category | flops | bytes accessed | tf_op | source)
XLA Modules:
  0.0 82.8 jit_solution(2475475044261997914)
XLA Ops:
  0.0 0.7 copy-done.3
  0.7 0.8 %copy-done = bf16[1024,32]{0,1:T(8,128)(2,1)S(1)} copy-done((bf16[1024,32]{0,1:T(8,128)(2,1)S(1)}, bf16[1024,32]{0,1:T(8,128)(2,1)}, u32[]{:S(2)}) %copy-start) | copy-done | bytes 65560
  1.5 0.8 %copy-done.2 = bf16[1024,32]{0,1:T(8,128)(2,1)S(1)} copy-done((bf16[1024,32]{0,1:T(8,128)(2,1)S(1)}, bf16[1024,32]{0,1:T(8,128)(2,1)}, u32[]{:S(2)}) %copy-start.2) | copy-done | bytes 65560
  2.4 2.1 %collective-permute-start = (bf16[96,512]{1,0:T(8,128)(2,1)S(1)}, bf16[96,512]{1,0:T(8,128)(2,1)S(1)}, u32[]{:S(2)}, u32[]{:S(2)}) collective-permute-start(bf16[96,512]{1,0:T(8,128)(2,1)S(1)} %first_pack.1.given_ref), channel_id=1, source_target_pairs={{0,1},{1,0},{2,3},{3,2},{4,5},{5,4},{6,7},{7,6},{8,9},{9,8},{10,11... | collective-permute-start | bytes 294920 | tf_op jit(solution)/shard_map/ppermute | solution.py:281
  4.5 2.8 %collective-permute-done.got_ref = bf16[96,512]{1,0:T(8,128)(2,1)S(1)} collective-permute-done((bf16[96,512]{1,0:T(8,128)(2,1)S(1)}, bf16[96,512]{1,0:T(8,128)(2,1)S(1)}, u32[]{:S(2)}, u32[]{:S(2)}) %collective-permute-start) | collective-permute-done | bytes 98336 | tf_op jit(solution)/shard_map/ppermute | solution.py:281
  7.3 0.1 second_pack.1
  7.5 3.3 %collective-permute-start.1 = (bf16[512,128]{1,0:T(8,128)(2,1)S(1)}, bf16[512,128]{1,0:T(8,128)(2,1)S(1)}, u32[]{:S(2)}, u32[]{:S(2)}) collective-permute-start(bf16[512,128]{1,0:T(8,128)(2,1)S(1)} %get-tuple-element.28.refs_0_), channel_id=1, source_target_pairs={{0,8},{4,12},{8,0},{12,4},{1,9},{5,13},{9,1},{13,5},{2,10},{6,14},... | collective-permute-start | bytes 393224 | tf_op jit(solution)/shard_map/ppermute | solution.py:281
  10.7 1.5 %collective-permute-start.2 = (bf16[512,128]{1,0:T(8,128)(2,1)S(1)}, bf16[512,128]{1,0:T(8,128)(2,1)S(1)}, u32[]{:S(2)}, u32[]{:S(2)}) collective-permute-start(bf16[512,128]{1,0:T(8,128)(2,1)S(1)} %get-tuple-element.27.refs_0_), channel_id=1, source_target_pairs={{0,16},{16,32},{32,48},{48,0},{1,17},{17,33},{33,49},{49,1},{2,18}... | collective-permute-start | bytes 393224 | tf_op jit(solution)/shard_map/ppermute | solution.py:281
  12.2 0.7 collective-permute-start.5
  12.9 2.6 %collective-permute-start.6 = (bf16[512,128]{1,0:T(8,128)(2,1)S(1)}, bf16[512,128]{1,0:T(8,128)(2,1)S(1)}, u32[]{:S(2)}, u32[]{:S(2)}) collective-permute-start(bf16[512,128]{1,0:T(8,128)(2,1)S(1)} %get-tuple-element.28.refs_0_), channel_id=1, source_target_pairs={{0,12},{4,0},{8,4},{12,8},{1,13},{5,1},{9,5},{13,9},{2,14},{6,2},{... | collective-permute-start | bytes 393224 | tf_op jit(solution)/shard_map/ppermute | solution.py:281
  16.2 0.7 collective-permute-done.2.refs_0_
  16.9 1.5 %collective-permute-done.5 = bf16[512,128]{1,0:T(8,128)(2,1)S(1)} collective-permute-done((bf16[512,128]{1,0:T(8,128)(2,1)S(1)}, bf16[512,128]{1,0:T(8,128)(2,1)S(1)}, u32[]{:S(2)}, u32[]{:S(2)}) %collective-permute-start.5) | collective-permute-done | bytes 131104 | tf_op jit(solution)/shard_map/ppermute | solution.py:281
  18.7 1.8 %collective-permute-start.3 = (bf16[512,128]{1,0:T(8,128)(2,1)S(1)}, bf16[512,128]{1,0:T(8,128)(2,1)S(1)}, u32[]{:S(2)}, u32[]{:S(2)}) collective-permute-start(bf16[512,128]{1,0:T(8,128)(2,1)S(1)} %get-tuple-element.27.refs_0_), channel_id=1, source_target_pairs={{0,48},{16,0},{32,16},{48,32},{1,49},{17,1},{33,17},{49,33},{2,50}... | collective-permute-start | bytes 393224 | tf_op jit(solution)/shard_map/ppermute | solution.py:281
  20.4 1.8 %collective-permute-start.4 = (bf16[512,128]{1,0:T(8,128)(2,1)S(1)}, bf16[512,128]{1,0:T(8,128)(2,1)S(1)}, u32[]{:S(2)}, u32[]{:S(2)}) collective-permute-start(bf16[512,128]{1,0:T(8,128)(2,1)S(1)} %get-tuple-element.27.refs_0_), channel_id=1, source_target_pairs={{0,32},{16,48},{32,0},{48,16},{1,33},{17,49},{33,1},{49,17},{2,34}... | collective-permute-start | bytes 393224 | tf_op jit(solution)/shard_map/ppermute | solution.py:281
  22.3 3.9 %collective-permute-start.7 = (bf16[2048,128]{1,0:T(8,128)(2,1)S(1)}, bf16[2048,128]{1,0:T(8,128)(2,1)S(1)}, u32[]{:S(2)}, u32[]{:S(2)}) collective-permute-start(bf16[2048,128]{1,0:T(8,128)(2,1)S(1)} %pad_maximum_fusion), channel_id=1, source_target_pairs={{0,64},{64,0},{1,65},{65,1},{2,66},{66,2},{3,67},{67,3},{4,68},{68... | collective-permute-start | bytes 1572872 | tf_op jit(solution)/shard_map/ppermute | solution.py:281
  26.1 0.5 collective-permute-done.3.refs_1_
  26.6 0.9 %collective-permute-done.4.refs_2_ = bf16[512,128]{1,0:T(8,128)(2,1)S(1)} collective-permute-done((bf16[512,128]{1,0:T(8,128)(2,1)S(1)}, bf16[512,128]{1,0:T(8,128)(2,1)S(1)}, u32[]{:S(2)}, u32[]{:S(2)}) %collective-permute-start.4) | collective-permute-done | bytes 131104 | tf_op jit(solution)/shard_map/ppermute | solution.py:281
  27.5 1.5 %ready_rows.3.left_ref = bf16[3,1024,128]{2,1,0:T(8,128)(2,1)S(1)} custom-call(f32[2]{0:T(128)S(1)} %pad_maximum_fusion.1.amp_ref, bf16[512,128]{1,0:T(8,128)(2,1)S(1)} %collective-permute-done.2.refs_0_, bf16[512,128]{1,0:T(8,128)(2,1)S(1)} %collective-permute-done.3.refs_1_, bf16[512,128]{1,0:T(8,128)(2,1)S(1)} %collective-permute-done.4.refs_2_), custom_call_target="tpu_custom_call" | custom-call | tf_op jit(solution)/shard_map/ready_rows/pallas_call | solution.py:47
  29.0 4.8 %add_tiles.4 = (f32[3,64,1024]{2,1,0:T(8,128)S(1)}, bf16[1024,128]{1,0:T(8,128)(2,1)S(1)}, bf16[64,1024]{1,0:T(8,128)(2,1)S(1)}) custom-call(f32[2]{0:T(128)S(1)} %pad_maximum_fusion.1.amp_ref, bf16[3,1024,128]{2,1,0:T(8,128)(2,1)S(1)} %ready_rows.3.left_ref, bf16[512,128]{1,0:T(8,128)(2,1)S(1)} %get-tuple-element.28.refs_0_, ...), custom_call_target="tpu_custom_call" | custom-call | flops 1610612736 | bytes 393216 | tf_op jit(solution)/shard_map/add_tiles/pallas_call | solution.py:205
  33.8 10.9 %add_tiles.5 = (f32[3,64,1024]{2,1,0:T(8,128)S(1)}, bf16[3072,128]{1,0:T(8,128)(2,1)S(1)}, bf16[64,3072]{1,0:T(8,128)(2,1)S(1)}) custom-call(f32[2]{0:T(128)S(1)} %pad_maximum_fusion.1.amp_ref, bf16[3,1024,128]{2,1,0:T(8,128)(2,1)S(1)} %ready_rows.3.left_ref, bf16[1536,128]{1,0:T(8,128)(2,1)S(1)} %constant_dynamic-update-slice_fusion.refs_0_, ...), custom_call_target="tpu_custom_call" | custom-call | flops 4831838208 | bytes 1179648 | tf_op jit(solution)/shard_map/add_tiles/pallas_call | solution.py:205
  44.7 0.3 collective-permute-start.10
  45.0 0.9 %ready_rows.2.left_ref = bf16[1,1024,128]{2,1,0:T(8,128)(2,1)S(1)} custom-call(f32[2]{0:T(128)S(1)} %pad_maximum_fusion.1.amp_ref, bf16[512,128]{1,0:T(8,128)(2,1)S(1)} %get-tuple-element.27.refs_0_), custom_call_target="tpu_custom_call" | custom-call | tf_op jit(solution)/shard_map/ready_rows/pallas_call | solution.py:47
  45.9 7.8 %add_tiles.6 = (f32[3,64,1024]{2,1,0:T(8,128)S(1)}, bf16[2048,128]{1,0:T(8,128)(2,1)S(1)}, bf16[64,2048]{1,0:T(8,128)(2,1)S(1)}) custom-call(f32[2]{0:T(128)S(1)} %pad_maximum_fusion.1.amp_ref, bf16[3,1024,128]{2,1,0:T(8,128)(2,1)S(1)} %ready_rows.3.left_ref, bf16[2048,128]{1,0:T(8,128)(2,1)S(1)} %collective-permute-done.7.refs_0_, ...), custom_call_target="tpu_custom_call" | custom-call | flops 3221225472 | bytes 786432 | tf_op jit(solution)/shard_map/add_tiles/pallas_call | solution.py:205
  53.7 8.0 %add_tiles.7 = (bf16[64,1024]{1,0:T(8,128)(2,1)S(1)}, bf16[64,1024]{1,0:T(8,128)(2,1)S(1)}, bf16[64,1024]{1,0:T(8,128)(2,1)S(1)}, bf16[2048,128]{1,0:T(8,128)(2,1)S(1)}, bf16[64,2048]{1,0:T(8,128)(2,1)S(1)}) custom-call(f32[2]{0:T(128)S(1)} %pad_maximum_fusion.1.amp_ref, bf16[3,1024,128]{2,1,0:T(8,128)(2,1)S(1)} %ready_rows.3.left_ref, ...), custom_call_target="tpu_custom_call" | custom-call | flops 3221225472 | bytes 786432 | tf_op jit(solution)/shard_map/add_tiles/pallas_call | solution.py:205
  61.8 2.9 %collective-permute-start.11 = (bf16[64,1024]{1,0:T(8,128)(2,1)S(1)}, bf16[64,1024]{1,0:T(8,128)(2,1)S(1)}, u32[]{:S(2)}, u32[]{:S(2)}) collective-permute-start(bf16[64,1024]{1,0:T(8,128)(2,1)S(1)} %get-tuple-element.44), channel_id=1, source_target_pairs={{0,48},{16,0},{32,16},{48,32},{1,49},{17,1},{33,17},{49,33},{2,50}... | collective-permute-start | bytes 393224 | tf_op jit(solution)/shard_map/ppermute | solution.py:281
  64.7 1.5 %collective-permute-start.13 = (bf16[64,1024]{1,0:T(8,128)(2,1)S(1)}, bf16[64,1024]{1,0:T(8,128)(2,1)S(1)}, u32[]{:S(2)}, u32[]{:S(2)}) collective-permute-start(bf16[64,1024]{1,0:T(8,128)(2,1)S(1)} %get-tuple-element.46), channel_id=1, source_target_pairs={{0,32},{16,48},{32,0},{48,16},{1,33},{17,49},{33,1},{49,17},{2,34}... | collective-permute-start | bytes 393224 | tf_op jit(solution)/shard_map/ppermute | solution.py:281
  66.2 6.6 %own_tiles.1.before_ref = f32[64,1024]{1,0:T(8,128)S(1)} custom-call(f32[2]{0:T(128)S(1)} %pad_maximum_fusion.1.amp_ref, bf16[1,1024,128]{2,1,0:T(8,128)(2,1)S(1)} %ready_rows.2.left_ref, bf16[1024,128]{1,0:T(8,128)(2,1)S(1)} %get-tuple-element.38.refs_0_, bf16[64,1024]{1,0:T(8,128)(2,1)S(1)} %get-tuple-element.39.refs_1_, ...), custom_call_target="tpu_custom_call" | custom-call | flops 3221225472 | bytes 2359296 | tf_op jit(solution)/shard_map/own_tiles/pallas_call | solution.py:232
  72.8 1.5 %collective-permute-done.12.refs_1_ = bf16[64,1024]{1,0:T(8,128)(2,1)S(1)} collective-permute-done((bf16[64,1024]{1,0:T(8,128)(2,1)S(1)}, bf16[64,1024]{1,0:T(8,128)(2,1)S(1)}, u32[]{:S(2)}, u32[]{:S(2)}) %collective-permute-start.12) | collective-permute-done | bytes 131104 | tf_op jit(solution)/shard_map/ppermute | solution.py:281
  74.3 2.8 %own_last.1 = (f32[32,1024]{1,0:T(8,128)S(1)}, f32[32,1024]{1,0:T(8,128)S(1)}) custom-call(f32[2]{0:T(128)S(1)} %pad_maximum_fusion.1.amp_ref, bf16[1,1024,128]{2,1,0:T(8,128)(2,1)S(1)} %ready_rows.2.left_ref, bf16[2048,128]{1,0:T(8,128)(2,1)S(1)} %get-tuple-element.36.right_ref, bf16[64,2048]{1,0:T(8,128)(2,1)S(1)} %get-tuple-element.37.vectors_ref, ...), custom_call_target="tpu_custom_call" | custom-call | flops 1073741824 | bytes 786432 | tf_op jit(solution)/shard_map/own_last/pallas_call | solution.py:261
  77.1 1.9 %collective-permute-start.14 = (f32[32,1024]{1,0:T(8,128)S(1)}, f32[32,1024]{1,0:T(8,128)S(1)}, u32[]{:S(2)}, u32[]{:S(2)}) collective-permute-start(f32[32,1024]{1,0:T(8,128)S(1)} %get-tuple-element.48), channel_id=1, source_target_pairs={{0,1},{1,0},{2,3},{3,2},{4,5},{5,4},{6,7},{7,6},{8,9},{9,8},{10,11... | collective-permute-start | bytes 393224 | tf_op jit(solution)/shard_map/ppermute | solution.py:281
  79.7 2.5 %collective-permute-done.14 = f32[32,1024]{1,0:T(8,128)S(1)} collective-permute-done((f32[32,1024]{1,0:T(8,128)S(1)}, f32[32,1024]{1,0:T(8,128)S(1)}, u32[]{:S(2)}, u32[]{:S(2)}) %collective-permute-start.14) | collective-permute-done | bytes 131104 | tf_op jit(solution)/shard_map/ppermute | solution.py:281
  82.2 0.7 bitcast_add_fusion
  (22 shorter events, 0.4 us)
Async XLA Ops:
  0.0 0.7 copy-start.3
  0.7 0.8 %copy-start = (bf16[1024,32]{0,1:T(8,128)(2,1)S(1)}, bf16[1024,32]{0,1:T(8,128)(2,1)}, u32[]{:S(2)}) copy-start(bf16[1024,32]{0,1:T(8,128)(2,1)} %param.6) | copy-start | bytes 196612
  1.5 0.8 %copy-start.2 = (bf16[1024,32]{0,1:T(8,128)(2,1)S(1)}, bf16[1024,32]{0,1:T(8,128)(2,1)}, u32[]{:S(2)}) copy-start(bf16[1024,32]{0,1:T(8,128)(2,1)} %param.5) | copy-start | bytes 196612
  2.3 5.0 %copy-start.1 = (bf16[1024,32]{0,1:T(8,128)(2,1)S(1)}, bf16[1024,32]{0,1:T(8,128)(2,1)}, u32[]{:S(2)}) copy-start(bf16[1024,32]{0,1:T(8,128)(2,1)} %param.6) | copy-start | bytes 196612
  2.4 4.9 %collective-permute-start = (bf16[96,512]{1,0:T(8,128)(2,1)S(1)}, bf16[96,512]{1,0:T(8,128)(2,1)S(1)}, u32[]{:S(2)}, u32[]{:S(2)}) collective-permute-start(bf16[96,512]{1,0:T(8,128)(2,1)S(1)} %first_pack.1.given_ref), channel_id=1, source_target_pairs={{0,1},{1,0},{2,3},{3,2},{4,5},{5,4},{6,7},{7,6},{8,9},{9,8},{10,11... | collective-permute-start | bytes 294920 | tf_op jit(solution)/shard_map/ppermute | solution.py:281
  7.5 8.7 %collective-permute-start.1 = (bf16[512,128]{1,0:T(8,128)(2,1)S(1)}, bf16[512,128]{1,0:T(8,128)(2,1)S(1)}, u32[]{:S(2)}, u32[]{:S(2)}) collective-permute-start(bf16[512,128]{1,0:T(8,128)(2,1)S(1)} %get-tuple-element.28.refs_0_), channel_id=1, source_target_pairs={{0,8},{4,12},{8,0},{12,4},{1,9},{5,13},{9,1},{13,5},{2,10},{6,14},... | collective-permute-start | bytes 393224 | tf_op jit(solution)/shard_map/ppermute | solution.py:281
  10.7 6.2 %collective-permute-start.2 = (bf16[512,128]{1,0:T(8,128)(2,1)S(1)}, bf16[512,128]{1,0:T(8,128)(2,1)S(1)}, u32[]{:S(2)}, u32[]{:S(2)}) collective-permute-start(bf16[512,128]{1,0:T(8,128)(2,1)S(1)} %get-tuple-element.27.refs_0_), channel_id=1, source_target_pairs={{0,16},{16,32},{32,48},{48,0},{1,17},{17,33},{33,49},{49,1},{2,18}... | collective-permute-start | bytes 393224 | tf_op jit(solution)/shard_map/ppermute | solution.py:281
  12.2 6.2 %collective-permute-start.5 = (bf16[512,128]{1,0:T(8,128)(2,1)S(1)}, bf16[512,128]{1,0:T(8,128)(2,1)S(1)}, u32[]{:S(2)}, u32[]{:S(2)}) collective-permute-start(bf16[512,128]{1,0:T(8,128)(2,1)S(1)} %get-tuple-element.28.refs_0_), channel_id=1, source_target_pairs={{0,4},{4,8},{8,12},{12,0},{1,5},{5,9},{9,13},{13,1},{2,6},{6,10},{... | collective-permute-start | bytes 393224 | tf_op jit(solution)/shard_map/ppermute | solution.py:281
  12.9 5.5 %collective-permute-start.6 = (bf16[512,128]{1,0:T(8,128)(2,1)S(1)}, bf16[512,128]{1,0:T(8,128)(2,1)S(1)}, u32[]{:S(2)}, u32[]{:S(2)}) collective-permute-start(bf16[512,128]{1,0:T(8,128)(2,1)S(1)} %get-tuple-element.28.refs_0_), channel_id=1, source_target_pairs={{0,12},{4,0},{8,4},{12,8},{1,13},{5,1},{9,5},{13,9},{2,14},{6,2},{... | collective-permute-start | bytes 393224 | tf_op jit(solution)/shard_map/ppermute | solution.py:281
  18.5 15.3 %collective-permute-start.8 = (bf16[1536,128]{1,0:T(8,128)(2,1)S(1)}, bf16[1536,128]{1,0:T(8,128)(2,1)S(1)}, u32[]{:S(2)}, u32[]{:S(2)}) collective-permute-start(bf16[1536,128]{1,0:T(8,128)(2,1)S(1)} %constant_dynamic-update-slice_fusion.refs_0_), channel_id=1, source_target_pairs={{0,2},{2,0},{1,3},{3,1},{4,6},{6,4},{5,7},{7,5},{8,10},{10,8},{9,1... | collective-permute-start | bytes 1179656 | tf_op jit(solution)/shard_map/ppermute | solution.py:281
  18.7 8.0 %collective-permute-start.3 = (bf16[512,128]{1,0:T(8,128)(2,1)S(1)}, bf16[512,128]{1,0:T(8,128)(2,1)S(1)}, u32[]{:S(2)}, u32[]{:S(2)}) collective-permute-start(bf16[512,128]{1,0:T(8,128)(2,1)S(1)} %get-tuple-element.27.refs_0_), channel_id=1, source_target_pairs={{0,48},{16,0},{32,16},{48,32},{1,49},{17,1},{33,17},{49,33},{2,50}... | collective-permute-start | bytes 393224 | tf_op jit(solution)/shard_map/ppermute | solution.py:281
  20.4 7.1 %collective-permute-start.4 = (bf16[512,128]{1,0:T(8,128)(2,1)S(1)}, bf16[512,128]{1,0:T(8,128)(2,1)S(1)}, u32[]{:S(2)}, u32[]{:S(2)}) collective-permute-start(bf16[512,128]{1,0:T(8,128)(2,1)S(1)} %get-tuple-element.27.refs_0_), channel_id=1, source_target_pairs={{0,32},{16,48},{32,0},{48,16},{1,33},{17,49},{33,1},{49,17},{2,34}... | collective-permute-start | bytes 393224 | tf_op jit(solution)/shard_map/ppermute | solution.py:281
  22.2 6.8 %collective-permute-start.9 = (bf16[512,128]{1,0:T(8,128)(2,1)S(1)}, bf16[512,128]{1,0:T(8,128)(2,1)S(1)}, u32[]{:S(2)}, u32[]{:S(2)}) collective-permute-start(bf16[512,128]{1,0:T(8,128)(2,1)S(1)} %get-tuple-element.28.refs_0_), channel_id=1, source_target_pairs={{0,2},{2,0},{1,3},{3,1},{4,6},{6,4},{5,7},{7,5},{8,10},{10,8},{9,1... | collective-permute-start | bytes 393224 | tf_op jit(solution)/shard_map/ppermute | solution.py:281
  22.3 22.4 %collective-permute-start.7 = (bf16[2048,128]{1,0:T(8,128)(2,1)S(1)}, bf16[2048,128]{1,0:T(8,128)(2,1)S(1)}, u32[]{:S(2)}, u32[]{:S(2)}) collective-permute-start(bf16[2048,128]{1,0:T(8,128)(2,1)S(1)} %pad_maximum_fusion), channel_id=1, source_target_pairs={{0,64},{64,0},{1,65},{65,1},{2,66},{66,2},{3,67},{67,3},{4,68},{68... | collective-permute-start | bytes 1572872 | tf_op jit(solution)/shard_map/ppermute | solution.py:281
  44.7 9.0 %collective-permute-start.10 = (bf16[2048,128]{1,0:T(8,128)(2,1)S(1)}, bf16[2048,128]{1,0:T(8,128)(2,1)S(1)}, u32[]{:S(2)}, u32[]{:S(2)}) collective-permute-start(bf16[2048,128]{1,0:T(8,128)(2,1)S(1)} %collective-permute-done.7.refs_0_), channel_id=1, source_target_pairs={{0,2},{2,0},{1,3},{3,1},{4,6},{6,4},{5,7},{7,5},{8,10},{10,8},{9,1... | collective-permute-start | bytes 1572872 | tf_op jit(solution)/shard_map/ppermute | solution.py:281
  61.8 11.0 %collective-permute-start.11 = (bf16[64,1024]{1,0:T(8,128)(2,1)S(1)}, bf16[64,1024]{1,0:T(8,128)(2,1)S(1)}, u32[]{:S(2)}, u32[]{:S(2)}) collective-permute-start(bf16[64,1024]{1,0:T(8,128)(2,1)S(1)} %get-tuple-element.44), channel_id=1, source_target_pairs={{0,48},{16,0},{32,16},{48,32},{1,49},{17,1},{33,17},{49,33},{2,50}... | collective-permute-start | bytes 393224 | tf_op jit(solution)/shard_map/ppermute | solution.py:281
  64.6 9.6 %collective-permute-start.12 = (bf16[64,1024]{1,0:T(8,128)(2,1)S(1)}, bf16[64,1024]{1,0:T(8,128)(2,1)S(1)}, u32[]{:S(2)}, u32[]{:S(2)}) collective-permute-start(bf16[64,1024]{1,0:T(8,128)(2,1)S(1)} %get-tuple-element.45), channel_id=1, source_target_pairs={{0,16},{16,32},{32,48},{48,0},{1,17},{17,33},{33,49},{49,1},{2,18}... | collective-permute-start | bytes 393224 | tf_op jit(solution)/shard_map/ppermute | solution.py:281
  64.7 9.6 %collective-permute-start.13 = (bf16[64,1024]{1,0:T(8,128)(2,1)S(1)}, bf16[64,1024]{1,0:T(8,128)(2,1)S(1)}, u32[]{:S(2)}, u32[]{:S(2)}) collective-permute-start(bf16[64,1024]{1,0:T(8,128)(2,1)S(1)} %get-tuple-element.46), channel_id=1, source_target_pairs={{0,32},{16,48},{32,0},{48,16},{1,33},{17,49},{33,1},{49,17},{2,34}... | collective-permute-start | bytes 393224 | tf_op jit(solution)/shard_map/ppermute | solution.py:281
  77.1 5.0 %collective-permute-start.14 = (f32[32,1024]{1,0:T(8,128)S(1)}, f32[32,1024]{1,0:T(8,128)S(1)}, u32[]{:S(2)}, u32[]{:S(2)}) collective-permute-start(f32[32,1024]{1,0:T(8,128)S(1)} %get-tuple-element.48), channel_id=1, source_target_pairs={{0,1},{1,0},{2,3},{3,2},{4,5},{5,4},{6,7},{7,6},{8,9},{9,8},{10,11... | collective-permute-start | bytes 393224 | tf_op jit(solution)/shard_map/ppermute | solution.py:281

commit v5 on v4

v5 whole, which is shorter than its diff:
```python
import jax
import jax.numpy as jnp
from jax import lax
from jax.experimental import pallas as pl
from jax.experimental.pallas import tpu as pltpu
from jax.sharding import Mesh, PartitionSpec as P

SIZES = (2, 4, 4, 2, 2)
NAMES = ("zh", "x", "y", "c", "zl")
BLK = ("zh", "x", "y", "c")
TM = 256
TN = 512
STEP = 512
LOG2E = 1.4426950408889634
LIFT = 64.0
F8 = jnp.float8_e4m3fn
F32 = jnp.float32
BF16 = jnp.bfloat16
PARAMS = pltpu.CompilerParams(vmem_limit_bytes=48 << 20)


def parts(wide, lanes_low):
    high = wide.astype(F8).astype(F32)
    return jnp.where(lanes_low, high, wide - high)


def lanes_of(shape):
    return lax.broadcasted_iota(jnp.int32, shape, 1) < 64


def ready_rows(amp, blocks):
    count = len(blocks)

    def body(amp_ref, *refs):
        left_ref, norm_ref = refs[count:]
        low = lanes_of((512, 128))
        for k in range(count):
            wide = refs[k][...].astype(F32)
            flipped = wide.T
            flipped = flipped * flipped
            turned = pltpu.roll(wide, 64, 1)
            for half in range(2):
                at = 512 * half
                same = jnp.where(low, wide, turned) if half == 0 else jnp.where(low, turned, wide)
                both = same * LIFT
                high = both.astype(F8)
                left_ref[k, at : at + 512, :128] = high
                left_ref[k, at : at + 512, 128:] = (both - high.astype(F32)).astype(F8)
                norm = jnp.sum(flipped[64 * half : 64 * half + 64], axis=0, keepdims=True)
                norm_ref[k, :, at : at + 512] = amp_ref[1] - (0.5 * LOG2E) * norm

    return pl.pallas_call(
        body,
        out_shape=(
            jax.ShapeDtypeStruct((count, 1024, 256), F8),
            jax.ShapeDtypeStruct((count, 1, 1024), F32),
        ),
        in_specs=[pl.BlockSpec(memory_space=pltpu.SMEM)]
        + [pl.BlockSpec(memory_space=pltpu.VMEM)] * count,
        out_specs=(pl.BlockSpec(memory_space=pltpu.VMEM),) * 2,
        compiler_params=PARAMS,
        name="ready_rows",
    )(amp, *blocks)


def first_pack(zl, points, vectors, lengthscale):
    def body(zl_ref, points_in, vectors_in, length_in, out_ref, kept_ref, points_ref, vectors_ref, length_ref, sems):
        copies = [
            pltpu.make_async_copy(length_in, length_ref, sems.at[0]),
            pltpu.make_async_copy(points_in, points_ref, sems.at[1]),
            pltpu.make_async_copy(vectors_in, vectors_ref, sems.at[2]),
        ]
        for copy in copies:
            copy.start()
        for copy in copies:
            copy.wait()
        at = zl_ref[0]
        lane = lax.broadcasted_iota(jnp.int32, (32, 64), 1)
        row = lax.broadcasted_iota(jnp.int32, (32, 64), 0)
        column = jnp.sum(jnp.where(lane == row + 32 * at, length_ref[...], 0.0), axis=1, keepdims=True)
        scaled = (points_ref[...].astype(F32) / column).astype(BF16)
        out_ref[:32] = scaled[:, :512]
        out_ref[32:64] = scaled[:, 512:]
        given = vectors_ref[...].astype(F32)
        out_ref[64:] = jnp.where(at == 0, given[:, 512:], given[:, :512]).astype(BF16)
        kept_ref[...] = jnp.where(at == 0, given[:, :512], given[:, 512:]).astype(BF16)

    return pl.pallas_call(
        body,
        out_shape=(jax.ShapeDtypeStruct((96, 512), BF16), jax.ShapeDtypeStruct((32, 512), BF16)),
        in_specs=[pl.BlockSpec(memory_space=pltpu.SMEM)] + [pl.BlockSpec(memory_space=pltpu.HBM)] * 3,
        out_specs=(pl.BlockSpec(memory_space=pltpu.VMEM),) * 2,
        scratch_shapes=[
            pltpu.VMEM((32, 1024), BF16),
            pltpu.VMEM((32, 1024), BF16),
            pltpu.VMEM((1, 64), F32),
            pltpu.SemaphoreType.DMA((3,)),
        ],
        compiler_params=PARAMS,
        name="first_pack",
    )(zl, points, vectors, lengthscale.reshape(1, 64))


def second_pack(zl, given, got, kept):
    def body(zl_ref, given_ref, got_ref, kept_ref, rows_ref, share_ref):
        first = zl_ref[0] == 0
        mine = given_ref[...].astype(F32)
        theirs = got_ref[...].astype(F32)
        whole = jnp.concatenate([mine[:32], theirs[:32], mine[32:64], theirs[32:64]], axis=0)
        rows_ref[...] = whole.T.astype(BF16)
        picked = jnp.concatenate(
            [
                jnp.where(first, whole[:64], whole[64:]),
                kept_ref[...].astype(F32),
                theirs[64:],
            ],
            axis=0,
        )
        share_ref[...] = picked.T.astype(BF16)

    packed = jax.ShapeDtypeStruct((512, 128), BF16)
    return pl.pallas_call(
        body,
        out_shape=(packed, packed),
        in_specs=[pl.BlockSpec(memory_space=pltpu.SMEM)] + [pl.BlockSpec(memory_space=pltpu.VMEM)] * 3,
        out_specs=(pl.BlockSpec(memory_space=pltpu.VMEM),) * 2,
        compiler_params=PARAMS,
        name="second_pack",
    )(zl, given, got, kept)


def one_block(left, row_norm, right, norm, vectors, top):
    inner = lax.dot_general(right, left, (((1,), (1,)), ((), ())), preferred_element_type=F32)
    wide_norm = jnp.concatenate([norm] * (left.shape[0] // 128), axis=1)
    exponent = (inner * (LOG2E / (LIFT * LIFT)) + row_norm) + wide_norm
    block = jnp.minimum(jnp.exp2(exponent).astype(BF16), top)
    return jnp.dot(vectors, block, preferred_element_type=F32)


def amplitude(amp_ref):
    return jnp.full((1, 1), amp_ref[0], F32).astype(BF16)


def tile_sum(amp_ref, left, row_norm, ready_refs):
    top = amplitude(amp_ref)
    sums = []
    for m in range(0, STEP, TM):
        result = jnp.zeros((64, TM), F32)
        for right_ref, norm_ref, vectors_ref in ready_refs:
            for at in range(0, right_ref.shape[0], TN):
                part = slice(at, at + TN)
                result += one_block(
                    left[m : m + TM], row_norm[:, m : m + TM],
                    right_ref[part, :], norm_ref[part, :], vectors_ref[:, part], top,
                )
        sums.append(result)
    return jnp.concatenate(sums, axis=1)


def ready_cols(raw_refs, right_ref, norm_ref, vectors_ref):
    low = lanes_of((512, 128))
    at = 0
    for ref in raw_refs:
        for sub in range(0, ref.shape[0], 512):
            part = slice(at, at + 512)
            wide = ref[sub : sub + 512, :].astype(F32)
            vectors_ref[:, part] = wide.T[64:, :].astype(BF16)
            narrow = parts(jnp.where(low, wide, pltpu.roll(wide, 64, 1)) * LIFT, low).astype(F8)
            right_ref[part, :128] = narrow
            right_ref[part, 128:] = narrow
            own = jnp.where(low, wide, 0.0)
            norm = (-0.5 * LOG2E) * jnp.sum(own * own, axis=1, keepdims=True)
            norm_ref[part, :] = jnp.broadcast_to(norm, (512, 128))
            at += 512


def ready_shapes(total):
    return [
        jax.ShapeDtypeStruct((total, 256), F8),
        jax.ShapeDtypeStruct((total, 128), F32),
        jax.ShapeDtypeStruct((64, total), BF16),
    ]


def whole(arrays):
    return [pl.BlockSpec(a.shape, lambda i: (0, 0)) for a in arrays]


SCALE = 512


def cost(rows, cols):
    return pl.CostEstimate(flops=rows * cols * SCALE, transcendentals=0, bytes_accessed=cols * 384)


def row_specs():
    per = 1024 // STEP
    return [
        pl.BlockSpec(memory_space=pltpu.SMEM),
        pl.BlockSpec((1, STEP, 256), lambda i: (i // per, i % per, 0)),
        pl.BlockSpec((1, 1, STEP), lambda i: (i // per, 0, i % per)),
    ]


def add_tiles(amp, left, raws, before, narrow):
    count = left[0].shape[0]
    total = sum(raw.shape[0] for raw in raws)
    per = 1024 // STEP
    old = [] if before is None else [before]
    sums = count if narrow else 1

    def body(amp_ref, left_ref, row_norm_ref, *refs):
        raw_refs = refs[: len(raws)]
        before_refs = refs[len(raws) : len(raws) + len(old)]
        sum_refs = refs[len(raws) + len(old) : len(raws) + len(old) + sums]
        ready_refs = refs[-3:]
        step = pl.program_id(0)

        @pl.when(step == 0)
        def _():
            ready_cols(raw_refs, *ready_refs)

        value = tile_sum(amp_ref, left_ref[0], row_norm_ref[0], [ready_refs])
        if before_refs:
            value += before_refs[0][0]
        if not narrow:
            sum_refs[0][0] = value
            return
        for k in range(count):

            @pl.when(step // per == k)
            def _():
                sum_refs[k][...] = value.astype(BF16)

    def place(k):
        return pl.BlockSpec((64, STEP), lambda i: (0, jnp.clip(i - k * per, 0, per - 1)))

    acc_spec = pl.BlockSpec((1, 64, STEP), lambda i: (i // per, 0, i % per))
    if narrow:
        sum_shapes = [jax.ShapeDtypeStruct((64, 1024), BF16)] * count
        sum_specs = [place(k) for k in range(count)]
    else:
        sum_shapes = [jax.ShapeDtypeStruct((count, 64, 1024), F32)]
        sum_specs = [acc_spec]
    ready = ready_shapes(total)
    out = pl.pallas_call(
        body,
        grid=(count * per,),
        out_shape=sum_shapes + ready,
        in_specs=row_specs() + whole(raws) + [acc_spec] * len(old),
        out_specs=sum_specs + whole(ready),
        compiler_params=PARAMS,
        cost_estimate=cost(1024 * count, total),
        name="add_tiles",
    )(amp, *left, *raws, *old)
    return out[:sums], tuple(out[sums:])


def own_tiles(amp, left, ready):
    flat = [part for group in ready for part in group]

    def body(amp_ref, left_ref, row_norm_ref, *refs):
        groups = [refs[3 * k : 3 * k + 3] for k in range(len(ready))]
        refs[-1][...] = tile_sum(amp_ref, left_ref[0], row_norm_ref[0], groups)

    return pl.pallas_call(
        body,
        grid=(1024 // STEP,),
        out_shape=jax.ShapeDtypeStruct((64, 1024), F32),
        in_specs=row_specs() + whole(flat),
        out_specs=pl.BlockSpec((64, STEP), lambda i: (0, i)),
        compiler_params=PARAMS,
        cost_estimate=cost(1024, sum(group[0].shape[0] for group in ready)),
        name="own_tiles",
    )(amp, *left, *flat)


def own_last(amp, left, ready, before, arrived):
    count = len(arrived)

    def body(amp_ref, left_ref, row_norm_ref, right_ref, norm_ref, vectors_ref, before_ref, *refs):
        mine_ref, theirs_ref = refs[count:]
        groups = [(right_ref, norm_ref, vectors_ref)]
        value = tile_sum(amp_ref, left_ref[0], row_norm_ref[0], groups) + before_ref[...]
        for ref in refs[:count]:
            value += ref[...].astype(F32)
        mine_ref[...] = value[:32]
        theirs_ref[...] = value[32:]

    out_spec = pl.BlockSpec((32, STEP), lambda i: (0, i))
    half = jax.ShapeDtypeStruct((32, 1024), F32)
    return pl.pallas_call(
        body,
        grid=(1024 // STEP,),
        out_shape=(half, half),
        in_specs=row_specs()
        + whole(ready)
        + [pl.BlockSpec((64, STEP), lambda i: (0, i))] * (count + 1),
        out_specs=(out_spec, out_spec),
        compiler_params=PARAMS,
        cost_estimate=cost(1024, ready[0].shape[0]),
        name="own_last",
    )(amp, *left, *ready, before, *arrived)


def shift(value, axis, by):
    size = SIZES[NAMES.index(axis)]
    return lax.ppermute(value, axis, [(i, (i + by) % size) for i in range(size)])


def per_device(points, vectors, lengthscale, outscale, noise):
    zl = lax.axis_index("zl").astype(jnp.int32).reshape(1)
    amp = jnp.concatenate([outscale, jnp.log(outscale) * LOG2E])

    given, kept = first_pack(zl, points.T, vectors.T, lengthscale)
    got = shift(given, "zl", 1)
    rows, share = second_pack(zl, given, got, kept)

    near = [shift(share, "y", by) for by in (1, -1, 2)]
    rows_in = [shift(rows, "x", by) for by in (1, -1, 2)]
    beside = shift(share, "c", 1)
    own_left = ready_rows(amp, [rows])
    near[2], rows_in[0], own_left = lax.optimization_barrier((near[2], rows_in[0], own_left))
    near = jnp.concatenate(near, axis=0)
    near_beside = shift(near, "c", 1)
    far = shift(jnp.concatenate([share, near], axis=0), "zh", 1)

    left = ready_rows(amp, rows_in)
    (acc,), ready0 = add_tiles(amp, left, [share, beside], None, False)
    (acc,), ready1 = add_tiles(amp, left, [near, near_beside], acc, False)
    far, acc = lax.optimization_barrier((far, acc))
    far_beside = shift(far, "c", 1)
    (acc,), ready2 = add_tiles(amp, left, [far], acc, False)
    sent, ready3 = add_tiles(amp, left, [far_beside], acc, True)
    arrived = [shift(part, "x", by) for part, by in zip(sent, (-1, 1, 2))]
    own = own_tiles(amp, own_left, [ready0, ready1, ready2])
    mine, theirs = own_last(amp, own_left, ready3, own, arrived)
    mine = mine + shift(theirs, "zl", 1)
    return mine.T + noise[0] * vectors.astype(F32)


def solution(mesh):
    fine = Mesh(mesh.devices.reshape(SIZES), NAMES)
    placed = (P(BLK, "zl"), P(BLK, "zl"), P(), P(), P())
    return jax.shard_map(
        per_device, mesh=fine, in_specs=placed, out_specs=P(BLK, "zl"), check_vma=False
    )
```

time: 83.2 us -> 84.8 us (1.019)
  Pallas kernels: 43.5 us -> 45 us
    pallas_call x9, Pallas kernels: 43.4 us -> 44.9 us  [the longest x4 33.7 us: add_tiles(): pl.pallas_call(body, grid=(count * per,), out_shape=sum_shapes + ready, i...]
where the time goes in v5:
time: 84.8 us; the launch traced here: 84 us
  Pallas kernels  45 us (53%)
  starting transfers between devices  24.3 us (29%)
  waiting for transfers between devices  9.98 us (12%)
  local copies, waits for them, and re-layouts  2.38 us (3%)
  between operations  1.52 us (2%)
    pallas_call x4, Pallas kernels, add_tiles(): pl.pallas_call(body, grid=(count * per,), out_shape=sum_shapes + ready, i...  33.7 us
    ppermute x15, starting transfers between devices, shift(): lax.ppermute(value, axis, [(i, (i + by) % size) for i in range(size)])  24.3 us
    ppermute x15, waiting for transfers between devices, shift(): lax.ppermute(value, axis, [(i, (i + by) % size) for i in range(size)])  9.98 us
    pallas_call x1, Pallas kernels, own_tiles(): pl.pallas_call(body, grid=(1024 // STEP,), out_shape=jax.ShapeDtypeStruct...  6.18 us
    pallas_call x1, Pallas kernels, own_last(): pl.pallas_call(body, grid=(1024 // STEP,), out_shape=(half, half), in_spe...  2.92 us
    unnamed x10, local copies, waits for them, and re-layouts  2.36 us
    pallas_call x2, Pallas kernels, ready_rows(): pl.pallas_call(body, out_shape=(jax.ShapeDtypeStruct((count, 1024, 256),...  1.82 us
  transfers between devices with their start and end apart: 15, of which 7 were waited for; matrix products, arithmetic and copies ran while one was open for 0% of the time, Pallas kernels for 39%

profile of v5, /device:TPU:0, one launch (start us, length us, event | category | flops | bytes accessed | tf_op | source)
XLA Modules:
  0.0 84.0 jit_solution(241380557398679119)
XLA Ops:
  0.0 0.8 copy-done
  0.8 0.8 copy-done.2
  1.7 0.7 copy-done.3
  2.3 0.3 first_pack.1
  2.6 2.1 %collective-permute-start = (bf16[96,512]{1,0:T(8,128)(2,1)S(1)}, bf16[96,512]{1,0:T(8,128)(2,1)S(1)}, u32[]{:S(2)}, u32[]{:S(2)}) collective-permute-start(bf16[96,512]{1,0:T(8,128)(2,1)S(1)} %get-tuple-element.39.given_ref), channel_id=1, source_target_pairs={{0,1},{1,0},{2,3},{3,2},{4,5},{5,4},{6,7},{7,6},{8,9},{9,8},{10,11... | collective-permute-start | bytes 294920 | tf_op jit(solution)/shard_map/ppermute | solution.py:308
  4.7 2.8 %collective-permute-done.got_ref = bf16[96,512]{1,0:T(8,128)(2,1)S(1)} collective-permute-done((bf16[96,512]{1,0:T(8,128)(2,1)S(1)}, bf16[96,512]{1,0:T(8,128)(2,1)S(1)}, u32[]{:S(2)}, u32[]{:S(2)}) %collective-permute-start) | collective-permute-done | bytes 98336 | tf_op jit(solution)/shard_map/ppermute | solution.py:308
  7.5 0.1 second_pack.1
  7.6 3.3 %collective-permute-start.1 = (bf16[512,128]{1,0:T(8,128)(2,1)S(1)}, bf16[512,128]{1,0:T(8,128)(2,1)S(1)}, u32[]{:S(2)}, u32[]{:S(2)}) collective-permute-start(bf16[512,128]{1,0:T(8,128)(2,1)S(1)} %get-tuple-element.41.refs_0_), channel_id=1, source_target_pairs={{0,8},{4,12},{8,0},{12,4},{1,9},{5,13},{9,1},{13,5},{2,10},{6,14},... | collective-permute-start | bytes 393224 | tf_op jit(solution)/shard_map/ppermute | solution.py:308
  10.9 1.5 %collective-permute-start.2 = (bf16[512,128]{1,0:T(8,128)(2,1)S(1)}, bf16[512,128]{1,0:T(8,128)(2,1)S(1)}, u32[]{:S(2)}, u32[]{:S(2)}) collective-permute-start(bf16[512,128]{1,0:T(8,128)(2,1)S(1)} %get-tuple-element.42.refs_0_), channel_id=1, source_target_pairs={{0,16},{16,32},{32,48},{48,0},{1,17},{17,33},{33,49},{49,1},{2,18}... | collective-permute-start | bytes 393224 | tf_op jit(solution)/shard_map/ppermute | solution.py:308
  12.4 0.7 collective-permute-start.5
  13.8 2.6 %collective-permute-start.6 = (bf16[512,128]{1,0:T(8,128)(2,1)S(1)}, bf16[512,128]{1,0:T(8,128)(2,1)S(1)}, u32[]{:S(2)}, u32[]{:S(2)}) collective-permute-start(bf16[512,128]{1,0:T(8,128)(2,1)S(1)} %get-tuple-element.41.refs_0_), channel_id=1, source_target_pairs={{0,12},{4,0},{8,4},{12,8},{1,13},{5,1},{9,5},{13,9},{2,14},{6,2},{... | collective-permute-start | bytes 393224 | tf_op jit(solution)/shard_map/ppermute | solution.py:308
  16.5 0.8 ready_rows.2
  17.3 1.3 %collective-permute-done.5 = bf16[512,128]{1,0:T(8,128)(2,1)S(1)} collective-permute-done((bf16[512,128]{1,0:T(8,128)(2,1)S(1)}, bf16[512,128]{1,0:T(8,128)(2,1)S(1)}, u32[]{:S(2)}, u32[]{:S(2)}) %collective-permute-start.5) | collective-permute-done | bytes 131104 | tf_op jit(solution)/shard_map/ppermute | solution.py:308
  18.6 0.3 collective-permute-done.6
  19.1 1.8 %collective-permute-start.3 = (bf16[512,128]{1,0:T(8,128)(2,1)S(1)}, bf16[512,128]{1,0:T(8,128)(2,1)S(1)}, u32[]{:S(2)}, u32[]{:S(2)}) collective-permute-start(bf16[512,128]{1,0:T(8,128)(2,1)S(1)} %get-tuple-element.42.refs_0_), channel_id=1, source_target_pairs={{0,48},{16,0},{32,16},{48,32},{1,49},{17,1},{33,17},{49,33},{2,50}... | collective-permute-start | bytes 393224 | tf_op jit(solution)/shard_map/ppermute | solution.py:308
  20.9 1.8 %collective-permute-start.4 = (bf16[512,128]{1,0:T(8,128)(2,1)S(1)}, bf16[512,128]{1,0:T(8,128)(2,1)S(1)}, u32[]{:S(2)}, u32[]{:S(2)}) collective-permute-start(bf16[512,128]{1,0:T(8,128)(2,1)S(1)} %get-tuple-element.42.refs_0_), channel_id=1, source_target_pairs={{0,32},{16,48},{32,0},{48,16},{1,33},{17,49},{33,1},{49,17},{2,34}... | collective-permute-start | bytes 393224 | tf_op jit(solution)/shard_map/ppermute | solution.py:308
  22.7 3.9 %collective-permute-start.7 = (bf16[2048,128]{1,0:T(8,128)(2,1)S(1)}, bf16[2048,128]{1,0:T(8,128)(2,1)S(1)}, u32[]{:S(2)}, u32[]{:S(2)}) collective-permute-start(bf16[2048,128]{1,0:T(8,128)(2,1)S(1)} %pad_maximum_fusion), channel_id=1, source_target_pairs={{0,64},{64,0},{1,65},{65,1},{2,66},{66,2},{3,67},{67,3},{4,68},{68... | collective-permute-start | bytes 1572872 | tf_op jit(solution)/shard_map/ppermute | solution.py:308
  26.6 0.5 collective-permute-done.3.refs_1_
  27.1 0.9 %collective-permute-done.4.refs_2_ = bf16[512,128]{1,0:T(8,128)(2,1)S(1)} collective-permute-done((bf16[512,128]{1,0:T(8,128)(2,1)S(1)}, bf16[512,128]{1,0:T(8,128)(2,1)S(1)}, u32[]{:S(2)}, u32[]{:S(2)}) %collective-permute-start.4) | collective-permute-done | bytes 131104 | tf_op jit(solution)/shard_map/ppermute | solution.py:308
  28.0 1.1 %ready_rows.3 = (f8e4m3fn[3,1024,256]{2,1,0:T(32,128)(4,1)S(1)}, f32[3,1,1024]{2,1,0:T(1,128)S(1)}) custom-call(f32[2]{0:T(128)S(1)} %pad_maximum_fusion.1.amp_ref, bf16[512,128]{1,0:T(8,128)(2,1)S(1)} %collective-permute-done.2.refs_0_, bf16[512,128]{1,0:T(8,128)(2,1)S(1)} %collective-permute-done.3.refs_1_, bf16[512,128]{1,0:T(8,128)(2,1)S(1)} %collective-permute-done.4.refs_2_), custom_call_target="tpu_custom_call" | custom-call | tf_op jit(solution)/shard_map/ready_rows/pallas_call | solution.py:52
  29.0 5.4 %add_tiles.4 = (f32[3,64,1024]{2,1,0:T(8,128)S(1)}, f8e4m3fn[1024,256]{1,0:T(32,128)(4,1)S(1)}, f32[1024,128]{1,0:T(8,128)S(1)}, bf16[64,1024]{1,0:T(8,128)(2,1)S(1)}) custom-call(f32[2]{0:T(128)S(1)} %pad_maximum_fusion.1.amp_ref, f8e4m3fn[3,1024,256]{2,1,0:T(32,128)(4,1)S(1)} %get-tuple-element.48.left_ref, ...), custom_call_target="tpu_custom_call" | custom-call | flops 1610612736 | bytes 393216 | tf_op jit(solution)/shard_map/add_tiles/pallas_call | solution.py:246
  34.4 11.2 %add_tiles.5 = (f32[3,64,1024]{2,1,0:T(8,128)S(1)}, f8e4m3fn[3072,256]{1,0:T(32,128)(4,1)S(1)}, f32[3072,128]{1,0:T(8,128)S(1)}, bf16[64,3072]{1,0:T(8,128)(2,1)S(1)}) custom-call(f32[2]{0:T(128)S(1)} %pad_maximum_fusion.1.amp_ref, f8e4m3fn[3,1024,256]{2,1,0:T(32,128)(4,1)S(1)} %get-tuple-element.48.left_ref, ...), custom_call_target="tpu_custom_call" | custom-call | flops 4831838208 | bytes 1179648 | tf_op jit(solution)/shard_map/add_tiles/pallas_call | solution.py:246
  45.8 8.4 %add_tiles.6 = (f32[3,64,1024]{2,1,0:T(8,128)S(1)}, f8e4m3fn[2048,256]{1,0:T(32,128)(4,1)S(1)}, f32[2048,128]{1,0:T(8,128)S(1)}, bf16[64,2048]{1,0:T(8,128)(2,1)S(1)}) custom-call(f32[2]{0:T(128)S(1)} %pad_maximum_fusion.1.amp_ref, f8e4m3fn[3,1024,256]{2,1,0:T(32,128)(4,1)S(1)} %get-tuple-element.48.left_ref, ...), custom_call_target="tpu_custom_call" | custom-call | flops 3221225472 | bytes 786432 | tf_op jit(solution)/shard_map/add_tiles/pallas_call | solution.py:246
  54.2 8.7 %add_tiles.7 = (bf16[64,1024]{1,0:T(8,128)(2,1)S(1)}, bf16[64,1024]{1,0:T(8,128)(2,1)S(1)}, bf16[64,1024]{1,0:T(8,128)(2,1)S(1)}, f8e4m3fn[2048,256]{1,0:T(32,12...) custom-call(f32[2]{0:T(128)S(1)} %pad_maximum_fusion.1.amp_ref, ...), custom_call_target="tpu_custom_call" | custom-call | flops 3221225472 | bytes 786432 | tf_op jit(solution)/shard_map/add_tiles/pallas_call | solution.py:246
  62.9 2.9 %collective-permute-start.11 = (bf16[64,1024]{1,0:T(8,128)(2,1)S(1)}, bf16[64,1024]{1,0:T(8,128)(2,1)S(1)}, u32[]{:S(2)}, u32[]{:S(2)}) collective-permute-start(bf16[64,1024]{1,0:T(8,128)(2,1)S(1)} %get-tuple-element.68), channel_id=1, source_target_pairs={{0,48},{16,0},{32,16},{48,32},{1,49},{17,1},{33,17},{49,33},{2,50}... | collective-permute-start | bytes 393224 | tf_op jit(solution)/shard_map/ppermute | solution.py:308
  65.7 1.7 %collective-permute-start.13 = (bf16[64,1024]{1,0:T(8,128)(2,1)S(1)}, bf16[64,1024]{1,0:T(8,128)(2,1)S(1)}, u32[]{:S(2)}, u32[]{:S(2)}) collective-permute-start(bf16[64,1024]{1,0:T(8,128)(2,1)S(1)} %get-tuple-element.70), channel_id=1, source_target_pairs={{0,32},{16,48},{32,0},{48,16},{1,33},{17,49},{33,1},{49,17},{2,34}... | collective-permute-start | bytes 393224 | tf_op jit(solution)/shard_map/ppermute | solution.py:308
  67.5 6.2 %own_tiles.1.before_ref = f32[64,1024]{1,0:T(8,128)S(1)} custom-call(f32[2]{0:T(128)S(1)} %pad_maximum_fusion.1.amp_ref, f8e4m3fn[1,1024,256]{2,1,0:T(32,128)(4,1)S(1)} %get-tuple-element.45.left_ref, f32[1,1,1024]{2,1,0:T(1,128)S(1)} %get-tuple-element.46.row_norm_ref, f8e4m3fn[1024,256]{1,0:T(32,128)(4,1)S(1)} %get-tuple-element.59.refs_0_, ...), custom_call_target="tpu_custom_call" | custom-call | flops 3221225472 | bytes 2359296 | tf_op jit(solution)/shard_map/own_tiles/pallas_call | solution.py:266
  73.7 1.7 %collective-permute-done.12.refs_1_ = bf16[64,1024]{1,0:T(8,128)(2,1)S(1)} collective-permute-done((bf16[64,1024]{1,0:T(8,128)(2,1)S(1)}, bf16[64,1024]{1,0:T(8,128)(2,1)S(1)}, u32[]{:S(2)}, u32[]{:S(2)}) %collective-permute-start.12) | collective-permute-done | bytes 131104 | tf_op jit(solution)/shard_map/ppermute | solution.py:308
  75.4 2.9 %own_last.1 = (f32[32,1024]{1,0:T(8,128)S(1)}, f32[32,1024]{1,0:T(8,128)S(1)}) custom-call(f32[2]{0:T(128)S(1)} %pad_maximum_fusion.1.amp_ref, f8e4m3fn[1,1024,256]{2,1,0:T(32,128)(4,1)S(1)} %get-tuple-element.45.left_ref, f32[1,1,1024]{2,1,0:T(1,128)S(1)} %get-tuple-element.46.row_norm_ref, f8e4m3fn[2048,256]{1,0:T(32,128)(4,1)S(1)} %get-tuple-element.56.right_ref, ...), custom_call_target="tpu_custom_call" | custom-call | flops 1073741824 | bytes 786432 | tf_op jit(solution)/shard_map/own_last/pallas_call | solution.py:292
  78.3 1.9 %collective-permute-start.14 = (f32[32,1024]{1,0:T(8,128)S(1)}, f32[32,1024]{1,0:T(8,128)S(1)}, u32[]{:S(2)}, u32[]{:S(2)}) collective-permute-start(f32[32,1024]{1,0:T(8,128)S(1)} %get-tuple-element.72), channel_id=1, source_target_pairs={{0,1},{1,0},{2,3},{3,2},{4,5},{5,4},{6,7},{7,6},{8,9},{9,8},{10,11... | collective-permute-start | bytes 393224 | tf_op jit(solution)/shard_map/ppermute | solution.py:308
  80.8 2.5 %collective-permute-done.14 = f32[32,1024]{1,0:T(8,128)S(1)} collective-permute-done((f32[32,1024]{1,0:T(8,128)S(1)}, f32[32,1024]{1,0:T(8,128)S(1)}, u32[]{:S(2)}, u32[]{:S(2)}) %collective-permute-start.14) | collective-permute-done | bytes 131104 | tf_op jit(solution)/shard_map/ppermute | solution.py:308
  83.3 0.7 bitcast_add_fusion
  (22 shorter events, 0.4 us)
Async XLA Ops:
  0.0 0.8 copy-start
  0.8 0.8 copy-start.2
  1.7 0.7 copy-start.3
  2.6 4.9 %collective-permute-start = (bf16[96,512]{1,0:T(8,128)(2,1)S(1)}, bf16[96,512]{1,0:T(8,128)(2,1)S(1)}, u32[]{:S(2)}, u32[]{:S(2)}) collective-permute-start(bf16[96,512]{1,0:T(8,128)(2,1)S(1)} %get-tuple-element.39.given_ref), channel_id=1, source_target_pairs={{0,1},{1,0},{2,3},{3,2},{4,5},{5,4},{6,7},{7,6},{8,9},{9,8},{10,11... | collective-permute-start | bytes 294920 | tf_op jit(solution)/shard_map/ppermute | solution.py:308
  7.6 9.6 %collective-permute-start.1 = (bf16[512,128]{1,0:T(8,128)(2,1)S(1)}, bf16[512,128]{1,0:T(8,128)(2,1)S(1)}, u32[]{:S(2)}, u32[]{:S(2)}) collective-permute-start(bf16[512,128]{1,0:T(8,128)(2,1)S(1)} %get-tuple-element.41.refs_0_), channel_id=1, source_target_pairs={{0,8},{4,12},{8,0},{12,4},{1,9},{5,13},{9,1},{13,5},{2,10},{6,14},... | collective-permute-start | bytes 393224 | tf_op jit(solution)/shard_map/ppermute | solution.py:308
  10.9 6.3 %collective-permute-start.2 = (bf16[512,128]{1,0:T(8,128)(2,1)S(1)}, bf16[512,128]{1,0:T(8,128)(2,1)S(1)}, u32[]{:S(2)}, u32[]{:S(2)}) collective-permute-start(bf16[512,128]{1,0:T(8,128)(2,1)S(1)} %get-tuple-element.42.refs_0_), channel_id=1, source_target_pairs={{0,16},{16,32},{32,48},{48,0},{1,17},{17,33},{33,49},{49,1},{2,18}... | collective-permute-start | bytes 393224 | tf_op jit(solution)/shard_map/ppermute | solution.py:308
  12.4 6.2 %collective-permute-start.5 = (bf16[512,128]{1,0:T(8,128)(2,1)S(1)}, bf16[512,128]{1,0:T(8,128)(2,1)S(1)}, u32[]{:S(2)}, u32[]{:S(2)}) collective-permute-start(bf16[512,128]{1,0:T(8,128)(2,1)S(1)} %get-tuple-element.41.refs_0_), channel_id=1, source_target_pairs={{0,4},{4,8},{8,12},{12,0},{1,5},{5,9},{9,13},{13,1},{2,6},{6,10},{... | collective-permute-start | bytes 393224 | tf_op jit(solution)/shard_map/ppermute | solution.py:308
  13.8 5.2 %collective-permute-start.6 = (bf16[512,128]{1,0:T(8,128)(2,1)S(1)}, bf16[512,128]{1,0:T(8,128)(2,1)S(1)}, u32[]{:S(2)}, u32[]{:S(2)}) collective-permute-start(bf16[512,128]{1,0:T(8,128)(2,1)S(1)} %get-tuple-element.41.refs_0_), channel_id=1, source_target_pairs={{0,12},{4,0},{8,4},{12,8},{1,13},{5,1},{9,5},{13,9},{2,14},{6,2},{... | collective-permute-start | bytes 393224 | tf_op jit(solution)/shard_map/ppermute | solution.py:308
  19.0 15.5 %collective-permute-start.8 = (bf16[1536,128]{1,0:T(8,128)(2,1)S(1)}, bf16[1536,128]{1,0:T(8,128)(2,1)S(1)}, u32[]{:S(2)}, u32[]{:S(2)}) collective-permute-start(bf16[1536,128]{1,0:T(8,128)(2,1)S(1)} %constant_dynamic-update-slice_fusion.refs_0_), channel_id=1, source_target_pairs={{0,2},{2,0},{1,3},{3,1},{4,6},{6,4},{5,7},{7,5},{8,10},{10,8},{9,1... | collective-permute-start | bytes 1179656 | tf_op jit(solution)/shard_map/ppermute | solution.py:308
  19.1 8.0 %collective-permute-start.3 = (bf16[512,128]{1,0:T(8,128)(2,1)S(1)}, bf16[512,128]{1,0:T(8,128)(2,1)S(1)}, u32[]{:S(2)}, u32[]{:S(2)}) collective-permute-start(bf16[512,128]{1,0:T(8,128)(2,1)S(1)} %get-tuple-element.42.refs_0_), channel_id=1, source_target_pairs={{0,48},{16,0},{32,16},{48,32},{1,49},{17,1},{33,17},{49,33},{2,50}... | collective-permute-start | bytes 393224 | tf_op jit(solution)/shard_map/ppermute | solution.py:308
  20.9 7.1 %collective-permute-start.4 = (bf16[512,128]{1,0:T(8,128)(2,1)S(1)}, bf16[512,128]{1,0:T(8,128)(2,1)S(1)}, u32[]{:S(2)}, u32[]{:S(2)}) collective-permute-start(bf16[512,128]{1,0:T(8,128)(2,1)S(1)} %get-tuple-element.42.refs_0_), channel_id=1, source_target_pairs={{0,32},{16,48},{32,0},{48,16},{1,33},{17,49},{33,1},{49,17},{2,34}... | collective-permute-start | bytes 393224 | tf_op jit(solution)/shard_map/ppermute | solution.py:308
  22.7 6.3 %collective-permute-start.9 = (bf16[512,128]{1,0:T(8,128)(2,1)S(1)}, bf16[512,128]{1,0:T(8,128)(2,1)S(1)}, u32[]{:S(2)}, u32[]{:S(2)}) collective-permute-start(bf16[512,128]{1,0:T(8,128)(2,1)S(1)} %get-tuple-element.41.refs_0_), channel_id=1, source_target_pairs={{0,2},{2,0},{1,3},{3,1},{4,6},{6,4},{5,7},{7,5},{8,10},{10,8},{9,1... | collective-permute-start | bytes 393224 | tf_op jit(solution)/shard_map/ppermute | solution.py:308
  22.7 22.9 %collective-permute-start.7 = (bf16[2048,128]{1,0:T(8,128)(2,1)S(1)}, bf16[2048,128]{1,0:T(8,128)(2,1)S(1)}, u32[]{:S(2)}, u32[]{:S(2)}) collective-permute-start(bf16[2048,128]{1,0:T(8,128)(2,1)S(1)} %pad_maximum_fusion), channel_id=1, source_target_pairs={{0,64},{64,0},{1,65},{65,1},{2,66},{66,2},{3,67},{67,3},{4,68},{68... | collective-permute-start | bytes 1572872 | tf_op jit(solution)/shard_map/ppermute | solution.py:308
  45.7 8.5 %collective-permute-start.10 = (bf16[2048,128]{1,0:T(8,128)(2,1)S(1)}, bf16[2048,128]{1,0:T(8,128)(2,1)S(1)}, u32[]{:S(2)}, u32[]{:S(2)}) collective-permute-start(bf16[2048,128]{1,0:T(8,128)(2,1)S(1)} %collective-permute-done.7.refs_0_), channel_id=1, source_target_pairs={{0,2},{2,0},{1,3},{3,1},{4,6},{6,4},{5,7},{7,5},{8,10},{10,8},{9,1... | collective-permute-start | bytes 1572872 | tf_op jit(solution)/shard_map/ppermute | solution.py:308
  62.9 10.8 %collective-permute-start.11 = (bf16[64,1024]{1,0:T(8,128)(2,1)S(1)}, bf16[64,1024]{1,0:T(8,128)(2,1)S(1)}, u32[]{:S(2)}, u32[]{:S(2)}) collective-permute-start(bf16[64,1024]{1,0:T(8,128)(2,1)S(1)} %get-tuple-element.68), channel_id=1, source_target_pairs={{0,48},{16,0},{32,16},{48,32},{1,49},{17,1},{33,17},{49,33},{2,50}... | collective-permute-start | bytes 393224 | tf_op jit(solution)/shard_map/ppermute | solution.py:308
  65.7 9.6 %collective-permute-start.12 = (bf16[64,1024]{1,0:T(8,128)(2,1)S(1)}, bf16[64,1024]{1,0:T(8,128)(2,1)S(1)}, u32[]{:S(2)}, u32[]{:S(2)}) collective-permute-start(bf16[64,1024]{1,0:T(8,128)(2,1)S(1)} %get-tuple-element.69), channel_id=1, source_target_pairs={{0,16},{16,32},{32,48},{48,0},{1,17},{17,33},{33,49},{49,1},{2,18}... | collective-permute-start | bytes 393224 | tf_op jit(solution)/shard_map/ppermute | solution.py:308
  65.7 9.6 %collective-permute-start.13 = (bf16[64,1024]{1,0:T(8,128)(2,1)S(1)}, bf16[64,1024]{1,0:T(8,128)(2,1)S(1)}, u32[]{:S(2)}, u32[]{:S(2)}) collective-permute-start(bf16[64,1024]{1,0:T(8,128)(2,1)S(1)} %get-tuple-element.70), channel_id=1, source_target_pairs={{0,32},{16,48},{32,0},{48,16},{1,33},{17,49},{33,1},{49,17},{2,34}... | collective-permute-start | bytes 393224 | tf_op jit(solution)/shard_map/ppermute | solution.py:308
  75.3 8.0 %copy-start.1 = (bf16[1024,32]{0,1:T(8,128)(2,1)S(1)}, bf16[1024,32]{0,1:T(8,128)(2,1)}, u32[]{:S(2)}) copy-start(bf16[1024,32]{0,1:T(8,128)(2,1)} %param.6) | copy-start | bytes 196612
  78.3 5.0 %collective-permute-start.14 = (f32[32,1024]{1,0:T(8,128)S(1)}, f32[32,1024]{1,0:T(8,128)S(1)}, u32[]{:S(2)}, u32[]{:S(2)}) collective-permute-start(f32[32,1024]{1,0:T(8,128)S(1)} %get-tuple-element.72), channel_id=1, source_target_pairs={{0,1},{1,0},{2,3},{3,2},{4,5},{5,4},{6,7},{7,6},{8,9},{9,8},{10,11... | collective-permute-start | bytes 393224 | tf_op jit(solution)/shard_map/ppermute | solution.py:308

commit v6 on v4

v6 whole, which is shorter than its diff:
```python
import jax
import jax.numpy as jnp
from jax import lax
from jax.experimental import pallas as pl
from jax.experimental.pallas import tpu as pltpu
from jax.sharding import Mesh, PartitionSpec as P

SIZES = (2, 4, 4, 2, 2)
NAMES = ("zh", "x", "y", "c", "zl")
BLK = ("zh", "x", "y", "c")
TM = 512
TN = 1024
F32 = jnp.float32
BF16 = jnp.bfloat16
PARAMS = pltpu.CompilerParams(vmem_limit_bytes=48 << 20)


SCALE = 512


def cost(rows, cols):
    return pl.CostEstimate(flops=rows * cols * SCALE, transcendentals=0, bytes_accessed=cols * 384)


def three_parts(wide):
    hi = wide.astype(BF16).astype(F32)
    mid = (wide - hi).astype(BF16).astype(F32)
    return hi, mid, wide - hi - mid


def with_norms(wide, offset, first, other):
    lane = lax.broadcasted_iota(jnp.int32, wide.shape, 1)
    wide = jnp.where(lane < 64, wide, 0.0)
    half = offset - 0.5 * jnp.sum(wide * wide, axis=1, keepdims=True)
    hi, mid, low = three_parts(half)
    ones = (lane >= other) & (lane < other + 3)
    wide = jnp.where(ones, 1.0, wide)
    wide = jnp.where(lane == first, hi, wide)
    wide = jnp.where(lane == first + 1, mid, wide)
    wide = jnp.where(lane == first + 2, low, wide)
    return wide.astype(BF16)


def ready_rows(amp, mines, theirs):
    count = len(mines)

    def body(amp_ref, *refs):
        theirs_ref, out_ref = refs[count:]
        for k in range(count):
            for half in range(2):
                low = 32 * half
                mine = refs[k][low : low + 32, :].astype(F32)
                other = theirs_ref[64 * k + low : 64 * k + low + 32, :].astype(F32)
                wide = jnp.concatenate([mine, other, mine, other], axis=0).T
                out_ref[k, 512 * half : 512 * half + 512] = with_norms(wide, amp_ref[1], 67, 64)

    return pl.pallas_call(
        body,
        out_shape=jax.ShapeDtypeStruct((count, 1024, 128), BF16),
        in_specs=[pl.BlockSpec(memory_space=pltpu.SMEM)]
        + [pl.BlockSpec(memory_space=pltpu.VMEM)] * (count + 1),
        out_specs=pl.BlockSpec(memory_space=pltpu.VMEM),
        compiler_params=PARAMS,
        name="ready_rows",
    )(amp, *mines, theirs)


def first_pack(zl, points, vectors, lengthscale):
    def body(zl_ref, points_ref, vectors_ref, length_ref, out_ref, kept_ref):
        at = zl_ref[0]
        lane = lax.broadcasted_iota(jnp.int32, (32, 64), 1)
        row = lax.broadcasted_iota(jnp.int32, (32, 64), 0)
        column = jnp.sum(jnp.where(lane == row + 32 * at, length_ref[...], 0.0), axis=1, keepdims=True)
        scaled = (points_ref[...].astype(F32) / column).astype(BF16)
        out_ref[:32] = scaled[:, :512]
        out_ref[32:64] = scaled[:, 512:]
        given = vectors_ref[...].astype(F32)
        out_ref[64:] = jnp.where(at == 0, given[:, 512:], given[:, :512]).astype(BF16)
        kept_ref[...] = jnp.where(at == 0, given[:, :512], given[:, 512:]).astype(BF16)

    return pl.pallas_call(
        body,
        out_shape=[jax.ShapeDtypeStruct((n, 512), BF16) for n in (96, 32)],
        in_specs=[pl.BlockSpec(memory_space=pltpu.SMEM)] + [pl.BlockSpec(memory_space=pltpu.VMEM)] * 3,
        out_specs=[pl.BlockSpec(memory_space=pltpu.VMEM)] * 2,
        compiler_params=PARAMS,
        name="first_pack",
    )(zl, points, vectors, lengthscale.reshape(1, 64))


def copy_of(parts, rows, token, weight):
    def body(token_ref, *refs):
        at = 0
        for ref in refs[:-1]:
            refs[-1][at : at + rows] = ref[:rows]
            at += rows

    return pl.pallas_call(
        body,
        out_shape=jax.ShapeDtypeStruct((rows * len(parts), parts[0].shape[1]), BF16),
        in_specs=[pl.BlockSpec(memory_space=pl.ANY)]
        + [pl.BlockSpec(memory_space=pltpu.VMEM)] * len(parts),
        out_specs=pl.BlockSpec(memory_space=pltpu.VMEM),
        compiler_params=PARAMS,
        cost_estimate=cost(weight, 1024),
        name="copy_of",
    )(token, *parts)


def second_pack(zl, amp, half, got, kept):
    def body(zl_ref, amp_ref, half_ref, got_ref, kept_ref, rows_ref, share_ref):
        first = zl_ref[0] == 0
        mine = half_ref[...].astype(F32)
        theirs = got_ref[...].astype(F32)
        low = jnp.concatenate([mine[:32], theirs[:32]], axis=0)
        high = jnp.concatenate([mine[32:], theirs[32:64]], axis=0)
        picked = jnp.where(first, low, high)
        share_ref[...] = jnp.concatenate([picked, kept_ref[...].astype(F32), theirs[64:]], axis=0).T.astype(BF16)
        for k, wide in enumerate((low, high)):
            wide = jnp.concatenate([wide, wide], axis=0).T
            rows_ref[0, 512 * k : 512 * k + 512] = with_norms(wide, amp_ref[1], 67, 64)

    return pl.pallas_call(
        body,
        out_shape=[jax.ShapeDtypeStruct((1, 1024, 128), BF16), jax.ShapeDtypeStruct((512, 128), BF16)],
        in_specs=[pl.BlockSpec(memory_space=pltpu.SMEM)] * 2 + [pl.BlockSpec(memory_space=pltpu.VMEM)] * 3,
        out_specs=[pl.BlockSpec(memory_space=pltpu.VMEM)] * 2,
        compiler_params=PARAMS,
        name="second_pack",
    )(zl, amp, half, got, kept)


def one_block(left, right, vectors, top):
    exponent = lax.dot_general(right, left, (((1,), (1,)), ((), ())), preferred_element_type=F32)
    block = jnp.minimum(jnp.exp(exponent).astype(BF16), top)
    return jnp.dot(vectors, block, preferred_element_type=F32)


def ready_sum(left, pairs, top):
    result = jnp.zeros((64, left.shape[0]), F32)
    for right_ref, vectors_ref in pairs:
        total = right_ref.shape[0]
        for at in range(0, total, TN):
            part = slice(at, min(at + TN, total))
            result += one_block(left, right_ref[part, :], vectors_ref[:, part], top)
    return result


def raw_sum(left, raws, right_ref, vectors_ref, top):
    total = right_ref.shape[0]
    result = jnp.zeros((64, left.shape[0]), F32)
    at = back = 0
    for ref, start in raws:
        for sub in range(start, ref.shape[0], 512):
            wide = ref[sub : sub + 512, :].astype(F32)
            right_ref[at : at + 512, :] = with_norms(wide, 0.0, 64, 67)
            vectors_ref[:, at : at + 512] = wide.T[64:, :].astype(BF16)
            at += 512
            if at - back == TN or at == total:
                result += one_block(left, right_ref[back:at, :], vectors_ref[:, back:at], top)
                back = at
    return result


def add_tiles(amp, left, ready, raws, before=None, narrow=False, weight=1024):
    count = left.shape[0]
    flat = [part for pair in ready for part in pair]
    total = sum(raw.shape[0] - start for raw, start in raws)
    cols = total + sum(right.shape[0] for right, _ in ready)
    per = 1024 // TM
    old = [] if before is None else [before]
    sums = count if narrow else 1
    ends = [len(flat), len(raws), len(old), sums]

    def body(amp_ref, left_ref, *refs):
        groups = []
        for size in ends:
            groups.append(refs[:size])
            refs = refs[size:]
        flat_refs, raw_refs, before_refs, sum_refs = groups
        pairs = [(flat_refs[2 * k], flat_refs[2 * k + 1]) for k in range(len(ready))]
        step = pl.program_id(0)
        top = jnp.full((1, 1), amp_ref[0], F32).astype(BF16)

        def put(value):
            if before_refs:
                value += before_refs[0][0]
            if not narrow:
                sum_refs[0][0] = value
                return
            for k in range(count):

                @pl.when(step // per == k)
                def _():
                    sum_refs[k][...] = value.astype(BF16)

        def tiles(fresh):
            value = ready_sum(left_ref[0], pairs if fresh or not raws else pairs + [tuple(refs)], top)
            if fresh:
                starts = [(ref, start) for ref, (_, start) in zip(raw_refs, raws)]
                value += raw_sum(left_ref[0], starts, *refs, top)
            put(value)

        if not raws:
            tiles(False)
            return

        @pl.when(step == 0)
        def _():
            tiles(True)

        @pl.when(step > 0)
        def _():
            tiles(False)

    def place(k):
        return pl.BlockSpec((64, TM), lambda i: (0, jnp.clip(i - k * per, 0, per - 1)))

    def whole(array):
        return pl.BlockSpec(array.shape, lambda i: (0, 0))

    acc_spec = pl.BlockSpec((1, 64, TM), lambda i: (i // per, 0, i % per))
    if narrow:
        sum_shapes = [jax.ShapeDtypeStruct((64, 1024), BF16)] * count
        sum_specs = [place(k) for k in range(count)]
    else:
        sum_shapes = [jax.ShapeDtypeStruct((count, 64, 1024), F32)]
        sum_specs = [acc_spec]
    made = []
    if raws:
        made = [jax.ShapeDtypeStruct((total, 128), BF16), jax.ShapeDtypeStruct((64, total), BF16)]
    out = pl.pallas_call(
        body,
        grid=(count * per,),
        out_shape=sum_shapes + made,
        in_specs=[
            pl.BlockSpec(memory_space=pltpu.SMEM),
            pl.BlockSpec((1, TM, 128), lambda i: (i // per, i % per, 0)),
        ]
        + [whole(part) for part in flat]
        + [whole(raw) for raw, _ in raws]
        + [acc_spec] * len(old),
        out_specs=sum_specs + [whole(part) for part in made],
        compiler_params=PARAMS,
        cost_estimate=cost(weight * count, cols),
        name="add_tiles",
    )(amp, left, *flat, *[raw for raw, _ in raws], *old)
    return (out[:sums] if narrow else out[0]), tuple(out[sums:])


def shift(value, axis, by):
    size = SIZES[NAMES.index(axis)]
    return lax.ppermute(value, axis, [(i, (i + by) % size) for i in range(size)])


def per_device(points, vectors, lengthscale, outscale, noise):
    zl = lax.axis_index("zl").astype(jnp.int32).reshape(1)
    amp = jnp.concatenate([outscale, jnp.log(outscale)])

    given, kept = first_pack(zl, points.T, vectors.T, lengthscale)
    got = shift(given, "zl", 1)
    half = copy_of([given], 64, kept, 4096)
    mines = [shift(half, "x", by) for by in (1, -1, 2)]
    own_left, share = second_pack(zl, amp, half, got, kept)

    beside = shift(share, "c", 1)
    near = [shift(share, "y", by) for by in (1, -1, 2)]
    mined = copy_of(mines, 64, share, 16)
    mined, beside = lax.optimization_barrier((mined, beside))
    theirs = shift(mined, "zl", 1)
    own, ready0 = add_tiles(amp, own_left, [], [(share, 0), (beside, 0)], weight=4096)
    near[0], near[1], near[2], own = lax.optimization_barrier((near[0], near[1], near[2], own))
    merged = jnp.concatenate([share] + near, axis=0)
    far = shift(merged, "zh", 1)
    merged_beside = shift(merged, "c", 1)
    own, ready1 = add_tiles(amp, own_left, [], [(merged, 512)], own, weight=64)

    theirs, own = lax.optimization_barrier((theirs, own))
    left = ready_rows(amp, mines, theirs)
    acc, ready2 = add_tiles(amp, left, [ready0, ready1], [(merged_beside, 512)])
    far, acc = lax.optimization_barrier((far, acc))
    far_beside = shift(far, "c", 1)
    acc, ready3 = add_tiles(amp, left, [], [(far, 0)], acc)
    sent, ready4 = add_tiles(amp, left, [], [(far_beside, 0)], acc, narrow=True)
    arrived = [shift(part, "x", by) for part, by in zip(sent, (-1, 1, 2))]
    own, _ = add_tiles(amp, own_left, [ready2, ready3, ready4], [], own)
    own = own[0]
    for part in arrived:
        own = own + part.astype(F32)
    result = own[:32] + shift(own[32:], "zl", 1)
    return result.T + noise[0] * vectors.astype(F32)


def solution(mesh):
    fine = Mesh(mesh.devices.reshape(SIZES), NAMES)
    placed = (P(BLK, "zl"), P(BLK, "zl"), P(), P(), P())
    return jax.shard_map(
        per_device, mesh=fine, in_specs=placed, out_specs=P(BLK, "zl"), check_vma=False
    )
```

time: 83.2 us -> 80.1 us (0.963)
  starting transfers between devices: 24.2 us -> 22.1 us
  waiting for transfers between devices: 10.4 us -> 9.01 us
    ppermute x15 -> x16, starting transfers between devices: 24.2 us -> 22.1 us  [shift(): lax.ppermute(value, axis, [(i, (i + by) % size) for i in range(size)])]
    ppermute x15 -> x16, waiting for transfers between devices: 10.4 us -> 9.01 us  [shift(): lax.ppermute(value, axis, [(i, (i + by) % size) for i in range(size)])]
    pallas_call x8 -> x10, Pallas kernels: 41.2 us -> 42.5 us  [the longest x6 41.4 us: add_tiles(): pl.pallas_call(body, grid=(count * per,), out_shape=sum_shapes + made, in...]
    pallas_call x2 -> x1, Pallas kernels: 2.37 us -> 1.46 us  [ready_rows(): pl.pallas_call(body, out_shape=jax.ShapeDtypeStruct((count, 1024, 128), B...]
    unnamed x10 -> x11, local copies, waits for them, and re-layouts: 2.37 us -> 2.39 us
  transfers between devices with their start and end apart: 15 -> 16, of which waited for: 7 -> 4; matrix products, arithmetic and copies ran while one was open for 0% -> 0% of each run, Pallas kernels for 39% -> 45%
where the time goes in v6:
time: 80.1 us; the launch traced here: 79.8 us
  Pallas kernels  43.9 us (55%)
  starting transfers between devices  22.1 us (28%)
  waiting for transfers between devices  9.01 us (11%)
  local copies, waits for them, and re-layouts  2.42 us (3%)
  between operations  1.57 us (2%)
  other arithmetic  0.81 us (1%)
    pallas_call x6, Pallas kernels, add_tiles(): pl.pallas_call(body, grid=(count * per,), out_shape=sum_shapes + made, in...  41.4 us
    ppermute x16, starting transfers between devices, shift(): lax.ppermute(value, axis, [(i, (i + by) % size) for i in range(size)])  22.1 us
    ppermute x16, waiting for transfers between devices, shift(): lax.ppermute(value, axis, [(i, (i + by) % size) for i in range(size)])  9.01 us
    unnamed x11, local copies, waits for them, and re-layouts  2.39 us
  transfers between devices with their start and end apart: 16, of which 4 were waited for; matrix products, arithmetic and copies ran while one was open for 0% of the time, Pallas kernels for 45%

profile of v6, /device:TPU:0, one launch (start us, length us, event | category | flops | bytes accessed | tf_op | source)
XLA Modules:
  0.0 79.8 jit_solution(9071010837047057046)
XLA Ops:
  0.0 0.7 copy-done.3
  0.7 0.8 %copy-done = bf16[1024,32]{0,1:T(8,128)(2,1)S(1)} copy-done((bf16[1024,32]{0,1:T(8,128)(2,1)S(1)}, bf16[1024,32]{0,1:T(8,128)(2,1)}, u32[]{:S(2)}) %copy-start) | copy-done | bytes 65560
  1.5 0.8 %copy-done.2 = bf16[1024,32]{0,1:T(8,128)(2,1)S(1)} copy-done((bf16[1024,32]{0,1:T(8,128)(2,1)S(1)}, bf16[1024,32]{0,1:T(8,128)(2,1)}, u32[]{:S(2)}) %copy-start.2) | copy-done | bytes 65560
  2.3 0.1 first_pack.1
  2.4 2.1 %collective-permute-start = (bf16[96,512]{1,0:T(8,128)(2,1)S(1)}, bf16[96,512]{1,0:T(8,128)(2,1)S(1)}, u32[]{:S(2)}, u32[]{:S(2)}) collective-permute-start(bf16[96,512]{1,0:T(8,128)(2,1)S(1)} %get-tuple-element.37.refs_0_), channel_id=1, source_target_pairs={{0,1},{1,0},{2,3},{3,2},{4,5},{5,4},{6,7},{7,6},{8,9},{9,8},{10,11... | collective-permute-start | bytes 294920 | tf_op jit(solution)/shard_map/ppermute | solution.py:253
  4.5 1.5 %collective-permute-start.1 = (bf16[64,512]{1,0:T(8,128)(2,1)S(1)}, bf16[64,512]{1,0:T(8,128)(2,1)S(1)}, u32[]{:S(2)}, u32[]{:S(2)}) collective-permute-start(bf16[64,512]{1,0:T(8,128)(2,1)S(1)} %copy_of.2.half_ref), channel_id=1, source_target_pairs={{0,16},{16,32},{32,48},{48,0},{1,17},{17,33},{33,49},{49,1},{2,18}... | collective-permute-start | bytes 196616 | tf_op jit(solution)/shard_map/ppermute | solution.py:253
  6.0 1.7 %collective-permute-start.2 = (bf16[64,512]{1,0:T(8,128)(2,1)S(1)}, bf16[64,512]{1,0:T(8,128)(2,1)S(1)}, u32[]{:S(2)}, u32[]{:S(2)}) collective-permute-start(bf16[64,512]{1,0:T(8,128)(2,1)S(1)} %copy_of.2.half_ref), channel_id=1, source_target_pairs={{0,48},{16,0},{32,16},{48,32},{1,49},{17,1},{33,17},{49,33},{2,50}... | collective-permute-start | bytes 196616 | tf_op jit(solution)/shard_map/ppermute | solution.py:253
  7.8 1.8 %collective-permute-start.3 = (bf16[64,512]{1,0:T(8,128)(2,1)S(1)}, bf16[64,512]{1,0:T(8,128)(2,1)S(1)}, u32[]{:S(2)}, u32[]{:S(2)}) collective-permute-start(bf16[64,512]{1,0:T(8,128)(2,1)S(1)} %copy_of.2.half_ref), channel_id=1, source_target_pairs={{0,32},{16,48},{32,0},{48,16},{1,33},{17,49},{33,1},{49,17},{2,34}... | collective-permute-start | bytes 196616 | tf_op jit(solution)/shard_map/ppermute | solution.py:253
  10.3 0.9 %second_pack.1 = (bf16[1,1024,128]{2,1,0:T(8,128)(2,1)S(1)}, bf16[512,128]{1,0:T(8,128)(2,1)S(1)}) custom-call(s32[1]{0:T(128)} %bitcast.zl_ref, f32[2]{0:T(128)S(1)} %pad_maximum_fusion.amp_ref, bf16[64,512]{1,0:T(8,128)(2,1)S(1)} %copy_of.2.half_ref, bf16[96,512]{1,0:T(8,128)(2,1)S(1)} %collective-permute-done.got_ref, ...), custom_call_target="tpu_custom_call" | custom-call | tf_op jit(solution)/shard_map/second_pack/pallas_call | solution.py:123
  11.3 0.1 collective-permute-start.4
  11.4 1.6 %collective-permute-start.6 = (bf16[512,128]{1,0:T(8,128)(2,1)S(1)}, bf16[512,128]{1,0:T(8,128)(2,1)S(1)}, u32[]{:S(2)}, u32[]{:S(2)}) collective-permute-start(bf16[512,128]{1,0:T(8,128)(2,1)S(1)} %get-tuple-element.39.token_ref.refs_0_), channel_id=1, source_target_pairs={{0,4},{4,8},{8,12},{12,0},{1,5},{5,9},{9,13},{13,1},{2,6},{6,10},{... | collective-permute-start | bytes 393224 | tf_op jit(solution)/shard_map/ppermute | solution.py:253
  13.0 1.7 %collective-permute-start.7 = (bf16[512,128]{1,0:T(8,128)(2,1)S(1)}, bf16[512,128]{1,0:T(8,128)(2,1)S(1)}, u32[]{:S(2)}, u32[]{:S(2)}) collective-permute-start(bf16[512,128]{1,0:T(8,128)(2,1)S(1)} %get-tuple-element.39.token_ref.refs_0_), channel_id=1, source_target_pairs={{0,12},{4,0},{8,4},{12,8},{1,13},{5,1},{9,5},{13,9},{2,14},{6,2},{... | collective-permute-start | bytes 393224 | tf_op jit(solution)/shard_map/ppermute | solution.py:253
  14.7 2.0 %collective-permute-start.8 = (bf16[512,128]{1,0:T(8,128)(2,1)S(1)}, bf16[512,128]{1,0:T(8,128)(2,1)S(1)}, u32[]{:S(2)}, u32[]{:S(2)}) collective-permute-start(bf16[512,128]{1,0:T(8,128)(2,1)S(1)} %get-tuple-element.39.token_ref.refs_0_), channel_id=1, source_target_pairs={{0,8},{4,12},{8,0},{12,4},{1,9},{5,13},{9,1},{13,5},{2,10},{6,14},... | collective-permute-start | bytes 393224 | tf_op jit(solution)/shard_map/ppermute | solution.py:253
  16.7 2.1 %add_tiles.6 = (f32[1,64,1024]{2,1,0:T(8,128)S(1)}, bf16[1024,128]{1,0:T(8,128)(2,1)S(1)}, bf16[64,1024]{1,0:T(8,128)(2,1)S(1)}) custom-call(f32[2]{0:T(128)S(1)} %pad_maximum_fusion.amp_ref, bf16[1,1024,128]{2,1,0:T(8,128)(2,1)S(1)} %get-tuple-element.38.left_ref, bf16[512,128]{1,0:T(8,128)(2,1)S(1)} %get-tuple-element.39.token_ref.refs_0_, ...), custom_call_target="tpu_custom_call" | custom-call | flops 2147483648 | bytes 393216 | tf_op jit(solution)/shard_map/add_tiles/pallas_call | solution.py:232
  18.8 0.5 collective-permute-done.7
  19.4 3.2 %collective-permute-done.8 = bf16[512,128]{1,0:T(8,128)(2,1)S(1)} collective-permute-done((bf16[512,128]{1,0:T(8,128)(2,1)S(1)}, bf16[512,128]{1,0:T(8,128)(2,1)S(1)}, u32[]{:S(2)}, u32[]{:S(2)}) %collective-permute-start.8) | collective-permute-done | bytes 131104 | tf_op jit(solution)/shard_map/ppermute | solution.py:253
  22.7 0.2 collective-permute-start.5
  22.9 3.9 %collective-permute-start.10 = (bf16[2048,128]{1,0:T(8,128)(2,1)S(1)}, bf16[2048,128]{1,0:T(8,128)(2,1)S(1)}, u32[]{:S(2)}, u32[]{:S(2)}) collective-permute-start(bf16[2048,128]{1,0:T(8,128)(2,1)S(1)} %constant_dynamic-update-slice_fusion.refs_0_), channel_id=1, source_target_pairs={{0,64},{64,0},{1,65},{65,1},{2,66},{66,2},{3,67},{67,3},{4,68},{68... | collective-permute-start | bytes 1572872 | tf_op jit(solution)/shard_map/ppermute | solution.py:253
  26.8 2.8 %add_tiles.7 = (f32[1,64,1024]{2,1,0:T(8,128)S(1)}, bf16[1536,128]{1,0:T(8,128)(2,1)S(1)}, bf16[64,1536]{1,0:T(8,128)(2,1)S(1)}) custom-call(f32[2]{0:T(128)S(1)} %pad_maximum_fusion.amp_ref, bf16[1,1024,128]{2,1,0:T(8,128)(2,1)S(1)} %get-tuple-element.38.left_ref, bf16[2048,128]{1,0:T(8,128)(2,1)S(1)} %constant_dynamic-update-slice_fusion.refs_0_, ...), custom_call_target="tpu_custom_call" | custom-call | flops 50331648 | bytes 589824 | tf_op jit(solution)/shard_map/add_tiles/pallas_call | solution.py:232
  29.6 1.0 %collective-permute-done.5.refs_3_ = bf16[192,512]{1,0:T(8,128)(2,1)S(1)} collective-permute-done((bf16[192,512]{1,0:T(8,128)(2,1)S(1)}, bf16[192,512]{1,0:T(8,128)(2,1)S(1)}, u32[]{:S(2)}, u32[]{:S(2)}) %collective-permute-start.5) | collective-permute-done | bytes 196640 | tf_op jit(solution)/shard_map/ppermute | solution.py:253
  30.5 1.5 %ready_rows.1.left_ref = bf16[3,1024,128]{2,1,0:T(8,128)(2,1)S(1)} custom-call(f32[2]{0:T(128)S(1)} %pad_maximum_fusion.amp_ref, bf16[64,512]{1,0:T(8,128)(2,1)S(1)} %collective-permute-done.1.refs_0_, bf16[64,512]{1,0:T(8,128)(2,1)S(1)} %collective-permute-done.2.refs_1_, bf16[64,512]{1,0:T(8,128)(2,1)S(1)} %collective-permute-done.3.refs_2_, ...), custom_call_target="tpu_custom_call" | custom-call | tf_op jit(solution)/shard_map/ready_rows/pallas_call | solution.py:57
  32.0 14.3 %add_tiles.8 = (f32[3,64,1024]{2,1,0:T(8,128)S(1)}, bf16[1536,128]{1,0:T(8,128)(2,1)S(1)}, bf16[64,1536]{1,0:T(8,128)(2,1)S(1)}) custom-call(f32[2]{0:T(128)S(1)} %pad_maximum_fusion.amp_ref, bf16[3,1024,128]{2,1,0:T(8,128)(2,1)S(1)} %ready_rows.1.left_ref, bf16[1024,128]{1,0:T(8,128)(2,1)S(1)} %get-tuple-element.49.refs_0_, ...), custom_call_target="tpu_custom_call" | custom-call | flops 6442450944 | bytes 1572864 | tf_op jit(solution)/shard_map/add_tiles/pallas_call | solution.py:232
  46.4 0.3 collective-permute-start.11
  46.6 7.8 %add_tiles.9 = (f32[3,64,1024]{2,1,0:T(8,128)S(1)}, bf16[2048,128]{1,0:T(8,128)(2,1)S(1)}, bf16[64,2048]{1,0:T(8,128)(2,1)S(1)}) custom-call(f32[2]{0:T(128)S(1)} %pad_maximum_fusion.amp_ref, bf16[3,1024,128]{2,1,0:T(8,128)(2,1)S(1)} %ready_rows.1.left_ref, bf16[2048,128]{1,0:T(8,128)(2,1)S(1)} %collective-permute-done.10.refs_0_, ...), custom_call_target="tpu_custom_call" | custom-call | flops 3221225472 | bytes 786432 | tf_op jit(solution)/shard_map/add_tiles/pallas_call | solution.py:232
  54.5 8.0 %add_tiles.10 = (bf16[64,1024]{1,0:T(8,128)(2,1)S(1)}, bf16[64,1024]{1,0:T(8,128)(2,1)S(1)}, bf16[64,1024]{1,0:T(8,128)(2,1)S(1)}, bf16[2048,128]{1,0:T(8,128)(2,1)S(1)}, bf16[64,2048]{1,0:T(8,128)(2,1)S(1)}) custom-call(f32[2]{0:T(128)S(1)} %pad_maximum_fusion.amp_ref, bf16[3,1024,128]{2,1,0:T(8,128)(2,1)S(1)} %ready_rows.1.left_ref, ...), custom_call_target="tpu_custom_call" | custom-call | flops 3221225472 | bytes 786432 | tf_op jit(solution)/shard_map/add_tiles/pallas_call | solution.py:232
  62.5 1.8 %collective-permute-start.14 = (bf16[64,1024]{1,0:T(8,128)(2,1)S(1)}, bf16[64,1024]{1,0:T(8,128)(2,1)S(1)}, u32[]{:S(2)}, u32[]{:S(2)}) collective-permute-start(bf16[64,1024]{1,0:T(8,128)(2,1)S(1)} %get-tuple-element.66), channel_id=1, source_target_pairs={{0,32},{16,48},{32,0},{48,16},{1,33},{17,49},{33,1},{49,17},{2,34}... | collective-permute-start | bytes 393224 | tf_op jit(solution)/shard_map/ppermute | solution.py:253
  64.3 0.3 collective-permute-start.13
  64.6 3.0 %collective-permute-start.12 = (bf16[64,1024]{1,0:T(8,128)(2,1)S(1)}, bf16[64,1024]{1,0:T(8,128)(2,1)S(1)}, u32[]{:S(2)}, u32[]{:S(2)}) collective-permute-start(bf16[64,1024]{1,0:T(8,128)(2,1)S(1)} %get-tuple-element.64), channel_id=1, source_target_pairs={{0,48},{16,0},{32,16},{48,32},{1,49},{17,1},{33,17},{49,33},{2,50}... | collective-permute-start | bytes 393224 | tf_op jit(solution)/shard_map/ppermute | solution.py:253
  67.6 6.3 %add_tiles.11 = f32[1,64,1024]{2,1,0:T(8,128)S(1)} custom-call(f32[2]{0:T(128)S(1)} %pad_maximum_fusion.amp_ref, bf16[1,1024,128]{2,1,0:T(8,128)(2,1)S(1)} %get-tuple-element.38.left_ref, bf16[1536,128]{1,0:T(8,128)(2,1)S(1)} %get-tuple-element.53.refs_0_, bf16[64,1536]{1,0:T(8,128)(2,1)S(1)} %get-tuple-element.54.refs_1_, ...), custom_call_target="tpu_custom_call" | custom-call | flops 2952790016 | bytes 2162688 | tf_op jit(solution)/shard_map/add_tiles/pallas_call | solution.py:232
  74.0 0.2 collective-permute-start.15
  74.9 4.3 %collective-permute-done.15 = f32[32,1024]{1,0:T(8,128)S(1)} collective-permute-done((f32[32,1024]{1,0:T(8,128)S(1)}, f32[32,1024]{1,0:T(8,128)S(1)}, u32[]{:S(2)}, u32[]{:S(2)}) %collective-permute-start.15) | collective-permute-done | bytes 131104 | tf_op jit(solution)/shard_map/ppermute | solution.py:253
  79.2 0.7 fusion.3
  (27 shorter events, 0.4 us)
Async XLA Ops:
  0.0 0.7 copy-start.3
  0.7 0.8 %copy-start = (bf16[1024,32]{0,1:T(8,128)(2,1)S(1)}, bf16[1024,32]{0,1:T(8,128)(2,1)}, u32[]{:S(2)}) copy-start(bf16[1024,32]{0,1:T(8,128)(2,1)} %param.6) | copy-start | bytes 196612
  1.5 0.8 %copy-start.2 = (bf16[1024,32]{0,1:T(8,128)(2,1)S(1)}, bf16[1024,32]{0,1:T(8,128)(2,1)}, u32[]{:S(2)}) copy-start(bf16[1024,32]{0,1:T(8,128)(2,1)} %param.5) | copy-start | bytes 196612
  2.4 7.9 %collective-permute-start = (bf16[96,512]{1,0:T(8,128)(2,1)S(1)}, bf16[96,512]{1,0:T(8,128)(2,1)S(1)}, u32[]{:S(2)}, u32[]{:S(2)}) collective-permute-start(bf16[96,512]{1,0:T(8,128)(2,1)S(1)} %get-tuple-element.37.refs_0_), channel_id=1, source_target_pairs={{0,1},{1,0},{2,3},{3,2},{4,5},{5,4},{6,7},{7,6},{8,9},{9,8},{10,11... | collective-permute-start | bytes 294920 | tf_op jit(solution)/shard_map/ppermute | solution.py:253
  4.5 8.5 %collective-permute-start.1 = (bf16[64,512]{1,0:T(8,128)(2,1)S(1)}, bf16[64,512]{1,0:T(8,128)(2,1)S(1)}, u32[]{:S(2)}, u32[]{:S(2)}) collective-permute-start(bf16[64,512]{1,0:T(8,128)(2,1)S(1)} %copy_of.2.half_ref), channel_id=1, source_target_pairs={{0,16},{16,32},{32,48},{48,0},{1,17},{17,33},{33,49},{49,1},{2,18}... | collective-permute-start | bytes 196616 | tf_op jit(solution)/shard_map/ppermute | solution.py:253
  6.0 8.7 %collective-permute-start.2 = (bf16[64,512]{1,0:T(8,128)(2,1)S(1)}, bf16[64,512]{1,0:T(8,128)(2,1)S(1)}, u32[]{:S(2)}, u32[]{:S(2)}) collective-permute-start(bf16[64,512]{1,0:T(8,128)(2,1)S(1)} %copy_of.2.half_ref), channel_id=1, source_target_pairs={{0,48},{16,0},{32,16},{48,32},{1,49},{17,1},{33,17},{49,33},{2,50}... | collective-permute-start | bytes 196616 | tf_op jit(solution)/shard_map/ppermute | solution.py:253
  7.8 8.9 %collective-permute-start.3 = (bf16[64,512]{1,0:T(8,128)(2,1)S(1)}, bf16[64,512]{1,0:T(8,128)(2,1)S(1)}, u32[]{:S(2)}, u32[]{:S(2)}) collective-permute-start(bf16[64,512]{1,0:T(8,128)(2,1)S(1)} %copy_of.2.half_ref), channel_id=1, source_target_pairs={{0,32},{16,48},{32,0},{48,16},{1,33},{17,49},{33,1},{49,17},{2,34}... | collective-permute-start | bytes 196616 | tf_op jit(solution)/shard_map/ppermute | solution.py:253
  11.3 5.4 %collective-permute-start.4 = (bf16[512,128]{1,0:T(8,128)(2,1)S(1)}, bf16[512,128]{1,0:T(8,128)(2,1)S(1)}, u32[]{:S(2)}, u32[]{:S(2)}) collective-permute-start(bf16[512,128]{1,0:T(8,128)(2,1)S(1)} %get-tuple-element.39.token_ref.refs_0_), channel_id=1, source_target_pairs={{0,2},{2,0},{1,3},{3,1},{4,6},{6,4},{5,7},{7,5},{8,10},{10,8},{9,1... | collective-permute-start | bytes 393224 | tf_op jit(solution)/shard_map/ppermute | solution.py:253
  11.4 7.4 %collective-permute-start.6 = (bf16[512,128]{1,0:T(8,128)(2,1)S(1)}, bf16[512,128]{1,0:T(8,128)(2,1)S(1)}, u32[]{:S(2)}, u32[]{:S(2)}) collective-permute-start(bf16[512,128]{1,0:T(8,128)(2,1)S(1)} %get-tuple-element.39.token_ref.refs_0_), channel_id=1, source_target_pairs={{0,4},{4,8},{8,12},{12,0},{1,5},{5,9},{9,13},{13,1},{2,6},{6,10},{... | collective-permute-start | bytes 393224 | tf_op jit(solution)/shard_map/ppermute | solution.py:253
  13.0 6.3 %collective-permute-start.7 = (bf16[512,128]{1,0:T(8,128)(2,1)S(1)}, bf16[512,128]{1,0:T(8,128)(2,1)S(1)}, u32[]{:S(2)}, u32[]{:S(2)}) collective-permute-start(bf16[512,128]{1,0:T(8,128)(2,1)S(1)} %get-tuple-element.39.token_ref.refs_0_), channel_id=1, source_target_pairs={{0,12},{4,0},{8,4},{12,8},{1,13},{5,1},{9,5},{13,9},{2,14},{6,2},{... | collective-permute-start | bytes 393224 | tf_op jit(solution)/shard_map/ppermute | solution.py:253
  14.7 7.9 %collective-permute-start.8 = (bf16[512,128]{1,0:T(8,128)(2,1)S(1)}, bf16[512,128]{1,0:T(8,128)(2,1)S(1)}, u32[]{:S(2)}, u32[]{:S(2)}) collective-permute-start(bf16[512,128]{1,0:T(8,128)(2,1)S(1)} %get-tuple-element.39.token_ref.refs_0_), channel_id=1, source_target_pairs={{0,8},{4,12},{8,0},{12,4},{1,9},{5,13},{9,1},{13,5},{2,10},{6,14},... | collective-permute-start | bytes 393224 | tf_op jit(solution)/shard_map/ppermute | solution.py:253
  22.6 9.4 %collective-permute-start.9 = (bf16[2048,128]{1,0:T(8,128)(2,1)S(1)}, bf16[2048,128]{1,0:T(8,128)(2,1)S(1)}, u32[]{:S(2)}, u32[]{:S(2)}) collective-permute-start(bf16[2048,128]{1,0:T(8,128)(2,1)S(1)} %constant_dynamic-update-slice_fusion.refs_0_), channel_id=1, source_target_pairs={{0,2},{2,0},{1,3},{3,1},{4,6},{6,4},{5,7},{7,5},{8,10},{10,8},{9,1... | collective-permute-start | bytes 1572872 | tf_op jit(solution)/shard_map/ppermute | solution.py:253
  22.7 7.8 %collective-permute-start.5 = (bf16[192,512]{1,0:T(8,128)(2,1)S(1)}, bf16[192,512]{1,0:T(8,128)(2,1)S(1)}, u32[]{:S(2)}, u32[]{:S(2)}) collective-permute-start(bf16[192,512]{1,0:T(8,128)(2,1)S(1)} %copy_of.3), channel_id=1, source_target_pairs={{0,1},{1,0},{2,3},{3,2},{4,5},{5,4},{6,7},{7,6},{8,9},{9,8},{10,11... | collective-permute-start | bytes 589832 | tf_op jit(solution)/shard_map/ppermute | solution.py:253
  22.9 23.4 %collective-permute-start.10 = (bf16[2048,128]{1,0:T(8,128)(2,1)S(1)}, bf16[2048,128]{1,0:T(8,128)(2,1)S(1)}, u32[]{:S(2)}, u32[]{:S(2)}) collective-permute-start(bf16[2048,128]{1,0:T(8,128)(2,1)S(1)} %constant_dynamic-update-slice_fusion.refs_0_), channel_id=1, source_target_pairs={{0,64},{64,0},{1,65},{65,1},{2,66},{66,2},{3,67},{67,3},{4,68},{68... | collective-permute-start | bytes 1572872 | tf_op jit(solution)/shard_map/ppermute | solution.py:253
  46.4 8.1 %collective-permute-start.11 = (bf16[2048,128]{1,0:T(8,128)(2,1)S(1)}, bf16[2048,128]{1,0:T(8,128)(2,1)S(1)}, u32[]{:S(2)}, u32[]{:S(2)}) collective-permute-start(bf16[2048,128]{1,0:T(8,128)(2,1)S(1)} %collective-permute-done.10.refs_0_), channel_id=1, source_target_pairs={{0,2},{2,0},{1,3},{3,1},{4,6},{6,4},{5,7},{7,5},{8,10},{10,8},{9,1... | collective-permute-start | bytes 1572872 | tf_op jit(solution)/shard_map/ppermute | solution.py:253
  62.5 11.4 %collective-permute-start.14 = (bf16[64,1024]{1,0:T(8,128)(2,1)S(1)}, bf16[64,1024]{1,0:T(8,128)(2,1)S(1)}, u32[]{:S(2)}, u32[]{:S(2)}) collective-permute-start(bf16[64,1024]{1,0:T(8,128)(2,1)S(1)} %get-tuple-element.66), channel_id=1, source_target_pairs={{0,32},{16,48},{32,0},{48,16},{1,33},{17,49},{33,1},{49,17},{2,34}... | collective-permute-start | bytes 393224 | tf_op jit(solution)/shard_map/ppermute | solution.py:253
  64.3 9.6 %collective-permute-start.13 = (bf16[64,1024]{1,0:T(8,128)(2,1)S(1)}, bf16[64,1024]{1,0:T(8,128)(2,1)S(1)}, u32[]{:S(2)}, u32[]{:S(2)}) collective-permute-start(bf16[64,1024]{1,0:T(8,128)(2,1)S(1)} %get-tuple-element.65), channel_id=1, source_target_pairs={{0,16},{16,32},{32,48},{48,0},{1,17},{17,33},{33,49},{49,1},{2,18}... | collective-permute-start | bytes 393224 | tf_op jit(solution)/shard_map/ppermute | solution.py:253
  64.6 9.3 %collective-permute-start.12 = (bf16[64,1024]{1,0:T(8,128)(2,1)S(1)}, bf16[64,1024]{1,0:T(8,128)(2,1)S(1)}, u32[]{:S(2)}, u32[]{:S(2)}) collective-permute-start(bf16[64,1024]{1,0:T(8,128)(2,1)S(1)} %get-tuple-element.64), channel_id=1, source_target_pairs={{0,48},{16,0},{32,16},{48,32},{1,49},{17,1},{33,17},{49,33},{2,50}... | collective-permute-start | bytes 393224 | tf_op jit(solution)/shard_map/ppermute | solution.py:253
  74.0 5.1 %copy-start.1 = (bf16[1024,32]{0,1:T(8,128)(2,1)S(1)}, bf16[1024,32]{0,1:T(8,128)(2,1)}, u32[]{:S(2)}) copy-start(bf16[1024,32]{0,1:T(8,128)(2,1)} %param.6) | copy-start | bytes 196612
  74.0 5.1 %collective-permute-start.15 = (f32[32,1024]{1,0:T(8,128)S(1)}, f32[32,1024]{1,0:T(8,128)S(1)}, u32[]{:S(2)}, u32[]{:S(2)}) collective-permute-start(f32[32,1024]{1,0:T(8,128)S(1)} %slice.9), channel_id=1, source_target_pairs={{0,1},{1,0},{2,3},{3,2},{4,5},{5,4},{6,7},{7,6},{8,9},{9,8},{10,11... | collective-permute-start | bytes 393224 | tf_op jit(solution)/shard_map/ppermute | solution.py:253

commit v7 on v6

--- a/solution.py
+++ b/solution.py
@@ -149,16 +149,20 @@
 def raw_sum(left, raws, right_ref, vectors_ref, top):
     total = right_ref.shape[0]
     result = jnp.zeros((64, left.shape[0]), F32)
-    at = back = 0
+    at = 0
+    rights, turned = [], []
     for ref, start in raws:
         for sub in range(start, ref.shape[0], 512):
             wide = ref[sub : sub + 512, :].astype(F32)
-            right_ref[at : at + 512, :] = with_norms(wide, 0.0, 64, 67)
-            vectors_ref[:, at : at + 512] = wide.T[64:, :].astype(BF16)
+            rights.append(with_norms(wide, 0.0, 64, 67))
+            turned.append(wide.T[64:, :].astype(BF16))
+            right_ref[at : at + 512, :] = rights[-1]
+            vectors_ref[:, at : at + 512] = turned[-1]
             at += 512
-            if at - back == TN or at == total:
-                result += one_block(left, right_ref[back:at, :], vectors_ref[:, back:at], top)
-                back = at
+            if len(rights) * 512 == TN or at == total:
+                right = jnp.concatenate(rights, axis=0)
+                result += one_block(left, right, jnp.concatenate(turned, axis=1), top)
+                rights, turned = [], []
     return result
 
 
@@ -260,11 +264,11 @@
     given, kept = first_pack(zl, points.T, vectors.T, lengthscale)
     got = shift(given, "zl", 1)
     half = copy_of([given], 64, kept, 4096)
-    mines = [shift(half, "x", by) for by in (1, -1, 2)]
+    mines = [shift(half, "x", by) for by in (2, 1, -1)]
     own_left, share = second_pack(zl, amp, half, got, kept)
 
     beside = shift(share, "c", 1)
-    near = [shift(share, "y", by) for by in (1, -1, 2)]
+    near = [shift(share, "y", by) for by in (2, 1, -1)]
     mined = copy_of(mines, 64, share, 16)
     mined, beside = lax.optimization_barrier((mined, beside))
     theirs = shift(mined, "zl", 1)
@@ -282,7 +286,7 @@
     far_beside = shift(far, "c", 1)
     acc, ready3 = add_tiles(amp, left, [], [(far, 0)], acc)
     sent, ready4 = add_tiles(amp, left, [], [(far_beside, 0)], acc, narrow=True)
-    arrived = [shift(part, "x", by) for part, by in zip(sent, (-1, 1, 2))]
+    arrived = [shift(part, "x", by) for part, by in zip(sent, (2, -1, 1))]
     own, _ = add_tiles(amp, own_left, [ready2, ready3, ready4], [], own)
     own = own[0]
     for part in arrived:

time: 80.1 us -> 79.1 us (0.988)
  waiting for transfers between devices: 9.01 us -> 7.63 us
    ppermute x16, waiting for transfers between devices: 9.01 us -> 7.63 us  [shift(): lax.ppermute(value, axis, [(i, (i + by) % size) for i in range(size)])]
  transfers between devices with their start and end apart: 16 -> 16, of which waited for: 4 -> 5; matrix products, arithmetic and copies ran while one was open for 0% -> 0% of each run, Pallas kernels for 45% -> 45%
where the time goes in v7:
time: 79.1 us; the launch traced here: 78.8 us
  Pallas kernels  43.5 us (55%)
  starting transfers between devices  22.8 us (29%)
  waiting for transfers between devices  7.63 us (10%)
  local copies, waits for them, and re-layouts  2.42 us (3%)
  between operations  1.56 us (2%)
  other arithmetic  0.81 us (1%)
    pallas_call x6, Pallas kernels, add_tiles(): pl.pallas_call(body, grid=(count * per,), out_shape=sum_shapes + made, in...  41 us
    ppermute x16, starting transfers between devices, shift(): lax.ppermute(value, axis, [(i, (i + by) % size) for i in range(size)])  22.8 us
    ppermute x16, waiting for transfers between devices, shift(): lax.ppermute(value, axis, [(i, (i + by) % size) for i in range(size)])  7.63 us
    unnamed x11, local copies, waits for them, and re-layouts  2.39 us
  transfers between devices with their start and end apart: 16, of which 5 were waited for; matrix products, arithmetic and copies ran while one was open for 0% of the time, Pallas kernels for 45%

profile of v7, /device:TPU:0, one launch (start us, length us, event | category | flops | bytes accessed | tf_op | source)
XLA Modules:
  0.0 78.8 jit_solution(15817342076165779306)
XLA Ops:
  0.0 0.7 copy-done.3
  0.7 0.8 %copy-done = bf16[1024,32]{0,1:T(8,128)(2,1)S(1)} copy-done((bf16[1024,32]{0,1:T(8,128)(2,1)S(1)}, bf16[1024,32]{0,1:T(8,128)(2,1)}, u32[]{:S(2)}) %copy-start) | copy-done | bytes 65560
  1.5 0.8 %copy-done.2 = bf16[1024,32]{0,1:T(8,128)(2,1)S(1)} copy-done((bf16[1024,32]{0,1:T(8,128)(2,1)S(1)}, bf16[1024,32]{0,1:T(8,128)(2,1)}, u32[]{:S(2)}) %copy-start.2) | copy-done | bytes 65560
  2.3 0.1 first_pack.1
  2.4 2.1 %collective-permute-start = (bf16[96,512]{1,0:T(8,128)(2,1)S(1)}, bf16[96,512]{1,0:T(8,128)(2,1)S(1)}, u32[]{:S(2)}, u32[]{:S(2)}) collective-permute-start(bf16[96,512]{1,0:T(8,128)(2,1)S(1)} %get-tuple-element.37.refs_0_), channel_id=1, source_target_pairs={{0,1},{1,0},{2,3},{3,2},{4,5},{5,4},{6,7},{7,6},{8,9},{9,8},{10,11... | collective-permute-start | bytes 294920 | tf_op jit(solution)/shard_map/ppermute | solution.py:257
  4.5 3.0 %collective-permute-start.1 = (bf16[64,512]{1,0:T(8,128)(2,1)S(1)}, bf16[64,512]{1,0:T(8,128)(2,1)S(1)}, u32[]{:S(2)}, u32[]{:S(2)}) collective-permute-start(bf16[64,512]{1,0:T(8,128)(2,1)S(1)} %copy_of.2.half_ref), channel_id=1, source_target_pairs={{0,32},{16,48},{32,0},{48,16},{1,33},{17,49},{33,1},{49,17},{2,34}... | collective-permute-start | bytes 196616 | tf_op jit(solution)/shard_map/ppermute | solution.py:257
  7.6 0.6 collective-permute-start.2
  8.1 2.6 %collective-permute-start.3 = (bf16[64,512]{1,0:T(8,128)(2,1)S(1)}, bf16[64,512]{1,0:T(8,128)(2,1)S(1)}, u32[]{:S(2)}, u32[]{:S(2)}) collective-permute-start(bf16[64,512]{1,0:T(8,128)(2,1)S(1)} %copy_of.2.half_ref), channel_id=1, source_target_pairs={{0,48},{16,0},{32,16},{48,32},{1,49},{17,1},{33,17},{49,33},{2,50}... | collective-permute-start | bytes 196616 | tf_op jit(solution)/shard_map/ppermute | solution.py:257
  11.6 0.9 %second_pack.1 = (bf16[1,1024,128]{2,1,0:T(8,128)(2,1)S(1)}, bf16[512,128]{1,0:T(8,128)(2,1)S(1)}) custom-call(s32[1]{0:T(128)} %bitcast.zl_ref, f32[2]{0:T(128)S(1)} %pad_maximum_fusion.amp_ref, bf16[64,512]{1,0:T(8,128)(2,1)S(1)} %copy_of.2.half_ref, bf16[96,512]{1,0:T(8,128)(2,1)S(1)} %collective-permute-done.got_ref, ...), custom_call_target="tpu_custom_call" | custom-call | tf_op jit(solution)/shard_map/second_pack/pallas_call | solution.py:123
  12.5 0.1 collective-permute-start.4
  12.6 3.3 %collective-permute-start.6 = (bf16[512,128]{1,0:T(8,128)(2,1)S(1)}, bf16[512,128]{1,0:T(8,128)(2,1)S(1)}, u32[]{:S(2)}, u32[]{:S(2)}) collective-permute-start(bf16[512,128]{1,0:T(8,128)(2,1)S(1)} %get-tuple-element.39.token_ref.refs_0_), channel_id=1, source_target_pairs={{0,8},{4,12},{8,0},{12,4},{1,9},{5,13},{9,1},{13,5},{2,10},{6,14},... | collective-permute-start | bytes 393224 | tf_op jit(solution)/shard_map/ppermute | solution.py:257
  15.9 0.7 collective-permute-start.7
  16.6 2.6 %collective-permute-start.8 = (bf16[512,128]{1,0:T(8,128)(2,1)S(1)}, bf16[512,128]{1,0:T(8,128)(2,1)S(1)}, u32[]{:S(2)}, u32[]{:S(2)}) collective-permute-start(bf16[512,128]{1,0:T(8,128)(2,1)S(1)} %get-tuple-element.39.token_ref.refs_0_), channel_id=1, source_target_pairs={{0,12},{4,0},{8,4},{12,8},{1,13},{5,1},{9,5},{13,9},{2,14},{6,2},{... | collective-permute-start | bytes 393224 | tf_op jit(solution)/shard_map/ppermute | solution.py:257
  19.2 2.1 %add_tiles.6 = (f32[1,64,1024]{2,1,0:T(8,128)S(1)}, bf16[1024,128]{1,0:T(8,128)(2,1)S(1)}, bf16[64,1024]{1,0:T(8,128)(2,1)S(1)}) custom-call(f32[2]{0:T(128)S(1)} %pad_maximum_fusion.amp_ref, bf16[1,1024,128]{2,1,0:T(8,128)(2,1)S(1)} %get-tuple-element.38.left_ref, bf16[512,128]{1,0:T(8,128)(2,1)S(1)} %get-tuple-element.39.token_ref.refs_0_, ...), custom_call_target="tpu_custom_call" | custom-call | flops 2147483648 | bytes 393216 | tf_op jit(solution)/shard_map/add_tiles/pallas_call | solution.py:236
  21.3 1.7 %collective-permute-done.7 = bf16[512,128]{1,0:T(8,128)(2,1)S(1)} collective-permute-done((bf16[512,128]{1,0:T(8,128)(2,1)S(1)}, bf16[512,128]{1,0:T(8,128)(2,1)S(1)}, u32[]{:S(2)}, u32[]{:S(2)}) %collective-permute-start.7) | collective-permute-done | bytes 131104 | tf_op jit(solution)/shard_map/ppermute | solution.py:257
  23.0 0.2 collective-permute-done.8
  23.2 0.1 collective-permute-start.9
  23.3 0.2 collective-permute-start.5
  23.5 3.9 %collective-permute-start.10 = (bf16[2048,128]{1,0:T(8,128)(2,1)S(1)}, bf16[2048,128]{1,0:T(8,128)(2,1)S(1)}, u32[]{:S(2)}, u32[]{:S(2)}) collective-permute-start(bf16[2048,128]{1,0:T(8,128)(2,1)S(1)} %constant_dynamic-update-slice_fusion.refs_0_), channel_id=1, source_target_pairs={{0,64},{64,0},{1,65},{65,1},{2,66},{66,2},{3,67},{67,3},{4,68},{68... | collective-permute-start | bytes 1572872 | tf_op jit(solution)/shard_map/ppermute | solution.py:257
  27.4 2.7 %add_tiles.7 = (f32[1,64,1024]{2,1,0:T(8,128)S(1)}, bf16[1536,128]{1,0:T(8,128)(2,1)S(1)}, bf16[64,1536]{1,0:T(8,128)(2,1)S(1)}) custom-call(f32[2]{0:T(128)S(1)} %pad_maximum_fusion.amp_ref, bf16[1,1024,128]{2,1,0:T(8,128)(2,1)S(1)} %get-tuple-element.38.left_ref, bf16[2048,128]{1,0:T(8,128)(2,1)S(1)} %constant_dynamic-update-slice_fusion.refs_0_, ...), custom_call_target="tpu_custom_call" | custom-call | flops 50331648 | bytes 589824 | tf_op jit(solution)/shard_map/add_tiles/pallas_call | solution.py:236
  30.1 1.0 %collective-permute-done.5.refs_3_ = bf16[192,512]{1,0:T(8,128)(2,1)S(1)} collective-permute-done((bf16[192,512]{1,0:T(8,128)(2,1)S(1)}, bf16[192,512]{1,0:T(8,128)(2,1)S(1)}, u32[]{:S(2)}, u32[]{:S(2)}) %collective-permute-start.5) | collective-permute-done | bytes 196640 | tf_op jit(solution)/shard_map/ppermute | solution.py:257
  31.1 1.5 %ready_rows.1.left_ref = bf16[3,1024,128]{2,1,0:T(8,128)(2,1)S(1)} custom-call(f32[2]{0:T(128)S(1)} %pad_maximum_fusion.amp_ref, bf16[64,512]{1,0:T(8,128)(2,1)S(1)} %collective-permute-done.1.refs_0_, bf16[64,512]{1,0:T(8,128)(2,1)S(1)} %collective-permute-done.2.refs_1_, bf16[64,512]{1,0:T(8,128)(2,1)S(1)} %collective-permute-done.3.refs_2_, ...), custom_call_target="tpu_custom_call" | custom-call | tf_op jit(solution)/shard_map/ready_rows/pallas_call | solution.py:57
  32.6 14.3 %add_tiles.8 = (f32[3,64,1024]{2,1,0:T(8,128)S(1)}, bf16[1536,128]{1,0:T(8,128)(2,1)S(1)}, bf16[64,1536]{1,0:T(8,128)(2,1)S(1)}) custom-call(f32[2]{0:T(128)S(1)} %pad_maximum_fusion.amp_ref, bf16[3,1024,128]{2,1,0:T(8,128)(2,1)S(1)} %ready_rows.1.left_ref, bf16[1024,128]{1,0:T(8,128)(2,1)S(1)} %get-tuple-element.49.refs_0_, ...), custom_call_target="tpu_custom_call" | custom-call | flops 6442450944 | bytes 1572864 | tf_op jit(solution)/shard_map/add_tiles/pallas_call | solution.py:236
  46.9 0.3 collective-permute-start.11
  47.2 7.7 %add_tiles.9 = (f32[3,64,1024]{2,1,0:T(8,128)S(1)}, bf16[2048,128]{1,0:T(8,128)(2,1)S(1)}, bf16[64,2048]{1,0:T(8,128)(2,1)S(1)}) custom-call(f32[2]{0:T(128)S(1)} %pad_maximum_fusion.amp_ref, bf16[3,1024,128]{2,1,0:T(8,128)(2,1)S(1)} %ready_rows.1.left_ref, bf16[2048,128]{1,0:T(8,128)(2,1)S(1)} %collective-permute-done.10.refs_0_, ...), custom_call_target="tpu_custom_call" | custom-call | flops 3221225472 | bytes 786432 | tf_op jit(solution)/shard_map/add_tiles/pallas_call | solution.py:236
  54.9 7.9 %add_tiles.10 = (bf16[64,1024]{1,0:T(8,128)(2,1)S(1)}, bf16[64,1024]{1,0:T(8,128)(2,1)S(1)}, bf16[64,1024]{1,0:T(8,128)(2,1)S(1)}, bf16[2048,128]{1,0:T(8,128)(2,1)S(1)}, bf16[64,2048]{1,0:T(8,128)(2,1)S(1)}) custom-call(f32[2]{0:T(128)S(1)} %pad_maximum_fusion.amp_ref, bf16[3,1024,128]{2,1,0:T(8,128)(2,1)S(1)} %ready_rows.1.left_ref, ...), custom_call_target="tpu_custom_call" | custom-call | flops 3221225472 | bytes 786432 | tf_op jit(solution)/shard_map/add_tiles/pallas_call | solution.py:236
  62.9 3.2 %collective-permute-start.13 = (bf16[64,1024]{1,0:T(8,128)(2,1)S(1)}, bf16[64,1024]{1,0:T(8,128)(2,1)S(1)}, u32[]{:S(2)}, u32[]{:S(2)}) collective-permute-start(bf16[64,1024]{1,0:T(8,128)(2,1)S(1)} %get-tuple-element.65), channel_id=1, source_target_pairs={{0,48},{16,0},{32,16},{48,32},{1,49},{17,1},{33,17},{49,33},{2,50}... | collective-permute-start | bytes 393224 | tf_op jit(solution)/shard_map/ppermute | solution.py:257
  66.2 6.3 %add_tiles.11 = f32[1,64,1024]{2,1,0:T(8,128)S(1)} custom-call(f32[2]{0:T(128)S(1)} %pad_maximum_fusion.amp_ref, bf16[1,1024,128]{2,1,0:T(8,128)(2,1)S(1)} %get-tuple-element.38.left_ref, bf16[1536,128]{1,0:T(8,128)(2,1)S(1)} %get-tuple-element.53.refs_0_, bf16[64,1536]{1,0:T(8,128)(2,1)S(1)} %get-tuple-element.54.refs_1_, ...), custom_call_target="tpu_custom_call" | custom-call | flops 2952790016 | bytes 2162688 | tf_op jit(solution)/shard_map/add_tiles/pallas_call | solution.py:236
  72.5 0.4 collective-permute-done.12
  73.1 0.2 collective-permute-start.15
  73.9 4.2 %collective-permute-done.15 = f32[32,1024]{1,0:T(8,128)S(1)} collective-permute-done((f32[32,1024]{1,0:T(8,128)S(1)}, f32[32,1024]{1,0:T(8,128)S(1)}, u32[]{:S(2)}, u32[]{:S(2)}) %collective-permute-start.15) | collective-permute-done | bytes 131104 | tf_op jit(solution)/shard_map/ppermute | solution.py:257
  78.1 0.7 fusion.3
  (27 shorter events, 0.3 us)
Async XLA Ops:
  0.0 0.7 copy-start.3
  0.7 0.8 %copy-start = (bf16[1024,32]{0,1:T(8,128)(2,1)S(1)}, bf16[1024,32]{0,1:T(8,128)(2,1)}, u32[]{:S(2)}) copy-start(bf16[1024,32]{0,1:T(8,128)(2,1)} %param.6) | copy-start | bytes 196612
  1.5 0.8 %copy-start.2 = (bf16[1024,32]{0,1:T(8,128)(2,1)S(1)}, bf16[1024,32]{0,1:T(8,128)(2,1)}, u32[]{:S(2)}) copy-start(bf16[1024,32]{0,1:T(8,128)(2,1)} %param.5) | copy-start | bytes 196612
  2.4 9.1 %collective-permute-start = (bf16[96,512]{1,0:T(8,128)(2,1)S(1)}, bf16[96,512]{1,0:T(8,128)(2,1)S(1)}, u32[]{:S(2)}, u32[]{:S(2)}) collective-permute-start(bf16[96,512]{1,0:T(8,128)(2,1)S(1)} %get-tuple-element.37.refs_0_), channel_id=1, source_target_pairs={{0,1},{1,0},{2,3},{3,2},{4,5},{5,4},{6,7},{7,6},{8,9},{9,8},{10,11... | collective-permute-start | bytes 294920 | tf_op jit(solution)/shard_map/ppermute | solution.py:257
  4.5 11.3 %collective-permute-start.1 = (bf16[64,512]{1,0:T(8,128)(2,1)S(1)}, bf16[64,512]{1,0:T(8,128)(2,1)S(1)}, u32[]{:S(2)}, u32[]{:S(2)}) collective-permute-start(bf16[64,512]{1,0:T(8,128)(2,1)S(1)} %copy_of.2.half_ref), channel_id=1, source_target_pairs={{0,32},{16,48},{32,0},{48,16},{1,33},{17,49},{33,1},{49,17},{2,34}... | collective-permute-start | bytes 196616 | tf_op jit(solution)/shard_map/ppermute | solution.py:257
  7.6 9.0 %collective-permute-start.2 = (bf16[64,512]{1,0:T(8,128)(2,1)S(1)}, bf16[64,512]{1,0:T(8,128)(2,1)S(1)}, u32[]{:S(2)}, u32[]{:S(2)}) collective-permute-start(bf16[64,512]{1,0:T(8,128)(2,1)S(1)} %copy_of.2.half_ref), channel_id=1, source_target_pairs={{0,16},{16,32},{32,48},{48,0},{1,17},{17,33},{33,49},{49,1},{2,18}... | collective-permute-start | bytes 196616 | tf_op jit(solution)/shard_map/ppermute | solution.py:257
  8.1 11.0 %collective-permute-start.3 = (bf16[64,512]{1,0:T(8,128)(2,1)S(1)}, bf16[64,512]{1,0:T(8,128)(2,1)S(1)}, u32[]{:S(2)}, u32[]{:S(2)}) collective-permute-start(bf16[64,512]{1,0:T(8,128)(2,1)S(1)} %copy_of.2.half_ref), channel_id=1, source_target_pairs={{0,48},{16,0},{32,16},{48,32},{1,49},{17,1},{33,17},{49,33},{2,50}... | collective-permute-start | bytes 196616 | tf_op jit(solution)/shard_map/ppermute | solution.py:257
  12.5 6.7 %collective-permute-start.4 = (bf16[512,128]{1,0:T(8,128)(2,1)S(1)}, bf16[512,128]{1,0:T(8,128)(2,1)S(1)}, u32[]{:S(2)}, u32[]{:S(2)}) collective-permute-start(bf16[512,128]{1,0:T(8,128)(2,1)S(1)} %get-tuple-element.39.token_ref.refs_0_), channel_id=1, source_target_pairs={{0,2},{2,0},{1,3},{3,1},{4,6},{6,4},{5,7},{7,5},{8,10},{10,8},{9,1... | collective-permute-start | bytes 393224 | tf_op jit(solution)/shard_map/ppermute | solution.py:257
  12.6 8.7 %collective-permute-start.6 = (bf16[512,128]{1,0:T(8,128)(2,1)S(1)}, bf16[512,128]{1,0:T(8,128)(2,1)S(1)}, u32[]{:S(2)}, u32[]{:S(2)}) collective-permute-start(bf16[512,128]{1,0:T(8,128)(2,1)S(1)} %get-tuple-element.39.token_ref.refs_0_), channel_id=1, source_target_pairs={{0,8},{4,12},{8,0},{12,4},{1,9},{5,13},{9,1},{13,5},{2,10},{6,14},... | collective-permute-start | bytes 393224 | tf_op jit(solution)/shard_map/ppermute | solution.py:257
  15.9 7.1 %collective-permute-start.7 = (bf16[512,128]{1,0:T(8,128)(2,1)S(1)}, bf16[512,128]{1,0:T(8,128)(2,1)S(1)}, u32[]{:S(2)}, u32[]{:S(2)}) collective-permute-start(bf16[512,128]{1,0:T(8,128)(2,1)S(1)} %get-tuple-element.39.token_ref.refs_0_), channel_id=1, source_target_pairs={{0,4},{4,8},{8,12},{12,0},{1,5},{5,9},{9,13},{13,1},{2,6},{6,10},{... | collective-permute-start | bytes 393224 | tf_op jit(solution)/shard_map/ppermute | solution.py:257
  16.6 6.6 %collective-permute-start.8 = (bf16[512,128]{1,0:T(8,128)(2,1)S(1)}, bf16[512,128]{1,0:T(8,128)(2,1)S(1)}, u32[]{:S(2)}, u32[]{:S(2)}) collective-permute-start(bf16[512,128]{1,0:T(8,128)(2,1)S(1)} %get-tuple-element.39.token_ref.refs_0_), channel_id=1, source_target_pairs={{0,12},{4,0},{8,4},{12,8},{1,13},{5,1},{9,5},{13,9},{2,14},{6,2},{... | collective-permute-start | bytes 393224 | tf_op jit(solution)/shard_map/ppermute | solution.py:257
  23.2 9.4 %collective-permute-start.9 = (bf16[2048,128]{1,0:T(8,128)(2,1)S(1)}, bf16[2048,128]{1,0:T(8,128)(2,1)S(1)}, u32[]{:S(2)}, u32[]{:S(2)}) collective-permute-start(bf16[2048,128]{1,0:T(8,128)(2,1)S(1)} %constant_dynamic-update-slice_fusion.refs_0_), channel_id=1, source_target_pairs={{0,2},{2,0},{1,3},{3,1},{4,6},{6,4},{5,7},{7,5},{8,10},{10,8},{9,1... | collective-permute-start | bytes 1572872 | tf_op jit(solution)/shard_map/ppermute | solution.py:257
  23.3 7.8 %collective-permute-start.5 = (bf16[192,512]{1,0:T(8,128)(2,1)S(1)}, bf16[192,512]{1,0:T(8,128)(2,1)S(1)}, u32[]{:S(2)}, u32[]{:S(2)}) collective-permute-start(bf16[192,512]{1,0:T(8,128)(2,1)S(1)} %copy_of.3), channel_id=1, source_target_pairs={{0,1},{1,0},{2,3},{3,2},{4,5},{5,4},{6,7},{7,6},{8,9},{9,8},{10,11... | collective-permute-start | bytes 589832 | tf_op jit(solution)/shard_map/ppermute | solution.py:257
  23.5 23.4 %collective-permute-start.10 = (bf16[2048,128]{1,0:T(8,128)(2,1)S(1)}, bf16[2048,128]{1,0:T(8,128)(2,1)S(1)}, u32[]{:S(2)}, u32[]{:S(2)}) collective-permute-start(bf16[2048,128]{1,0:T(8,128)(2,1)S(1)} %constant_dynamic-update-slice_fusion.refs_0_), channel_id=1, source_target_pairs={{0,64},{64,0},{1,65},{65,1},{2,66},{66,2},{3,67},{67,3},{4,68},{68... | collective-permute-start | bytes 1572872 | tf_op jit(solution)/shard_map/ppermute | solution.py:257
  46.9 8.0 %collective-permute-start.11 = (bf16[2048,128]{1,0:T(8,128)(2,1)S(1)}, bf16[2048,128]{1,0:T(8,128)(2,1)S(1)}, u32[]{:S(2)}, u32[]{:S(2)}) collective-permute-start(bf16[2048,128]{1,0:T(8,128)(2,1)S(1)} %collective-permute-done.10.refs_0_), channel_id=1, source_target_pairs={{0,2},{2,0},{1,3},{3,1},{4,6},{6,4},{5,7},{7,5},{8,10},{10,8},{9,1... | collective-permute-start | bytes 1572872 | tf_op jit(solution)/shard_map/ppermute | solution.py:257
  62.8 9.7 %collective-permute-start.14 = (bf16[64,1024]{1,0:T(8,128)(2,1)S(1)}, bf16[64,1024]{1,0:T(8,128)(2,1)S(1)}, u32[]{:S(2)}, u32[]{:S(2)}) collective-permute-start(bf16[64,1024]{1,0:T(8,128)(2,1)S(1)} %get-tuple-element.66), channel_id=1, source_target_pairs={{0,16},{16,32},{32,48},{48,0},{1,17},{17,33},{33,49},{49,1},{2,18}... | collective-permute-start | bytes 393224 | tf_op jit(solution)/shard_map/ppermute | solution.py:257
  62.9 9.6 %collective-permute-start.13 = (bf16[64,1024]{1,0:T(8,128)(2,1)S(1)}, bf16[64,1024]{1,0:T(8,128)(2,1)S(1)}, u32[]{:S(2)}, u32[]{:S(2)}) collective-permute-start(bf16[64,1024]{1,0:T(8,128)(2,1)S(1)} %get-tuple-element.65), channel_id=1, source_target_pairs={{0,48},{16,0},{32,16},{48,32},{1,49},{17,1},{33,17},{49,33},{2,50}... | collective-permute-start | bytes 393224 | tf_op jit(solution)/shard_map/ppermute | solution.py:257
  66.1 6.8 %collective-permute-start.12 = (bf16[64,1024]{1,0:T(8,128)(2,1)S(1)}, bf16[64,1024]{1,0:T(8,128)(2,1)S(1)}, u32[]{:S(2)}, u32[]{:S(2)}) collective-permute-start(bf16[64,1024]{1,0:T(8,128)(2,1)S(1)} %get-tuple-element.64), channel_id=1, source_target_pairs={{0,32},{16,48},{32,0},{48,16},{1,33},{17,49},{33,1},{49,17},{2,34}... | collective-permute-start | bytes 393224 | tf_op jit(solution)/shard_map/ppermute | solution.py:257
  73.0 5.1 %copy-start.1 = (bf16[1024,32]{0,1:T(8,128)(2,1)S(1)}, bf16[1024,32]{0,1:T(8,128)(2,1)}, u32[]{:S(2)}) copy-start(bf16[1024,32]{0,1:T(8,128)(2,1)} %param.6) | copy-start | bytes 196612
  73.1 5.0 %collective-permute-start.15 = (f32[32,1024]{1,0:T(8,128)S(1)}, f32[32,1024]{1,0:T(8,128)S(1)}, u32[]{:S(2)}, u32[]{:S(2)}) collective-permute-start(f32[32,1024]{1,0:T(8,128)S(1)} %slice.9), channel_id=1, source_target_pairs={{0,1},{1,0},{2,3},{3,2},{4,5},{5,4},{6,7},{7,6},{8,9},{9,8},{10,11... | collective-permute-start | bytes 393224 | tf_op jit(solution)/shard_map/ppermute | solution.py:257

commit v8 on v7

--- a/solution.py
+++ b/solution.py
@@ -12,6 +12,7 @@
 TN = 1024
 F32 = jnp.float32
 BF16 = jnp.bfloat16
+ALONE = pltpu.CompilerParams(vmem_limit_bytes=60 << 20)
 PARAMS = pltpu.CompilerParams(vmem_limit_bytes=48 << 20)
 
 
@@ -66,7 +67,16 @@
 
 
 def first_pack(zl, points, vectors, lengthscale):
-    def body(zl_ref, points_ref, vectors_ref, length_ref, out_ref, kept_ref):
+    def body(zl_ref, points_in, vectors_in, length_in, out_ref, kept_ref, points_ref, vectors_ref, length_ref, sems):
+        copies = [
+            pltpu.make_async_copy(length_in, length_ref, sems.at[0]),
+            pltpu.make_async_copy(points_in, points_ref, sems.at[1]),
+            pltpu.make_async_copy(vectors_in, vectors_ref, sems.at[2]),
+        ]
+        for copy in copies:
+            copy.start()
+        for copy in copies:
+            copy.wait()
         at = zl_ref[0]
         lane = lax.broadcasted_iota(jnp.int32, (32, 64), 1)
         row = lax.broadcasted_iota(jnp.int32, (32, 64), 0)
@@ -80,12 +90,36 @@
 
     return pl.pallas_call(
         body,
-        out_shape=[jax.ShapeDtypeStruct((n, 512), BF16) for n in (96, 32)],
-        in_specs=[pl.BlockSpec(memory_space=pltpu.SMEM)] + [pl.BlockSpec(memory_space=pltpu.VMEM)] * 3,
-        out_specs=[pl.BlockSpec(memory_space=pltpu.VMEM)] * 2,
-        compiler_params=PARAMS,
+        out_shape=(jax.ShapeDtypeStruct((96, 512), BF16), jax.ShapeDtypeStruct((32, 512), BF16)),
+        in_specs=[pl.BlockSpec(memory_space=pltpu.SMEM)] + [pl.BlockSpec(memory_space=pltpu.HBM)] * 3,
+        out_specs=(pl.BlockSpec(memory_space=pltpu.VMEM),) * 2,
+        scratch_shapes=[
+            pltpu.VMEM((32, 1024), BF16),
+            pltpu.VMEM((32, 1024), BF16),
+            pltpu.VMEM((1, 64), F32),
+            pltpu.SemaphoreType.DMA((3,)),
+        ],
+        compiler_params=ALONE,
         name="first_pack",
     )(zl, points, vectors, lengthscale.reshape(1, 64))
+
+
+def features_of(given):
+    def body(given_ref, out_ref, sem):
+        copy = pltpu.make_async_copy(given_ref.at[:64], out_ref, sem)
+        copy.start()
+        copy.wait()
+
+    return pl.pallas_call(
+        body,
+        out_shape=jax.ShapeDtypeStruct((64, 512), BF16),
+        in_specs=[pl.BlockSpec(memory_space=pltpu.HBM)],
+        out_specs=pl.BlockSpec(memory_space=pltpu.HBM),
+        scratch_shapes=[pltpu.SemaphoreType.DMA],
+        compiler_params=ALONE,
+        cost_estimate=cost(4096, 1024),
+        name="features_of",
+    )(given)
 
 
 def copy_of(parts, rows, token, weight):
@@ -110,7 +144,7 @@
 def second_pack(zl, amp, half, got, kept):
     def body(zl_ref, amp_ref, half_ref, got_ref, kept_ref, rows_ref, share_ref):
         first = zl_ref[0] == 0
-        mine = half_ref[...].astype(F32)
+        mine = half_ref[:64].astype(F32)
         theirs = got_ref[...].astype(F32)
         low = jnp.concatenate([mine[:32], theirs[:32]], axis=0)
         high = jnp.concatenate([mine[32:], theirs[32:64]], axis=0)
@@ -146,14 +180,21 @@
     return result
 
 
+def swapped(wide):
+    lane = lax.broadcasted_iota(jnp.int32, wide.shape, 1)
+    return jnp.where(lane % 64 < 32, pltpu.roll(wide, 96, 1), pltpu.roll(wide, 32, 1))
+
+
 def raw_sum(left, raws, right_ref, vectors_ref, top):
     total = right_ref.shape[0]
     result = jnp.zeros((64, left.shape[0]), F32)
     at = 0
     rights, turned = [], []
-    for ref, start in raws:
+    for ref, start, swap in raws:
         for sub in range(start, ref.shape[0], 512):
             wide = ref[sub : sub + 512, :].astype(F32)
+            if swap:
+                wide = swapped(wide)
             rights.append(with_norms(wide, 0.0, 64, 67))
             turned.append(wide.T[64:, :].astype(BF16))
             right_ref[at : at + 512, :] = rights[-1]
@@ -166,7 +207,7 @@
     return result
 
 
-def add_tiles(amp, left, ready, raws, before=None, narrow=False, weight=1024):
+def add_tiles(amp, left, ready, raws, before=None, narrow=False, weight=1024, swap=False):
     count = left.shape[0]
     flat = [part for pair in ready for part in pair]
     total = sum(raw.shape[0] - start for raw, start in raws)
@@ -201,7 +242,7 @@
         def tiles(fresh):
             value = ready_sum(left_ref[0], pairs if fresh or not raws else pairs + [tuple(refs)], top)
             if fresh:
-                starts = [(ref, start) for ref, (_, start) in zip(raw_refs, raws)]
+                starts = [(ref, start, swap) for ref, (_, start) in zip(raw_refs, raws)]
                 value += raw_sum(left_ref[0], starts, *refs, top)
             put(value)
 
@@ -257,15 +298,19 @@
     return lax.ppermute(value, axis, [(i, (i + by) % size) for i in range(size)])
 
 
+def cross(value):
+    return lax.ppermute(value, ("zh", "zl"), [(i, 3 - i) for i in range(4)])
+
+
 def per_device(points, vectors, lengthscale, outscale, noise):
     zl = lax.axis_index("zl").astype(jnp.int32).reshape(1)
     amp = jnp.concatenate([outscale, jnp.log(outscale)])
 
     given, kept = first_pack(zl, points.T, vectors.T, lengthscale)
     got = shift(given, "zl", 1)
-    half = copy_of([given], 64, kept, 4096)
-    mines = [shift(half, "x", by) for by in (2, 1, -1)]
-    own_left, share = second_pack(zl, amp, half, got, kept)
+    half = features_of(given)
+    mines = [shift(half, "x", by) for by in (1, -1, 2)]
+    own_left, share = second_pack(zl, amp, given, got, kept)
 
     beside = shift(share, "c", 1)
     near = [shift(share, "y", by) for by in (2, 1, -1)]
@@ -275,7 +320,7 @@
     own, ready0 = add_tiles(amp, own_left, [], [(share, 0), (beside, 0)], weight=4096)
     near[0], near[1], near[2], own = lax.optimization_barrier((near[0], near[1], near[2], own))
     merged = jnp.concatenate([share] + near, axis=0)
-    far = shift(merged, "zh", 1)
+    far = cross(merged)
     merged_beside = shift(merged, "c", 1)
     own, ready1 = add_tiles(amp, own_left, [], [(merged, 512)], own, weight=64)
 
@@ -284,9 +329,9 @@
     acc, ready2 = add_tiles(amp, left, [ready0, ready1], [(merged_beside, 512)])
     far, acc = lax.optimization_barrier((far, acc))
     far_beside = shift(far, "c", 1)
-    acc, ready3 = add_tiles(amp, left, [], [(far, 0)], acc)
-    sent, ready4 = add_tiles(amp, left, [], [(far_beside, 0)], acc, narrow=True)
-    arrived = [shift(part, "x", by) for part, by in zip(sent, (2, -1, 1))]
+    acc, ready3 = add_tiles(amp, left, [], [(far, 0)], acc, swap=True)
+    sent, ready4 = add_tiles(amp, left, [], [(far_beside, 0)], acc, narrow=True, swap=True)
+    arrived = [shift(part, "x", by) for part, by in zip(sent, (-1, 1, 2))]
     own, _ = add_tiles(amp, own_left, [ready2, ready3, ready4], [], own)
     own = own[0]
     for part in arrived:

time: 79.1 us -> 85.1 us (1.076)
  Pallas kernels: 43.5 us -> 52.2 us
  local copies, waits for them, and re-layouts: 2.42 us -> 0.09 us
  waiting for transfers between devices: 7.63 us -> 6.45 us
  starting transfers between devices: 22.8 us -> 23.8 us
    pallas_call x1 -> x2, Pallas kernels: 0.1 us -> 4.74 us  [the longest x1 3.09 us: features_of(): pl.pallas_call(body, out_shape=jax.ShapeDtypeStruct((64, 512), BF16), in_...]
    pallas_call x6, Pallas kernels: 41 us -> 45.1 us  [add_tiles(): pl.pallas_call(body, grid=(count * per,), out_shape=sum_shapes + made, in...]
    ppermute x0 -> x1, starting transfers between devices: none -> 4.04 us  [cross(): return lax.ppermute(value, ('zh', 'zl'), [(i, 3 - i) for i in range(4)])]
    ppermute x16 -> x15, starting transfers between devices: 22.8 us -> 19.7 us  [shift(): lax.ppermute(value, axis, [(i, (i + by) % size) for i in range(size)])]
    unnamed x11 -> x9, local copies, waits for them, and re-layouts: 2.39 us -> 0.06 us
    ppermute x16 -> x15, waiting for transfers between devices: 7.63 us -> 6.44 us  [shift(): lax.ppermute(value, axis, [(i, (i + by) % size) for i in range(size)])]
  transfers between devices with their start and end apart: 16 -> 16, of which waited for: 5 -> 4; matrix products, arithmetic and copies ran while one was open for 0% -> 0% of each run, Pallas kernels for 45% -> 48%
where the time goes in v8:
time: 85.1 us; the launch traced here: 84.9 us
  Pallas kernels  52.2 us (61%)
  starting transfers between devices  23.8 us (28%)
  waiting for transfers between devices  6.45 us (8%)
  between operations  1.59 us (2%)
    pallas_call x6, Pallas kernels, add_tiles(): pl.pallas_call(body, grid=(count * per,), out_shape=sum_shapes + made, in...  45.1 us
    ppermute x15, starting transfers between devices, shift(): lax.ppermute(value, axis, [(i, (i + by) % size) for i in range(size)])  19.7 us
    ppermute x15, waiting for transfers between devices, shift(): lax.ppermute(value, axis, [(i, (i + by) % size) for i in range(size)])  6.44 us
    ppermute x1, starting transfers between devices, cross(): return lax.ppermute(value, ('zh', 'zl'), [(i, 3 - i) for i in range(4)])  4.04 us
    pallas_call x1, Pallas kernels, features_of(): pl.pallas_call(body, out_shape=jax.ShapeDtypeStruct((64, 512), BF16), in_...  3.09 us
  transfers between devices with their start and end apart: 16, of which 4 were waited for; matrix products, arithmetic and copies ran while one was open for 0% of the time, Pallas kernels for 48%

profile of v8, /device:TPU:0, one launch (start us, length us, event | category | flops | bytes accessed | tf_op | source)
XLA Modules:
  0.0 84.9 jit_solution(17079263224152895850)
XLA Ops:
  0.0 1.6 %first_pack.1 = (bf16[96,512]{1,0:T(8,128)(2,1)}, bf16[32,512]{1,0:T(8,128)(2,1)}) custom-call(s32[1]{0:T(128)} %bitcast.zl_ref, bf16[32,1024]{1,0:T(8,128)(2,1)} %bitcast.17, bf16[32,1024]{1,0:T(8,128)(2,1)} %bitcast.16, f32[1,64]{1,0:T(1,128)} %bitcast.18), custom_call_target="tpu_custom_call" | custom-call | tf_op jit(solution)/shard_map/first_pack/pallas_call | solution.py:91
  1.7 2.1 %collective-permute-start = (bf16[96,512]{1,0:T(8,128)(2,1)}, bf16[96,512]{1,0:T(8,128)(2,1)S(1)}, u32[]{:S(2)}, u32[]{:S(2)}) collective-permute-start(bf16[96,512]{1,0:T(8,128)(2,1)} %get-tuple-element.36.half_ref.given_ref), channel_id=1, source_target_pairs={{0,1},{1,0},{2,3},{3,2},{4,5},{5,4},{6,7},{7,6},{8,9},{9,8},{10,11... | collective-permute-start | bytes 294920 | tf_op jit(solution)/shard_map/ppermute | solution.py:298
  3.8 3.1 %features_of.1 = bf16[64,512]{1,0:T(8,128)(2,1)} custom-call(bf16[96,512]{1,0:T(8,128)(2,1)} %get-tuple-element.36.half_ref.given_ref), custom_call_target="tpu_custom_call" | custom-call | flops 2147483648 | bytes 393216 | tf_op jit(solution)/shard_map/features_of/pallas_call | solution.py:113
  6.9 1.6 %collective-permute-start.1 = (bf16[64,512]{1,0:T(8,128)(2,1)}, bf16[64,512]{1,0:T(8,128)(2,1)S(1)}, u32[]{:S(2)}, u32[]{:S(2)}) collective-permute-start(bf16[64,512]{1,0:T(8,128)(2,1)} %features_of.1), channel_id=1, source_target_pairs={{0,16},{16,32},{32,48},{48,0},{1,17},{17,33},{33,49},{49,1},{2,18}... | collective-permute-start | bytes 196616 | tf_op jit(solution)/shard_map/ppermute | solution.py:298
  8.4 1.7 %collective-permute-start.2 = (bf16[64,512]{1,0:T(8,128)(2,1)}, bf16[64,512]{1,0:T(8,128)(2,1)S(1)}, u32[]{:S(2)}, u32[]{:S(2)}) collective-permute-start(bf16[64,512]{1,0:T(8,128)(2,1)} %features_of.1), channel_id=1, source_target_pairs={{0,48},{16,0},{32,16},{48,32},{1,49},{17,1},{33,17},{49,33},{2,50}... | collective-permute-start | bytes 196616 | tf_op jit(solution)/shard_map/ppermute | solution.py:298
  10.2 1.8 %collective-permute-start.3 = (bf16[64,512]{1,0:T(8,128)(2,1)}, bf16[64,512]{1,0:T(8,128)(2,1)S(1)}, u32[]{:S(2)}, u32[]{:S(2)}) collective-permute-start(bf16[64,512]{1,0:T(8,128)(2,1)} %features_of.1), channel_id=1, source_target_pairs={{0,32},{16,48},{32,0},{48,16},{1,33},{17,49},{33,1},{49,17},{2,34}... | collective-permute-start | bytes 196616 | tf_op jit(solution)/shard_map/ppermute | solution.py:298
  12.7 0.1 pad_maximum_fusion.amp_ref
  12.8 0.9 %second_pack.1 = (bf16[1,1024,128]{2,1,0:T(8,128)(2,1)S(1)}, bf16[512,128]{1,0:T(8,128)(2,1)S(1)}) custom-call(s32[1]{0:T(128)} %bitcast.zl_ref, f32[2]{0:T(128)S(1)} %pad_maximum_fusion.amp_ref, bf16[96,512]{1,0:T(8,128)(2,1)S(1)} %copy-done, bf16[96,512]{1,0:T(8,128)(2,1)S(1)} %collective-permute-done.got_ref, bf16[32,512]{1,0:T(8,128)(2,1)S(1)} %copy-done.1), custom_call_target="tpu_custom_call" | custom-call | tf_op jit(solution)/shard_map/second_pack/pallas_call | solution.py:157
  13.7 0.1 collective-permute-start.4
  13.8 3.3 %collective-permute-start.6 = (bf16[512,128]{1,0:T(8,128)(2,1)S(1)}, bf16[512,128]{1,0:T(8,128)(2,1)S(1)}, u32[]{:S(2)}, u32[]{:S(2)}) collective-permute-start(bf16[512,128]{1,0:T(8,128)(2,1)S(1)} %get-tuple-element.39.token_ref.refs_0_), channel_id=1, source_target_pairs={{0,8},{4,12},{8,0},{12,4},{1,9},{5,13},{9,1},{13,5},{2,10},{6,14},... | collective-permute-start | bytes 393224 | tf_op jit(solution)/shard_map/ppermute | solution.py:298
  17.1 0.7 collective-permute-start.7
  17.8 2.6 %collective-permute-start.8 = (bf16[512,128]{1,0:T(8,128)(2,1)S(1)}, bf16[512,128]{1,0:T(8,128)(2,1)S(1)}, u32[]{:S(2)}, u32[]{:S(2)}) collective-permute-start(bf16[512,128]{1,0:T(8,128)(2,1)S(1)} %get-tuple-element.39.token_ref.refs_0_), channel_id=1, source_target_pairs={{0,12},{4,0},{8,4},{12,8},{1,13},{5,1},{9,5},{13,9},{2,14},{6,2},{... | collective-permute-start | bytes 393224 | tf_op jit(solution)/shard_map/ppermute | solution.py:298
  20.4 2.1 %add_tiles.6 = (f32[1,64,1024]{2,1,0:T(8,128)S(1)}, bf16[1024,128]{1,0:T(8,128)(2,1)S(1)}, bf16[64,1024]{1,0:T(8,128)(2,1)S(1)}) custom-call(f32[2]{0:T(128)S(1)} %pad_maximum_fusion.amp_ref, bf16[1,1024,128]{2,1,0:T(8,128)(2,1)S(1)} %get-tuple-element.38.left_ref, bf16[512,128]{1,0:T(8,128)(2,1)S(1)} %get-tuple-element.39.token_ref.refs_0_, ...), custom_call_target="tpu_custom_call" | custom-call | flops 2147483648 | bytes 393216 | tf_op jit(solution)/shard_map/add_tiles/pallas_call | solution.py:277
  22.5 1.7 %collective-permute-done.7 = bf16[512,128]{1,0:T(8,128)(2,1)S(1)} collective-permute-done((bf16[512,128]{1,0:T(8,128)(2,1)S(1)}, bf16[512,128]{1,0:T(8,128)(2,1)S(1)}, u32[]{:S(2)}, u32[]{:S(2)}) %collective-permute-start.7) | collective-permute-done | bytes 131104 | tf_op jit(solution)/shard_map/ppermute | solution.py:298
  24.2 0.2 collective-permute-done.8
  24.4 0.1 collective-permute-start.9
  24.5 0.2 collective-permute-start.5
  24.7 4.0 %collective-permute-start.10 = (bf16[2048,128]{1,0:T(8,128)(2,1)S(1)}, bf16[2048,128]{1,0:T(8,128)(2,1)S(1)}, u32[]{:S(2)}, u32[]{:S(2)}) collective-permute-start(bf16[2048,128]{1,0:T(8,128)(2,1)S(1)} %constant_dynamic-update-slice_fusion.refs_0_), channel_id=1, source_target_pairs={{0,65},{1,64},{64,1},{65,0},{2,67},{3,66},{66,3},{67,2},{4,69},{5,... | collective-permute-start | bytes 1572872 | tf_op jit(solution)/shard_map/ppermute | solution.py:302
  28.8 2.7 %add_tiles.7 = (f32[1,64,1024]{2,1,0:T(8,128)S(1)}, bf16[1536,128]{1,0:T(8,128)(2,1)S(1)}, bf16[64,1536]{1,0:T(8,128)(2,1)S(1)}) custom-call(f32[2]{0:T(128)S(1)} %pad_maximum_fusion.amp_ref, bf16[1,1024,128]{2,1,0:T(8,128)(2,1)S(1)} %get-tuple-element.38.left_ref, bf16[2048,128]{1,0:T(8,128)(2,1)S(1)} %constant_dynamic-update-slice_fusion.refs_0_, ...), custom_call_target="tpu_custom_call" | custom-call | flops 50331648 | bytes 589824 | tf_op jit(solution)/shard_map/add_tiles/pallas_call | solution.py:277
  31.5 0.4 collective-permute-done.5.refs_3_
  31.9 1.5 %ready_rows.1.left_ref = bf16[3,1024,128]{2,1,0:T(8,128)(2,1)S(1)} custom-call(f32[2]{0:T(128)S(1)} %pad_maximum_fusion.amp_ref, bf16[64,512]{1,0:T(8,128)(2,1)S(1)} %collective-permute-done.1.refs_0_, bf16[64,512]{1,0:T(8,128)(2,1)S(1)} %collective-permute-done.2.refs_1_, bf16[64,512]{1,0:T(8,128)(2,1)S(1)} %collective-permute-done.3.refs_2_, ...), custom_call_target="tpu_custom_call" | custom-call | tf_op jit(solution)/shard_map/ready_rows/pallas_call | solution.py:58
  33.3 14.3 %add_tiles.8 = (f32[3,64,1024]{2,1,0:T(8,128)S(1)}, bf16[1536,128]{1,0:T(8,128)(2,1)S(1)}, bf16[64,1536]{1,0:T(8,128)(2,1)S(1)}) custom-call(f32[2]{0:T(128)S(1)} %pad_maximum_fusion.amp_ref, bf16[3,1024,128]{2,1,0:T(8,128)(2,1)S(1)} %ready_rows.1.left_ref, bf16[1024,128]{1,0:T(8,128)(2,1)S(1)} %get-tuple-element.49.refs_0_, ...), custom_call_target="tpu_custom_call" | custom-call | flops 6442450944 | bytes 1572864 | tf_op jit(solution)/shard_map/add_tiles/pallas_call | solution.py:277
  47.6 0.3 collective-permute-start.11
  47.9 9.8 %add_tiles.9 = (f32[3,64,1024]{2,1,0:T(8,128)S(1)}, bf16[2048,128]{1,0:T(8,128)(2,1)S(1)}, bf16[64,2048]{1,0:T(8,128)(2,1)S(1)}) custom-call(f32[2]{0:T(128)S(1)} %pad_maximum_fusion.amp_ref, bf16[3,1024,128]{2,1,0:T(8,128)(2,1)S(1)} %ready_rows.1.left_ref, bf16[2048,128]{1,0:T(8,128)(2,1)S(1)} %collective-permute-done.10.refs_0_, ...), custom_call_target="tpu_custom_call" | custom-call | flops 3221225472 | bytes 786432 | tf_op jit(solution)/shard_map/add_tiles/pallas_call | solution.py:277
  57.7 9.9 %add_tiles.10 = (bf16[64,1024]{1,0:T(8,128)(2,1)S(1)}, bf16[64,1024]{1,0:T(8,128)(2,1)S(1)}, bf16[64,1024]{1,0:T(8,128)(2,1)S(1)}, bf16[2048,128]{1,0:T(8,128)(2,1)S(1)}, bf16[64,2048]{1,0:T(8,128)(2,1)S(1)}) custom-call(f32[2]{0:T(128)S(1)} %pad_maximum_fusion.amp_ref, bf16[3,1024,128]{2,1,0:T(8,128)(2,1)S(1)} %ready_rows.1.left_ref, ...), custom_call_target="tpu_custom_call" | custom-call | flops 3221225472 | bytes 786432 | tf_op jit(solution)/shard_map/add_tiles/pallas_call | solution.py:277
  67.6 1.8 %collective-permute-start.14 = (bf16[64,1024]{1,0:T(8,128)(2,1)S(1)}, bf16[64,1024]{1,0:T(8,128)(2,1)S(1)}, u32[]{:S(2)}, u32[]{:S(2)}) collective-permute-start(bf16[64,1024]{1,0:T(8,128)(2,1)S(1)} %get-tuple-element.66), channel_id=1, source_target_pairs={{0,32},{16,48},{32,0},{48,16},{1,33},{17,49},{33,1},{49,17},{2,34}... | collective-permute-start | bytes 393224 | tf_op jit(solution)/shard_map/ppermute | solution.py:298
  69.4 0.3 collective-permute-start.13
  69.7 3.0 %collective-permute-start.12 = (bf16[64,1024]{1,0:T(8,128)(2,1)S(1)}, bf16[64,1024]{1,0:T(8,128)(2,1)S(1)}, u32[]{:S(2)}, u32[]{:S(2)}) collective-permute-start(bf16[64,1024]{1,0:T(8,128)(2,1)S(1)} %get-tuple-element.64), channel_id=1, source_target_pairs={{0,48},{16,0},{32,16},{48,32},{1,49},{17,1},{33,17},{49,33},{2,50}... | collective-permute-start | bytes 393224 | tf_op jit(solution)/shard_map/ppermute | solution.py:298
  72.7 6.3 %add_tiles.11 = f32[1,64,1024]{2,1,0:T(8,128)S(1)} custom-call(f32[2]{0:T(128)S(1)} %pad_maximum_fusion.amp_ref, bf16[1,1024,128]{2,1,0:T(8,128)(2,1)S(1)} %get-tuple-element.38.left_ref, bf16[1536,128]{1,0:T(8,128)(2,1)S(1)} %get-tuple-element.53.refs_0_, bf16[64,1536]{1,0:T(8,128)(2,1)S(1)} %get-tuple-element.54.refs_1_, ...), custom_call_target="tpu_custom_call" | custom-call | flops 2952790016 | bytes 2162688 | tf_op jit(solution)/shard_map/add_tiles/pallas_call | solution.py:277
  79.1 0.3 collective-permute-start.15
  80.1 4.1 %collective-permute-done.15 = f32[32,1024]{1,0:T(8,128)S(1)} collective-permute-done((f32[32,1024]{1,0:T(8,128)S(1)}, f32[32,1024]{1,0:T(8,128)S(1)}, u32[]{:S(2)}, u32[]{:S(2)}) %collective-permute-start.15) | collective-permute-done | bytes 131104 | tf_op jit(solution)/shard_map/ppermute | solution.py:298
  84.3 0.7 fusion.3
  (25 shorter events, 0.2 us)
Async XLA Ops:
  1.7 11.1 %copy-start = (bf16[96,512]{1,0:T(8,128)(2,1)S(1)}, bf16[96,512]{1,0:T(8,128)(2,1)}, u32[]{:S(2)}) copy-start(bf16[96,512]{1,0:T(8,128)(2,1)} %get-tuple-element.36.half_ref.given_ref) | copy-start | bytes 294916
  1.7 11.1 %copy-start.1 = (bf16[32,512]{1,0:T(8,128)(2,1)S(1)}, bf16[32,512]{1,0:T(8,128)(2,1)}, u32[]{:S(2)}) copy-start(bf16[32,512]{1,0:T(8,128)(2,1)} %get-tuple-element.37.kept_ref) | copy-start | bytes 98308
  1.7 11.1 %collective-permute-start = (bf16[96,512]{1,0:T(8,128)(2,1)}, bf16[96,512]{1,0:T(8,128)(2,1)S(1)}, u32[]{:S(2)}, u32[]{:S(2)}) collective-permute-start(bf16[96,512]{1,0:T(8,128)(2,1)} %get-tuple-element.36.half_ref.given_ref), channel_id=1, source_target_pairs={{0,1},{1,0},{2,3},{3,2},{4,5},{5,4},{6,7},{7,6},{8,9},{9,8},{10,11... | collective-permute-start | bytes 294920 | tf_op jit(solution)/shard_map/ppermute | solution.py:298
  6.9 10.2 %collective-permute-start.1 = (bf16[64,512]{1,0:T(8,128)(2,1)}, bf16[64,512]{1,0:T(8,128)(2,1)S(1)}, u32[]{:S(2)}, u32[]{:S(2)}) collective-permute-start(bf16[64,512]{1,0:T(8,128)(2,1)} %features_of.1), channel_id=1, source_target_pairs={{0,16},{16,32},{32,48},{48,0},{1,17},{17,33},{33,49},{49,1},{2,18}... | collective-permute-start | bytes 196616 | tf_op jit(solution)/shard_map/ppermute | solution.py:298
  8.4 9.3 %collective-permute-start.2 = (bf16[64,512]{1,0:T(8,128)(2,1)}, bf16[64,512]{1,0:T(8,128)(2,1)S(1)}, u32[]{:S(2)}, u32[]{:S(2)}) collective-permute-start(bf16[64,512]{1,0:T(8,128)(2,1)} %features_of.1), channel_id=1, source_target_pairs={{0,48},{16,0},{32,16},{48,32},{1,49},{17,1},{33,17},{49,33},{2,50}... | collective-permute-start | bytes 196616 | tf_op jit(solution)/shard_map/ppermute | solution.py:298
  10.2 10.2 %collective-permute-start.3 = (bf16[64,512]{1,0:T(8,128)(2,1)}, bf16[64,512]{1,0:T(8,128)(2,1)S(1)}, u32[]{:S(2)}, u32[]{:S(2)}) collective-permute-start(bf16[64,512]{1,0:T(8,128)(2,1)} %features_of.1), channel_id=1, source_target_pairs={{0,32},{16,48},{32,0},{48,16},{1,33},{17,49},{33,1},{49,17},{2,34}... | collective-permute-start | bytes 196616 | tf_op jit(solution)/shard_map/ppermute | solution.py:298
  13.7 6.7 %collective-permute-start.4 = (bf16[512,128]{1,0:T(8,128)(2,1)S(1)}, bf16[512,128]{1,0:T(8,128)(2,1)S(1)}, u32[]{:S(2)}, u32[]{:S(2)}) collective-permute-start(bf16[512,128]{1,0:T(8,128)(2,1)S(1)} %get-tuple-element.39.token_ref.refs_0_), channel_id=1, source_target_pairs={{0,2},{2,0},{1,3},{3,1},{4,6},{6,4},{5,7},{7,5},{8,10},{10,8},{9,1... | collective-permute-start | bytes 393224 | tf_op jit(solution)/shard_map/ppermute | solution.py:298
  13.8 8.7 %collective-permute-start.6 = (bf16[512,128]{1,0:T(8,128)(2,1)S(1)}, bf16[512,128]{1,0:T(8,128)(2,1)S(1)}, u32[]{:S(2)}, u32[]{:S(2)}) collective-permute-start(bf16[512,128]{1,0:T(8,128)(2,1)S(1)} %get-tuple-element.39.token_ref.refs_0_), channel_id=1, source_target_pairs={{0,8},{4,12},{8,0},{12,4},{1,9},{5,13},{9,1},{13,5},{2,10},{6,14},... | collective-permute-start | bytes 393224 | tf_op jit(solution)/shard_map/ppermute | solution.py:298
  17.1 7.1 %collective-permute-start.7 = (bf16[512,128]{1,0:T(8,128)(2,1)S(1)}, bf16[512,128]{1,0:T(8,128)(2,1)S(1)}, u32[]{:S(2)}, u32[]{:S(2)}) collective-permute-start(bf16[512,128]{1,0:T(8,128)(2,1)S(1)} %get-tuple-element.39.token_ref.refs_0_), channel_id=1, source_target_pairs={{0,4},{4,8},{8,12},{12,0},{1,5},{5,9},{9,13},{13,1},{2,6},{6,10},{... | collective-permute-start | bytes 393224 | tf_op jit(solution)/shard_map/ppermute | solution.py:298
  17.8 6.6 %collective-permute-start.8 = (bf16[512,128]{1,0:T(8,128)(2,1)S(1)}, bf16[512,128]{1,0:T(8,128)(2,1)S(1)}, u32[]{:S(2)}, u32[]{:S(2)}) collective-permute-start(bf16[512,128]{1,0:T(8,128)(2,1)S(1)} %get-tuple-element.39.token_ref.refs_0_), channel_id=1, source_target_pairs={{0,12},{4,0},{8,4},{12,8},{1,13},{5,1},{9,5},{13,9},{2,14},{6,2},{... | collective-permute-start | bytes 393224 | tf_op jit(solution)/shard_map/ppermute | solution.py:298
  24.4 8.9 %collective-permute-start.9 = (bf16[2048,128]{1,0:T(8,128)(2,1)S(1)}, bf16[2048,128]{1,0:T(8,128)(2,1)S(1)}, u32[]{:S(2)}, u32[]{:S(2)}) collective-permute-start(bf16[2048,128]{1,0:T(8,128)(2,1)S(1)} %constant_dynamic-update-slice_fusion.refs_0_), channel_id=1, source_target_pairs={{0,2},{2,0},{1,3},{3,1},{4,6},{6,4},{5,7},{7,5},{8,10},{10,8},{9,1... | collective-permute-start | bytes 1572872 | tf_op jit(solution)/shard_map/ppermute | solution.py:298
  24.5 7.3 %collective-permute-start.5 = (bf16[192,512]{1,0:T(8,128)(2,1)S(1)}, bf16[192,512]{1,0:T(8,128)(2,1)S(1)}, u32[]{:S(2)}, u32[]{:S(2)}) collective-permute-start(bf16[192,512]{1,0:T(8,128)(2,1)S(1)} %copy_of.1), channel_id=1, source_target_pairs={{0,1},{1,0},{2,3},{3,2},{4,5},{5,4},{6,7},{7,6},{8,9},{9,8},{10,11... | collective-permute-start | bytes 589832 | tf_op jit(solution)/shard_map/ppermute | solution.py:298
  24.7 22.9 %collective-permute-start.10 = (bf16[2048,128]{1,0:T(8,128)(2,1)S(1)}, bf16[2048,128]{1,0:T(8,128)(2,1)S(1)}, u32[]{:S(2)}, u32[]{:S(2)}) collective-permute-start(bf16[2048,128]{1,0:T(8,128)(2,1)S(1)} %constant_dynamic-update-slice_fusion.refs_0_), channel_id=1, source_target_pairs={{0,65},{1,64},{64,1},{65,0},{2,67},{3,66},{66,3},{67,2},{4,69},{5,... | collective-permute-start | bytes 1572872 | tf_op jit(solution)/shard_map/ppermute | solution.py:302
  47.6 10.0 %collective-permute-start.11 = (bf16[2048,128]{1,0:T(8,128)(2,1)S(1)}, bf16[2048,128]{1,0:T(8,128)(2,1)S(1)}, u32[]{:S(2)}, u32[]{:S(2)}) collective-permute-start(bf16[2048,128]{1,0:T(8,128)(2,1)S(1)} %collective-permute-done.10.refs_0_), channel_id=1, source_target_pairs={{0,2},{2,0},{1,3},{3,1},{4,6},{6,4},{5,7},{7,5},{8,10},{10,8},{9,1... | collective-permute-start | bytes 1572872 | tf_op jit(solution)/shard_map/ppermute | solution.py:298
  67.6 11.4 %collective-permute-start.14 = (bf16[64,1024]{1,0:T(8,128)(2,1)S(1)}, bf16[64,1024]{1,0:T(8,128)(2,1)S(1)}, u32[]{:S(2)}, u32[]{:S(2)}) collective-permute-start(bf16[64,1024]{1,0:T(8,128)(2,1)S(1)} %get-tuple-element.66), channel_id=1, source_target_pairs={{0,32},{16,48},{32,0},{48,16},{1,33},{17,49},{33,1},{49,17},{2,34}... | collective-permute-start | bytes 393224 | tf_op jit(solution)/shard_map/ppermute | solution.py:298
  69.4 9.6 %collective-permute-start.13 = (bf16[64,1024]{1,0:T(8,128)(2,1)S(1)}, bf16[64,1024]{1,0:T(8,128)(2,1)S(1)}, u32[]{:S(2)}, u32[]{:S(2)}) collective-permute-start(bf16[64,1024]{1,0:T(8,128)(2,1)S(1)} %get-tuple-element.65), channel_id=1, source_target_pairs={{0,16},{16,32},{32,48},{48,0},{1,17},{17,33},{33,49},{49,1},{2,18}... | collective-permute-start | bytes 393224 | tf_op jit(solution)/shard_map/ppermute | solution.py:298
  69.7 9.3 %collective-permute-start.12 = (bf16[64,1024]{1,0:T(8,128)(2,1)S(1)}, bf16[64,1024]{1,0:T(8,128)(2,1)S(1)}, u32[]{:S(2)}, u32[]{:S(2)}) collective-permute-start(bf16[64,1024]{1,0:T(8,128)(2,1)S(1)} %get-tuple-element.64), channel_id=1, source_target_pairs={{0,48},{16,0},{32,16},{48,32},{1,49},{17,1},{33,17},{49,33},{2,50}... | collective-permute-start | bytes 393224 | tf_op jit(solution)/shard_map/ppermute | solution.py:298
  79.1 5.1 %copy-start.2 = (bf16[1024,32]{0,1:T(8,128)(2,1)S(1)}, bf16[1024,32]{0,1:T(8,128)(2,1)}, u32[]{:S(2)}) copy-start(bf16[1024,32]{0,1:T(8,128)(2,1)} %param.6) | copy-start | bytes 196612
  79.1 5.1 %collective-permute-start.15 = (f32[32,1024]{1,0:T(8,128)S(1)}, f32[32,1024]{1,0:T(8,128)S(1)}, u32[]{:S(2)}, u32[]{:S(2)}) collective-permute-start(f32[32,1024]{1,0:T(8,128)S(1)} %slice.9), channel_id=1, source_target_pairs={{0,1},{1,0},{2,3},{3,2},{4,5},{5,4},{6,7},{7,6},{8,9},{9,8},{10,11... | collective-permute-start | bytes 393224 | tf_op jit(solution)/shard_map/ppermute | solution.py:298

commit v9 on v7

--- a/solution.py
+++ b/solution.py
@@ -28,17 +28,25 @@
     return hi, mid, wide - hi - mid
 
 
-def with_norms(wide, offset, first, other):
+def put_row(ref, k, at, wide, offset):
     lane = lax.broadcasted_iota(jnp.int32, wide.shape, 1)
     wide = jnp.where(lane < 64, wide, 0.0)
     half = offset - 0.5 * jnp.sum(wide * wide, axis=1, keepdims=True)
-    hi, mid, low = three_parts(half)
-    ones = (lane >= other) & (lane < other + 3)
-    wide = jnp.where(ones, 1.0, wide)
-    wide = jnp.where(lane == first, hi, wide)
-    wide = jnp.where(lane == first + 1, mid, wide)
-    wide = jnp.where(lane == first + 2, low, wide)
-    return wide.astype(BF16)
+    for place, part in enumerate(three_parts(half)):
+        wide = jnp.where(lane == 64 + place, part, wide)
+    ref[k, at : at + 512, :128] = wide.astype(BF16)
+    ref[k, at : at + 512, 128:] = jnp.full((512, 128), -0.5, BF16)
+
+
+def column(raw):
+    lane = lax.broadcasted_iota(jnp.int32, raw.shape, 1)
+    wide = raw.astype(F32)
+    square = wide * wide
+    high = square.astype(BF16)
+    low = square - high.astype(F32)
+    second = jnp.where(lane < 64, high.astype(F32), pltpu.roll(low, 64, 1)).astype(BF16)
+    first = jnp.where(lane < 64, wide, 1.0).astype(BF16)
+    return jnp.concatenate([first, second], axis=1)
 
 
 def ready_rows(amp, mines, theirs):
@@ -52,11 +60,11 @@
                 mine = refs[k][low : low + 32, :].astype(F32)
                 other = theirs_ref[64 * k + low : 64 * k + low + 32, :].astype(F32)
                 wide = jnp.concatenate([mine, other, mine, other], axis=0).T
-                out_ref[k, 512 * half : 512 * half + 512] = with_norms(wide, amp_ref[1], 67, 64)
+                put_row(out_ref, k, 512 * half, wide, amp_ref[1])
 
     return pl.pallas_call(
         body,
-        out_shape=jax.ShapeDtypeStruct((count, 1024, 128), BF16),
+        out_shape=jax.ShapeDtypeStruct((count, 1024, 256), BF16),
         in_specs=[pl.BlockSpec(memory_space=pltpu.SMEM)]
         + [pl.BlockSpec(memory_space=pltpu.VMEM)] * (count + 1),
         out_specs=pl.BlockSpec(memory_space=pltpu.VMEM),
@@ -65,8 +73,21 @@
     )(amp, *mines, theirs)
 
 
+def kept_in_hbm(array):
+    return pltpu.with_memory_space_constraint(array, pltpu.HBM)
+
+
 def first_pack(zl, points, vectors, lengthscale):
-    def body(zl_ref, points_ref, vectors_ref, length_ref, out_ref, kept_ref):
+    def body(zl_ref, points_in, vectors_in, length_in, out_ref, kept_ref, points_ref, vectors_ref, length_ref, sems):
+        copies = [
+            pltpu.make_async_copy(length_in, length_ref, sems.at[0]),
+            pltpu.make_async_copy(points_in, points_ref, sems.at[1]),
+            pltpu.make_async_copy(vectors_in, vectors_ref, sems.at[2]),
+        ]
+        for copy in copies:
+            copy.start()
+        for copy in copies:
+            copy.wait()
         at = zl_ref[0]
         lane = lax.broadcasted_iota(jnp.int32, (32, 64), 1)
         row = lax.broadcasted_iota(jnp.int32, (32, 64), 0)
@@ -80,12 +101,18 @@
 
     return pl.pallas_call(
         body,
-        out_shape=[jax.ShapeDtypeStruct((n, 512), BF16) for n in (96, 32)],
-        in_specs=[pl.BlockSpec(memory_space=pltpu.SMEM)] + [pl.BlockSpec(memory_space=pltpu.VMEM)] * 3,
-        out_specs=[pl.BlockSpec(memory_space=pltpu.VMEM)] * 2,
+        out_shape=(jax.ShapeDtypeStruct((96, 512), BF16), jax.ShapeDtypeStruct((32, 512), BF16)),
+        in_specs=[pl.BlockSpec(memory_space=pltpu.SMEM)] + [pl.BlockSpec(memory_space=pltpu.HBM)] * 3,
+        out_specs=(pl.BlockSpec(memory_space=pltpu.VMEM),) * 2,
+        scratch_shapes=[
+            pltpu.VMEM((32, 1024), BF16),
+            pltpu.VMEM((32, 1024), BF16),
+            pltpu.VMEM((1, 64), F32),
+            pltpu.SemaphoreType.DMA((3,)),
+        ],
         compiler_params=PARAMS,
         name="first_pack",
-    )(zl, points, vectors, lengthscale.reshape(1, 64))
+    )(zl, *(kept_in_hbm(a) for a in (points, vectors, lengthscale.reshape(1, 64))))
 
 
 def copy_of(parts, rows, token, weight):
@@ -118,11 +145,11 @@
         share_ref[...] = jnp.concatenate([picked, kept_ref[...].astype(F32), theirs[64:]], axis=0).T.astype(BF16)
         for k, wide in enumerate((low, high)):
             wide = jnp.concatenate([wide, wide], axis=0).T
-            rows_ref[0, 512 * k : 512 * k + 512] = with_norms(wide, amp_ref[1], 67, 64)
+            put_row(rows_ref, 0, 512 * k, wide, amp_ref[1])
 
     return pl.pallas_call(
         body,
-        out_shape=[jax.ShapeDtypeStruct((1, 1024, 128), BF16), jax.ShapeDtypeStruct((512, 128), BF16)],
+        out_shape=[jax.ShapeDtypeStruct((1, 1024, 256), BF16), jax.ShapeDtypeStruct((512, 128), BF16)],
         in_specs=[pl.BlockSpec(memory_space=pltpu.SMEM)] * 2 + [pl.BlockSpec(memory_space=pltpu.VMEM)] * 3,
         out_specs=[pl.BlockSpec(memory_space=pltpu.VMEM)] * 2,
         compiler_params=PARAMS,
@@ -153,9 +180,9 @@
     rights, turned = [], []
     for ref, start in raws:
         for sub in range(start, ref.shape[0], 512):
-            wide = ref[sub : sub + 512, :].astype(F32)
-            rights.append(with_norms(wide, 0.0, 64, 67))
-            turned.append(wide.T[64:, :].astype(BF16))
+            raw = ref[sub : sub + 512, :]
+            rights.append(column(raw))
+            turned.append(raw.astype(F32).T[64:, :].astype(BF16))
             right_ref[at : at + 512, :] = rights[-1]
             vectors_ref[:, at : at + 512] = turned[-1]
             at += 512
@@ -232,14 +259,14 @@
         sum_specs = [acc_spec]
     made = []
     if raws:
-        made = [jax.ShapeDtypeStruct((total, 128), BF16), jax.ShapeDtypeStruct((64, total), BF16)]
+        made = [jax.ShapeDtypeStruct((total, 256), BF16), jax.ShapeDtypeStruct((64, total), BF16)]
     out = pl.pallas_call(
         body,
         grid=(count * per,),
         out_shape=sum_shapes + made,
         in_specs=[
             pl.BlockSpec(memory_space=pltpu.SMEM),
-            pl.BlockSpec((1, TM, 128), lambda i: (i // per, i % per, 0)),
+            pl.BlockSpec((1, TM, 256), lambda i: (i // per, i % per, 0)),
         ]
         + [whole(part) for part in flat]
         + [whole(raw) for raw, _ in raws]

time: 79.1 us -> 79 us (level)
  local copies, waits for them, and re-layouts: 2.42 us -> 0.08 us
  Pallas kernels: 43.5 us -> 45.8 us
    unnamed x11 -> x5, local copies, waits for them, and re-layouts: 2.39 us -> 0.05 us
    pallas_call x6, Pallas kernels: 41 us -> 42.3 us  [add_tiles(): pl.pallas_call(body, grid=(count * per,), out_shape=sum_shapes + made, in...]
    pallas_call x3, Pallas kernels: 2.5 us -> 3.52 us  [the longest x1 1.55 us: ready_rows(): pl.pallas_call(body, out_shape=jax.ShapeDtypeStruct((count, 1024, 256), B...]
  transfers between devices with their start and end apart: 16 -> 16, of which waited for: 5 -> 5; matrix products, arithmetic and copies ran while one was open for 0% -> 0% of each run, Pallas kernels for 45% -> 47%
where the time goes in v9:
time: 79 us; the launch traced here: 78.7 us
  Pallas kernels  45.8 us (58%)
  starting transfers between devices  22.8 us (29%)
  waiting for transfers between devices  7.56 us (10%)
  between operations  1.56 us (2%)
  other arithmetic  0.82 us (1%)
    pallas_call x6, Pallas kernels, add_tiles(): pl.pallas_call(body, grid=(count * per,), out_shape=sum_shapes + made, in...  42.3 us
    ppermute x16, starting transfers between devices, shift(): lax.ppermute(value, axis, [(i, (i + by) % size) for i in range(size)])  22.8 us
    ppermute x16, waiting for transfers between devices, shift(): lax.ppermute(value, axis, [(i, (i + by) % size) for i in range(size)])  7.56 us
  transfers between devices with their start and end apart: 16, of which 5 were waited for; matrix products, arithmetic and copies ran while one was open for 0% of the time, Pallas kernels for 47%

profile of v9, /device:TPU:0, one launch (start us, length us, event | category | flops | bytes accessed | tf_op | source)
XLA Modules:
  0.0 78.7 jit_solution(1272332748385626587)
XLA Ops:
  0.0 1.0 %first_pack.1 = (bf16[96,512]{1,0:T(8,128)(2,1)S(1)}, bf16[32,512]{1,0:T(8,128)(2,1)S(1)}) custom-call(s32[1]{0:T(128)} %bitcast.zl_ref, bf16[32,1024]{1,0:T(8,128)(2,1)} %bitcast.17, bf16[32,1024]{1,0:T(8,128)(2,1)} %bitcast.16, f32[1,64]{1,0:T(1,128)} %bitcast.18), custom_call_target="tpu_custom_call" | custom-call | tf_op jit(solution)/shard_map/first_pack/pallas_call | solution.py:102
  1.0 2.1 %collective-permute-start = (bf16[96,512]{1,0:T(8,128)(2,1)S(1)}, bf16[96,512]{1,0:T(8,128)(2,1)S(1)}, u32[]{:S(2)}, u32[]{:S(2)}) collective-permute-start(bf16[96,512]{1,0:T(8,128)(2,1)S(1)} %get-tuple-element.37.refs_0_), channel_id=1, source_target_pairs={{0,1},{1,0},{2,3},{3,2},{4,5},{5,4},{6,7},{7,6},{8,9},{9,8},{10,11... | collective-permute-start | bytes 294920 | tf_op jit(solution)/shard_map/ppermute | solution.py:284
  3.1 3.0 %collective-permute-start.1 = (bf16[64,512]{1,0:T(8,128)(2,1)S(1)}, bf16[64,512]{1,0:T(8,128)(2,1)S(1)}, u32[]{:S(2)}, u32[]{:S(2)}) collective-permute-start(bf16[64,512]{1,0:T(8,128)(2,1)S(1)} %copy_of.2.half_ref), channel_id=1, source_target_pairs={{0,32},{16,48},{32,0},{48,16},{1,33},{17,49},{33,1},{49,17},{2,34}... | collective-permute-start | bytes 196616 | tf_op jit(solution)/shard_map/ppermute | solution.py:284
  6.1 0.6 collective-permute-start.2
  6.7 2.6 %collective-permute-start.3 = (bf16[64,512]{1,0:T(8,128)(2,1)S(1)}, bf16[64,512]{1,0:T(8,128)(2,1)S(1)}, u32[]{:S(2)}, u32[]{:S(2)}) collective-permute-start(bf16[64,512]{1,0:T(8,128)(2,1)S(1)} %copy_of.2.half_ref), channel_id=1, source_target_pairs={{0,48},{16,0},{32,16},{48,32},{1,49},{17,1},{33,17},{49,33},{2,50}... | collective-permute-start | bytes 196616 | tf_op jit(solution)/shard_map/ppermute | solution.py:284
  10.1 0.1 pad_maximum_fusion.amp_ref
  10.1 1.0 %second_pack.1 = (bf16[1,1024,256]{2,1,0:T(8,128)(2,1)S(1)}, bf16[512,128]{1,0:T(8,128)(2,1)S(1)}) custom-call(s32[1]{0:T(128)} %bitcast.zl_ref, f32[2]{0:T(128)S(1)} %pad_maximum_fusion.amp_ref, bf16[64,512]{1,0:T(8,128)(2,1)S(1)} %copy_of.2.half_ref, bf16[96,512]{1,0:T(8,128)(2,1)S(1)} %collective-permute-done.got_ref, ...), custom_call_target="tpu_custom_call" | custom-call | tf_op jit(solution)/shard_map/second_pack/pallas_call | solution.py:150
  11.1 0.1 collective-permute-start.4
  11.2 3.3 %collective-permute-start.6 = (bf16[512,128]{1,0:T(8,128)(2,1)S(1)}, bf16[512,128]{1,0:T(8,128)(2,1)S(1)}, u32[]{:S(2)}, u32[]{:S(2)}) collective-permute-start(bf16[512,128]{1,0:T(8,128)(2,1)S(1)} %get-tuple-element.39.token_ref.refs_0_), channel_id=1, source_target_pairs={{0,8},{4,12},{8,0},{12,4},{1,9},{5,13},{9,1},{13,5},{2,10},{6,14},... | collective-permute-start | bytes 393224 | tf_op jit(solution)/shard_map/ppermute | solution.py:284
  14.5 0.7 collective-permute-start.7
  15.2 2.6 %collective-permute-start.8 = (bf16[512,128]{1,0:T(8,128)(2,1)S(1)}, bf16[512,128]{1,0:T(8,128)(2,1)S(1)}, u32[]{:S(2)}, u32[]{:S(2)}) collective-permute-start(bf16[512,128]{1,0:T(8,128)(2,1)S(1)} %get-tuple-element.39.token_ref.refs_0_), channel_id=1, source_target_pairs={{0,12},{4,0},{8,4},{12,8},{1,13},{5,1},{9,5},{13,9},{2,14},{6,2},{... | collective-permute-start | bytes 393224 | tf_op jit(solution)/shard_map/ppermute | solution.py:284
  17.8 2.1 %add_tiles.6 = (f32[1,64,1024]{2,1,0:T(8,128)S(1)}, bf16[1024,256]{1,0:T(8,128)(2,1)S(1)}, bf16[64,1024]{1,0:T(8,128)(2,1)S(1)}) custom-call(f32[2]{0:T(128)S(1)} %pad_maximum_fusion.amp_ref, bf16[1,1024,256]{2,1,0:T(8,128)(2,1)S(1)} %get-tuple-element.38.left_ref, bf16[512,128]{1,0:T(8,128)(2,1)S(1)} %get-tuple-element.39.token_ref.refs_0_, ...), custom_call_target="tpu_custom_call" | custom-call | flops 2147483648 | bytes 393216 | tf_op jit(solution)/shard_map/add_tiles/pallas_call | solution.py:263
  19.8 1.7 %collective-permute-done.7 = bf16[512,128]{1,0:T(8,128)(2,1)S(1)} collective-permute-done((bf16[512,128]{1,0:T(8,128)(2,1)S(1)}, bf16[512,128]{1,0:T(8,128)(2,1)S(1)}, u32[]{:S(2)}, u32[]{:S(2)}) %collective-permute-start.7) | collective-permute-done | bytes 131104 | tf_op jit(solution)/shard_map/ppermute | solution.py:284
  21.6 0.2 collective-permute-done.8
  21.8 0.1 collective-permute-start.9
  21.9 0.2 collective-permute-start.5
  22.1 3.9 %collective-permute-start.10 = (bf16[2048,128]{1,0:T(8,128)(2,1)S(1)}, bf16[2048,128]{1,0:T(8,128)(2,1)S(1)}, u32[]{:S(2)}, u32[]{:S(2)}) collective-permute-start(bf16[2048,128]{1,0:T(8,128)(2,1)S(1)} %constant_dynamic-update-slice_fusion.refs_0_), channel_id=1, source_target_pairs={{0,64},{64,0},{1,65},{65,1},{2,66},{66,2},{3,67},{67,3},{4,68},{68... | collective-permute-start | bytes 1572872 | tf_op jit(solution)/shard_map/ppermute | solution.py:284
  26.0 2.7 %add_tiles.7 = (f32[1,64,1024]{2,1,0:T(8,128)S(1)}, bf16[1536,256]{1,0:T(8,128)(2,1)S(1)}, bf16[64,1536]{1,0:T(8,128)(2,1)S(1)}) custom-call(f32[2]{0:T(128)S(1)} %pad_maximum_fusion.amp_ref, bf16[1,1024,256]{2,1,0:T(8,128)(2,1)S(1)} %get-tuple-element.38.left_ref, bf16[2048,128]{1,0:T(8,128)(2,1)S(1)} %constant_dynamic-update-slice_fusion.refs_0_, ...), custom_call_target="tpu_custom_call" | custom-call | flops 50331648 | bytes 589824 | tf_op jit(solution)/shard_map/add_tiles/pallas_call | solution.py:263
  28.7 1.0 %collective-permute-done.5.refs_3_ = bf16[192,512]{1,0:T(8,128)(2,1)S(1)} collective-permute-done((bf16[192,512]{1,0:T(8,128)(2,1)S(1)}, bf16[192,512]{1,0:T(8,128)(2,1)S(1)}, u32[]{:S(2)}, u32[]{:S(2)}) %collective-permute-start.5) | collective-permute-done | bytes 196640 | tf_op jit(solution)/shard_map/ppermute | solution.py:284
  29.7 1.6 %ready_rows.1.left_ref = bf16[3,1024,256]{2,1,0:T(8,128)(2,1)S(1)} custom-call(f32[2]{0:T(128)S(1)} %pad_maximum_fusion.amp_ref, bf16[64,512]{1,0:T(8,128)(2,1)S(1)} %collective-permute-done.1.refs_0_, bf16[64,512]{1,0:T(8,128)(2,1)S(1)} %collective-permute-done.2.refs_1_, bf16[64,512]{1,0:T(8,128)(2,1)S(1)} %collective-permute-done.3.refs_2_, ...), custom_call_target="tpu_custom_call" | custom-call | tf_op jit(solution)/shard_map/ready_rows/pallas_call | solution.py:65
  31.3 15.1 %add_tiles.8 = (f32[3,64,1024]{2,1,0:T(8,128)S(1)}, bf16[1536,256]{1,0:T(8,128)(2,1)S(1)}, bf16[64,1536]{1,0:T(8,128)(2,1)S(1)}) custom-call(f32[2]{0:T(128)S(1)} %pad_maximum_fusion.amp_ref, bf16[3,1024,256]{2,1,0:T(8,128)(2,1)S(1)} %ready_rows.1.left_ref, bf16[1024,256]{1,0:T(8,128)(2,1)S(1)} %get-tuple-element.49.refs_0_, ...), custom_call_target="tpu_custom_call" | custom-call | flops 6442450944 | bytes 1572864 | tf_op jit(solution)/shard_map/add_tiles/pallas_call | solution.py:263
  46.4 0.3 collective-permute-start.11
  46.7 7.8 %add_tiles.9 = (f32[3,64,1024]{2,1,0:T(8,128)S(1)}, bf16[2048,256]{1,0:T(8,128)(2,1)S(1)}, bf16[64,2048]{1,0:T(8,128)(2,1)S(1)}) custom-call(f32[2]{0:T(128)S(1)} %pad_maximum_fusion.amp_ref, bf16[3,1024,256]{2,1,0:T(8,128)(2,1)S(1)} %ready_rows.1.left_ref, bf16[2048,128]{1,0:T(8,128)(2,1)S(1)} %collective-permute-done.10.refs_0_, ...), custom_call_target="tpu_custom_call" | custom-call | flops 3221225472 | bytes 786432 | tf_op jit(solution)/shard_map/add_tiles/pallas_call | solution.py:263
  54.5 8.0 %add_tiles.10 = (bf16[64,1024]{1,0:T(8,128)(2,1)S(1)}, bf16[64,1024]{1,0:T(8,128)(2,1)S(1)}, bf16[64,1024]{1,0:T(8,128)(2,1)S(1)}, bf16[2048,256]{1,0:T(8,128)(2,1)S(1)}, bf16[64,2048]{1,0:T(8,128)(2,1)S(1)}) custom-call(f32[2]{0:T(128)S(1)} %pad_maximum_fusion.amp_ref, bf16[3,1024,256]{2,1,0:T(8,128)(2,1)S(1)} %ready_rows.1.left_ref, ...), custom_call_target="tpu_custom_call" | custom-call | flops 3221225472 | bytes 786432 | tf_op jit(solution)/shard_map/add_tiles/pallas_call | solution.py:263
  62.5 0.1 collective-permute-start.14
  62.5 3.2 %collective-permute-start.13 = (bf16[64,1024]{1,0:T(8,128)(2,1)S(1)}, bf16[64,1024]{1,0:T(8,128)(2,1)S(1)}, u32[]{:S(2)}, u32[]{:S(2)}) collective-permute-start(bf16[64,1024]{1,0:T(8,128)(2,1)S(1)} %get-tuple-element.65), channel_id=1, source_target_pairs={{0,48},{16,0},{32,16},{48,32},{1,49},{17,1},{33,17},{49,33},{2,50}... | collective-permute-start | bytes 393224 | tf_op jit(solution)/shard_map/ppermute | solution.py:284
  65.8 6.7 %add_tiles.11 = f32[1,64,1024]{2,1,0:T(8,128)S(1)} custom-call(f32[2]{0:T(128)S(1)} %pad_maximum_fusion.amp_ref, bf16[1,1024,256]{2,1,0:T(8,128)(2,1)S(1)} %get-tuple-element.38.left_ref, bf16[1536,256]{1,0:T(8,128)(2,1)S(1)} %get-tuple-element.53.refs_0_, bf16[64,1536]{1,0:T(8,128)(2,1)S(1)} %get-tuple-element.54.refs_1_, ...), custom_call_target="tpu_custom_call" | custom-call | flops 2952790016 | bytes 2162688 | tf_op jit(solution)/shard_map/add_tiles/pallas_call | solution.py:263
  72.5 0.1 collective-permute-done.12
  72.6 0.1 fusion.1
  72.7 0.2 collective-permute-start.15
  73.5 4.5 %collective-permute-done.15 = f32[32,1024]{1,0:T(8,128)S(1)} collective-permute-done((f32[32,1024]{1,0:T(8,128)S(1)}, f32[32,1024]{1,0:T(8,128)S(1)}, u32[]{:S(2)}, u32[]{:S(2)}) %collective-permute-start.15) | collective-permute-done | bytes 131104 | tf_op jit(solution)/shard_map/ppermute | solution.py:284
  78.0 0.7 fusion.3
  (21 shorter events, 0.1 us)
Async XLA Ops:
  1.0 9.1 %collective-permute-start = (bf16[96,512]{1,0:T(8,128)(2,1)S(1)}, bf16[96,512]{1,0:T(8,128)(2,1)S(1)}, u32[]{:S(2)}, u32[]{:S(2)}) collective-permute-start(bf16[96,512]{1,0:T(8,128)(2,1)S(1)} %get-tuple-element.37.refs_0_), channel_id=1, source_target_pairs={{0,1},{1,0},{2,3},{3,2},{4,5},{5,4},{6,7},{7,6},{8,9},{9,8},{10,11... | collective-permute-start | bytes 294920 | tf_op jit(solution)/shard_map/ppermute | solution.py:284
  3.1 11.4 %collective-permute-start.1 = (bf16[64,512]{1,0:T(8,128)(2,1)S(1)}, bf16[64,512]{1,0:T(8,128)(2,1)S(1)}, u32[]{:S(2)}, u32[]{:S(2)}) collective-permute-start(bf16[64,512]{1,0:T(8,128)(2,1)S(1)} %copy_of.2.half_ref), channel_id=1, source_target_pairs={{0,32},{16,48},{32,0},{48,16},{1,33},{17,49},{33,1},{49,17},{2,34}... | collective-permute-start | bytes 196616 | tf_op jit(solution)/shard_map/ppermute | solution.py:284
  6.1 9.0 %collective-permute-start.2 = (bf16[64,512]{1,0:T(8,128)(2,1)S(1)}, bf16[64,512]{1,0:T(8,128)(2,1)S(1)}, u32[]{:S(2)}, u32[]{:S(2)}) collective-permute-start(bf16[64,512]{1,0:T(8,128)(2,1)S(1)} %copy_of.2.half_ref), channel_id=1, source_target_pairs={{0,16},{16,32},{32,48},{48,0},{1,17},{17,33},{33,49},{49,1},{2,18}... | collective-permute-start | bytes 196616 | tf_op jit(solution)/shard_map/ppermute | solution.py:284
  6.7 11.0 %collective-permute-start.3 = (bf16[64,512]{1,0:T(8,128)(2,1)S(1)}, bf16[64,512]{1,0:T(8,128)(2,1)S(1)}, u32[]{:S(2)}, u32[]{:S(2)}) collective-permute-start(bf16[64,512]{1,0:T(8,128)(2,1)S(1)} %copy_of.2.half_ref), channel_id=1, source_target_pairs={{0,48},{16,0},{32,16},{48,32},{1,49},{17,1},{33,17},{49,33},{2,50}... | collective-permute-start | bytes 196616 | tf_op jit(solution)/shard_map/ppermute | solution.py:284
  11.1 6.7 %collective-permute-start.4 = (bf16[512,128]{1,0:T(8,128)(2,1)S(1)}, bf16[512,128]{1,0:T(8,128)(2,1)S(1)}, u32[]{:S(2)}, u32[]{:S(2)}) collective-permute-start(bf16[512,128]{1,0:T(8,128)(2,1)S(1)} %get-tuple-element.39.token_ref.refs_0_), channel_id=1, source_target_pairs={{0,2},{2,0},{1,3},{3,1},{4,6},{6,4},{5,7},{7,5},{8,10},{10,8},{9,1... | collective-permute-start | bytes 393224 | tf_op jit(solution)/shard_map/ppermute | solution.py:284
  11.2 8.6 %collective-permute-start.6 = (bf16[512,128]{1,0:T(8,128)(2,1)S(1)}, bf16[512,128]{1,0:T(8,128)(2,1)S(1)}, u32[]{:S(2)}, u32[]{:S(2)}) collective-permute-start(bf16[512,128]{1,0:T(8,128)(2,1)S(1)} %get-tuple-element.39.token_ref.refs_0_), channel_id=1, source_target_pairs={{0,8},{4,12},{8,0},{12,4},{1,9},{5,13},{9,1},{13,5},{2,10},{6,14},... | collective-permute-start | bytes 393224 | tf_op jit(solution)/shard_map/ppermute | solution.py:284
  14.5 7.1 %collective-permute-start.7 = (bf16[512,128]{1,0:T(8,128)(2,1)S(1)}, bf16[512,128]{1,0:T(8,128)(2,1)S(1)}, u32[]{:S(2)}, u32[]{:S(2)}) collective-permute-start(bf16[512,128]{1,0:T(8,128)(2,1)S(1)} %get-tuple-element.39.token_ref.refs_0_), channel_id=1, source_target_pairs={{0,4},{4,8},{8,12},{12,0},{1,5},{5,9},{9,13},{13,1},{2,6},{6,10},{... | collective-permute-start | bytes 393224 | tf_op jit(solution)/shard_map/ppermute | solution.py:284
  15.2 6.6 %collective-permute-start.8 = (bf16[512,128]{1,0:T(8,128)(2,1)S(1)}, bf16[512,128]{1,0:T(8,128)(2,1)S(1)}, u32[]{:S(2)}, u32[]{:S(2)}) collective-permute-start(bf16[512,128]{1,0:T(8,128)(2,1)S(1)} %get-tuple-element.39.token_ref.refs_0_), channel_id=1, source_target_pairs={{0,12},{4,0},{8,4},{12,8},{1,13},{5,1},{9,5},{13,9},{2,14},{6,2},{... | collective-permute-start | bytes 393224 | tf_op jit(solution)/shard_map/ppermute | solution.py:284
  21.8 9.4 %collective-permute-start.9 = (bf16[2048,128]{1,0:T(8,128)(2,1)S(1)}, bf16[2048,128]{1,0:T(8,128)(2,1)S(1)}, u32[]{:S(2)}, u32[]{:S(2)}) collective-permute-start(bf16[2048,128]{1,0:T(8,128)(2,1)S(1)} %constant_dynamic-update-slice_fusion.refs_0_), channel_id=1, source_target_pairs={{0,2},{2,0},{1,3},{3,1},{4,6},{6,4},{5,7},{7,5},{8,10},{10,8},{9,1... | collective-permute-start | bytes 1572872 | tf_op jit(solution)/shard_map/ppermute | solution.py:284
  21.9 7.8 %collective-permute-start.5 = (bf16[192,512]{1,0:T(8,128)(2,1)S(1)}, bf16[192,512]{1,0:T(8,128)(2,1)S(1)}, u32[]{:S(2)}, u32[]{:S(2)}) collective-permute-start(bf16[192,512]{1,0:T(8,128)(2,1)S(1)} %copy_of.3), channel_id=1, source_target_pairs={{0,1},{1,0},{2,3},{3,2},{4,5},{5,4},{6,7},{7,6},{8,9},{9,8},{10,11... | collective-permute-start | bytes 589832 | tf_op jit(solution)/shard_map/ppermute | solution.py:284
  22.1 24.3 %collective-permute-start.10 = (bf16[2048,128]{1,0:T(8,128)(2,1)S(1)}, bf16[2048,128]{1,0:T(8,128)(2,1)S(1)}, u32[]{:S(2)}, u32[]{:S(2)}) collective-permute-start(bf16[2048,128]{1,0:T(8,128)(2,1)S(1)} %constant_dynamic-update-slice_fusion.refs_0_), channel_id=1, source_target_pairs={{0,64},{64,0},{1,65},{65,1},{2,66},{66,2},{3,67},{67,3},{4,68},{68... | collective-permute-start | bytes 1572872 | tf_op jit(solution)/shard_map/ppermute | solution.py:284
  46.4 8.1 %collective-permute-start.11 = (bf16[2048,128]{1,0:T(8,128)(2,1)S(1)}, bf16[2048,128]{1,0:T(8,128)(2,1)S(1)}, u32[]{:S(2)}, u32[]{:S(2)}) collective-permute-start(bf16[2048,128]{1,0:T(8,128)(2,1)S(1)} %collective-permute-done.10.refs_0_), channel_id=1, source_target_pairs={{0,2},{2,0},{1,3},{3,1},{4,6},{6,4},{5,7},{7,5},{8,10},{10,8},{9,1... | collective-permute-start | bytes 1572872 | tf_op jit(solution)/shard_map/ppermute | solution.py:284
  62.5 10.0 %collective-permute-start.14 = (bf16[64,1024]{1,0:T(8,128)(2,1)S(1)}, bf16[64,1024]{1,0:T(8,128)(2,1)S(1)}, u32[]{:S(2)}, u32[]{:S(2)}) collective-permute-start(bf16[64,1024]{1,0:T(8,128)(2,1)S(1)} %get-tuple-element.66), channel_id=1, source_target_pairs={{0,16},{16,32},{32,48},{48,0},{1,17},{17,33},{33,49},{49,1},{2,18}... | collective-permute-start | bytes 393224 | tf_op jit(solution)/shard_map/ppermute | solution.py:284
  62.5 10.0 %collective-permute-start.13 = (bf16[64,1024]{1,0:T(8,128)(2,1)S(1)}, bf16[64,1024]{1,0:T(8,128)(2,1)S(1)}, u32[]{:S(2)}, u32[]{:S(2)}) collective-permute-start(bf16[64,1024]{1,0:T(8,128)(2,1)S(1)} %get-tuple-element.65), channel_id=1, source_target_pairs={{0,48},{16,0},{32,16},{48,32},{1,49},{17,1},{33,17},{49,33},{2,50}... | collective-permute-start | bytes 393224 | tf_op jit(solution)/shard_map/ppermute | solution.py:284
  65.8 6.8 %collective-permute-start.12 = (bf16[64,1024]{1,0:T(8,128)(2,1)S(1)}, bf16[64,1024]{1,0:T(8,128)(2,1)S(1)}, u32[]{:S(2)}, u32[]{:S(2)}) collective-permute-start(bf16[64,1024]{1,0:T(8,128)(2,1)S(1)} %get-tuple-element.64), channel_id=1, source_target_pairs={{0,32},{16,48},{32,0},{48,16},{1,33},{17,49},{33,1},{49,17},{2,34}... | collective-permute-start | bytes 393224 | tf_op jit(solution)/shard_map/ppermute | solution.py:284
  65.8 12.2 %copy-start = (bf16[1024,32]{0,1:T(8,128)(2,1)S(1)}, bf16[1024,32]{0,1:T(8,128)(2,1)}, u32[]{:S(2)}) copy-start(bf16[1024,32]{0,1:T(8,128)(2,1)} %param.6) | copy-start | bytes 196612
  72.7 5.3 %collective-permute-start.15 = (f32[32,1024]{1,0:T(8,128)S(1)}, f32[32,1024]{1,0:T(8,128)S(1)}, u32[]{:S(2)}, u32[]{:S(2)}) collective-permute-start(f32[32,1024]{1,0:T(8,128)S(1)} %slice.9), channel_id=1, source_target_pairs={{0,1},{1,0},{2,3},{3,2},{4,5},{5,4},{6,7},{7,6},{8,9},{9,8},{10,11... | collective-permute-start | bytes 393224 | tf_op jit(solution)/shard_map/ppermute | solution.py:284

commit v10 on v9

--- a/solution.py
+++ b/solution.py
@@ -28,25 +28,14 @@
     return hi, mid, wide - hi - mid
 
 
-def put_row(ref, k, at, wide, offset):
-    lane = lax.broadcasted_iota(jnp.int32, wide.shape, 1)
-    wide = jnp.where(lane < 64, wide, 0.0)
-    half = offset - 0.5 * jnp.sum(wide * wide, axis=1, keepdims=True)
+def with_parts(features, offset, first):
+    half = offset - 0.5 * jnp.sum(features * features, axis=0, keepdims=True)
+    shape = (8, features.shape[1])
+    row = lax.broadcasted_iota(jnp.int32, shape, 0)
+    tail = jnp.where(row < 6, 1.0, 0.0)
     for place, part in enumerate(three_parts(half)):
-        wide = jnp.where(lane == 64 + place, part, wide)
-    ref[k, at : at + 512, :128] = wide.astype(BF16)
-    ref[k, at : at + 512, 128:] = jnp.full((512, 128), -0.5, BF16)
-
-
-def column(raw):
-    lane = lax.broadcasted_iota(jnp.int32, raw.shape, 1)
-    wide = raw.astype(F32)
-    square = wide * wide
-    high = square.astype(BF16)
-    low = square - high.astype(F32)
-    second = jnp.where(lane < 64, high.astype(F32), pltpu.roll(low, 64, 1)).astype(BF16)
-    first = jnp.where(lane < 64, wide, 1.0).astype(BF16)
-    return jnp.concatenate([first, second], axis=1)
+        tail = jnp.where(row == first + place, part, tail)
+    return jnp.concatenate([features, tail, jnp.zeros((56, features.shape[1]), F32)], axis=0)
 
 
 def ready_rows(amp, mines, theirs):
@@ -59,12 +48,12 @@
                 low = 32 * half
                 mine = refs[k][low : low + 32, :].astype(F32)
                 other = theirs_ref[64 * k + low : 64 * k + low + 32, :].astype(F32)
-                wide = jnp.concatenate([mine, other, mine, other], axis=0).T
-                put_row(out_ref, k, 512 * half, wide, amp_ref[1])
+                features = jnp.concatenate([mine, other], axis=0)
+                out_ref[k, :, 512 * half : 512 * half + 512] = with_parts(features, amp_ref[1], 3).astype(BF16)
 
     return pl.pallas_call(
         body,
-        out_shape=jax.ShapeDtypeStruct((count, 1024, 256), BF16),
+        out_shape=jax.ShapeDtypeStruct((count, 128, 1024), BF16),
         in_specs=[pl.BlockSpec(memory_space=pltpu.SMEM)]
         + [pl.BlockSpec(memory_space=pltpu.VMEM)] * (count + 1),
         out_specs=pl.BlockSpec(memory_space=pltpu.VMEM),
@@ -142,14 +131,13 @@
         low = jnp.concatenate([mine[:32], theirs[:32]], axis=0)
         high = jnp.concatenate([mine[32:], theirs[32:64]], axis=0)
         picked = jnp.where(first, low, high)
-        share_ref[...] = jnp.concatenate([picked, kept_ref[...].astype(F32), theirs[64:]], axis=0).T.astype(BF16)
-        for k, wide in enumerate((low, high)):
-            wide = jnp.concatenate([wide, wide], axis=0).T
-            put_row(rows_ref, 0, 512 * k, wide, amp_ref[1])
+        share_ref[...] = jnp.concatenate([picked, kept_ref[...].astype(F32), theirs[64:]], axis=0).astype(BF16)
+        for k, features in enumerate((low, high)):
+            rows_ref[0, :, 512 * k : 512 * k + 512] = with_parts(features, amp_ref[1], 3).astype(BF16)
 
     return pl.pallas_call(
         body,
-        out_shape=[jax.ShapeDtypeStruct((1, 1024, 256), BF16), jax.ShapeDtypeStruct((512, 128), BF16)],
+        out_shape=[jax.ShapeDtypeStruct((1, 128, 1024), BF16), jax.ShapeDtypeStruct((128, 512), BF16)],
         in_specs=[pl.BlockSpec(memory_space=pltpu.SMEM)] * 2 + [pl.BlockSpec(memory_space=pltpu.VMEM)] * 3,
         out_specs=[pl.BlockSpec(memory_space=pltpu.VMEM)] * 2,
         compiler_params=PARAMS,
@@ -158,13 +146,13 @@
 
 
 def one_block(left, right, vectors, top):
-    exponent = lax.dot_general(right, left, (((1,), (1,)), ((), ())), preferred_element_type=F32)
+    exponent = jnp.dot(right, left, preferred_element_type=F32)
     block = jnp.minimum(jnp.exp(exponent).astype(BF16), top)
     return jnp.dot(vectors, block, preferred_element_type=F32)
 
 
 def ready_sum(left, pairs, top):
-    result = jnp.zeros((64, left.shape[0]), F32)
+    result = jnp.zeros((64, left.shape[1]), F32)
     for right_ref, vectors_ref in pairs:
         total = right_ref.shape[0]
         for at in range(0, total, TN):
@@ -175,14 +163,14 @@
 
 def raw_sum(left, raws, right_ref, vectors_ref, top):
     total = right_ref.shape[0]
-    result = jnp.zeros((64, left.shape[0]), F32)
+    result = jnp.zeros((64, left.shape[1]), F32)
     at = 0
     rights, turned = [], []
     for ref, start in raws:
-        for sub in range(start, ref.shape[0], 512):
-            raw = ref[sub : sub + 512, :]
-            rights.append(column(raw))
-            turned.append(raw.astype(F32).T[64:, :].astype(BF16))
+        for sub in range(128 * start, ref.shape[0], 128):
+            features = ref[sub : sub + 64, :].astype(F32)
+            rights.append(with_parts(features, 0.0, 0).T.astype(BF16))
+            turned.append(ref[sub + 64 : sub + 128, :])
             right_ref[at : at + 512, :] = rights[-1]
             vectors_ref[:, at : at + 512] = turned[-1]
             at += 512
@@ -196,7 +184,7 @@
 def add_tiles(amp, left, ready, raws, before=None, narrow=False, weight=1024):
     count = left.shape[0]
     flat = [part for pair in ready for part in pair]
-    total = sum(raw.shape[0] - start for raw, start in raws)
+    total = sum(4 * raw.shape[0] - 512 * start for raw, start in raws)
     cols = total + sum(right.shape[0] for right, _ in ready)
     per = 1024 // TM
     old = [] if before is None else [before]
@@ -259,14 +247,14 @@
         sum_specs = [acc_spec]
     made = []
     if raws:
-        made = [jax.ShapeDtypeStruct((total, 256), BF16), jax.ShapeDtypeStruct((64, total), BF16)]
+        made = [jax.ShapeDtypeStruct((total, 128), BF16), jax.ShapeDtypeStruct((64, total), BF16)]
     out = pl.pallas_call(
         body,
         grid=(count * per,),
         out_shape=sum_shapes + made,
         in_specs=[
             pl.BlockSpec(memory_space=pltpu.SMEM),
-            pl.BlockSpec((1, TM, 256), lambda i: (i // per, i % per, 0)),
+            pl.BlockSpec((1, 128, TM), lambda i: (i // per, 0, i % per)),
         ]
         + [whole(part) for part in flat]
         + [whole(raw) for raw, _ in raws]
@@ -304,21 +292,23 @@
     merged = jnp.concatenate([share] + near, axis=0)
     far = shift(merged, "zh", 1)
     merged_beside = shift(merged, "c", 1)
-    own, ready1 = add_tiles(amp, own_left, [], [(merged, 512)], own, weight=64)
+    own, ready1 = add_tiles(amp, own_left, [], [(merged, 1)], own, weight=64)
 
     theirs, own = lax.optimization_barrier((theirs, own))
     left = ready_rows(amp, mines, theirs)
-    acc, ready2 = add_tiles(amp, left, [ready0, ready1], [(merged_beside, 512)])
+    acc, ready2 = add_tiles(amp, left, [ready0, ready1], [(merged_beside, 1)])
     far, acc = lax.optimization_barrier((far, acc))
     far_beside = shift(far, "c", 1)
     acc, ready3 = add_tiles(amp, left, [], [(far, 0)], acc)
     sent, ready4 = add_tiles(amp, left, [], [(far_beside, 0)], acc, narrow=True)
     arrived = [shift(part, "x", by) for part, by in zip(sent, (2, -1, 1))]
     own, _ = add_tiles(amp, own_left, [ready2, ready3, ready4], [], own)
-    own = own[0]
+    mine, theirs = own[0, :32], own[0, 32:]
     for part in arrived:
-        own = own + part.astype(F32)
-    result = own[:32] + shift(own[32:], "zl", 1)
+        theirs = theirs + part[32:].astype(F32)
+    for part in arrived:
+        mine = mine + part[:32].astype(F32)
+    result = mine + shift(theirs, "zl", 1)
     return result.T + noise[0] * vectors.astype(F32)
 
 

time: 79 us -> 75.3 us (0.953)
  Pallas kernels: 45.8 us -> 42 us
    pallas_call x6, Pallas kernels: 42.3 us -> 39.7 us  [add_tiles(): pl.pallas_call(body, grid=(count * per,), out_shape=sum_shapes + made, in...]
    pallas_call x2, Pallas kernels: 2.51 us -> 1.25 us  [the longest x1 0.66 us: ready_rows(): pl.pallas_call(body, out_shape=jax.ShapeDtypeStruct((count, 128, 1024), B...]
  transfers between devices with their start and end apart: 16 -> 16, of which waited for: 5 -> 5; matrix products, arithmetic and copies ran while one was open for 0% -> 0% of each run, Pallas kernels for 47% -> 44%
where the time goes in v10:
time: 75.3 us; the launch traced here: 75.2 us
  Pallas kernels  42 us (56%)
  starting transfers between devices  22.8 us (30%)
  waiting for transfers between devices  7.96 us (11%)
  between operations  1.55 us (2%)
  other arithmetic  0.81 us (1%)
    pallas_call x6, Pallas kernels, add_tiles(): pl.pallas_call(body, grid=(count * per,), out_shape=sum_shapes + made, in...  39.7 us
    ppermute x16, starting transfers between devices, shift(): lax.ppermute(value, axis, [(i, (i + by) % size) for i in range(size)])  22.8 us
    ppermute x16, waiting for transfers between devices, shift(): lax.ppermute(value, axis, [(i, (i + by) % size) for i in range(size)])  7.96 us
  transfers between devices with their start and end apart: 16, of which 5 were waited for; matrix products, arithmetic and copies ran while one was open for 0% of the time, Pallas kernels for 44%

profile of v10, /device:TPU:0, one launch (start us, length us, event | category | flops | bytes accessed | tf_op | source)
XLA Modules:
  0.0 75.2 jit_solution(7143999804356543950)
XLA Ops:
  0.0 1.0 %first_pack.1 = (bf16[96,512]{1,0:T(8,128)(2,1)S(1)}, bf16[32,512]{1,0:T(8,128)(2,1)S(1)}) custom-call(s32[1]{0:T(128)} %bitcast.zl_ref, bf16[32,1024]{1,0:T(8,128)(2,1)} %bitcast.33, bf16[32,1024]{1,0:T(8,128)(2,1)} %bitcast.32, f32[1,64]{1,0:T(1,128)} %bitcast.34), custom_call_target="tpu_custom_call" | custom-call | tf_op jit(solution)/shard_map/first_pack/pallas_call | solution.py:91
  1.0 2.1 %collective-permute-start = (bf16[96,512]{1,0:T(8,128)(2,1)S(1)}, bf16[96,512]{1,0:T(8,128)(2,1)S(1)}, u32[]{:S(2)}, u32[]{:S(2)}) collective-permute-start(bf16[96,512]{1,0:T(8,128)(2,1)S(1)} %get-tuple-element.37.refs_0_), channel_id=1, source_target_pairs={{0,1},{1,0},{2,3},{3,2},{4,5},{5,4},{6,7},{7,6},{8,9},{9,8},{10,11... | collective-permute-start | bytes 294920 | tf_op jit(solution)/shard_map/ppermute | solution.py:272
  3.1 3.0 %collective-permute-start.1 = (bf16[64,512]{1,0:T(8,128)(2,1)S(1)}, bf16[64,512]{1,0:T(8,128)(2,1)S(1)}, u32[]{:S(2)}, u32[]{:S(2)}) collective-permute-start(bf16[64,512]{1,0:T(8,128)(2,1)S(1)} %copy_of.2.half_ref), channel_id=1, source_target_pairs={{0,32},{16,48},{32,0},{48,16},{1,33},{17,49},{33,1},{49,17},{2,34}... | collective-permute-start | bytes 196616 | tf_op jit(solution)/shard_map/ppermute | solution.py:272
  6.1 0.6 collective-permute-start.2
  6.7 2.6 %collective-permute-start.3 = (bf16[64,512]{1,0:T(8,128)(2,1)S(1)}, bf16[64,512]{1,0:T(8,128)(2,1)S(1)}, u32[]{:S(2)}, u32[]{:S(2)}) collective-permute-start(bf16[64,512]{1,0:T(8,128)(2,1)S(1)} %copy_of.2.half_ref), channel_id=1, source_target_pairs={{0,48},{16,0},{32,16},{48,32},{1,49},{17,1},{33,17},{49,33},{2,50}... | collective-permute-start | bytes 196616 | tf_op jit(solution)/shard_map/ppermute | solution.py:272
  10.1 0.1 pad_maximum_fusion.amp_ref
  10.1 0.6 second_pack.1
  10.7 0.1 collective-permute-start.4
  10.8 3.3 %collective-permute-start.6 = (bf16[128,512]{1,0:T(8,128)(2,1)S(1)}, bf16[128,512]{1,0:T(8,128)(2,1)S(1)}, u32[]{:S(2)}, u32[]{:S(2)}) collective-permute-start(bf16[128,512]{1,0:T(8,128)(2,1)S(1)} %get-tuple-element.39.token_ref.refs_0_), channel_id=1, source_target_pairs={{0,8},{4,12},{8,0},{12,4},{1,9},{5,13},{9,1},{13,5},{2,10},{6,14},... | collective-permute-start | bytes 393224 | tf_op jit(solution)/shard_map/ppermute | solution.py:272
  14.1 0.7 collective-permute-start.7
  14.8 2.6 %collective-permute-start.8 = (bf16[128,512]{1,0:T(8,128)(2,1)S(1)}, bf16[128,512]{1,0:T(8,128)(2,1)S(1)}, u32[]{:S(2)}, u32[]{:S(2)}) collective-permute-start(bf16[128,512]{1,0:T(8,128)(2,1)S(1)} %get-tuple-element.39.token_ref.refs_0_), channel_id=1, source_target_pairs={{0,12},{4,0},{8,4},{12,8},{1,13},{5,1},{9,5},{13,9},{2,14},{6,2},{... | collective-permute-start | bytes 393224 | tf_op jit(solution)/shard_map/ppermute | solution.py:272
  17.4 2.0 %add_tiles.6 = (f32[1,64,1024]{2,1,0:T(8,128)S(1)}, bf16[1024,128]{1,0:T(8,128)(2,1)S(1)}, bf16[64,1024]{1,0:T(8,128)(2,1)S(1)}) custom-call(f32[2]{0:T(128)S(1)} %pad_maximum_fusion.amp_ref, bf16[1,128,1024]{2,1,0:T(8,128)(2,1)S(1)} %get-tuple-element.38.left_ref, bf16[128,512]{1,0:T(8,128)(2,1)S(1)} %get-tuple-element.39.token_ref.refs_0_, ...), custom_call_target="tpu_custom_call" | custom-call | flops 2147483648 | bytes 393216 | tf_op jit(solution)/shard_map/add_tiles/pallas_call | solution.py:251
  19.4 1.8 %collective-permute-done.7 = bf16[128,512]{1,0:T(8,128)(2,1)S(1)} collective-permute-done((bf16[128,512]{1,0:T(8,128)(2,1)S(1)}, bf16[128,512]{1,0:T(8,128)(2,1)S(1)}, u32[]{:S(2)}, u32[]{:S(2)}) %collective-permute-start.7) | collective-permute-done | bytes 131104 | tf_op jit(solution)/shard_map/ppermute | solution.py:272
  21.2 0.2 collective-permute-done.8
  21.5 0.1 collective-permute-start.9
  21.5 0.2 collective-permute-start.5
  21.7 3.9 %collective-permute-start.10 = (bf16[512,512]{1,0:T(8,128)(2,1)S(1)}, bf16[512,512]{1,0:T(8,128)(2,1)S(1)}, u32[]{:S(2)}, u32[]{:S(2)}) collective-permute-start(bf16[512,512]{1,0:T(8,128)(2,1)S(1)} %constant_dynamic-update-slice_fusion.refs_0_), channel_id=1, source_target_pairs={{0,64},{64,0},{1,65},{65,1},{2,66},{66,2},{3,67},{67,3},{4,68},{68... | collective-permute-start | bytes 1572872 | tf_op jit(solution)/shard_map/ppermute | solution.py:272
  25.6 2.6 %add_tiles.7 = (f32[1,64,1024]{2,1,0:T(8,128)S(1)}, bf16[1536,128]{1,0:T(8,128)(2,1)S(1)}, bf16[64,1536]{1,0:T(8,128)(2,1)S(1)}) custom-call(f32[2]{0:T(128)S(1)} %pad_maximum_fusion.amp_ref, bf16[1,128,1024]{2,1,0:T(8,128)(2,1)S(1)} %get-tuple-element.38.left_ref, bf16[512,512]{1,0:T(8,128)(2,1)S(1)} %constant_dynamic-update-slice_fusion.refs_0_, ...), custom_call_target="tpu_custom_call" | custom-call | flops 50331648 | bytes 589824 | tf_op jit(solution)/shard_map/add_tiles/pallas_call | solution.py:251
  28.2 1.1 %collective-permute-done.5.refs_3_ = bf16[192,512]{1,0:T(8,128)(2,1)S(1)} collective-permute-done((bf16[192,512]{1,0:T(8,128)(2,1)S(1)}, bf16[192,512]{1,0:T(8,128)(2,1)S(1)}, u32[]{:S(2)}, u32[]{:S(2)}) %collective-permute-start.5) | collective-permute-done | bytes 196640 | tf_op jit(solution)/shard_map/ppermute | solution.py:272
  29.3 0.7 ready_rows.1.left_ref
  30.0 13.8 %add_tiles.8 = (f32[3,64,1024]{2,1,0:T(8,128)S(1)}, bf16[1536,128]{1,0:T(8,128)(2,1)S(1)}, bf16[64,1536]{1,0:T(8,128)(2,1)S(1)}) custom-call(f32[2]{0:T(128)S(1)} %pad_maximum_fusion.amp_ref, bf16[3,128,1024]{2,1,0:T(8,128)(2,1)S(1)} %ready_rows.1.left_ref, bf16[1024,128]{1,0:T(8,128)(2,1)S(1)} %get-tuple-element.49.refs_0_, ...), custom_call_target="tpu_custom_call" | custom-call | flops 6442450944 | bytes 1572864 | tf_op jit(solution)/shard_map/add_tiles/pallas_call | solution.py:251
  43.8 0.3 collective-permute-start.11
  44.1 7.5 %add_tiles.9 = (f32[3,64,1024]{2,1,0:T(8,128)S(1)}, bf16[2048,128]{1,0:T(8,128)(2,1)S(1)}, bf16[64,2048]{1,0:T(8,128)(2,1)S(1)}) custom-call(f32[2]{0:T(128)S(1)} %pad_maximum_fusion.amp_ref, bf16[3,128,1024]{2,1,0:T(8,128)(2,1)S(1)} %ready_rows.1.left_ref, bf16[512,512]{1,0:T(8,128)(2,1)S(1)} %collective-permute-done.10.refs_0_, ...), custom_call_target="tpu_custom_call" | custom-call | flops 3221225472 | bytes 786432 | tf_op jit(solution)/shard_map/add_tiles/pallas_call | solution.py:251
  51.6 7.7 %add_tiles.10 = (bf16[64,1024]{1,0:T(8,128)(2,1)S(1)}, bf16[64,1024]{1,0:T(8,128)(2,1)S(1)}, bf16[64,1024]{1,0:T(8,128)(2,1)S(1)}, bf16[2048,128]{1,0:T(8,128)(2,1)S(1)}, bf16[64,2048]{1,0:T(8,128)(2,1)S(1)}) custom-call(f32[2]{0:T(128)S(1)} %pad_maximum_fusion.amp_ref, bf16[3,128,1024]{2,1,0:T(8,128)(2,1)S(1)} %ready_rows.1.left_ref, ...), custom_call_target="tpu_custom_call" | custom-call | flops 3221225472 | bytes 786432 | tf_op jit(solution)/shard_map/add_tiles/pallas_call | solution.py:251
  59.3 0.1 collective-permute-start.14
  59.3 3.2 %collective-permute-start.13 = (bf16[64,1024]{1,0:T(8,128)(2,1)S(1)}, bf16[64,1024]{1,0:T(8,128)(2,1)S(1)}, u32[]{:S(2)}, u32[]{:S(2)}) collective-permute-start(bf16[64,1024]{1,0:T(8,128)(2,1)S(1)} %get-tuple-element.65), channel_id=1, source_target_pairs={{0,48},{16,0},{32,16},{48,32},{1,49},{17,1},{33,17},{49,33},{2,50}... | collective-permute-start | bytes 393224 | tf_op jit(solution)/shard_map/ppermute | solution.py:272
  62.6 6.2 %add_tiles.11 = f32[1,64,1024]{2,1,0:T(8,128)S(1)} custom-call(f32[2]{0:T(128)S(1)} %pad_maximum_fusion.amp_ref, bf16[1,128,1024]{2,1,0:T(8,128)(2,1)S(1)} %get-tuple-element.38.left_ref, bf16[1536,128]{1,0:T(8,128)(2,1)S(1)} %get-tuple-element.53.refs_0_, bf16[64,1536]{1,0:T(8,128)(2,1)S(1)} %get-tuple-element.54.refs_1_, ...), custom_call_target="tpu_custom_call" | custom-call | flops 2952790016 | bytes 2162688 | tf_op jit(solution)/shard_map/add_tiles/pallas_call | solution.py:251
  68.7 0.0 copy-start
  68.8 0.6 collective-permute-done.12
  69.4 0.2 collective-permute-start.15
  70.2 4.2 %collective-permute-done.15 = f32[32,1024]{1,0:T(8,128)S(1)} collective-permute-done((f32[32,1024]{1,0:T(8,128)S(1)}, f32[32,1024]{1,0:T(8,128)S(1)}, u32[]{:S(2)}, u32[]{:S(2)}) %collective-permute-start.15) | collective-permute-done | bytes 131104 | tf_op jit(solution)/shard_map/ppermute | solution.py:272
  74.5 0.7 fusion.8
  (20 shorter events, 0.1 us)
Async XLA Ops:
  1.0 9.1 %collective-permute-start = (bf16[96,512]{1,0:T(8,128)(2,1)S(1)}, bf16[96,512]{1,0:T(8,128)(2,1)S(1)}, u32[]{:S(2)}, u32[]{:S(2)}) collective-permute-start(bf16[96,512]{1,0:T(8,128)(2,1)S(1)} %get-tuple-element.37.refs_0_), channel_id=1, source_target_pairs={{0,1},{1,0},{2,3},{3,2},{4,5},{5,4},{6,7},{7,6},{8,9},{9,8},{10,11... | collective-permute-start | bytes 294920 | tf_op jit(solution)/shard_map/ppermute | solution.py:272
  3.1 11.0 %collective-permute-start.1 = (bf16[64,512]{1,0:T(8,128)(2,1)S(1)}, bf16[64,512]{1,0:T(8,128)(2,1)S(1)}, u32[]{:S(2)}, u32[]{:S(2)}) collective-permute-start(bf16[64,512]{1,0:T(8,128)(2,1)S(1)} %copy_of.2.half_ref), channel_id=1, source_target_pairs={{0,32},{16,48},{32,0},{48,16},{1,33},{17,49},{33,1},{49,17},{2,34}... | collective-permute-start | bytes 196616 | tf_op jit(solution)/shard_map/ppermute | solution.py:272
  6.1 8.7 %collective-permute-start.2 = (bf16[64,512]{1,0:T(8,128)(2,1)S(1)}, bf16[64,512]{1,0:T(8,128)(2,1)S(1)}, u32[]{:S(2)}, u32[]{:S(2)}) collective-permute-start(bf16[64,512]{1,0:T(8,128)(2,1)S(1)} %copy_of.2.half_ref), channel_id=1, source_target_pairs={{0,16},{16,32},{32,48},{48,0},{1,17},{17,33},{33,49},{49,1},{2,18}... | collective-permute-start | bytes 196616 | tf_op jit(solution)/shard_map/ppermute | solution.py:272
  6.7 10.6 %collective-permute-start.3 = (bf16[64,512]{1,0:T(8,128)(2,1)S(1)}, bf16[64,512]{1,0:T(8,128)(2,1)S(1)}, u32[]{:S(2)}, u32[]{:S(2)}) collective-permute-start(bf16[64,512]{1,0:T(8,128)(2,1)S(1)} %copy_of.2.half_ref), channel_id=1, source_target_pairs={{0,48},{16,0},{32,16},{48,32},{1,49},{17,1},{33,17},{49,33},{2,50}... | collective-permute-start | bytes 196616 | tf_op jit(solution)/shard_map/ppermute | solution.py:272
  10.7 6.7 %collective-permute-start.4 = (bf16[128,512]{1,0:T(8,128)(2,1)S(1)}, bf16[128,512]{1,0:T(8,128)(2,1)S(1)}, u32[]{:S(2)}, u32[]{:S(2)}) collective-permute-start(bf16[128,512]{1,0:T(8,128)(2,1)S(1)} %get-tuple-element.39.token_ref.refs_0_), channel_id=1, source_target_pairs={{0,2},{2,0},{1,3},{3,1},{4,6},{6,4},{5,7},{7,5},{8,10},{10,8},{9,1... | collective-permute-start | bytes 393224 | tf_op jit(solution)/shard_map/ppermute | solution.py:272
  10.8 8.6 %collective-permute-start.6 = (bf16[128,512]{1,0:T(8,128)(2,1)S(1)}, bf16[128,512]{1,0:T(8,128)(2,1)S(1)}, u32[]{:S(2)}, u32[]{:S(2)}) collective-permute-start(bf16[128,512]{1,0:T(8,128)(2,1)S(1)} %get-tuple-element.39.token_ref.refs_0_), channel_id=1, source_target_pairs={{0,8},{4,12},{8,0},{12,4},{1,9},{5,13},{9,1},{13,5},{2,10},{6,14},... | collective-permute-start | bytes 393224 | tf_op jit(solution)/shard_map/ppermute | solution.py:272
  14.1 7.1 %collective-permute-start.7 = (bf16[128,512]{1,0:T(8,128)(2,1)S(1)}, bf16[128,512]{1,0:T(8,128)(2,1)S(1)}, u32[]{:S(2)}, u32[]{:S(2)}) collective-permute-start(bf16[128,512]{1,0:T(8,128)(2,1)S(1)} %get-tuple-element.39.token_ref.refs_0_), channel_id=1, source_target_pairs={{0,4},{4,8},{8,12},{12,0},{1,5},{5,9},{9,13},{13,1},{2,6},{6,10},{... | collective-permute-start | bytes 393224 | tf_op jit(solution)/shard_map/ppermute | solution.py:272
  14.8 6.6 %collective-permute-start.8 = (bf16[128,512]{1,0:T(8,128)(2,1)S(1)}, bf16[128,512]{1,0:T(8,128)(2,1)S(1)}, u32[]{:S(2)}, u32[]{:S(2)}) collective-permute-start(bf16[128,512]{1,0:T(8,128)(2,1)S(1)} %get-tuple-element.39.token_ref.refs_0_), channel_id=1, source_target_pairs={{0,12},{4,0},{8,4},{12,8},{1,13},{5,1},{9,5},{13,9},{2,14},{6,2},{... | collective-permute-start | bytes 393224 | tf_op jit(solution)/shard_map/ppermute | solution.py:272
  21.5 8.5 %collective-permute-start.9 = (bf16[512,512]{1,0:T(8,128)(2,1)S(1)}, bf16[512,512]{1,0:T(8,128)(2,1)S(1)}, u32[]{:S(2)}, u32[]{:S(2)}) collective-permute-start(bf16[512,512]{1,0:T(8,128)(2,1)S(1)} %constant_dynamic-update-slice_fusion.refs_0_), channel_id=1, source_target_pairs={{0,2},{2,0},{1,3},{3,1},{4,6},{6,4},{5,7},{7,5},{8,10},{10,8},{9,1... | collective-permute-start | bytes 1572872 | tf_op jit(solution)/shard_map/ppermute | solution.py:272
  21.5 7.8 %collective-permute-start.5 = (bf16[192,512]{1,0:T(8,128)(2,1)S(1)}, bf16[192,512]{1,0:T(8,128)(2,1)S(1)}, u32[]{:S(2)}, u32[]{:S(2)}) collective-permute-start(bf16[192,512]{1,0:T(8,128)(2,1)S(1)} %copy_of.3), channel_id=1, source_target_pairs={{0,1},{1,0},{2,3},{3,2},{4,5},{5,4},{6,7},{7,6},{8,9},{9,8},{10,11... | collective-permute-start | bytes 589832 | tf_op jit(solution)/shard_map/ppermute | solution.py:272
  21.7 22.1 %collective-permute-start.10 = (bf16[512,512]{1,0:T(8,128)(2,1)S(1)}, bf16[512,512]{1,0:T(8,128)(2,1)S(1)}, u32[]{:S(2)}, u32[]{:S(2)}) collective-permute-start(bf16[512,512]{1,0:T(8,128)(2,1)S(1)} %constant_dynamic-update-slice_fusion.refs_0_), channel_id=1, source_target_pairs={{0,64},{64,0},{1,65},{65,1},{2,66},{66,2},{3,67},{67,3},{4,68},{68... | collective-permute-start | bytes 1572872 | tf_op jit(solution)/shard_map/ppermute | solution.py:272
  43.8 7.8 %collective-permute-start.11 = (bf16[512,512]{1,0:T(8,128)(2,1)S(1)}, bf16[512,512]{1,0:T(8,128)(2,1)S(1)}, u32[]{:S(2)}, u32[]{:S(2)}) collective-permute-start(bf16[512,512]{1,0:T(8,128)(2,1)S(1)} %collective-permute-done.10.refs_0_), channel_id=1, source_target_pairs={{0,2},{2,0},{1,3},{3,1},{4,6},{6,4},{5,7},{7,5},{8,10},{10,8},{9,1... | collective-permute-start | bytes 1572872 | tf_op jit(solution)/shard_map/ppermute | solution.py:272
  59.3 9.5 %collective-permute-start.14 = (bf16[64,1024]{1,0:T(8,128)(2,1)S(1)}, bf16[64,1024]{1,0:T(8,128)(2,1)S(1)}, u32[]{:S(2)}, u32[]{:S(2)}) collective-permute-start(bf16[64,1024]{1,0:T(8,128)(2,1)S(1)} %get-tuple-element.66), channel_id=1, source_target_pairs={{0,16},{16,32},{32,48},{48,0},{1,17},{17,33},{33,49},{49,1},{2,18}... | collective-permute-start | bytes 393224 | tf_op jit(solution)/shard_map/ppermute | solution.py:272
  59.3 9.4 %collective-permute-start.13 = (bf16[64,1024]{1,0:T(8,128)(2,1)S(1)}, bf16[64,1024]{1,0:T(8,128)(2,1)S(1)}, u32[]{:S(2)}, u32[]{:S(2)}) collective-permute-start(bf16[64,1024]{1,0:T(8,128)(2,1)S(1)} %get-tuple-element.65), channel_id=1, source_target_pairs={{0,48},{16,0},{32,16},{48,32},{1,49},{17,1},{33,17},{49,33},{2,50}... | collective-permute-start | bytes 393224 | tf_op jit(solution)/shard_map/ppermute | solution.py:272
  62.6 6.8 %collective-permute-start.12 = (bf16[64,1024]{1,0:T(8,128)(2,1)S(1)}, bf16[64,1024]{1,0:T(8,128)(2,1)S(1)}, u32[]{:S(2)}, u32[]{:S(2)}) collective-permute-start(bf16[64,1024]{1,0:T(8,128)(2,1)S(1)} %get-tuple-element.64), channel_id=1, source_target_pairs={{0,32},{16,48},{32,0},{48,16},{1,33},{17,49},{33,1},{49,17},{2,34}... | collective-permute-start | bytes 393224 | tf_op jit(solution)/shard_map/ppermute | solution.py:272
  68.7 5.7 %copy-start = (bf16[1024,32]{0,1:T(8,128)(2,1)S(1)}, bf16[1024,32]{0,1:T(8,128)(2,1)}, u32[]{:S(2)}) copy-start(bf16[1024,32]{0,1:T(8,128)(2,1)} %param.6) | copy-start | bytes 196612
  69.4 5.0 %collective-permute-start.15 = (f32[32,1024]{1,0:T(8,128)S(1)}, f32[32,1024]{1,0:T(8,128)S(1)}, u32[]{:S(2)}, u32[]{:S(2)}) collective-permute-start(f32[32,1024]{1,0:T(8,128)S(1)} %fusion.2), channel_id=1, source_target_pairs={{0,1},{1,0},{2,3},{3,2},{4,5},{5,4},{6,7},{7,6},{8,9},{9,8},{10,11... | collective-permute-start | bytes 393224 | tf_op jit(solution)/shard_map/ppermute | solution.py:272

commit v11 on v10

--- a/solution.py
+++ b/solution.py
@@ -151,19 +151,20 @@
     return jnp.dot(vectors, block, preferred_element_type=F32)
 
 
-def ready_sum(left, pairs, top):
-    result = jnp.zeros((64, left.shape[1]), F32)
+def ready_sum(lefts, pairs, top):
+    sums = [jnp.zeros((64, TM), F32) for _ in lefts]
     for right_ref, vectors_ref in pairs:
         total = right_ref.shape[0]
         for at in range(0, total, TN):
             part = slice(at, min(at + TN, total))
-            result += one_block(left, right_ref[part, :], vectors_ref[:, part], top)
-    return result
-
-
-def raw_sum(left, raws, right_ref, vectors_ref, top):
+            for k, left in enumerate(lefts):
+                sums[k] += one_block(left, right_ref[part, :], vectors_ref[:, part], top)
+    return sums
+
+
+def raw_sum(lefts, raws, right_ref, vectors_ref, top):
     total = right_ref.shape[0]
-    result = jnp.zeros((64, left.shape[1]), F32)
+    sums = [jnp.zeros((64, TM), F32) for _ in lefts]
     at = 0
     rights, turned = [], []
     for ref, start in raws:
@@ -176,9 +177,11 @@
             at += 512
             if len(rights) * 512 == TN or at == total:
                 right = jnp.concatenate(rights, axis=0)
-                result += one_block(left, right, jnp.concatenate(turned, axis=1), top)
+                vectors = jnp.concatenate(turned, axis=1)
+                for k, left in enumerate(lefts):
+                    sums[k] += one_block(left, right, vectors, top)
                 rights, turned = [], []
-    return result
+    return sums
 
 
 def add_tiles(amp, left, ready, raws, before=None, narrow=False, weight=1024):
@@ -186,7 +189,6 @@
     flat = [part for pair in ready for part in pair]
     total = sum(4 * raw.shape[0] - 512 * start for raw, start in raws)
     cols = total + sum(right.shape[0] for right, _ in ready)
-    per = 1024 // TM
     old = [] if before is None else [before]
     sums = count if narrow else 1
     ends = [len(flat), len(raws), len(old), sums]
@@ -209,16 +211,17 @@
                 return
             for k in range(count):
 
-                @pl.when(step // per == k)
+                @pl.when(step == k)
                 def _():
                     sum_refs[k][...] = value.astype(BF16)
 
         def tiles(fresh):
-            value = ready_sum(left_ref[0], pairs if fresh or not raws else pairs + [tuple(refs)], top)
+            lefts = [left_ref[0, :, at : at + TM] for at in range(0, 1024, TM)]
+            sums = ready_sum(lefts, pairs if fresh or not raws else pairs + [tuple(refs)], top)
             if fresh:
                 starts = [(ref, start) for ref, (_, start) in zip(raw_refs, raws)]
-                value += raw_sum(left_ref[0], starts, *refs, top)
-            put(value)
+                sums = [a + b for a, b in zip(sums, raw_sum(lefts, starts, *refs, top))]
+            put(jnp.concatenate(sums, axis=1))
 
         if not raws:
             tiles(False)
@@ -232,16 +235,14 @@
         def _():
             tiles(False)
 
-    def place(k):
-        return pl.BlockSpec((64, TM), lambda i: (0, jnp.clip(i - k * per, 0, per - 1)))
 
     def whole(array):
         return pl.BlockSpec(array.shape, lambda i: (0, 0))
 
-    acc_spec = pl.BlockSpec((1, 64, TM), lambda i: (i // per, 0, i % per))
+    acc_spec = pl.BlockSpec((1, 64, 1024), lambda i: (i, 0, 0))
     if narrow:
         sum_shapes = [jax.ShapeDtypeStruct((64, 1024), BF16)] * count
-        sum_specs = [place(k) for k in range(count)]
+        sum_specs = [whole(part) for part in sum_shapes]
     else:
         sum_shapes = [jax.ShapeDtypeStruct((count, 64, 1024), F32)]
         sum_specs = [acc_spec]
@@ -250,11 +251,11 @@
         made = [jax.ShapeDtypeStruct((total, 128), BF16), jax.ShapeDtypeStruct((64, total), BF16)]
     out = pl.pallas_call(
         body,
-        grid=(count * per,),
+        grid=(count,),
         out_shape=sum_shapes + made,
         in_specs=[
             pl.BlockSpec(memory_space=pltpu.SMEM),
-            pl.BlockSpec((1, 128, TM), lambda i: (i // per, 0, i % per)),
+            pl.BlockSpec((1, 128, 1024), lambda i: (i, 0, 0)),
         ]
         + [whole(part) for part in flat]
         + [whole(raw) for raw, _ in raws]
@@ -279,7 +280,7 @@
     given, kept = first_pack(zl, points.T, vectors.T, lengthscale)
     got = shift(given, "zl", 1)
     half = copy_of([given], 64, kept, 4096)
-    mines = [shift(half, "x", by) for by in (2, 1, -1)]
+    mines = [shift(half, "x", by) for by in (1, -1, 2)]
     own_left, share = second_pack(zl, amp, half, got, kept)
 
     beside = shift(share, "c", 1)
@@ -301,7 +302,7 @@
     far_beside = shift(far, "c", 1)
     acc, ready3 = add_tiles(amp, left, [], [(far, 0)], acc)
     sent, ready4 = add_tiles(amp, left, [], [(far_beside, 0)], acc, narrow=True)
-    arrived = [shift(part, "x", by) for part, by in zip(sent, (2, -1, 1))]
+    arrived = [shift(sent[k], "x", by) for k, by in ((2, 2), (0, -1), (1, 1))]
     own, _ = add_tiles(amp, own_left, [ready2, ready3, ready4], [], own)
     mine, theirs = own[0, :32], own[0, 32:]
     for part in arrived:

time: 75.3 us -> 71.6 us (0.951)
  Pallas kernels: 42 us -> 38.5 us
    pallas_call x6, Pallas kernels: 39.7 us -> 36.2 us  [add_tiles(): pl.pallas_call(body, grid=(count,), out_shape=sum_shapes + made, in_specs...]
  transfers between devices with their start and end apart: 16 -> 16, of which waited for: 5 -> 5; matrix products, arithmetic and copies ran while one was open for 0% -> 0% of each run, Pallas kernels for 44% -> 43%
where the time goes in v11:
time: 71.6 us; the launch traced here: 71.4 us
  Pallas kernels  38.5 us (54%)
  starting transfers between devices  22.1 us (31%)
  waiting for transfers between devices  8.38 us (12%)
  between operations  1.52 us (2%)
  other arithmetic  0.81 us (1%)
    pallas_call x6, Pallas kernels, add_tiles(): pl.pallas_call(body, grid=(count,), out_shape=sum_shapes + made, in_specs...  36.2 us
    ppermute x16, starting transfers between devices, shift(): lax.ppermute(value, axis, [(i, (i + by) % size) for i in range(size)])  22.1 us
    ppermute x16, waiting for transfers between devices, shift(): lax.ppermute(value, axis, [(i, (i + by) % size) for i in range(size)])  8.38 us
  transfers between devices with their start and end apart: 16, of which 5 were waited for; matrix products, arithmetic and copies ran while one was open for 0% of the time, Pallas kernels for 43%

profile of v11, /device:TPU:0, one launch (start us, length us, event | category | flops | bytes accessed | tf_op | source)
XLA Modules:
  0.0 71.4 jit_solution(6219811098089496947)
XLA Ops:
  0.0 1.0 %first_pack.1 = (bf16[96,512]{1,0:T(8,128)(2,1)S(1)}, bf16[32,512]{1,0:T(8,128)(2,1)S(1)}) custom-call(s32[1]{0:T(128)} %bitcast.zl_ref, bf16[32,1024]{1,0:T(8,128)(2,1)} %bitcast.33, bf16[32,1024]{1,0:T(8,128)(2,1)} %bitcast.32, f32[1,64]{1,0:T(1,128)} %bitcast.34), custom_call_target="tpu_custom_call" | custom-call | tf_op jit(solution)/shard_map/first_pack/pallas_call | solution.py:91
  1.0 2.1 %collective-permute-start = (bf16[96,512]{1,0:T(8,128)(2,1)S(1)}, bf16[96,512]{1,0:T(8,128)(2,1)S(1)}, u32[]{:S(2)}, u32[]{:S(2)}) collective-permute-start(bf16[96,512]{1,0:T(8,128)(2,1)S(1)} %get-tuple-element.37.refs_0_), channel_id=1, source_target_pairs={{0,1},{1,0},{2,3},{3,2},{4,5},{5,4},{6,7},{7,6},{8,9},{9,8},{10,11... | collective-permute-start | bytes 294920 | tf_op jit(solution)/shard_map/ppermute | solution.py:273
  3.1 1.5 %collective-permute-start.1 = (bf16[64,512]{1,0:T(8,128)(2,1)S(1)}, bf16[64,512]{1,0:T(8,128)(2,1)S(1)}, u32[]{:S(2)}, u32[]{:S(2)}) collective-permute-start(bf16[64,512]{1,0:T(8,128)(2,1)S(1)} %copy_of.2.half_ref), channel_id=1, source_target_pairs={{0,16},{16,32},{32,48},{48,0},{1,17},{17,33},{33,49},{49,1},{2,18}... | collective-permute-start | bytes 196616 | tf_op jit(solution)/shard_map/ppermute | solution.py:273
  4.6 1.7 %collective-permute-start.2 = (bf16[64,512]{1,0:T(8,128)(2,1)S(1)}, bf16[64,512]{1,0:T(8,128)(2,1)S(1)}, u32[]{:S(2)}, u32[]{:S(2)}) collective-permute-start(bf16[64,512]{1,0:T(8,128)(2,1)S(1)} %copy_of.2.half_ref), channel_id=1, source_target_pairs={{0,48},{16,0},{32,16},{48,32},{1,49},{17,1},{33,17},{49,33},{2,50}... | collective-permute-start | bytes 196616 | tf_op jit(solution)/shard_map/ppermute | solution.py:273
  6.3 1.8 %collective-permute-start.3 = (bf16[64,512]{1,0:T(8,128)(2,1)S(1)}, bf16[64,512]{1,0:T(8,128)(2,1)S(1)}, u32[]{:S(2)}, u32[]{:S(2)}) collective-permute-start(bf16[64,512]{1,0:T(8,128)(2,1)S(1)} %copy_of.2.half_ref), channel_id=1, source_target_pairs={{0,32},{16,48},{32,0},{48,16},{1,33},{17,49},{33,1},{49,17},{2,34}... | collective-permute-start | bytes 196616 | tf_op jit(solution)/shard_map/ppermute | solution.py:273
  8.9 0.1 pad_maximum_fusion.amp_ref
  8.9 0.6 second_pack.1
  9.5 0.1 collective-permute-start.4
  9.6 3.3 %collective-permute-start.6 = (bf16[128,512]{1,0:T(8,128)(2,1)S(1)}, bf16[128,512]{1,0:T(8,128)(2,1)S(1)}, u32[]{:S(2)}, u32[]{:S(2)}) collective-permute-start(bf16[128,512]{1,0:T(8,128)(2,1)S(1)} %get-tuple-element.39.token_ref.refs_0_), channel_id=1, source_target_pairs={{0,8},{4,12},{8,0},{12,4},{1,9},{5,13},{9,1},{13,5},{2,10},{6,14},... | collective-permute-start | bytes 393224 | tf_op jit(solution)/shard_map/ppermute | solution.py:273
  12.9 0.7 collective-permute-start.7
  13.6 2.6 %collective-permute-start.8 = (bf16[128,512]{1,0:T(8,128)(2,1)S(1)}, bf16[128,512]{1,0:T(8,128)(2,1)S(1)}, u32[]{:S(2)}, u32[]{:S(2)}) collective-permute-start(bf16[128,512]{1,0:T(8,128)(2,1)S(1)} %get-tuple-element.39.token_ref.refs_0_), channel_id=1, source_target_pairs={{0,12},{4,0},{8,4},{12,8},{1,13},{5,1},{9,5},{13,9},{2,14},{6,2},{... | collective-permute-start | bytes 393224 | tf_op jit(solution)/shard_map/ppermute | solution.py:273
  16.2 1.7 %add_tiles.6 = (f32[1,64,1024]{2,1,0:T(8,128)S(1)}, bf16[1024,128]{1,0:T(8,128)(2,1)S(1)}, bf16[64,1024]{1,0:T(8,128)(2,1)S(1)}) custom-call(f32[2]{0:T(128)S(1)} %pad_maximum_fusion.amp_ref, bf16[1,128,1024]{2,1,0:T(8,128)(2,1)S(1)} %get-tuple-element.38.left_ref, bf16[128,512]{1,0:T(8,128)(2,1)S(1)} %get-tuple-element.39.token_ref.refs_0_, ...), custom_call_target="tpu_custom_call" | custom-call | flops 2147483648 | bytes 393216 | tf_op jit(solution)/shard_map/add_tiles/pallas_call | solution.py:252
  17.9 2.1 %collective-permute-done.7 = bf16[128,512]{1,0:T(8,128)(2,1)S(1)} collective-permute-done((bf16[128,512]{1,0:T(8,128)(2,1)S(1)}, bf16[128,512]{1,0:T(8,128)(2,1)S(1)}, u32[]{:S(2)}, u32[]{:S(2)}) %collective-permute-start.7) | collective-permute-done | bytes 131104 | tf_op jit(solution)/shard_map/ppermute | solution.py:273
  20.0 0.2 collective-permute-done.8
  20.2 0.1 collective-permute-start.9
  20.3 0.2 collective-permute-start.5
  20.5 3.9 %collective-permute-start.10 = (bf16[512,512]{1,0:T(8,128)(2,1)S(1)}, bf16[512,512]{1,0:T(8,128)(2,1)S(1)}, u32[]{:S(2)}, u32[]{:S(2)}) collective-permute-start(bf16[512,512]{1,0:T(8,128)(2,1)S(1)} %constant_dynamic-update-slice_fusion.refs_0_), channel_id=1, source_target_pairs={{0,64},{64,0},{1,65},{65,1},{2,66},{66,2},{3,67},{67,3},{4,68},{68... | collective-permute-start | bytes 1572872 | tf_op jit(solution)/shard_map/ppermute | solution.py:273
  24.4 2.3 %add_tiles.7 = (f32[1,64,1024]{2,1,0:T(8,128)S(1)}, bf16[1536,128]{1,0:T(8,128)(2,1)S(1)}, bf16[64,1536]{1,0:T(8,128)(2,1)S(1)}) custom-call(f32[2]{0:T(128)S(1)} %pad_maximum_fusion.amp_ref, bf16[1,128,1024]{2,1,0:T(8,128)(2,1)S(1)} %get-tuple-element.38.left_ref, bf16[512,512]{1,0:T(8,128)(2,1)S(1)} %constant_dynamic-update-slice_fusion.refs_0_, ...), custom_call_target="tpu_custom_call" | custom-call | flops 50331648 | bytes 589824 | tf_op jit(solution)/shard_map/add_tiles/pallas_call | solution.py:252
  26.7 1.4 %collective-permute-done.5.refs_3_ = bf16[192,512]{1,0:T(8,128)(2,1)S(1)} collective-permute-done((bf16[192,512]{1,0:T(8,128)(2,1)S(1)}, bf16[192,512]{1,0:T(8,128)(2,1)S(1)}, u32[]{:S(2)}, u32[]{:S(2)}) %collective-permute-start.5) | collective-permute-done | bytes 196640 | tf_op jit(solution)/shard_map/ppermute | solution.py:273
  28.1 0.7 ready_rows.1.left_ref
  28.8 13.0 %add_tiles.8 = (f32[3,64,1024]{2,1,0:T(8,128)S(1)}, bf16[1536,128]{1,0:T(8,128)(2,1)S(1)}, bf16[64,1536]{1,0:T(8,128)(2,1)S(1)}) custom-call(f32[2]{0:T(128)S(1)} %pad_maximum_fusion.amp_ref, bf16[3,128,1024]{2,1,0:T(8,128)(2,1)S(1)} %ready_rows.1.left_ref, bf16[1024,128]{1,0:T(8,128)(2,1)S(1)} %get-tuple-element.49.refs_0_, ...), custom_call_target="tpu_custom_call" | custom-call | flops 6442450944 | bytes 1572864 | tf_op jit(solution)/shard_map/add_tiles/pallas_call | solution.py:252
  41.8 0.3 collective-permute-start.11
  42.1 6.6 %add_tiles.9 = (f32[3,64,1024]{2,1,0:T(8,128)S(1)}, bf16[2048,128]{1,0:T(8,128)(2,1)S(1)}, bf16[64,2048]{1,0:T(8,128)(2,1)S(1)}) custom-call(f32[2]{0:T(128)S(1)} %pad_maximum_fusion.amp_ref, bf16[3,128,1024]{2,1,0:T(8,128)(2,1)S(1)} %ready_rows.1.left_ref, bf16[512,512]{1,0:T(8,128)(2,1)S(1)} %collective-permute-done.10.refs_0_, ...), custom_call_target="tpu_custom_call" | custom-call | flops 3221225472 | bytes 786432 | tf_op jit(solution)/shard_map/add_tiles/pallas_call | solution.py:252
  48.8 6.7 %add_tiles.10 = (bf16[64,1024]{1,0:T(8,128)(2,1)S(1)}, bf16[64,1024]{1,0:T(8,128)(2,1)S(1)}, bf16[64,1024]{1,0:T(8,128)(2,1)S(1)}, bf16[2048,128]{1,0:T(8,128)(2,1)S(1)}, bf16[64,2048]{1,0:T(8,128)(2,1)S(1)}) custom-call(f32[2]{0:T(128)S(1)} %pad_maximum_fusion.amp_ref, bf16[3,128,1024]{2,1,0:T(8,128)(2,1)S(1)} %ready_rows.1.left_ref, ...), custom_call_target="tpu_custom_call" | custom-call | flops 3221225472 | bytes 786432 | tf_op jit(solution)/shard_map/add_tiles/pallas_call | solution.py:252
  55.5 0.7 collective-permute-start.14
  56.1 2.6 %collective-permute-start.13 = (bf16[64,1024]{1,0:T(8,128)(2,1)S(1)}, bf16[64,1024]{1,0:T(8,128)(2,1)S(1)}, u32[]{:S(2)}, u32[]{:S(2)}) collective-permute-start(bf16[64,1024]{1,0:T(8,128)(2,1)S(1)} %get-tuple-element.65), channel_id=1, source_target_pairs={{0,48},{16,0},{32,16},{48,32},{1,49},{17,1},{33,17},{49,33},{2,50}... | collective-permute-start | bytes 393224 | tf_op jit(solution)/shard_map/ppermute | solution.py:273
  58.8 0.5 collective-permute-start.12
  59.3 5.9 %add_tiles.11 = f32[1,64,1024]{2,1,0:T(8,128)S(1)} custom-call(f32[2]{0:T(128)S(1)} %pad_maximum_fusion.amp_ref, bf16[1,128,1024]{2,1,0:T(8,128)(2,1)S(1)} %get-tuple-element.38.left_ref, bf16[1536,128]{1,0:T(8,128)(2,1)S(1)} %get-tuple-element.53.refs_0_, bf16[64,1536]{1,0:T(8,128)(2,1)S(1)} %get-tuple-element.54.refs_1_, ...), custom_call_target="tpu_custom_call" | custom-call | flops 2952790016 | bytes 2162688 | tf_op jit(solution)/shard_map/add_tiles/pallas_call | solution.py:252
  65.2 0.4 collective-permute-done.12
  65.6 0.2 collective-permute-start.15
  66.5 4.2 %collective-permute-done.15 = f32[32,1024]{1,0:T(8,128)S(1)} collective-permute-done((f32[32,1024]{1,0:T(8,128)S(1)}, f32[32,1024]{1,0:T(8,128)S(1)}, u32[]{:S(2)}, u32[]{:S(2)}) %collective-permute-start.15) | collective-permute-done | bytes 131104 | tf_op jit(solution)/shard_map/ppermute | solution.py:273
  70.7 0.7 fusion.8
  (20 shorter events, 0.1 us)
Async XLA Ops:
  1.0 7.9 %collective-permute-start = (bf16[96,512]{1,0:T(8,128)(2,1)S(1)}, bf16[96,512]{1,0:T(8,128)(2,1)S(1)}, u32[]{:S(2)}, u32[]{:S(2)}) collective-permute-start(bf16[96,512]{1,0:T(8,128)(2,1)S(1)} %get-tuple-element.37.refs_0_), channel_id=1, source_target_pairs={{0,1},{1,0},{2,3},{3,2},{4,5},{5,4},{6,7},{7,6},{8,9},{9,8},{10,11... | collective-permute-start | bytes 294920 | tf_op jit(solution)/shard_map/ppermute | solution.py:273
  3.1 9.8 %collective-permute-start.1 = (bf16[64,512]{1,0:T(8,128)(2,1)S(1)}, bf16[64,512]{1,0:T(8,128)(2,1)S(1)}, u32[]{:S(2)}, u32[]{:S(2)}) collective-permute-start(bf16[64,512]{1,0:T(8,128)(2,1)S(1)} %copy_of.2.half_ref), channel_id=1, source_target_pairs={{0,16},{16,32},{32,48},{48,0},{1,17},{17,33},{33,49},{49,1},{2,18}... | collective-permute-start | bytes 196616 | tf_op jit(solution)/shard_map/ppermute | solution.py:273
  4.6 9.0 %collective-permute-start.2 = (bf16[64,512]{1,0:T(8,128)(2,1)S(1)}, bf16[64,512]{1,0:T(8,128)(2,1)S(1)}, u32[]{:S(2)}, u32[]{:S(2)}) collective-permute-start(bf16[64,512]{1,0:T(8,128)(2,1)S(1)} %copy_of.2.half_ref), channel_id=1, source_target_pairs={{0,48},{16,0},{32,16},{48,32},{1,49},{17,1},{33,17},{49,33},{2,50}... | collective-permute-start | bytes 196616 | tf_op jit(solution)/shard_map/ppermute | solution.py:273
  6.3 9.8 %collective-permute-start.3 = (bf16[64,512]{1,0:T(8,128)(2,1)S(1)}, bf16[64,512]{1,0:T(8,128)(2,1)S(1)}, u32[]{:S(2)}, u32[]{:S(2)}) collective-permute-start(bf16[64,512]{1,0:T(8,128)(2,1)S(1)} %copy_of.2.half_ref), channel_id=1, source_target_pairs={{0,32},{16,48},{32,0},{48,16},{1,33},{17,49},{33,1},{49,17},{2,34}... | collective-permute-start | bytes 196616 | tf_op jit(solution)/shard_map/ppermute | solution.py:273
  9.5 6.7 %collective-permute-start.4 = (bf16[128,512]{1,0:T(8,128)(2,1)S(1)}, bf16[128,512]{1,0:T(8,128)(2,1)S(1)}, u32[]{:S(2)}, u32[]{:S(2)}) collective-permute-start(bf16[128,512]{1,0:T(8,128)(2,1)S(1)} %get-tuple-element.39.token_ref.refs_0_), channel_id=1, source_target_pairs={{0,2},{2,0},{1,3},{3,1},{4,6},{6,4},{5,7},{7,5},{8,10},{10,8},{9,1... | collective-permute-start | bytes 393224 | tf_op jit(solution)/shard_map/ppermute | solution.py:273
  9.6 8.2 %collective-permute-start.6 = (bf16[128,512]{1,0:T(8,128)(2,1)S(1)}, bf16[128,512]{1,0:T(8,128)(2,1)S(1)}, u32[]{:S(2)}, u32[]{:S(2)}) collective-permute-start(bf16[128,512]{1,0:T(8,128)(2,1)S(1)} %get-tuple-element.39.token_ref.refs_0_), channel_id=1, source_target_pairs={{0,8},{4,12},{8,0},{12,4},{1,9},{5,13},{9,1},{13,5},{2,10},{6,14},... | collective-permute-start | bytes 393224 | tf_op jit(solution)/shard_map/ppermute | solution.py:273
  12.9 7.1 %collective-permute-start.7 = (bf16[128,512]{1,0:T(8,128)(2,1)S(1)}, bf16[128,512]{1,0:T(8,128)(2,1)S(1)}, u32[]{:S(2)}, u32[]{:S(2)}) collective-permute-start(bf16[128,512]{1,0:T(8,128)(2,1)S(1)} %get-tuple-element.39.token_ref.refs_0_), channel_id=1, source_target_pairs={{0,4},{4,8},{8,12},{12,0},{1,5},{5,9},{9,13},{13,1},{2,6},{6,10},{... | collective-permute-start | bytes 393224 | tf_op jit(solution)/shard_map/ppermute | solution.py:273
  13.6 6.6 %collective-permute-start.8 = (bf16[128,512]{1,0:T(8,128)(2,1)S(1)}, bf16[128,512]{1,0:T(8,128)(2,1)S(1)}, u32[]{:S(2)}, u32[]{:S(2)}) collective-permute-start(bf16[128,512]{1,0:T(8,128)(2,1)S(1)} %get-tuple-element.39.token_ref.refs_0_), channel_id=1, source_target_pairs={{0,12},{4,0},{8,4},{12,8},{1,13},{5,1},{9,5},{13,9},{2,14},{6,2},{... | collective-permute-start | bytes 393224 | tf_op jit(solution)/shard_map/ppermute | solution.py:273
  20.2 8.5 %collective-permute-start.9 = (bf16[512,512]{1,0:T(8,128)(2,1)S(1)}, bf16[512,512]{1,0:T(8,128)(2,1)S(1)}, u32[]{:S(2)}, u32[]{:S(2)}) collective-permute-start(bf16[512,512]{1,0:T(8,128)(2,1)S(1)} %constant_dynamic-update-slice_fusion.refs_0_), channel_id=1, source_target_pairs={{0,2},{2,0},{1,3},{3,1},{4,6},{6,4},{5,7},{7,5},{8,10},{10,8},{9,1... | collective-permute-start | bytes 1572872 | tf_op jit(solution)/shard_map/ppermute | solution.py:273
  20.3 7.8 %collective-permute-start.5 = (bf16[192,512]{1,0:T(8,128)(2,1)S(1)}, bf16[192,512]{1,0:T(8,128)(2,1)S(1)}, u32[]{:S(2)}, u32[]{:S(2)}) collective-permute-start(bf16[192,512]{1,0:T(8,128)(2,1)S(1)} %copy_of.3), channel_id=1, source_target_pairs={{0,1},{1,0},{2,3},{3,2},{4,5},{5,4},{6,7},{7,6},{8,9},{9,8},{10,11... | collective-permute-start | bytes 589832 | tf_op jit(solution)/shard_map/ppermute | solution.py:273
  20.5 21.3 %collective-permute-start.10 = (bf16[512,512]{1,0:T(8,128)(2,1)S(1)}, bf16[512,512]{1,0:T(8,128)(2,1)S(1)}, u32[]{:S(2)}, u32[]{:S(2)}) collective-permute-start(bf16[512,512]{1,0:T(8,128)(2,1)S(1)} %constant_dynamic-update-slice_fusion.refs_0_), channel_id=1, source_target_pairs={{0,64},{64,0},{1,65},{65,1},{2,66},{66,2},{3,67},{67,3},{4,68},{68... | collective-permute-start | bytes 1572872 | tf_op jit(solution)/shard_map/ppermute | solution.py:273
  41.8 7.0 %collective-permute-start.11 = (bf16[512,512]{1,0:T(8,128)(2,1)S(1)}, bf16[512,512]{1,0:T(8,128)(2,1)S(1)}, u32[]{:S(2)}, u32[]{:S(2)}) collective-permute-start(bf16[512,512]{1,0:T(8,128)(2,1)S(1)} %collective-permute-done.10.refs_0_), channel_id=1, source_target_pairs={{0,2},{2,0},{1,3},{3,1},{4,6},{6,4},{5,7},{7,5},{8,10},{10,8},{9,1... | collective-permute-start | bytes 1572872 | tf_op jit(solution)/shard_map/ppermute | solution.py:273
  55.5 9.7 %collective-permute-start.14 = (bf16[64,1024]{1,0:T(8,128)(2,1)S(1)}, bf16[64,1024]{1,0:T(8,128)(2,1)S(1)}, u32[]{:S(2)}, u32[]{:S(2)}) collective-permute-start(bf16[64,1024]{1,0:T(8,128)(2,1)S(1)} %get-tuple-element.66), channel_id=1, source_target_pairs={{0,16},{16,32},{32,48},{48,0},{1,17},{17,33},{33,49},{49,1},{2,18}... | collective-permute-start | bytes 393224 | tf_op jit(solution)/shard_map/ppermute | solution.py:273
  56.1 9.1 %collective-permute-start.13 = (bf16[64,1024]{1,0:T(8,128)(2,1)S(1)}, bf16[64,1024]{1,0:T(8,128)(2,1)S(1)}, u32[]{:S(2)}, u32[]{:S(2)}) collective-permute-start(bf16[64,1024]{1,0:T(8,128)(2,1)S(1)} %get-tuple-element.65), channel_id=1, source_target_pairs={{0,48},{16,0},{32,16},{48,32},{1,49},{17,1},{33,17},{49,33},{2,50}... | collective-permute-start | bytes 393224 | tf_op jit(solution)/shard_map/ppermute | solution.py:273
  58.8 6.8 %collective-permute-start.12 = (bf16[64,1024]{1,0:T(8,128)(2,1)S(1)}, bf16[64,1024]{1,0:T(8,128)(2,1)S(1)}, u32[]{:S(2)}, u32[]{:S(2)}) collective-permute-start(bf16[64,1024]{1,0:T(8,128)(2,1)S(1)} %get-tuple-element.64), channel_id=1, source_target_pairs={{0,32},{16,48},{32,0},{48,16},{1,33},{17,49},{33,1},{49,17},{2,34}... | collective-permute-start | bytes 393224 | tf_op jit(solution)/shard_map/ppermute | solution.py:273
  65.2 5.5 %copy-start = (bf16[1024,32]{0,1:T(8,128)(2,1)S(1)}, bf16[1024,32]{0,1:T(8,128)(2,1)}, u32[]{:S(2)}) copy-start(bf16[1024,32]{0,1:T(8,128)(2,1)} %param.6) | copy-start | bytes 196612
  65.6 5.0 %collective-permute-start.15 = (f32[32,1024]{1,0:T(8,128)S(1)}, f32[32,1024]{1,0:T(8,128)S(1)}, u32[]{:S(2)}, u32[]{:S(2)}) collective-permute-start(f32[32,1024]{1,0:T(8,128)S(1)} %fusion.2), channel_id=1, source_target_pairs={{0,1},{1,0},{2,3},{3,2},{4,5},{5,4},{6,7},{7,6},{8,9},{9,8},{10,11... | collective-permute-start | bytes 393224 | tf_op jit(solution)/shard_map/ppermute | solution.py:273

commit v12 on v11

--- a/solution.py
+++ b/solution.py
@@ -309,7 +309,7 @@
         theirs = theirs + part[32:].astype(F32)
     for part in arrived:
         mine = mine + part[:32].astype(F32)
-    result = mine + shift(theirs, "zl", 1)
+    result = mine + shift(theirs.astype(BF16), "zl", 1).astype(F32)
     return result.T + noise[0] * vectors.astype(F32)
 
 

time: 71.6 us -> 70.9 us (level)
  transfers between devices with their start and end apart: 16 -> 16, of which waited for: 5 -> 5; matrix products, arithmetic and copies ran while one was open for 0% -> 0% of each run, Pallas kernels for 43% -> 44%
where the time goes in v12:
time: 70.9 us; the launch traced here: 70.7 us
  Pallas kernels  38.5 us (54%)
  starting transfers between devices  22.1 us (31%)
  waiting for transfers between devices  7.68 us (11%)
  between operations  1.52 us (2%)
  other arithmetic  0.82 us (1%)
    pallas_call x6, Pallas kernels, add_tiles(): pl.pallas_call(body, grid=(count,), out_shape=sum_shapes + made, in_specs...  36.2 us
    ppermute x16, starting transfers between devices, shift(): lax.ppermute(value, axis, [(i, (i + by) % size) for i in range(size)])  22.1 us
    ppermute x16, waiting for transfers between devices, shift(): lax.ppermute(value, axis, [(i, (i + by) % size) for i in range(size)])  7.68 us
  transfers between devices with their start and end apart: 16, of which 5 were waited for; matrix products, arithmetic and copies ran while one was open for 0% of the time, Pallas kernels for 44%

profile of v12, /device:TPU:0, one launch (start us, length us, event | category | flops | bytes accessed | tf_op | source)
XLA Modules:
  0.0 70.7 jit_solution(3862638017228755558)
XLA Ops:
  0.0 1.0 %first_pack.1 = (bf16[96,512]{1,0:T(8,128)(2,1)S(1)}, bf16[32,512]{1,0:T(8,128)(2,1)S(1)}) custom-call(s32[1]{0:T(128)} %bitcast.zl_ref, bf16[32,1024]{1,0:T(8,128)(2,1)} %bitcast.35, bf16[32,1024]{1,0:T(8,128)(2,1)} %bitcast.34, f32[1,64]{1,0:T(1,128)} %bitcast.36), custom_call_target="tpu_custom_call" | custom-call | tf_op jit(solution)/shard_map/first_pack/pallas_call | solution.py:91
  1.0 2.1 %collective-permute-start = (bf16[96,512]{1,0:T(8,128)(2,1)S(1)}, bf16[96,512]{1,0:T(8,128)(2,1)S(1)}, u32[]{:S(2)}, u32[]{:S(2)}) collective-permute-start(bf16[96,512]{1,0:T(8,128)(2,1)S(1)} %get-tuple-element.37.refs_0_), channel_id=1, source_target_pairs={{0,1},{1,0},{2,3},{3,2},{4,5},{5,4},{6,7},{7,6},{8,9},{9,8},{10,11... | collective-permute-start | bytes 294920 | tf_op jit(solution)/shard_map/ppermute | solution.py:273
  3.1 1.5 %collective-permute-start.1 = (bf16[64,512]{1,0:T(8,128)(2,1)S(1)}, bf16[64,512]{1,0:T(8,128)(2,1)S(1)}, u32[]{:S(2)}, u32[]{:S(2)}) collective-permute-start(bf16[64,512]{1,0:T(8,128)(2,1)S(1)} %copy_of.2.half_ref), channel_id=1, source_target_pairs={{0,16},{16,32},{32,48},{48,0},{1,17},{17,33},{33,49},{49,1},{2,18}... | collective-permute-start | bytes 196616 | tf_op jit(solution)/shard_map/ppermute | solution.py:273
  4.6 1.7 %collective-permute-start.2 = (bf16[64,512]{1,0:T(8,128)(2,1)S(1)}, bf16[64,512]{1,0:T(8,128)(2,1)S(1)}, u32[]{:S(2)}, u32[]{:S(2)}) collective-permute-start(bf16[64,512]{1,0:T(8,128)(2,1)S(1)} %copy_of.2.half_ref), channel_id=1, source_target_pairs={{0,48},{16,0},{32,16},{48,32},{1,49},{17,1},{33,17},{49,33},{2,50}... | collective-permute-start | bytes 196616 | tf_op jit(solution)/shard_map/ppermute | solution.py:273
  6.3 1.8 %collective-permute-start.3 = (bf16[64,512]{1,0:T(8,128)(2,1)S(1)}, bf16[64,512]{1,0:T(8,128)(2,1)S(1)}, u32[]{:S(2)}, u32[]{:S(2)}) collective-permute-start(bf16[64,512]{1,0:T(8,128)(2,1)S(1)} %copy_of.2.half_ref), channel_id=1, source_target_pairs={{0,32},{16,48},{32,0},{48,16},{1,33},{17,49},{33,1},{49,17},{2,34}... | collective-permute-start | bytes 196616 | tf_op jit(solution)/shard_map/ppermute | solution.py:273
  8.9 0.1 pad_maximum_fusion.amp_ref
  8.9 0.6 second_pack.1
  9.5 0.1 collective-permute-start.4
  9.6 3.3 %collective-permute-start.6 = (bf16[128,512]{1,0:T(8,128)(2,1)S(1)}, bf16[128,512]{1,0:T(8,128)(2,1)S(1)}, u32[]{:S(2)}, u32[]{:S(2)}) collective-permute-start(bf16[128,512]{1,0:T(8,128)(2,1)S(1)} %get-tuple-element.39.token_ref.refs_0_), channel_id=1, source_target_pairs={{0,8},{4,12},{8,0},{12,4},{1,9},{5,13},{9,1},{13,5},{2,10},{6,14},... | collective-permute-start | bytes 393224 | tf_op jit(solution)/shard_map/ppermute | solution.py:273
  12.9 0.7 collective-permute-start.7
  13.6 2.6 %collective-permute-start.8 = (bf16[128,512]{1,0:T(8,128)(2,1)S(1)}, bf16[128,512]{1,0:T(8,128)(2,1)S(1)}, u32[]{:S(2)}, u32[]{:S(2)}) collective-permute-start(bf16[128,512]{1,0:T(8,128)(2,1)S(1)} %get-tuple-element.39.token_ref.refs_0_), channel_id=1, source_target_pairs={{0,12},{4,0},{8,4},{12,8},{1,13},{5,1},{9,5},{13,9},{2,14},{6,2},{... | collective-permute-start | bytes 393224 | tf_op jit(solution)/shard_map/ppermute | solution.py:273
  16.2 1.7 %add_tiles.6 = (f32[1,64,1024]{2,1,0:T(8,128)S(1)}, bf16[1024,128]{1,0:T(8,128)(2,1)S(1)}, bf16[64,1024]{1,0:T(8,128)(2,1)S(1)}) custom-call(f32[2]{0:T(128)S(1)} %pad_maximum_fusion.amp_ref, bf16[1,128,1024]{2,1,0:T(8,128)(2,1)S(1)} %get-tuple-element.38.left_ref, bf16[128,512]{1,0:T(8,128)(2,1)S(1)} %get-tuple-element.39.token_ref.refs_0_, ...), custom_call_target="tpu_custom_call" | custom-call | flops 2147483648 | bytes 393216 | tf_op jit(solution)/shard_map/add_tiles/pallas_call | solution.py:252
  17.9 2.1 %collective-permute-done.7 = bf16[128,512]{1,0:T(8,128)(2,1)S(1)} collective-permute-done((bf16[128,512]{1,0:T(8,128)(2,1)S(1)}, bf16[128,512]{1,0:T(8,128)(2,1)S(1)}, u32[]{:S(2)}, u32[]{:S(2)}) %collective-permute-start.7) | collective-permute-done | bytes 131104 | tf_op jit(solution)/shard_map/ppermute | solution.py:273
  20.0 0.2 collective-permute-done.8
  20.2 0.1 collective-permute-start.9
  20.3 0.2 collective-permute-start.5
  20.5 3.9 %collective-permute-start.10 = (bf16[512,512]{1,0:T(8,128)(2,1)S(1)}, bf16[512,512]{1,0:T(8,128)(2,1)S(1)}, u32[]{:S(2)}, u32[]{:S(2)}) collective-permute-start(bf16[512,512]{1,0:T(8,128)(2,1)S(1)} %constant_dynamic-update-slice_fusion.refs_0_), channel_id=1, source_target_pairs={{0,64},{64,0},{1,65},{65,1},{2,66},{66,2},{3,67},{67,3},{4,68},{68... | collective-permute-start | bytes 1572872 | tf_op jit(solution)/shard_map/ppermute | solution.py:273
  24.4 2.3 %add_tiles.7 = (f32[1,64,1024]{2,1,0:T(8,128)S(1)}, bf16[1536,128]{1,0:T(8,128)(2,1)S(1)}, bf16[64,1536]{1,0:T(8,128)(2,1)S(1)}) custom-call(f32[2]{0:T(128)S(1)} %pad_maximum_fusion.amp_ref, bf16[1,128,1024]{2,1,0:T(8,128)(2,1)S(1)} %get-tuple-element.38.left_ref, bf16[512,512]{1,0:T(8,128)(2,1)S(1)} %constant_dynamic-update-slice_fusion.refs_0_, ...), custom_call_target="tpu_custom_call" | custom-call | flops 50331648 | bytes 589824 | tf_op jit(solution)/shard_map/add_tiles/pallas_call | solution.py:252
  26.7 1.4 %collective-permute-done.5.refs_3_ = bf16[192,512]{1,0:T(8,128)(2,1)S(1)} collective-permute-done((bf16[192,512]{1,0:T(8,128)(2,1)S(1)}, bf16[192,512]{1,0:T(8,128)(2,1)S(1)}, u32[]{:S(2)}, u32[]{:S(2)}) %collective-permute-start.5) | collective-permute-done | bytes 196640 | tf_op jit(solution)/shard_map/ppermute | solution.py:273
  28.1 0.7 ready_rows.1.left_ref
  28.8 13.0 %add_tiles.8 = (f32[3,64,1024]{2,1,0:T(8,128)S(1)}, bf16[1536,128]{1,0:T(8,128)(2,1)S(1)}, bf16[64,1536]{1,0:T(8,128)(2,1)S(1)}) custom-call(f32[2]{0:T(128)S(1)} %pad_maximum_fusion.amp_ref, bf16[3,128,1024]{2,1,0:T(8,128)(2,1)S(1)} %ready_rows.1.left_ref, bf16[1024,128]{1,0:T(8,128)(2,1)S(1)} %get-tuple-element.49.refs_0_, ...), custom_call_target="tpu_custom_call" | custom-call | flops 6442450944 | bytes 1572864 | tf_op jit(solution)/shard_map/add_tiles/pallas_call | solution.py:252
  41.8 0.3 collective-permute-start.11
  42.1 6.6 %add_tiles.9 = (f32[3,64,1024]{2,1,0:T(8,128)S(1)}, bf16[2048,128]{1,0:T(8,128)(2,1)S(1)}, bf16[64,2048]{1,0:T(8,128)(2,1)S(1)}) custom-call(f32[2]{0:T(128)S(1)} %pad_maximum_fusion.amp_ref, bf16[3,128,1024]{2,1,0:T(8,128)(2,1)S(1)} %ready_rows.1.left_ref, bf16[512,512]{1,0:T(8,128)(2,1)S(1)} %collective-permute-done.10.refs_0_, ...), custom_call_target="tpu_custom_call" | custom-call | flops 3221225472 | bytes 786432 | tf_op jit(solution)/shard_map/add_tiles/pallas_call | solution.py:252
  48.8 6.7 %add_tiles.10 = (bf16[64,1024]{1,0:T(8,128)(2,1)S(1)}, bf16[64,1024]{1,0:T(8,128)(2,1)S(1)}, bf16[64,1024]{1,0:T(8,128)(2,1)S(1)}, bf16[2048,128]{1,0:T(8,128)(2,1)S(1)}, bf16[64,2048]{1,0:T(8,128)(2,1)S(1)}) custom-call(f32[2]{0:T(128)S(1)} %pad_maximum_fusion.amp_ref, bf16[3,128,1024]{2,1,0:T(8,128)(2,1)S(1)} %ready_rows.1.left_ref, ...), custom_call_target="tpu_custom_call" | custom-call | flops 3221225472 | bytes 786432 | tf_op jit(solution)/shard_map/add_tiles/pallas_call | solution.py:252
  55.5 0.7 collective-permute-start.14
  56.1 2.6 %collective-permute-start.13 = (bf16[64,1024]{1,0:T(8,128)(2,1)S(1)}, bf16[64,1024]{1,0:T(8,128)(2,1)S(1)}, u32[]{:S(2)}, u32[]{:S(2)}) collective-permute-start(bf16[64,1024]{1,0:T(8,128)(2,1)S(1)} %get-tuple-element.65), channel_id=1, source_target_pairs={{0,48},{16,0},{32,16},{48,32},{1,49},{17,1},{33,17},{49,33},{2,50}... | collective-permute-start | bytes 393224 | tf_op jit(solution)/shard_map/ppermute | solution.py:273
  58.8 0.5 collective-permute-start.12
  59.3 5.9 %add_tiles.11 = f32[1,64,1024]{2,1,0:T(8,128)S(1)} custom-call(f32[2]{0:T(128)S(1)} %pad_maximum_fusion.amp_ref, bf16[1,128,1024]{2,1,0:T(8,128)(2,1)S(1)} %get-tuple-element.38.left_ref, bf16[1536,128]{1,0:T(8,128)(2,1)S(1)} %get-tuple-element.53.refs_0_, bf16[64,1536]{1,0:T(8,128)(2,1)S(1)} %get-tuple-element.54.refs_1_, ...), custom_call_target="tpu_custom_call" | custom-call | flops 2952790016 | bytes 2162688 | tf_op jit(solution)/shard_map/add_tiles/pallas_call | solution.py:252
  65.2 0.4 collective-permute-done.12
  65.6 0.2 collective-permute-start.15
  66.5 3.5 %collective-permute-done.15 = bf16[32,1024]{1,0:T(8,128)(2,1)S(1)} collective-permute-done((bf16[32,1024]{1,0:T(8,128)(2,1)S(1)}, bf16[32,1024]{1,0:T(8,128)(2,1)S(1)}, u32[]{:S(2)}, u32[]{:S(2)}) %collective-permute-start.15) | collective-permute-done | bytes 65568 | tf_op jit(solution)/shard_map/ppermute | solution.py:273
  70.0 0.7 %fusion.9 = f32[1024,32]{0,1:T(8,128)} fusion(f32[1,64,1024]{2,1,0:T(8,128)S(1)} %add_tiles.11, bf16[1024,32]{0,1:T(8,128)(2,1)S(1)} %copy-done, bf16[32,1024]{1,0:T(8,128)(2,1)S(1)} %collective-permute-done.15, bf16[64,1024]{1,0:T(8,128)(2,1)S(1)} %collective-permute-done.14, bf16[64,1024]{1,0:T(8,128)(2,1)S(1)} %collective-permute-done.13, ...), kind=kLoop, calls=%fused_computation.11 | loop fusion | flops 360448 | bytes 589828 | tf_op jit(solution)/shard_map/add | solution.py:313
  (20 shorter events, 0.1 us)
Async XLA Ops:
  1.0 7.9 %collective-permute-start = (bf16[96,512]{1,0:T(8,128)(2,1)S(1)}, bf16[96,512]{1,0:T(8,128)(2,1)S(1)}, u32[]{:S(2)}, u32[]{:S(2)}) collective-permute-start(bf16[96,512]{1,0:T(8,128)(2,1)S(1)} %get-tuple-element.37.refs_0_), channel_id=1, source_target_pairs={{0,1},{1,0},{2,3},{3,2},{4,5},{5,4},{6,7},{7,6},{8,9},{9,8},{10,11... | collective-permute-start | bytes 294920 | tf_op jit(solution)/shard_map/ppermute | solution.py:273
  3.1 9.8 %collective-permute-start.1 = (bf16[64,512]{1,0:T(8,128)(2,1)S(1)}, bf16[64,512]{1,0:T(8,128)(2,1)S(1)}, u32[]{:S(2)}, u32[]{:S(2)}) collective-permute-start(bf16[64,512]{1,0:T(8,128)(2,1)S(1)} %copy_of.2.half_ref), channel_id=1, source_target_pairs={{0,16},{16,32},{32,48},{48,0},{1,17},{17,33},{33,49},{49,1},{2,18}... | collective-permute-start | bytes 196616 | tf_op jit(solution)/shard_map/ppermute | solution.py:273
  4.6 9.0 %collective-permute-start.2 = (bf16[64,512]{1,0:T(8,128)(2,1)S(1)}, bf16[64,512]{1,0:T(8,128)(2,1)S(1)}, u32[]{:S(2)}, u32[]{:S(2)}) collective-permute-start(bf16[64,512]{1,0:T(8,128)(2,1)S(1)} %copy_of.2.half_ref), channel_id=1, source_target_pairs={{0,48},{16,0},{32,16},{48,32},{1,49},{17,1},{33,17},{49,33},{2,50}... | collective-permute-start | bytes 196616 | tf_op jit(solution)/shard_map/ppermute | solution.py:273
  6.3 9.8 %collective-permute-start.3 = (bf16[64,512]{1,0:T(8,128)(2,1)S(1)}, bf16[64,512]{1,0:T(8,128)(2,1)S(1)}, u32[]{:S(2)}, u32[]{:S(2)}) collective-permute-start(bf16[64,512]{1,0:T(8,128)(2,1)S(1)} %copy_of.2.half_ref), channel_id=1, source_target_pairs={{0,32},{16,48},{32,0},{48,16},{1,33},{17,49},{33,1},{49,17},{2,34}... | collective-permute-start | bytes 196616 | tf_op jit(solution)/shard_map/ppermute | solution.py:273
  9.5 6.7 %collective-permute-start.4 = (bf16[128,512]{1,0:T(8,128)(2,1)S(1)}, bf16[128,512]{1,0:T(8,128)(2,1)S(1)}, u32[]{:S(2)}, u32[]{:S(2)}) collective-permute-start(bf16[128,512]{1,0:T(8,128)(2,1)S(1)} %get-tuple-element.39.token_ref.refs_0_), channel_id=1, source_target_pairs={{0,2},{2,0},{1,3},{3,1},{4,6},{6,4},{5,7},{7,5},{8,10},{10,8},{9,1... | collective-permute-start | bytes 393224 | tf_op jit(solution)/shard_map/ppermute | solution.py:273
  9.6 8.2 %collective-permute-start.6 = (bf16[128,512]{1,0:T(8,128)(2,1)S(1)}, bf16[128,512]{1,0:T(8,128)(2,1)S(1)}, u32[]{:S(2)}, u32[]{:S(2)}) collective-permute-start(bf16[128,512]{1,0:T(8,128)(2,1)S(1)} %get-tuple-element.39.token_ref.refs_0_), channel_id=1, source_target_pairs={{0,8},{4,12},{8,0},{12,4},{1,9},{5,13},{9,1},{13,5},{2,10},{6,14},... | collective-permute-start | bytes 393224 | tf_op jit(solution)/shard_map/ppermute | solution.py:273
  12.9 7.1 %collective-permute-start.7 = (bf16[128,512]{1,0:T(8,128)(2,1)S(1)}, bf16[128,512]{1,0:T(8,128)(2,1)S(1)}, u32[]{:S(2)}, u32[]{:S(2)}) collective-permute-start(bf16[128,512]{1,0:T(8,128)(2,1)S(1)} %get-tuple-element.39.token_ref.refs_0_), channel_id=1, source_target_pairs={{0,4},{4,8},{8,12},{12,0},{1,5},{5,9},{9,13},{13,1},{2,6},{6,10},{... | collective-permute-start | bytes 393224 | tf_op jit(solution)/shard_map/ppermute | solution.py:273
  13.6 6.6 %collective-permute-start.8 = (bf16[128,512]{1,0:T(8,128)(2,1)S(1)}, bf16[128,512]{1,0:T(8,128)(2,1)S(1)}, u32[]{:S(2)}, u32[]{:S(2)}) collective-permute-start(bf16[128,512]{1,0:T(8,128)(2,1)S(1)} %get-tuple-element.39.token_ref.refs_0_), channel_id=1, source_target_pairs={{0,12},{4,0},{8,4},{12,8},{1,13},{5,1},{9,5},{13,9},{2,14},{6,2},{... | collective-permute-start | bytes 393224 | tf_op jit(solution)/shard_map/ppermute | solution.py:273
  20.2 8.5 %collective-permute-start.9 = (bf16[512,512]{1,0:T(8,128)(2,1)S(1)}, bf16[512,512]{1,0:T(8,128)(2,1)S(1)}, u32[]{:S(2)}, u32[]{:S(2)}) collective-permute-start(bf16[512,512]{1,0:T(8,128)(2,1)S(1)} %constant_dynamic-update-slice_fusion.refs_0_), channel_id=1, source_target_pairs={{0,2},{2,0},{1,3},{3,1},{4,6},{6,4},{5,7},{7,5},{8,10},{10,8},{9,1... | collective-permute-start | bytes 1572872 | tf_op jit(solution)/shard_map/ppermute | solution.py:273
  20.3 7.8 %collective-permute-start.5 = (bf16[192,512]{1,0:T(8,128)(2,1)S(1)}, bf16[192,512]{1,0:T(8,128)(2,1)S(1)}, u32[]{:S(2)}, u32[]{:S(2)}) collective-permute-start(bf16[192,512]{1,0:T(8,128)(2,1)S(1)} %copy_of.3), channel_id=1, source_target_pairs={{0,1},{1,0},{2,3},{3,2},{4,5},{5,4},{6,7},{7,6},{8,9},{9,8},{10,11... | collective-permute-start | bytes 589832 | tf_op jit(solution)/shard_map/ppermute | solution.py:273
  20.5 21.3 %collective-permute-start.10 = (bf16[512,512]{1,0:T(8,128)(2,1)S(1)}, bf16[512,512]{1,0:T(8,128)(2,1)S(1)}, u32[]{:S(2)}, u32[]{:S(2)}) collective-permute-start(bf16[512,512]{1,0:T(8,128)(2,1)S(1)} %constant_dynamic-update-slice_fusion.refs_0_), channel_id=1, source_target_pairs={{0,64},{64,0},{1,65},{65,1},{2,66},{66,2},{3,67},{67,3},{4,68},{68... | collective-permute-start | bytes 1572872 | tf_op jit(solution)/shard_map/ppermute | solution.py:273
  41.8 7.0 %collective-permute-start.11 = (bf16[512,512]{1,0:T(8,128)(2,1)S(1)}, bf16[512,512]{1,0:T(8,128)(2,1)S(1)}, u32[]{:S(2)}, u32[]{:S(2)}) collective-permute-start(bf16[512,512]{1,0:T(8,128)(2,1)S(1)} %collective-permute-done.10.refs_0_), channel_id=1, source_target_pairs={{0,2},{2,0},{1,3},{3,1},{4,6},{6,4},{5,7},{7,5},{8,10},{10,8},{9,1... | collective-permute-start | bytes 1572872 | tf_op jit(solution)/shard_map/ppermute | solution.py:273
  55.5 9.7 %collective-permute-start.14 = (bf16[64,1024]{1,0:T(8,128)(2,1)S(1)}, bf16[64,1024]{1,0:T(8,128)(2,1)S(1)}, u32[]{:S(2)}, u32[]{:S(2)}) collective-permute-start(bf16[64,1024]{1,0:T(8,128)(2,1)S(1)} %get-tuple-element.66), channel_id=1, source_target_pairs={{0,16},{16,32},{32,48},{48,0},{1,17},{17,33},{33,49},{49,1},{2,18}... | collective-permute-start | bytes 393224 | tf_op jit(solution)/shard_map/ppermute | solution.py:273
  56.1 9.1 %collective-permute-start.13 = (bf16[64,1024]{1,0:T(8,128)(2,1)S(1)}, bf16[64,1024]{1,0:T(8,128)(2,1)S(1)}, u32[]{:S(2)}, u32[]{:S(2)}) collective-permute-start(bf16[64,1024]{1,0:T(8,128)(2,1)S(1)} %get-tuple-element.65), channel_id=1, source_target_pairs={{0,48},{16,0},{32,16},{48,32},{1,49},{17,1},{33,17},{49,33},{2,50}... | collective-permute-start | bytes 393224 | tf_op jit(solution)/shard_map/ppermute | solution.py:273
  58.8 6.8 %collective-permute-start.12 = (bf16[64,1024]{1,0:T(8,128)(2,1)S(1)}, bf16[64,1024]{1,0:T(8,128)(2,1)S(1)}, u32[]{:S(2)}, u32[]{:S(2)}) collective-permute-start(bf16[64,1024]{1,0:T(8,128)(2,1)S(1)} %get-tuple-element.64), channel_id=1, source_target_pairs={{0,32},{16,48},{32,0},{48,16},{1,33},{17,49},{33,1},{49,17},{2,34}... | collective-permute-start | bytes 393224 | tf_op jit(solution)/shard_map/ppermute | solution.py:273
  65.2 4.8 %copy-start = (bf16[1024,32]{0,1:T(8,128)(2,1)S(1)}, bf16[1024,32]{0,1:T(8,128)(2,1)}, u32[]{:S(2)}) copy-start(bf16[1024,32]{0,1:T(8,128)(2,1)} %param.6) | copy-start | bytes 196612
  65.6 4.3 %collective-permute-start.15 = (bf16[32,1024]{1,0:T(8,128)(2,1)S(1)}, bf16[32,1024]{1,0:T(8,128)(2,1)S(1)}, u32[]{:S(2)}, u32[]{:S(2)}) collective-permute-start(bf16[32,1024]{1,0:T(8,128)(2,1)S(1)} %fusion.3), channel_id=1, source_target_pairs={{0,1},{1,0},{2,3},{3,2},{4,5},{5,4},{6,7},{7,6},{8,9},{9,8},{10,11... | collective-permute-start | bytes 196616 | tf_op jit(solution)/shard_map/ppermute | solution.py:273

commit v13 on v11

--- a/solution.py
+++ b/solution.py
@@ -38,11 +38,14 @@
     return jnp.concatenate([features, tail, jnp.zeros((56, features.shape[1]), F32)], axis=0)
 
 
-def ready_rows(amp, mines, theirs):
+def ready_rows(amp, mines, theirs, entire):
     count = len(mines)
 
     def body(amp_ref, *refs):
-        theirs_ref, out_ref = refs[count:]
+        theirs_ref, entire_ref, out_ref = refs[count:]
+        for half in range(2):
+            features = entire_ref[64 * half : 64 * half + 64, :].astype(F32)
+            out_ref[count, :, 512 * half : 512 * half + 512] = with_parts(features, amp_ref[1], 3).astype(BF16)
         for k in range(count):
             for half in range(2):
                 low = 32 * half
@@ -53,13 +56,13 @@
 
     return pl.pallas_call(
         body,
-        out_shape=jax.ShapeDtypeStruct((count, 128, 1024), BF16),
+        out_shape=jax.ShapeDtypeStruct((count + 1, 128, 1024), BF16),
         in_specs=[pl.BlockSpec(memory_space=pltpu.SMEM)]
-        + [pl.BlockSpec(memory_space=pltpu.VMEM)] * (count + 1),
+        + [pl.BlockSpec(memory_space=pltpu.VMEM)] * (count + 2),
         out_specs=pl.BlockSpec(memory_space=pltpu.VMEM),
         compiler_params=PARAMS,
         name="ready_rows",
-    )(amp, *mines, theirs)
+    )(amp, *mines, theirs, entire)
 
 
 def kept_in_hbm(array):
@@ -124,12 +127,13 @@
 
 
 def second_pack(zl, amp, half, got, kept):
-    def body(zl_ref, amp_ref, half_ref, got_ref, kept_ref, rows_ref, share_ref):
+    def body(zl_ref, amp_ref, half_ref, got_ref, kept_ref, rows_ref, share_ref, entire_ref):
         first = zl_ref[0] == 0
         mine = half_ref[...].astype(F32)
         theirs = got_ref[...].astype(F32)
         low = jnp.concatenate([mine[:32], theirs[:32]], axis=0)
         high = jnp.concatenate([mine[32:], theirs[32:64]], axis=0)
+        entire_ref[...] = jnp.concatenate([low, high], axis=0).astype(BF16)
         picked = jnp.where(first, low, high)
         share_ref[...] = jnp.concatenate([picked, kept_ref[...].astype(F32), theirs[64:]], axis=0).astype(BF16)
         for k, features in enumerate((low, high)):
@@ -137,9 +141,9 @@
 
     return pl.pallas_call(
         body,
-        out_shape=[jax.ShapeDtypeStruct((1, 128, 1024), BF16), jax.ShapeDtypeStruct((128, 512), BF16)],
+        out_shape=[jax.ShapeDtypeStruct((1, 128, 1024), BF16)] + [jax.ShapeDtypeStruct((128, 512), BF16)] * 2,
         in_specs=[pl.BlockSpec(memory_space=pltpu.SMEM)] * 2 + [pl.BlockSpec(memory_space=pltpu.VMEM)] * 3,
-        out_specs=[pl.BlockSpec(memory_space=pltpu.VMEM)] * 2,
+        out_specs=[pl.BlockSpec(memory_space=pltpu.VMEM)] * 3,
         compiler_params=PARAMS,
         name="second_pack",
     )(zl, amp, half, got, kept)
@@ -280,13 +284,14 @@
     given, kept = first_pack(zl, points.T, vectors.T, lengthscale)
     got = shift(given, "zl", 1)
     half = copy_of([given], 64, kept, 4096)
-    mines = [shift(half, "x", by) for by in (1, -1, 2)]
-    own_left, share = second_pack(zl, amp, half, got, kept)
+    mines = [shift(half, "x", by) for by in (1, -1)]
+    own_left, share, entire = second_pack(zl, amp, half, got, kept)
 
     beside = shift(share, "c", 1)
     near = [shift(share, "y", by) for by in (2, 1, -1)]
+    entire = shift(entire, "x", 2)
     mined = copy_of(mines, 64, share, 16)
-    mined, beside = lax.optimization_barrier((mined, beside))
+    mined, beside, entire = lax.optimization_barrier((mined, beside, entire))
     theirs = shift(mined, "zl", 1)
     own, ready0 = add_tiles(amp, own_left, [], [(share, 0), (beside, 0)], weight=4096)
     near[0], near[1], near[2], own = lax.optimization_barrier((near[0], near[1], near[2], own))
@@ -296,7 +301,7 @@
     own, ready1 = add_tiles(amp, own_left, [], [(merged, 1)], own, weight=64)
 
     theirs, own = lax.optimization_barrier((theirs, own))
-    left = ready_rows(amp, mines, theirs)
+    left = ready_rows(amp, mines, theirs, entire)
     acc, ready2 = add_tiles(amp, left, [ready0, ready1], [(merged_beside, 1)])
     far, acc = lax.optimization_barrier((far, acc))
     far_beside = shift(far, "c", 1)

time: 71.6 us -> 71.3 us (level)
  waiting for transfers between devices: 8.38 us -> 7.27 us
  starting transfers between devices: 22.1 us -> 23 us
    ppermute x16, waiting for transfers between devices: 8.38 us -> 7.27 us  [shift(): lax.ppermute(value, axis, [(i, (i + by) % size) for i in range(size)])]
    ppermute x16, starting transfers between devices: 22.1 us -> 23 us  [shift(): lax.ppermute(value, axis, [(i, (i + by) % size) for i in range(size)])]
  transfers between devices with their start and end apart: 16 -> 16, of which waited for: 5 -> 3; matrix products, arithmetic and copies ran while one was open for 0% -> 0% of each run, Pallas kernels for 43% -> 43%
where the time goes in v13:
time: 71.3 us; the launch traced here: 71.2 us
  Pallas kernels  38.5 us (54%)
  starting transfers between devices  23 us (32%)
  waiting for transfers between devices  7.27 us (10%)
  between operations  1.52 us (2%)
  other arithmetic  0.82 us (1%)
    pallas_call x6, Pallas kernels, add_tiles(): pl.pallas_call(body, grid=(count,), out_shape=sum_shapes + made, in_specs...  36.2 us
    ppermute x16, starting transfers between devices, shift(): lax.ppermute(value, axis, [(i, (i + by) % size) for i in range(size)])  23 us
    ppermute x16, waiting for transfers between devices, shift(): lax.ppermute(value, axis, [(i, (i + by) % size) for i in range(size)])  7.27 us
  transfers between devices with their start and end apart: 16, of which 3 were waited for; matrix products, arithmetic and copies ran while one was open for 0% of the time, Pallas kernels for 43%

profile of v13, /device:TPU:0, one launch (start us, length us, event | category | flops | bytes accessed | tf_op | source)
XLA Modules:
  0.0 71.2 jit_solution(12063073650553372084)
XLA Ops:
  0.0 1.0 %first_pack.1 = (bf16[96,512]{1,0:T(8,128)(2,1)S(1)}, bf16[32,512]{1,0:T(8,128)(2,1)S(1)}) custom-call(s32[1]{0:T(128)} %bitcast.zl_ref, bf16[32,1024]{1,0:T(8,128)(2,1)} %bitcast.33, bf16[32,1024]{1,0:T(8,128)(2,1)} %bitcast.32, f32[1,64]{1,0:T(1,128)} %bitcast.34), custom_call_target="tpu_custom_call" | custom-call | tf_op jit(solution)/shard_map/first_pack/pallas_call | solution.py:94
  1.0 2.1 %collective-permute-start = (bf16[96,512]{1,0:T(8,128)(2,1)S(1)}, bf16[96,512]{1,0:T(8,128)(2,1)S(1)}, u32[]{:S(2)}, u32[]{:S(2)}) collective-permute-start(bf16[96,512]{1,0:T(8,128)(2,1)S(1)} %get-tuple-element.39.refs_0_), channel_id=1, source_target_pairs={{0,1},{1,0},{2,3},{3,2},{4,5},{5,4},{6,7},{7,6},{8,9},{9,8},{10,11... | collective-permute-start | bytes 294920 | tf_op jit(solution)/shard_map/ppermute | solution.py:277
  3.1 1.5 %collective-permute-start.1 = (bf16[64,512]{1,0:T(8,128)(2,1)S(1)}, bf16[64,512]{1,0:T(8,128)(2,1)S(1)}, u32[]{:S(2)}, u32[]{:S(2)}) collective-permute-start(bf16[64,512]{1,0:T(8,128)(2,1)S(1)} %copy_of.2.half_ref), channel_id=1, source_target_pairs={{0,16},{16,32},{32,48},{48,0},{1,17},{17,33},{33,49},{49,1},{2,18}... | collective-permute-start | bytes 196616 | tf_op jit(solution)/shard_map/ppermute | solution.py:277
  4.6 1.7 %collective-permute-start.2 = (bf16[64,512]{1,0:T(8,128)(2,1)S(1)}, bf16[64,512]{1,0:T(8,128)(2,1)S(1)}, u32[]{:S(2)}, u32[]{:S(2)}) collective-permute-start(bf16[64,512]{1,0:T(8,128)(2,1)S(1)} %copy_of.2.half_ref), channel_id=1, source_target_pairs={{0,48},{16,0},{32,16},{48,32},{1,49},{17,1},{33,17},{49,33},{2,50}... | collective-permute-start | bytes 196616 | tf_op jit(solution)/shard_map/ppermute | solution.py:277
  7.0 0.1 pad_maximum_fusion.amp_ref
  7.1 0.6 second_pack.1
  7.7 0.1 collective-permute-start.3
  7.8 1.9 %collective-permute-start.4 = (bf16[128,512]{1,0:T(8,128)(2,1)S(1)}, bf16[128,512]{1,0:T(8,128)(2,1)S(1)}, u32[]{:S(2)}, u32[]{:S(2)}) collective-permute-start(bf16[128,512]{1,0:T(8,128)(2,1)S(1)} %get-tuple-element.42), channel_id=1, source_target_pairs={{0,32},{16,48},{32,0},{48,16},{1,33},{17,49},{33,1},{49,17},{2,34}... | collective-permute-start | bytes 393224 | tf_op jit(solution)/shard_map/ppermute | solution.py:277
  9.7 3.2 %collective-permute-start.6 = (bf16[128,512]{1,0:T(8,128)(2,1)S(1)}, bf16[128,512]{1,0:T(8,128)(2,1)S(1)}, u32[]{:S(2)}, u32[]{:S(2)}) collective-permute-start(bf16[128,512]{1,0:T(8,128)(2,1)S(1)} %get-tuple-element.41.token_ref.refs_0_), channel_id=1, source_target_pairs={{0,8},{4,12},{8,0},{12,4},{1,9},{5,13},{9,1},{13,5},{2,10},{6,14},... | collective-permute-start | bytes 393224 | tf_op jit(solution)/shard_map/ppermute | solution.py:277
  12.9 0.7 collective-permute-start.7
  13.6 2.6 %collective-permute-start.8 = (bf16[128,512]{1,0:T(8,128)(2,1)S(1)}, bf16[128,512]{1,0:T(8,128)(2,1)S(1)}, u32[]{:S(2)}, u32[]{:S(2)}) collective-permute-start(bf16[128,512]{1,0:T(8,128)(2,1)S(1)} %get-tuple-element.41.token_ref.refs_0_), channel_id=1, source_target_pairs={{0,12},{4,0},{8,4},{12,8},{1,13},{5,1},{9,5},{13,9},{2,14},{6,2},{... | collective-permute-start | bytes 393224 | tf_op jit(solution)/shard_map/ppermute | solution.py:277
  16.2 1.7 %add_tiles.6 = (f32[1,64,1024]{2,1,0:T(8,128)S(1)}, bf16[1024,128]{1,0:T(8,128)(2,1)S(1)}, bf16[64,1024]{1,0:T(8,128)(2,1)S(1)}) custom-call(f32[2]{0:T(128)S(1)} %pad_maximum_fusion.amp_ref, bf16[1,128,1024]{2,1,0:T(8,128)(2,1)S(1)} %get-tuple-element.40.left_ref, bf16[128,512]{1,0:T(8,128)(2,1)S(1)} %get-tuple-element.41.token_ref.refs_0_, ...), custom_call_target="tpu_custom_call" | custom-call | flops 2147483648 | bytes 393216 | tf_op jit(solution)/shard_map/add_tiles/pallas_call | solution.py:256
  17.9 2.0 %collective-permute-done.7 = bf16[128,512]{1,0:T(8,128)(2,1)S(1)} collective-permute-done((bf16[128,512]{1,0:T(8,128)(2,1)S(1)}, bf16[128,512]{1,0:T(8,128)(2,1)S(1)}, u32[]{:S(2)}, u32[]{:S(2)}) %collective-permute-start.7) | collective-permute-done | bytes 131104 | tf_op jit(solution)/shard_map/ppermute | solution.py:277
  19.9 0.0 collective-permute-done.8
  20.0 0.1 collective-permute-start.9
  20.1 1.9 %collective-permute-start.5 = (bf16[128,512]{1,0:T(8,128)(2,1)S(1)}, bf16[128,512]{1,0:T(8,128)(2,1)S(1)}, u32[]{:S(2)}, u32[]{:S(2)}) collective-permute-start(bf16[128,512]{1,0:T(8,128)(2,1)S(1)} %copy_of.3), channel_id=1, source_target_pairs={{0,1},{1,0},{2,3},{3,2},{4,5},{5,4},{6,7},{7,6},{8,9},{9,8},{10,11... | collective-permute-start | bytes 393224 | tf_op jit(solution)/shard_map/ppermute | solution.py:277
  22.0 3.6 %collective-permute-start.10 = (bf16[512,512]{1,0:T(8,128)(2,1)S(1)}, bf16[512,512]{1,0:T(8,128)(2,1)S(1)}, u32[]{:S(2)}, u32[]{:S(2)}) collective-permute-start(bf16[512,512]{1,0:T(8,128)(2,1)S(1)} %constant_dynamic-update-slice_fusion.refs_0_), channel_id=1, source_target_pairs={{0,64},{64,0},{1,65},{65,1},{2,66},{66,2},{3,67},{67,3},{4,68},{68... | collective-permute-start | bytes 1572872 | tf_op jit(solution)/shard_map/ppermute | solution.py:277
  25.5 2.3 %add_tiles.7 = (f32[1,64,1024]{2,1,0:T(8,128)S(1)}, bf16[1536,128]{1,0:T(8,128)(2,1)S(1)}, bf16[64,1536]{1,0:T(8,128)(2,1)S(1)}) custom-call(f32[2]{0:T(128)S(1)} %pad_maximum_fusion.amp_ref, bf16[1,128,1024]{2,1,0:T(8,128)(2,1)S(1)} %get-tuple-element.40.left_ref, bf16[512,512]{1,0:T(8,128)(2,1)S(1)} %constant_dynamic-update-slice_fusion.refs_0_, ...), custom_call_target="tpu_custom_call" | custom-call | flops 50331648 | bytes 589824 | tf_op jit(solution)/shard_map/add_tiles/pallas_call | solution.py:256
  27.9 0.7 ready_rows.1.left_ref
  28.5 13.0 %add_tiles.8 = (f32[3,64,1024]{2,1,0:T(8,128)S(1)}, bf16[1536,128]{1,0:T(8,128)(2,1)S(1)}, bf16[64,1536]{1,0:T(8,128)(2,1)S(1)}) custom-call(f32[2]{0:T(128)S(1)} %pad_maximum_fusion.amp_ref, bf16[3,128,1024]{2,1,0:T(8,128)(2,1)S(1)} %ready_rows.1.left_ref, bf16[1024,128]{1,0:T(8,128)(2,1)S(1)} %get-tuple-element.53.refs_0_, ...), custom_call_target="tpu_custom_call" | custom-call | flops 6442450944 | bytes 1572864 | tf_op jit(solution)/shard_map/add_tiles/pallas_call | solution.py:256
  41.6 0.3 collective-permute-start.11
  41.9 6.7 %add_tiles.9 = (f32[3,64,1024]{2,1,0:T(8,128)S(1)}, bf16[2048,128]{1,0:T(8,128)(2,1)S(1)}, bf16[64,2048]{1,0:T(8,128)(2,1)S(1)}) custom-call(f32[2]{0:T(128)S(1)} %pad_maximum_fusion.amp_ref, bf16[3,128,1024]{2,1,0:T(8,128)(2,1)S(1)} %ready_rows.1.left_ref, bf16[512,512]{1,0:T(8,128)(2,1)S(1)} %collective-permute-done.10.refs_0_, ...), custom_call_target="tpu_custom_call" | custom-call | flops 3221225472 | bytes 786432 | tf_op jit(solution)/shard_map/add_tiles/pallas_call | solution.py:256
  48.5 6.7 %add_tiles.10 = (bf16[64,1024]{1,0:T(8,128)(2,1)S(1)}, bf16[64,1024]{1,0:T(8,128)(2,1)S(1)}, bf16[64,1024]{1,0:T(8,128)(2,1)S(1)}, bf16[2048,128]{1,0:T(8,128)(2,1)S(1)}, bf16[64,2048]{1,0:T(8,128)(2,1)S(1)}) custom-call(f32[2]{0:T(128)S(1)} %pad_maximum_fusion.amp_ref, bf16[3,128,1024]{2,1,0:T(8,128)(2,1)S(1)} %ready_rows.1.left_ref, ...), custom_call_target="tpu_custom_call" | custom-call | flops 3221225472 | bytes 786432 | tf_op jit(solution)/shard_map/add_tiles/pallas_call | solution.py:256
  55.2 0.6 collective-permute-start.14
  55.9 2.7 %collective-permute-start.13 = (bf16[64,1024]{1,0:T(8,128)(2,1)S(1)}, bf16[64,1024]{1,0:T(8,128)(2,1)S(1)}, u32[]{:S(2)}, u32[]{:S(2)}) collective-permute-start(bf16[64,1024]{1,0:T(8,128)(2,1)S(1)} %get-tuple-element.69), channel_id=1, source_target_pairs={{0,48},{16,0},{32,16},{48,32},{1,49},{17,1},{33,17},{49,33},{2,50}... | collective-permute-start | bytes 393224 | tf_op jit(solution)/shard_map/ppermute | solution.py:277
  58.6 0.0 collective-permute-start.12
  58.6 5.9 %add_tiles.11 = f32[1,64,1024]{2,1,0:T(8,128)S(1)} custom-call(f32[2]{0:T(128)S(1)} %pad_maximum_fusion.amp_ref, bf16[1,128,1024]{2,1,0:T(8,128)(2,1)S(1)} %get-tuple-element.40.left_ref, bf16[1536,128]{1,0:T(8,128)(2,1)S(1)} %get-tuple-element.57.refs_0_, bf16[64,1536]{1,0:T(8,128)(2,1)S(1)} %get-tuple-element.58.refs_1_, ...), custom_call_target="tpu_custom_call" | custom-call | flops 2952790016 | bytes 2162688 | tf_op jit(solution)/shard_map/add_tiles/pallas_call | solution.py:256
  64.5 0.0 collective-permute-done.13
  64.5 0.9 %collective-permute-done.12 = bf16[64,1024]{1,0:T(8,128)(2,1)S(1)} collective-permute-done((bf16[64,1024]{1,0:T(8,128)(2,1)S(1)}, bf16[64,1024]{1,0:T(8,128)(2,1)S(1)}, u32[]{:S(2)}, u32[]{:S(2)}) %collective-permute-start.12) | collective-permute-done | bytes 131104 | tf_op jit(solution)/shard_map/ppermute | solution.py:277
  65.4 0.1 collective-permute-start.15
  66.2 4.3 %collective-permute-done.15 = f32[32,1024]{1,0:T(8,128)S(1)} collective-permute-done((f32[32,1024]{1,0:T(8,128)S(1)}, f32[32,1024]{1,0:T(8,128)S(1)}, u32[]{:S(2)}, u32[]{:S(2)}) %collective-permute-start.15) | collective-permute-done | bytes 131104 | tf_op jit(solution)/shard_map/ppermute | solution.py:277
  70.5 0.7 fusion.8
  (20 shorter events, 0.1 us)
Async XLA Ops:
  1.0 6.1 %collective-permute-start = (bf16[96,512]{1,0:T(8,128)(2,1)S(1)}, bf16[96,512]{1,0:T(8,128)(2,1)S(1)}, u32[]{:S(2)}, u32[]{:S(2)}) collective-permute-start(bf16[96,512]{1,0:T(8,128)(2,1)S(1)} %get-tuple-element.39.refs_0_), channel_id=1, source_target_pairs={{0,1},{1,0},{2,3},{3,2},{4,5},{5,4},{6,7},{7,6},{8,9},{9,8},{10,11... | collective-permute-start | bytes 294920 | tf_op jit(solution)/shard_map/ppermute | solution.py:277
  3.1 9.8 %collective-permute-start.1 = (bf16[64,512]{1,0:T(8,128)(2,1)S(1)}, bf16[64,512]{1,0:T(8,128)(2,1)S(1)}, u32[]{:S(2)}, u32[]{:S(2)}) collective-permute-start(bf16[64,512]{1,0:T(8,128)(2,1)S(1)} %copy_of.2.half_ref), channel_id=1, source_target_pairs={{0,16},{16,32},{32,48},{48,0},{1,17},{17,33},{33,49},{49,1},{2,18}... | collective-permute-start | bytes 196616 | tf_op jit(solution)/shard_map/ppermute | solution.py:277
  4.6 9.0 %collective-permute-start.2 = (bf16[64,512]{1,0:T(8,128)(2,1)S(1)}, bf16[64,512]{1,0:T(8,128)(2,1)S(1)}, u32[]{:S(2)}, u32[]{:S(2)}) collective-permute-start(bf16[64,512]{1,0:T(8,128)(2,1)S(1)} %copy_of.2.half_ref), channel_id=1, source_target_pairs={{0,48},{16,0},{32,16},{48,32},{1,49},{17,1},{33,17},{49,33},{2,50}... | collective-permute-start | bytes 196616 | tf_op jit(solution)/shard_map/ppermute | solution.py:277
  7.7 8.5 %collective-permute-start.3 = (bf16[128,512]{1,0:T(8,128)(2,1)S(1)}, bf16[128,512]{1,0:T(8,128)(2,1)S(1)}, u32[]{:S(2)}, u32[]{:S(2)}) collective-permute-start(bf16[128,512]{1,0:T(8,128)(2,1)S(1)} %get-tuple-element.41.token_ref.refs_0_), channel_id=1, source_target_pairs={{0,2},{2,0},{1,3},{3,1},{4,6},{6,4},{5,7},{7,5},{8,10},{10,8},{9,1... | collective-permute-start | bytes 393224 | tf_op jit(solution)/shard_map/ppermute | solution.py:277
  7.8 8.4 %collective-permute-start.4 = (bf16[128,512]{1,0:T(8,128)(2,1)S(1)}, bf16[128,512]{1,0:T(8,128)(2,1)S(1)}, u32[]{:S(2)}, u32[]{:S(2)}) collective-permute-start(bf16[128,512]{1,0:T(8,128)(2,1)S(1)} %get-tuple-element.42), channel_id=1, source_target_pairs={{0,32},{16,48},{32,0},{48,16},{1,33},{17,49},{33,1},{49,17},{2,34}... | collective-permute-start | bytes 393224 | tf_op jit(solution)/shard_map/ppermute | solution.py:277
  9.7 8.2 %collective-permute-start.6 = (bf16[128,512]{1,0:T(8,128)(2,1)S(1)}, bf16[128,512]{1,0:T(8,128)(2,1)S(1)}, u32[]{:S(2)}, u32[]{:S(2)}) collective-permute-start(bf16[128,512]{1,0:T(8,128)(2,1)S(1)} %get-tuple-element.41.token_ref.refs_0_), channel_id=1, source_target_pairs={{0,8},{4,12},{8,0},{12,4},{1,9},{5,13},{9,1},{13,5},{2,10},{6,14},... | collective-permute-start | bytes 393224 | tf_op jit(solution)/shard_map/ppermute | solution.py:277
  12.9 7.0 %collective-permute-start.7 = (bf16[128,512]{1,0:T(8,128)(2,1)S(1)}, bf16[128,512]{1,0:T(8,128)(2,1)S(1)}, u32[]{:S(2)}, u32[]{:S(2)}) collective-permute-start(bf16[128,512]{1,0:T(8,128)(2,1)S(1)} %get-tuple-element.41.token_ref.refs_0_), channel_id=1, source_target_pairs={{0,4},{4,8},{8,12},{12,0},{1,5},{5,9},{9,13},{13,1},{2,6},{6,10},{... | collective-permute-start | bytes 393224 | tf_op jit(solution)/shard_map/ppermute | solution.py:277
  13.6 6.3 %collective-permute-start.8 = (bf16[128,512]{1,0:T(8,128)(2,1)S(1)}, bf16[128,512]{1,0:T(8,128)(2,1)S(1)}, u32[]{:S(2)}, u32[]{:S(2)}) collective-permute-start(bf16[128,512]{1,0:T(8,128)(2,1)S(1)} %get-tuple-element.41.token_ref.refs_0_), channel_id=1, source_target_pairs={{0,12},{4,0},{8,4},{12,8},{1,13},{5,1},{9,5},{13,9},{2,14},{6,2},{... | collective-permute-start | bytes 393224 | tf_op jit(solution)/shard_map/ppermute | solution.py:277
  20.0 8.6 %collective-permute-start.9 = (bf16[512,512]{1,0:T(8,128)(2,1)S(1)}, bf16[512,512]{1,0:T(8,128)(2,1)S(1)}, u32[]{:S(2)}, u32[]{:S(2)}) collective-permute-start(bf16[512,512]{1,0:T(8,128)(2,1)S(1)} %constant_dynamic-update-slice_fusion.refs_0_), channel_id=1, source_target_pairs={{0,2},{2,0},{1,3},{3,1},{4,6},{6,4},{5,7},{7,5},{8,10},{10,8},{9,1... | collective-permute-start | bytes 1572872 | tf_op jit(solution)/shard_map/ppermute | solution.py:277
  20.1 7.8 %collective-permute-start.5 = (bf16[128,512]{1,0:T(8,128)(2,1)S(1)}, bf16[128,512]{1,0:T(8,128)(2,1)S(1)}, u32[]{:S(2)}, u32[]{:S(2)}) collective-permute-start(bf16[128,512]{1,0:T(8,128)(2,1)S(1)} %copy_of.3), channel_id=1, source_target_pairs={{0,1},{1,0},{2,3},{3,2},{4,5},{5,4},{6,7},{7,6},{8,9},{9,8},{10,11... | collective-permute-start | bytes 393224 | tf_op jit(solution)/shard_map/ppermute | solution.py:277
  22.0 19.6 %collective-permute-start.10 = (bf16[512,512]{1,0:T(8,128)(2,1)S(1)}, bf16[512,512]{1,0:T(8,128)(2,1)S(1)}, u32[]{:S(2)}, u32[]{:S(2)}) collective-permute-start(bf16[512,512]{1,0:T(8,128)(2,1)S(1)} %constant_dynamic-update-slice_fusion.refs_0_), channel_id=1, source_target_pairs={{0,64},{64,0},{1,65},{65,1},{2,66},{66,2},{3,67},{67,3},{4,68},{68... | collective-permute-start | bytes 1572872 | tf_op jit(solution)/shard_map/ppermute | solution.py:277
  41.6 7.0 %collective-permute-start.11 = (bf16[512,512]{1,0:T(8,128)(2,1)S(1)}, bf16[512,512]{1,0:T(8,128)(2,1)S(1)}, u32[]{:S(2)}, u32[]{:S(2)}) collective-permute-start(bf16[512,512]{1,0:T(8,128)(2,1)S(1)} %collective-permute-done.10.refs_0_), channel_id=1, source_target_pairs={{0,2},{2,0},{1,3},{3,1},{4,6},{6,4},{5,7},{7,5},{8,10},{10,8},{9,1... | collective-permute-start | bytes 1572872 | tf_op jit(solution)/shard_map/ppermute | solution.py:277
  55.2 9.2 %collective-permute-start.14 = (bf16[64,1024]{1,0:T(8,128)(2,1)S(1)}, bf16[64,1024]{1,0:T(8,128)(2,1)S(1)}, u32[]{:S(2)}, u32[]{:S(2)}) collective-permute-start(bf16[64,1024]{1,0:T(8,128)(2,1)S(1)} %get-tuple-element.70), channel_id=1, source_target_pairs={{0,16},{16,32},{32,48},{48,0},{1,17},{17,33},{33,49},{49,1},{2,18}... | collective-permute-start | bytes 393224 | tf_op jit(solution)/shard_map/ppermute | solution.py:277
  55.9 8.6 %collective-permute-start.13 = (bf16[64,1024]{1,0:T(8,128)(2,1)S(1)}, bf16[64,1024]{1,0:T(8,128)(2,1)S(1)}, u32[]{:S(2)}, u32[]{:S(2)}) collective-permute-start(bf16[64,1024]{1,0:T(8,128)(2,1)S(1)} %get-tuple-element.69), channel_id=1, source_target_pairs={{0,48},{16,0},{32,16},{48,32},{1,49},{17,1},{33,17},{49,33},{2,50}... | collective-permute-start | bytes 393224 | tf_op jit(solution)/shard_map/ppermute | solution.py:277
  58.6 6.8 %collective-permute-start.12 = (bf16[64,1024]{1,0:T(8,128)(2,1)S(1)}, bf16[64,1024]{1,0:T(8,128)(2,1)S(1)}, u32[]{:S(2)}, u32[]{:S(2)}) collective-permute-start(bf16[64,1024]{1,0:T(8,128)(2,1)S(1)} %get-tuple-element.68), channel_id=1, source_target_pairs={{0,32},{16,48},{32,0},{48,16},{1,33},{17,49},{33,1},{49,17},{2,34}... | collective-permute-start | bytes 393224 | tf_op jit(solution)/shard_map/ppermute | solution.py:277
  64.5 6.0 %copy-start = (bf16[1024,32]{0,1:T(8,128)(2,1)S(1)}, bf16[1024,32]{0,1:T(8,128)(2,1)}, u32[]{:S(2)}) copy-start(bf16[1024,32]{0,1:T(8,128)(2,1)} %param.6) | copy-start | bytes 196612
  65.4 5.0 %collective-permute-start.15 = (f32[32,1024]{1,0:T(8,128)S(1)}, f32[32,1024]{1,0:T(8,128)S(1)}, u32[]{:S(2)}, u32[]{:S(2)}) collective-permute-start(f32[32,1024]{1,0:T(8,128)S(1)} %fusion.2), channel_id=1, source_target_pairs={{0,1},{1,0},{2,3},{3,2},{4,5},{5,4},{6,7},{7,6},{8,9},{9,8},{10,11... | collective-permute-start | bytes 393224 | tf_op jit(solution)/shard_map/ppermute | solution.py:277

commit v14 on v13

--- a/solution.py
+++ b/solution.py
@@ -298,11 +298,8 @@
     merged = jnp.concatenate([share] + near, axis=0)
     far = shift(merged, "zh", 1)
     merged_beside = shift(merged, "c", 1)
-    own, ready1 = add_tiles(amp, own_left, [], [(merged, 1)], own, weight=64)
-
-    theirs, own = lax.optimization_barrier((theirs, own))
     left = ready_rows(amp, mines, theirs, entire)
-    acc, ready2 = add_tiles(amp, left, [ready0, ready1], [(merged_beside, 1)])
+    acc, ready2 = add_tiles(amp, left, [ready0], [(merged, 1), (merged_beside, 1)])
     far, acc = lax.optimization_barrier((far, acc))
     far_beside = shift(far, "c", 1)
     acc, ready3 = add_tiles(amp, left, [], [(far, 0)], acc)

time: 71.3 us -> 70.9 us (level)
  Pallas kernels: 38.5 us -> 36.6 us
  waiting for transfers between devices: 7.27 us -> 8.65 us
    pallas_call x6 -> x5, Pallas kernels: 36.2 us -> 34.3 us  [add_tiles(): pl.pallas_call(body, grid=(count,), out_shape=sum_shapes + made, in_specs...]
    ppermute x16, waiting for transfers between devices: 7.27 us -> 8.65 us  [shift(): lax.ppermute(value, axis, [(i, (i + by) % size) for i in range(size)])]
  transfers between devices with their start and end apart: 16 -> 16, of which waited for: 3 -> 4; matrix products, arithmetic and copies ran while one was open for 0% -> 0% of each run, Pallas kernels for 43% -> 41%
where the time goes in v14:
time: 70.9 us; the launch traced here: 70.6 us
  Pallas kernels  36.6 us (52%)
  starting transfers between devices  23 us (32%)
  waiting for transfers between devices  8.65 us (12%)
  between operations  1.52 us (2%)
  other arithmetic  0.82 us (1%)
    pallas_call x5, Pallas kernels, add_tiles(): pl.pallas_call(body, grid=(count,), out_shape=sum_shapes + made, in_specs...  34.3 us
    ppermute x16, starting transfers between devices, shift(): lax.ppermute(value, axis, [(i, (i + by) % size) for i in range(size)])  23 us
    ppermute x16, waiting for transfers between devices, shift(): lax.ppermute(value, axis, [(i, (i + by) % size) for i in range(size)])  8.65 us
  transfers between devices with their start and end apart: 16, of which 4 were waited for; matrix products, arithmetic and copies ran while one was open for 0% of the time, Pallas kernels for 41%

profile of v14, /device:TPU:0, one launch (start us, length us, event | category | flops | bytes accessed | tf_op | source)
XLA Modules:
  0.0 70.6 jit_solution(12013945702268783596)
XLA Ops:
  0.0 1.0 %first_pack.1 = (bf16[96,512]{1,0:T(8,128)(2,1)S(1)}, bf16[32,512]{1,0:T(8,128)(2,1)S(1)}) custom-call(s32[1]{0:T(128)} %bitcast.zl_ref, bf16[32,1024]{1,0:T(8,128)(2,1)} %bitcast.33, bf16[32,1024]{1,0:T(8,128)(2,1)} %bitcast.32, f32[1,64]{1,0:T(1,128)} %bitcast.34), custom_call_target="tpu_custom_call" | custom-call | tf_op jit(solution)/shard_map/first_pack/pallas_call | solution.py:94
  1.0 2.1 %collective-permute-start = (bf16[96,512]{1,0:T(8,128)(2,1)S(1)}, bf16[96,512]{1,0:T(8,128)(2,1)S(1)}, u32[]{:S(2)}, u32[]{:S(2)}) collective-permute-start(bf16[96,512]{1,0:T(8,128)(2,1)S(1)} %get-tuple-element.34.refs_0_), channel_id=1, source_target_pairs={{0,1},{1,0},{2,3},{3,2},{4,5},{5,4},{6,7},{7,6},{8,9},{9,8},{10,11... | collective-permute-start | bytes 294920 | tf_op jit(solution)/shard_map/ppermute | solution.py:277
  3.1 1.5 %collective-permute-start.1 = (bf16[64,512]{1,0:T(8,128)(2,1)S(1)}, bf16[64,512]{1,0:T(8,128)(2,1)S(1)}, u32[]{:S(2)}, u32[]{:S(2)}) collective-permute-start(bf16[64,512]{1,0:T(8,128)(2,1)S(1)} %copy_of.2.half_ref), channel_id=1, source_target_pairs={{0,16},{16,32},{32,48},{48,0},{1,17},{17,33},{33,49},{49,1},{2,18}... | collective-permute-start | bytes 196616 | tf_op jit(solution)/shard_map/ppermute | solution.py:277
  4.6 1.7 %collective-permute-start.2 = (bf16[64,512]{1,0:T(8,128)(2,1)S(1)}, bf16[64,512]{1,0:T(8,128)(2,1)S(1)}, u32[]{:S(2)}, u32[]{:S(2)}) collective-permute-start(bf16[64,512]{1,0:T(8,128)(2,1)S(1)} %copy_of.2.half_ref), channel_id=1, source_target_pairs={{0,48},{16,0},{32,16},{48,32},{1,49},{17,1},{33,17},{49,33},{2,50}... | collective-permute-start | bytes 196616 | tf_op jit(solution)/shard_map/ppermute | solution.py:277
  7.0 0.1 pad_maximum_fusion.amp_ref
  7.1 0.6 second_pack.1
  7.7 0.1 collective-permute-start.3
  7.8 1.9 %collective-permute-start.4 = (bf16[128,512]{1,0:T(8,128)(2,1)S(1)}, bf16[128,512]{1,0:T(8,128)(2,1)S(1)}, u32[]{:S(2)}, u32[]{:S(2)}) collective-permute-start(bf16[128,512]{1,0:T(8,128)(2,1)S(1)} %get-tuple-element.37), channel_id=1, source_target_pairs={{0,32},{16,48},{32,0},{48,16},{1,33},{17,49},{33,1},{49,17},{2,34}... | collective-permute-start | bytes 393224 | tf_op jit(solution)/shard_map/ppermute | solution.py:277
  9.7 3.2 %collective-permute-start.6 = (bf16[128,512]{1,0:T(8,128)(2,1)S(1)}, bf16[128,512]{1,0:T(8,128)(2,1)S(1)}, u32[]{:S(2)}, u32[]{:S(2)}) collective-permute-start(bf16[128,512]{1,0:T(8,128)(2,1)S(1)} %get-tuple-element.36.token_ref.refs_0_), channel_id=1, source_target_pairs={{0,8},{4,12},{8,0},{12,4},{1,9},{5,13},{9,1},{13,5},{2,10},{6,14},... | collective-permute-start | bytes 393224 | tf_op jit(solution)/shard_map/ppermute | solution.py:277
  12.9 0.0 collective-permute-done.1.refs_0_
  12.9 0.7 collective-permute-start.7
  13.6 2.6 %collective-permute-start.8 = (bf16[128,512]{1,0:T(8,128)(2,1)S(1)}, bf16[128,512]{1,0:T(8,128)(2,1)S(1)}, u32[]{:S(2)}, u32[]{:S(2)}) collective-permute-start(bf16[128,512]{1,0:T(8,128)(2,1)S(1)} %get-tuple-element.36.token_ref.refs_0_), channel_id=1, source_target_pairs={{0,12},{4,0},{8,4},{12,8},{1,13},{5,1},{9,5},{13,9},{2,14},{6,2},{... | collective-permute-start | bytes 393224 | tf_op jit(solution)/shard_map/ppermute | solution.py:277
  16.2 1.7 %add_tiles.5 = (f32[1,64,1024]{2,1,0:T(8,128)S(1)}, bf16[1024,128]{1,0:T(8,128)(2,1)S(1)}, bf16[64,1024]{1,0:T(8,128)(2,1)S(1)}) custom-call(f32[2]{0:T(128)S(1)} %pad_maximum_fusion.amp_ref, bf16[1,128,1024]{2,1,0:T(8,128)(2,1)S(1)} %get-tuple-element.35.left_ref, bf16[128,512]{1,0:T(8,128)(2,1)S(1)} %get-tuple-element.36.token_ref.refs_0_, ...), custom_call_target="tpu_custom_call" | custom-call | flops 2147483648 | bytes 393216 | tf_op jit(solution)/shard_map/add_tiles/pallas_call | solution.py:256
  17.9 2.0 %collective-permute-done.7 = bf16[128,512]{1,0:T(8,128)(2,1)S(1)} collective-permute-done((bf16[128,512]{1,0:T(8,128)(2,1)S(1)}, bf16[128,512]{1,0:T(8,128)(2,1)S(1)}, u32[]{:S(2)}, u32[]{:S(2)}) %collective-permute-start.7) | collective-permute-done | bytes 131104 | tf_op jit(solution)/shard_map/ppermute | solution.py:277
  19.9 0.0 collective-permute-done.8
  20.0 0.1 collective-permute-start.9
  20.1 1.9 %collective-permute-start.5 = (bf16[128,512]{1,0:T(8,128)(2,1)S(1)}, bf16[128,512]{1,0:T(8,128)(2,1)S(1)}, u32[]{:S(2)}, u32[]{:S(2)}) collective-permute-start(bf16[128,512]{1,0:T(8,128)(2,1)S(1)} %copy_of.3), channel_id=1, source_target_pairs={{0,1},{1,0},{2,3},{3,2},{4,5},{5,4},{6,7},{7,6},{8,9},{9,8},{10,11... | collective-permute-start | bytes 393224 | tf_op jit(solution)/shard_map/ppermute | solution.py:277
  22.0 3.6 %collective-permute-start.10 = (bf16[512,512]{1,0:T(8,128)(2,1)S(1)}, bf16[512,512]{1,0:T(8,128)(2,1)S(1)}, u32[]{:S(2)}, u32[]{:S(2)}) collective-permute-start(bf16[512,512]{1,0:T(8,128)(2,1)S(1)} %constant_dynamic-update-slice_fusion.refs_2_), channel_id=1, source_target_pairs={{0,64},{64,0},{1,65},{65,1},{2,66},{66,2},{3,67},{67,3},{4,68},{68... | collective-permute-start | bytes 1572872 | tf_op jit(solution)/shard_map/ppermute | solution.py:277
  25.5 0.5 collective-permute-done.5.refs_2_
  26.0 0.7 ready_rows.1.left_ref
  26.7 12.1 %add_tiles.6 = (f32[3,64,1024]{2,1,0:T(8,128)S(1)}, bf16[3072,128]{1,0:T(8,128)(2,1)S(1)}, bf16[64,3072]{1,0:T(8,128)(2,1)S(1)}) custom-call(f32[2]{0:T(128)S(1)} %pad_maximum_fusion.amp_ref, bf16[3,128,1024]{2,1,0:T(8,128)(2,1)S(1)} %ready_rows.1.left_ref, bf16[1024,128]{1,0:T(8,128)(2,1)S(1)} %get-tuple-element.41.refs_0_, ...), custom_call_target="tpu_custom_call" | custom-call | flops 6442450944 | bytes 1572864 | tf_op jit(solution)/shard_map/add_tiles/pallas_call | solution.py:256
  38.8 1.7 %collective-permute-done.10.refs_0_ = bf16[512,512]{1,0:T(8,128)(2,1)S(1)} collective-permute-done((bf16[512,512]{1,0:T(8,128)(2,1)S(1)}, bf16[512,512]{1,0:T(8,128)(2,1)S(1)}, u32[]{:S(2)}, u32[]{:S(2)}) %collective-permute-start.10) | collective-permute-done | bytes 524320 | tf_op jit(solution)/shard_map/ppermute | solution.py:277
  40.6 0.0 collective-permute-start.11
  40.6 6.7 %add_tiles.7 = (f32[3,64,1024]{2,1,0:T(8,128)S(1)}, bf16[2048,128]{1,0:T(8,128)(2,1)S(1)}, bf16[64,2048]{1,0:T(8,128)(2,1)S(1)}) custom-call(f32[2]{0:T(128)S(1)} %pad_maximum_fusion.amp_ref, bf16[3,128,1024]{2,1,0:T(8,128)(2,1)S(1)} %ready_rows.1.left_ref, bf16[512,512]{1,0:T(8,128)(2,1)S(1)} %collective-permute-done.10.refs_0_, ...), custom_call_target="tpu_custom_call" | custom-call | flops 3221225472 | bytes 786432 | tf_op jit(solution)/shard_map/add_tiles/pallas_call | solution.py:256
  47.2 6.7 %add_tiles.8 = (bf16[64,1024]{1,0:T(8,128)(2,1)S(1)}, bf16[64,1024]{1,0:T(8,128)(2,1)S(1)}, bf16[64,1024]{1,0:T(8,128)(2,1)S(1)}, bf16[2048,128]{1,0:T(8,128)(2,1)S(1)}, bf16[64,2048]{1,0:T(8,128)(2,1)S(1)}) custom-call(f32[2]{0:T(128)S(1)} %pad_maximum_fusion.amp_ref, bf16[3,128,1024]{2,1,0:T(8,128)(2,1)S(1)} %ready_rows.1.left_ref, ...), custom_call_target="tpu_custom_call" | custom-call | flops 3221225472 | bytes 786432 | tf_op jit(solution)/shard_map/add_tiles/pallas_call | solution.py:256
  53.9 0.6 collective-permute-start.14
  54.6 2.7 %collective-permute-start.13 = (bf16[64,1024]{1,0:T(8,128)(2,1)S(1)}, bf16[64,1024]{1,0:T(8,128)(2,1)S(1)}, u32[]{:S(2)}, u32[]{:S(2)}) collective-permute-start(bf16[64,1024]{1,0:T(8,128)(2,1)S(1)} %get-tuple-element.59), channel_id=1, source_target_pairs={{0,48},{16,0},{32,16},{48,32},{1,49},{17,1},{33,17},{49,33},{2,50}... | collective-permute-start | bytes 393224 | tf_op jit(solution)/shard_map/ppermute | solution.py:277
  57.3 0.0 collective-permute-start.12
  57.3 7.2 %add_tiles.9 = f32[1,64,1024]{2,1,0:T(8,128)S(1)} custom-call(f32[2]{0:T(128)S(1)} %pad_maximum_fusion.amp_ref, bf16[1,128,1024]{2,1,0:T(8,128)(2,1)S(1)} %get-tuple-element.35.left_ref, bf16[3072,128]{1,0:T(8,128)(2,1)S(1)} %get-tuple-element.47.refs_0_, bf16[64,3072]{1,0:T(8,128)(2,1)S(1)} %get-tuple-element.48.refs_1_, ...), custom_call_target="tpu_custom_call" | custom-call | flops 3758096384 | bytes 2752512 | tf_op jit(solution)/shard_map/add_tiles/pallas_call | solution.py:256
  64.5 0.4 collective-permute-start.15
  65.5 4.4 %collective-permute-done.15 = f32[32,1024]{1,0:T(8,128)S(1)} collective-permute-done((f32[32,1024]{1,0:T(8,128)S(1)}, f32[32,1024]{1,0:T(8,128)S(1)}, u32[]{:S(2)}, u32[]{:S(2)}) %collective-permute-start.15) | collective-permute-done | bytes 131104 | tf_op jit(solution)/shard_map/ppermute | solution.py:277
  69.9 0.7 %fusion.8 = f32[1024,32]{0,1:T(8,128)} fusion(f32[32,1024]{1,0:T(8,128)S(1)} %collective-permute-done.15, f32[1,64,1024]{2,1,0:T(8,128)S(1)} %add_tiles.9, bf16[1024,32]{0,1:T(8,128)(2,1)S(1)} %copy-done, bf16[64,1024]{1,0:T(8,128)(2,1)S(1)} %collective-permute-done.14, bf16[64,1024]{1,0:T(8,128)(2,1)S(1)} %collective-permute-done.13, ...), kind=kLoop, calls=%fused_computation.10 | loop fusion | flops 327680 | bytes 655364 | tf_op jit(solution)/shard_map/add | solution.py:315
  (19 shorter events, 0.1 us)
Async XLA Ops:
  1.0 6.1 %collective-permute-start = (bf16[96,512]{1,0:T(8,128)(2,1)S(1)}, bf16[96,512]{1,0:T(8,128)(2,1)S(1)}, u32[]{:S(2)}, u32[]{:S(2)}) collective-permute-start(bf16[96,512]{1,0:T(8,128)(2,1)S(1)} %get-tuple-element.34.refs_0_), channel_id=1, source_target_pairs={{0,1},{1,0},{2,3},{3,2},{4,5},{5,4},{6,7},{7,6},{8,9},{9,8},{10,11... | collective-permute-start | bytes 294920 | tf_op jit(solution)/shard_map/ppermute | solution.py:277
  3.1 9.8 %collective-permute-start.1 = (bf16[64,512]{1,0:T(8,128)(2,1)S(1)}, bf16[64,512]{1,0:T(8,128)(2,1)S(1)}, u32[]{:S(2)}, u32[]{:S(2)}) collective-permute-start(bf16[64,512]{1,0:T(8,128)(2,1)S(1)} %copy_of.2.half_ref), channel_id=1, source_target_pairs={{0,16},{16,32},{32,48},{48,0},{1,17},{17,33},{33,49},{49,1},{2,18}... | collective-permute-start | bytes 196616 | tf_op jit(solution)/shard_map/ppermute | solution.py:277
  4.6 9.0 %collective-permute-start.2 = (bf16[64,512]{1,0:T(8,128)(2,1)S(1)}, bf16[64,512]{1,0:T(8,128)(2,1)S(1)}, u32[]{:S(2)}, u32[]{:S(2)}) collective-permute-start(bf16[64,512]{1,0:T(8,128)(2,1)S(1)} %copy_of.2.half_ref), channel_id=1, source_target_pairs={{0,48},{16,0},{32,16},{48,32},{1,49},{17,1},{33,17},{49,33},{2,50}... | collective-permute-start | bytes 196616 | tf_op jit(solution)/shard_map/ppermute | solution.py:277
  7.7 8.5 %collective-permute-start.3 = (bf16[128,512]{1,0:T(8,128)(2,1)S(1)}, bf16[128,512]{1,0:T(8,128)(2,1)S(1)}, u32[]{:S(2)}, u32[]{:S(2)}) collective-permute-start(bf16[128,512]{1,0:T(8,128)(2,1)S(1)} %get-tuple-element.36.token_ref.refs_0_), channel_id=1, source_target_pairs={{0,2},{2,0},{1,3},{3,1},{4,6},{6,4},{5,7},{7,5},{8,10},{10,8},{9,1... | collective-permute-start | bytes 393224 | tf_op jit(solution)/shard_map/ppermute | solution.py:277
  7.8 8.4 %collective-permute-start.4 = (bf16[128,512]{1,0:T(8,128)(2,1)S(1)}, bf16[128,512]{1,0:T(8,128)(2,1)S(1)}, u32[]{:S(2)}, u32[]{:S(2)}) collective-permute-start(bf16[128,512]{1,0:T(8,128)(2,1)S(1)} %get-tuple-element.37), channel_id=1, source_target_pairs={{0,32},{16,48},{32,0},{48,16},{1,33},{17,49},{33,1},{49,17},{2,34}... | collective-permute-start | bytes 393224 | tf_op jit(solution)/shard_map/ppermute | solution.py:277
  9.7 8.2 %collective-permute-start.6 = (bf16[128,512]{1,0:T(8,128)(2,1)S(1)}, bf16[128,512]{1,0:T(8,128)(2,1)S(1)}, u32[]{:S(2)}, u32[]{:S(2)}) collective-permute-start(bf16[128,512]{1,0:T(8,128)(2,1)S(1)} %get-tuple-element.36.token_ref.refs_0_), channel_id=1, source_target_pairs={{0,8},{4,12},{8,0},{12,4},{1,9},{5,13},{9,1},{13,5},{2,10},{6,14},... | collective-permute-start | bytes 393224 | tf_op jit(solution)/shard_map/ppermute | solution.py:277
  12.9 7.0 %collective-permute-start.7 = (bf16[128,512]{1,0:T(8,128)(2,1)S(1)}, bf16[128,512]{1,0:T(8,128)(2,1)S(1)}, u32[]{:S(2)}, u32[]{:S(2)}) collective-permute-start(bf16[128,512]{1,0:T(8,128)(2,1)S(1)} %get-tuple-element.36.token_ref.refs_0_), channel_id=1, source_target_pairs={{0,4},{4,8},{8,12},{12,0},{1,5},{5,9},{9,13},{13,1},{2,6},{6,10},{... | collective-permute-start | bytes 393224 | tf_op jit(solution)/shard_map/ppermute | solution.py:277
  13.6 6.3 %collective-permute-start.8 = (bf16[128,512]{1,0:T(8,128)(2,1)S(1)}, bf16[128,512]{1,0:T(8,128)(2,1)S(1)}, u32[]{:S(2)}, u32[]{:S(2)}) collective-permute-start(bf16[128,512]{1,0:T(8,128)(2,1)S(1)} %get-tuple-element.36.token_ref.refs_0_), channel_id=1, source_target_pairs={{0,12},{4,0},{8,4},{12,8},{1,13},{5,1},{9,5},{13,9},{2,14},{6,2},{... | collective-permute-start | bytes 393224 | tf_op jit(solution)/shard_map/ppermute | solution.py:277
  20.0 6.7 %collective-permute-start.9 = (bf16[512,512]{1,0:T(8,128)(2,1)S(1)}, bf16[512,512]{1,0:T(8,128)(2,1)S(1)}, u32[]{:S(2)}, u32[]{:S(2)}) collective-permute-start(bf16[512,512]{1,0:T(8,128)(2,1)S(1)} %constant_dynamic-update-slice_fusion.refs_2_), channel_id=1, source_target_pairs={{0,2},{2,0},{1,3},{3,1},{4,6},{6,4},{5,7},{7,5},{8,10},{10,8},{9,1... | collective-permute-start | bytes 1572872 | tf_op jit(solution)/shard_map/ppermute | solution.py:277
  20.1 6.0 %collective-permute-start.5 = (bf16[128,512]{1,0:T(8,128)(2,1)S(1)}, bf16[128,512]{1,0:T(8,128)(2,1)S(1)}, u32[]{:S(2)}, u32[]{:S(2)}) collective-permute-start(bf16[128,512]{1,0:T(8,128)(2,1)S(1)} %copy_of.3), channel_id=1, source_target_pairs={{0,1},{1,0},{2,3},{3,2},{4,5},{5,4},{6,7},{7,6},{8,9},{9,8},{10,11... | collective-permute-start | bytes 393224 | tf_op jit(solution)/shard_map/ppermute | solution.py:277
  22.0 18.6 %collective-permute-start.10 = (bf16[512,512]{1,0:T(8,128)(2,1)S(1)}, bf16[512,512]{1,0:T(8,128)(2,1)S(1)}, u32[]{:S(2)}, u32[]{:S(2)}) collective-permute-start(bf16[512,512]{1,0:T(8,128)(2,1)S(1)} %constant_dynamic-update-slice_fusion.refs_2_), channel_id=1, source_target_pairs={{0,64},{64,0},{1,65},{65,1},{2,66},{66,2},{3,67},{67,3},{4,68},{68... | collective-permute-start | bytes 1572872 | tf_op jit(solution)/shard_map/ppermute | solution.py:277
  40.6 6.7 %collective-permute-start.11 = (bf16[512,512]{1,0:T(8,128)(2,1)S(1)}, bf16[512,512]{1,0:T(8,128)(2,1)S(1)}, u32[]{:S(2)}, u32[]{:S(2)}) collective-permute-start(bf16[512,512]{1,0:T(8,128)(2,1)S(1)} %collective-permute-done.10.refs_0_), channel_id=1, source_target_pairs={{0,2},{2,0},{1,3},{3,1},{4,6},{6,4},{5,7},{7,5},{8,10},{10,8},{9,1... | collective-permute-start | bytes 1572872 | tf_op jit(solution)/shard_map/ppermute | solution.py:277
  53.9 10.5 %collective-permute-start.14 = (bf16[64,1024]{1,0:T(8,128)(2,1)S(1)}, bf16[64,1024]{1,0:T(8,128)(2,1)S(1)}, u32[]{:S(2)}, u32[]{:S(2)}) collective-permute-start(bf16[64,1024]{1,0:T(8,128)(2,1)S(1)} %get-tuple-element.60), channel_id=1, source_target_pairs={{0,16},{16,32},{32,48},{48,0},{1,17},{17,33},{33,49},{49,1},{2,18}... | collective-permute-start | bytes 393224 | tf_op jit(solution)/shard_map/ppermute | solution.py:277
  54.6 9.8 %collective-permute-start.13 = (bf16[64,1024]{1,0:T(8,128)(2,1)S(1)}, bf16[64,1024]{1,0:T(8,128)(2,1)S(1)}, u32[]{:S(2)}, u32[]{:S(2)}) collective-permute-start(bf16[64,1024]{1,0:T(8,128)(2,1)S(1)} %get-tuple-element.59), channel_id=1, source_target_pairs={{0,48},{16,0},{32,16},{48,32},{1,49},{17,1},{33,17},{49,33},{2,50}... | collective-permute-start | bytes 393224 | tf_op jit(solution)/shard_map/ppermute | solution.py:277
  57.3 7.2 %collective-permute-start.12 = (bf16[64,1024]{1,0:T(8,128)(2,1)S(1)}, bf16[64,1024]{1,0:T(8,128)(2,1)S(1)}, u32[]{:S(2)}, u32[]{:S(2)}) collective-permute-start(bf16[64,1024]{1,0:T(8,128)(2,1)S(1)} %get-tuple-element.58), channel_id=1, source_target_pairs={{0,32},{16,48},{32,0},{48,16},{1,33},{17,49},{33,1},{49,17},{2,34}... | collective-permute-start | bytes 393224 | tf_op jit(solution)/shard_map/ppermute | solution.py:277
  64.4 5.5 %copy-start = (bf16[1024,32]{0,1:T(8,128)(2,1)S(1)}, bf16[1024,32]{0,1:T(8,128)(2,1)}, u32[]{:S(2)}) copy-start(bf16[1024,32]{0,1:T(8,128)(2,1)} %param.6) | copy-start | bytes 196612
  64.5 5.4 %collective-permute-start.15 = (f32[32,1024]{1,0:T(8,128)S(1)}, f32[32,1024]{1,0:T(8,128)S(1)}, u32[]{:S(2)}, u32[]{:S(2)}) collective-permute-start(f32[32,1024]{1,0:T(8,128)S(1)} %fusion.2), channel_id=1, source_target_pairs={{0,1},{1,0},{2,3},{3,2},{4,5},{5,4},{6,7},{7,6},{8,9},{9,8},{10,11... | collective-permute-start | bytes 393224 | tf_op jit(solution)/shard_map/ppermute | solution.py:277

commit v15 on v14

--- a/solution.py
+++ b/solution.py
@@ -157,9 +157,8 @@
 
 def ready_sum(lefts, pairs, top):
     sums = [jnp.zeros((64, TM), F32) for _ in lefts]
-    for right_ref, vectors_ref in pairs:
-        total = right_ref.shape[0]
-        for at in range(0, total, TN):
+    for right_ref, vectors_ref, low, total in pairs:
+        for at in range(low, total, TN):
             part = slice(at, min(at + TN, total))
             for k, left in enumerate(lefts):
                 sums[k] += one_block(left, right_ref[part, :], vectors_ref[:, part], top)
@@ -190,9 +189,10 @@
 
 def add_tiles(amp, left, ready, raws, before=None, narrow=False, weight=1024):
     count = left.shape[0]
-    flat = [part for pair in ready for part in pair]
+    flat = [part for pair in ready for part in pair[:2]]
+    ranges = [pair[2:] or (0, pair[0].shape[0]) for pair in ready]
     total = sum(4 * raw.shape[0] - 512 * start for raw, start in raws)
-    cols = total + sum(right.shape[0] for right, _ in ready)
+    cols = total + sum(stop - low for low, stop in ranges)
     old = [] if before is None else [before]
     sums = count if narrow else 1
     ends = [len(flat), len(raws), len(old), sums]
@@ -203,7 +203,7 @@
             groups.append(refs[:size])
             refs = refs[size:]
         flat_refs, raw_refs, before_refs, sum_refs = groups
-        pairs = [(flat_refs[2 * k], flat_refs[2 * k + 1]) for k in range(len(ready))]
+        pairs = [(flat_refs[2 * k], flat_refs[2 * k + 1], *ranges[k]) for k in range(len(ready))]
         step = pl.program_id(0)
         top = jnp.full((1, 1), amp_ref[0], F32).astype(BF16)
 
@@ -221,7 +221,7 @@
 
         def tiles(fresh):
             lefts = [left_ref[0, :, at : at + TM] for at in range(0, 1024, TM)]
-            sums = ready_sum(lefts, pairs if fresh or not raws else pairs + [tuple(refs)], top)
+            sums = ready_sum(lefts, pairs if fresh or not raws else pairs + [(*refs, 0, total)], top)
             if fresh:
                 starts = [(ref, start) for ref, (_, start) in zip(raw_refs, raws)]
                 sums = [a + b for a, b in zip(sums, raw_sum(lefts, starts, *refs, top))]
@@ -300,12 +300,13 @@
     merged_beside = shift(merged, "c", 1)
     left = ready_rows(amp, mines, theirs, entire)
     acc, ready2 = add_tiles(amp, left, [ready0], [(merged, 1), (merged_beside, 1)])
-    far, acc = lax.optimization_barrier((far, acc))
+    own, _ = add_tiles(amp, own_left, [(*ready2, 0, 1536)], [], own)
+    far, acc, own = lax.optimization_barrier((far, acc, own))
     far_beside = shift(far, "c", 1)
     acc, ready3 = add_tiles(amp, left, [], [(far, 0)], acc)
     sent, ready4 = add_tiles(amp, left, [], [(far_beside, 0)], acc, narrow=True)
     arrived = [shift(sent[k], "x", by) for k, by in ((2, 2), (0, -1), (1, 1))]
-    own, _ = add_tiles(amp, own_left, [ready2, ready3, ready4], [], own)
+    own, _ = add_tiles(amp, own_left, [(*ready2, 1536, 3072), ready3, ready4], [], own)
     mine, theirs = own[0, :32], own[0, 32:]
     for part in arrived:
         theirs = theirs + part[32:].astype(F32)

time: 70.9 us -> 71.1 us (level)
  waiting for transfers between devices: 8.65 us -> 5.56 us
  starting transfers between devices: 23 us -> 25.2 us
  Pallas kernels: 36.6 us -> 37.6 us
    ppermute x16, waiting for transfers between devices: 8.65 us -> 5.56 us  [shift(): lax.ppermute(value, axis, [(i, (i + by) % size) for i in range(size)])]
    ppermute x16, starting transfers between devices: 23 us -> 25.2 us  [shift(): lax.ppermute(value, axis, [(i, (i + by) % size) for i in range(size)])]
    pallas_call x5 -> x6, Pallas kernels: 34.3 us -> 35.3 us  [add_tiles(): pl.pallas_call(body, grid=(count,), out_shape=sum_shapes + made, in_specs...]
  transfers between devices with their start and end apart: 16 -> 16, of which waited for: 4 -> 4; matrix products, arithmetic and copies ran while one was open for 0% -> 0% of each run, Pallas kernels for 41% -> 42%
where the time goes in v15:
time: 71.1 us; the launch traced here: 70.7 us
  Pallas kernels  37.6 us (53%)
  starting transfers between devices  25.2 us (35%)
  waiting for transfers between devices  5.56 us (8%)
  between operations  1.52 us (2%)
  other arithmetic  0.82 us (1%)
    pallas_call x6, Pallas kernels, add_tiles(): pl.pallas_call(body, grid=(count,), out_shape=sum_shapes + made, in_specs...  35.3 us
    ppermute x16, starting transfers between devices, shift(): lax.ppermute(value, axis, [(i, (i + by) % size) for i in range(size)])  25.2 us
    ppermute x16, waiting for transfers between devices, shift(): lax.ppermute(value, axis, [(i, (i + by) % size) for i in range(size)])  5.56 us
  transfers between devices with their start and end apart: 16, of which 4 were waited for; matrix products, arithmetic and copies ran while one was open for 0% of the time, Pallas kernels for 42%

profile of v15, /device:TPU:0, one launch (start us, length us, event | category | flops | bytes accessed | tf_op | source)
XLA Modules:
  0.0 70.7 jit_solution(5196277798588195841)
XLA Ops:
  0.0 1.0 %first_pack.1 = (bf16[96,512]{1,0:T(8,128)(2,1)S(1)}, bf16[32,512]{1,0:T(8,128)(2,1)S(1)}) custom-call(s32[1]{0:T(128)} %bitcast.zl_ref, bf16[32,1024]{1,0:T(8,128)(2,1)} %bitcast.33, bf16[32,1024]{1,0:T(8,128)(2,1)} %bitcast.32, f32[1,64]{1,0:T(1,128)} %bitcast.34), custom_call_target="tpu_custom_call" | custom-call | tf_op jit(solution)/shard_map/first_pack/pallas_call | solution.py:94
  1.0 2.1 %collective-permute-start = (bf16[96,512]{1,0:T(8,128)(2,1)S(1)}, bf16[96,512]{1,0:T(8,128)(2,1)S(1)}, u32[]{:S(2)}, u32[]{:S(2)}) collective-permute-start(bf16[96,512]{1,0:T(8,128)(2,1)S(1)} %get-tuple-element.35.refs_0_), channel_id=1, source_target_pairs={{0,1},{1,0},{2,3},{3,2},{4,5},{5,4},{6,7},{7,6},{8,9},{9,8},{10,11... | collective-permute-start | bytes 294920 | tf_op jit(solution)/shard_map/ppermute | solution.py:277
  3.1 1.5 %collective-permute-start.1 = (bf16[64,512]{1,0:T(8,128)(2,1)S(1)}, bf16[64,512]{1,0:T(8,128)(2,1)S(1)}, u32[]{:S(2)}, u32[]{:S(2)}) collective-permute-start(bf16[64,512]{1,0:T(8,128)(2,1)S(1)} %copy_of.2.half_ref), channel_id=1, source_target_pairs={{0,16},{16,32},{32,48},{48,0},{1,17},{17,33},{33,49},{49,1},{2,18}... | collective-permute-start | bytes 196616 | tf_op jit(solution)/shard_map/ppermute | solution.py:277
  4.6 1.7 %collective-permute-start.2 = (bf16[64,512]{1,0:T(8,128)(2,1)S(1)}, bf16[64,512]{1,0:T(8,128)(2,1)S(1)}, u32[]{:S(2)}, u32[]{:S(2)}) collective-permute-start(bf16[64,512]{1,0:T(8,128)(2,1)S(1)} %copy_of.2.half_ref), channel_id=1, source_target_pairs={{0,48},{16,0},{32,16},{48,32},{1,49},{17,1},{33,17},{49,33},{2,50}... | collective-permute-start | bytes 196616 | tf_op jit(solution)/shard_map/ppermute | solution.py:277
  7.0 0.1 pad_maximum_fusion.amp_ref
  7.1 0.6 second_pack.1
  7.7 0.1 collective-permute-start.3
  7.8 1.9 %collective-permute-start.4 = (bf16[128,512]{1,0:T(8,128)(2,1)S(1)}, bf16[128,512]{1,0:T(8,128)(2,1)S(1)}, u32[]{:S(2)}, u32[]{:S(2)}) collective-permute-start(bf16[128,512]{1,0:T(8,128)(2,1)S(1)} %get-tuple-element.38), channel_id=1, source_target_pairs={{0,32},{16,48},{32,0},{48,16},{1,33},{17,49},{33,1},{49,17},{2,34}... | collective-permute-start | bytes 393224 | tf_op jit(solution)/shard_map/ppermute | solution.py:277
  9.7 3.2 %collective-permute-start.6 = (bf16[128,512]{1,0:T(8,128)(2,1)S(1)}, bf16[128,512]{1,0:T(8,128)(2,1)S(1)}, u32[]{:S(2)}, u32[]{:S(2)}) collective-permute-start(bf16[128,512]{1,0:T(8,128)(2,1)S(1)} %get-tuple-element.37.token_ref.refs_0_), channel_id=1, source_target_pairs={{0,8},{4,12},{8,0},{12,4},{1,9},{5,13},{9,1},{13,5},{2,10},{6,14},... | collective-permute-start | bytes 393224 | tf_op jit(solution)/shard_map/ppermute | solution.py:277
  12.9 0.7 collective-permute-start.7
  13.6 2.6 %collective-permute-start.8 = (bf16[128,512]{1,0:T(8,128)(2,1)S(1)}, bf16[128,512]{1,0:T(8,128)(2,1)S(1)}, u32[]{:S(2)}, u32[]{:S(2)}) collective-permute-start(bf16[128,512]{1,0:T(8,128)(2,1)S(1)} %get-tuple-element.37.token_ref.refs_0_), channel_id=1, source_target_pairs={{0,12},{4,0},{8,4},{12,8},{1,13},{5,1},{9,5},{13,9},{2,14},{6,2},{... | collective-permute-start | bytes 393224 | tf_op jit(solution)/shard_map/ppermute | solution.py:277
  16.2 1.7 %add_tiles.6 = (f32[1,64,1024]{2,1,0:T(8,128)S(1)}, bf16[1024,128]{1,0:T(8,128)(2,1)S(1)}, bf16[64,1024]{1,0:T(8,128)(2,1)S(1)}) custom-call(f32[2]{0:T(128)S(1)} %pad_maximum_fusion.amp_ref, bf16[1,128,1024]{2,1,0:T(8,128)(2,1)S(1)} %get-tuple-element.36.left_ref, bf16[128,512]{1,0:T(8,128)(2,1)S(1)} %get-tuple-element.37.token_ref.refs_0_, ...), custom_call_target="tpu_custom_call" | custom-call | flops 2147483648 | bytes 393216 | tf_op jit(solution)/shard_map/add_tiles/pallas_call | solution.py:256
  17.9 2.0 %collective-permute-done.7 = bf16[128,512]{1,0:T(8,128)(2,1)S(1)} collective-permute-done((bf16[128,512]{1,0:T(8,128)(2,1)S(1)}, bf16[128,512]{1,0:T(8,128)(2,1)S(1)}, u32[]{:S(2)}, u32[]{:S(2)}) %collective-permute-start.7) | collective-permute-done | bytes 131104 | tf_op jit(solution)/shard_map/ppermute | solution.py:277
  19.9 0.0 collective-permute-done.8
  20.0 0.1 collective-permute-start.9
  20.1 1.9 %collective-permute-start.5 = (bf16[128,512]{1,0:T(8,128)(2,1)S(1)}, bf16[128,512]{1,0:T(8,128)(2,1)S(1)}, u32[]{:S(2)}, u32[]{:S(2)}) collective-permute-start(bf16[128,512]{1,0:T(8,128)(2,1)S(1)} %copy_of.3), channel_id=1, source_target_pairs={{0,1},{1,0},{2,3},{3,2},{4,5},{5,4},{6,7},{7,6},{8,9},{9,8},{10,11... | collective-permute-start | bytes 393224 | tf_op jit(solution)/shard_map/ppermute | solution.py:277
  22.0 3.6 %collective-permute-start.10 = (bf16[512,512]{1,0:T(8,128)(2,1)S(1)}, bf16[512,512]{1,0:T(8,128)(2,1)S(1)}, u32[]{:S(2)}, u32[]{:S(2)}) collective-permute-start(bf16[512,512]{1,0:T(8,128)(2,1)S(1)} %constant_dynamic-update-slice_fusion.refs_2_), channel_id=1, source_target_pairs={{0,64},{64,0},{1,65},{65,1},{2,66},{66,2},{3,67},{67,3},{4,68},{68... | collective-permute-start | bytes 1572872 | tf_op jit(solution)/shard_map/ppermute | solution.py:277
  25.5 0.5 collective-permute-done.5.refs_2_
  26.0 0.7 ready_rows.1.left_ref
  26.7 12.2 %add_tiles.7 = (f32[3,64,1024]{2,1,0:T(8,128)S(1)}, bf16[3072,128]{1,0:T(8,128)(2,1)S(1)}, bf16[64,3072]{1,0:T(8,128)(2,1)S(1)}) custom-call(f32[2]{0:T(128)S(1)} %pad_maximum_fusion.amp_ref, bf16[3,128,1024]{2,1,0:T(8,128)(2,1)S(1)} %ready_rows.1.left_ref, bf16[1024,128]{1,0:T(8,128)(2,1)S(1)} %get-tuple-element.42.refs_0_, ...), custom_call_target="tpu_custom_call" | custom-call | flops 6442450944 | bytes 1572864 | tf_op jit(solution)/shard_map/add_tiles/pallas_call | solution.py:256
  38.9 2.2 %add_tiles.8.refs_6_ = f32[1,64,1024]{2,1,0:T(8,128)S(1)} custom-call(f32[2]{0:T(128)S(1)} %pad_maximum_fusion.amp_ref, bf16[1,128,1024]{2,1,0:T(8,128)(2,1)S(1)} %get-tuple-element.36.left_ref, bf16[3072,128]{1,0:T(8,128)(2,1)S(1)} %get-tuple-element.48.refs_0_, bf16[64,3072]{1,0:T(8,128)(2,1)S(1)} %get-tuple-element.49.refs_1_, ...), custom_call_target="tpu_custom_call" | custom-call | flops 805306368 | bytes 589824 | tf_op jit(solution)/shard_map/add_tiles/pallas_call | solution.py:256
  41.1 0.3 collective-permute-start.11
  41.4 6.7 %add_tiles.9 = (f32[3,64,1024]{2,1,0:T(8,128)S(1)}, bf16[2048,128]{1,0:T(8,128)(2,1)S(1)}, bf16[64,2048]{1,0:T(8,128)(2,1)S(1)}) custom-call(f32[2]{0:T(128)S(1)} %pad_maximum_fusion.amp_ref, bf16[3,128,1024]{2,1,0:T(8,128)(2,1)S(1)} %ready_rows.1.left_ref, bf16[512,512]{1,0:T(8,128)(2,1)S(1)} %collective-permute-done.10.refs_0_, ...), custom_call_target="tpu_custom_call" | custom-call | flops 3221225472 | bytes 786432 | tf_op jit(solution)/shard_map/add_tiles/pallas_call | solution.py:256
  48.1 6.7 %add_tiles.10 = (bf16[64,1024]{1,0:T(8,128)(2,1)S(1)}, bf16[64,1024]{1,0:T(8,128)(2,1)S(1)}, bf16[64,1024]{1,0:T(8,128)(2,1)S(1)}, bf16[2048,128]{1,0:T(8,128)(2,1)S(1)}, bf16[64,2048]{1,0:T(8,128)(2,1)S(1)}) custom-call(f32[2]{0:T(128)S(1)} %pad_maximum_fusion.amp_ref, bf16[3,128,1024]{2,1,0:T(8,128)(2,1)S(1)} %ready_rows.1.left_ref, ...), custom_call_target="tpu_custom_call" | custom-call | flops 3221225472 | bytes 786432 | tf_op jit(solution)/shard_map/add_tiles/pallas_call | solution.py:256
  54.8 0.6 collective-permute-start.14
  55.4 2.7 %collective-permute-start.13 = (bf16[64,1024]{1,0:T(8,128)(2,1)S(1)}, bf16[64,1024]{1,0:T(8,128)(2,1)S(1)}, u32[]{:S(2)}, u32[]{:S(2)}) collective-permute-start(bf16[64,1024]{1,0:T(8,128)(2,1)S(1)} %get-tuple-element.61), channel_id=1, source_target_pairs={{0,48},{16,0},{32,16},{48,32},{1,49},{17,1},{33,17},{49,33},{2,50}... | collective-permute-start | bytes 393224 | tf_op jit(solution)/shard_map/ppermute | solution.py:277
  58.1 0.5 collective-permute-start.12
  58.5 5.9 %add_tiles.11 = f32[1,64,1024]{2,1,0:T(8,128)S(1)} custom-call(f32[2]{0:T(128)S(1)} %pad_maximum_fusion.amp_ref, bf16[1,128,1024]{2,1,0:T(8,128)(2,1)S(1)} %get-tuple-element.36.left_ref, bf16[3072,128]{1,0:T(8,128)(2,1)S(1)} %get-tuple-element.48.refs_0_, bf16[64,3072]{1,0:T(8,128)(2,1)S(1)} %get-tuple-element.49.refs_1_, ...), custom_call_target="tpu_custom_call" | custom-call | flops 2952790016 | bytes 2162688 | tf_op jit(solution)/shard_map/add_tiles/pallas_call | solution.py:256
  64.5 0.4 collective-permute-done.12
  64.9 1.8 %collective-permute-start.15 = (f32[32,1024]{1,0:T(8,128)S(1)}, f32[32,1024]{1,0:T(8,128)S(1)}, u32[]{:S(2)}, u32[]{:S(2)}) collective-permute-start(f32[32,1024]{1,0:T(8,128)S(1)} %fusion.2), channel_id=1, source_target_pairs={{0,1},{1,0},{2,3},{3,2},{4,5},{5,4},{6,7},{7,6},{8,9},{9,8},{10,11... | collective-permute-start | bytes 393224 | tf_op jit(solution)/shard_map/ppermute | solution.py:277
  67.4 2.6 %collective-permute-done.15 = f32[32,1024]{1,0:T(8,128)S(1)} collective-permute-done((f32[32,1024]{1,0:T(8,128)S(1)}, f32[32,1024]{1,0:T(8,128)S(1)}, u32[]{:S(2)}, u32[]{:S(2)}) %collective-permute-start.15) | collective-permute-done | bytes 131104 | tf_op jit(solution)/shard_map/ppermute | solution.py:277
  70.0 0.7 %fusion.8 = f32[1024,32]{0,1:T(8,128)} fusion(f32[32,1024]{1,0:T(8,128)S(1)} %collective-permute-done.15, f32[1,64,1024]{2,1,0:T(8,128)S(1)} %add_tiles.11, bf16[1024,32]{0,1:T(8,128)(2,1)S(1)} %copy-done, bf16[64,1024]{1,0:T(8,128)(2,1)S(1)} %collective-permute-done.14, bf16[64,1024]{1,0:T(8,128)(2,1)S(1)} %collective-permute-done.13, ...), kind=kLoop, calls=%fused_computation.10 | loop fusion | flops 327680 | bytes 655364 | tf_op jit(solution)/shard_map/add | solution.py:316
  (20 shorter events, 0.1 us)
Async XLA Ops:
  1.0 6.1 %collective-permute-start = (bf16[96,512]{1,0:T(8,128)(2,1)S(1)}, bf16[96,512]{1,0:T(8,128)(2,1)S(1)}, u32[]{:S(2)}, u32[]{:S(2)}) collective-permute-start(bf16[96,512]{1,0:T(8,128)(2,1)S(1)} %get-tuple-element.35.refs_0_), channel_id=1, source_target_pairs={{0,1},{1,0},{2,3},{3,2},{4,5},{5,4},{6,7},{7,6},{8,9},{9,8},{10,11... | collective-permute-start | bytes 294920 | tf_op jit(solution)/shard_map/ppermute | solution.py:277
  3.1 9.8 %collective-permute-start.1 = (bf16[64,512]{1,0:T(8,128)(2,1)S(1)}, bf16[64,512]{1,0:T(8,128)(2,1)S(1)}, u32[]{:S(2)}, u32[]{:S(2)}) collective-permute-start(bf16[64,512]{1,0:T(8,128)(2,1)S(1)} %copy_of.2.half_ref), channel_id=1, source_target_pairs={{0,16},{16,32},{32,48},{48,0},{1,17},{17,33},{33,49},{49,1},{2,18}... | collective-permute-start | bytes 196616 | tf_op jit(solution)/shard_map/ppermute | solution.py:277
  4.6 9.0 %collective-permute-start.2 = (bf16[64,512]{1,0:T(8,128)(2,1)S(1)}, bf16[64,512]{1,0:T(8,128)(2,1)S(1)}, u32[]{:S(2)}, u32[]{:S(2)}) collective-permute-start(bf16[64,512]{1,0:T(8,128)(2,1)S(1)} %copy_of.2.half_ref), channel_id=1, source_target_pairs={{0,48},{16,0},{32,16},{48,32},{1,49},{17,1},{33,17},{49,33},{2,50}... | collective-permute-start | bytes 196616 | tf_op jit(solution)/shard_map/ppermute | solution.py:277
  7.7 8.5 %collective-permute-start.3 = (bf16[128,512]{1,0:T(8,128)(2,1)S(1)}, bf16[128,512]{1,0:T(8,128)(2,1)S(1)}, u32[]{:S(2)}, u32[]{:S(2)}) collective-permute-start(bf16[128,512]{1,0:T(8,128)(2,1)S(1)} %get-tuple-element.37.token_ref.refs_0_), channel_id=1, source_target_pairs={{0,2},{2,0},{1,3},{3,1},{4,6},{6,4},{5,7},{7,5},{8,10},{10,8},{9,1... | collective-permute-start | bytes 393224 | tf_op jit(solution)/shard_map/ppermute | solution.py:277
  7.8 8.4 %collective-permute-start.4 = (bf16[128,512]{1,0:T(8,128)(2,1)S(1)}, bf16[128,512]{1,0:T(8,128)(2,1)S(1)}, u32[]{:S(2)}, u32[]{:S(2)}) collective-permute-start(bf16[128,512]{1,0:T(8,128)(2,1)S(1)} %get-tuple-element.38), channel_id=1, source_target_pairs={{0,32},{16,48},{32,0},{48,16},{1,33},{17,49},{33,1},{49,17},{2,34}... | collective-permute-start | bytes 393224 | tf_op jit(solution)/shard_map/ppermute | solution.py:277
  9.7 8.2 %collective-permute-start.6 = (bf16[128,512]{1,0:T(8,128)(2,1)S(1)}, bf16[128,512]{1,0:T(8,128)(2,1)S(1)}, u32[]{:S(2)}, u32[]{:S(2)}) collective-permute-start(bf16[128,512]{1,0:T(8,128)(2,1)S(1)} %get-tuple-element.37.token_ref.refs_0_), channel_id=1, source_target_pairs={{0,8},{4,12},{8,0},{12,4},{1,9},{5,13},{9,1},{13,5},{2,10},{6,14},... | collective-permute-start | bytes 393224 | tf_op jit(solution)/shard_map/ppermute | solution.py:277
  12.9 7.0 %collective-permute-start.7 = (bf16[128,512]{1,0:T(8,128)(2,1)S(1)}, bf16[128,512]{1,0:T(8,128)(2,1)S(1)}, u32[]{:S(2)}, u32[]{:S(2)}) collective-permute-start(bf16[128,512]{1,0:T(8,128)(2,1)S(1)} %get-tuple-element.37.token_ref.refs_0_), channel_id=1, source_target_pairs={{0,4},{4,8},{8,12},{12,0},{1,5},{5,9},{9,13},{13,1},{2,6},{6,10},{... | collective-permute-start | bytes 393224 | tf_op jit(solution)/shard_map/ppermute | solution.py:277
  13.6 6.3 %collective-permute-start.8 = (bf16[128,512]{1,0:T(8,128)(2,1)S(1)}, bf16[128,512]{1,0:T(8,128)(2,1)S(1)}, u32[]{:S(2)}, u32[]{:S(2)}) collective-permute-start(bf16[128,512]{1,0:T(8,128)(2,1)S(1)} %get-tuple-element.37.token_ref.refs_0_), channel_id=1, source_target_pairs={{0,12},{4,0},{8,4},{12,8},{1,13},{5,1},{9,5},{13,9},{2,14},{6,2},{... | collective-permute-start | bytes 393224 | tf_op jit(solution)/shard_map/ppermute | solution.py:277
  20.0 6.7 %collective-permute-start.9 = (bf16[512,512]{1,0:T(8,128)(2,1)S(1)}, bf16[512,512]{1,0:T(8,128)(2,1)S(1)}, u32[]{:S(2)}, u32[]{:S(2)}) collective-permute-start(bf16[512,512]{1,0:T(8,128)(2,1)S(1)} %constant_dynamic-update-slice_fusion.refs_2_), channel_id=1, source_target_pairs={{0,2},{2,0},{1,3},{3,1},{4,6},{6,4},{5,7},{7,5},{8,10},{10,8},{9,1... | collective-permute-start | bytes 1572872 | tf_op jit(solution)/shard_map/ppermute | solution.py:277
  20.1 6.0 %collective-permute-start.5 = (bf16[128,512]{1,0:T(8,128)(2,1)S(1)}, bf16[128,512]{1,0:T(8,128)(2,1)S(1)}, u32[]{:S(2)}, u32[]{:S(2)}) collective-permute-start(bf16[128,512]{1,0:T(8,128)(2,1)S(1)} %copy_of.3), channel_id=1, source_target_pairs={{0,1},{1,0},{2,3},{3,2},{4,5},{5,4},{6,7},{7,6},{8,9},{9,8},{10,11... | collective-permute-start | bytes 393224 | tf_op jit(solution)/shard_map/ppermute | solution.py:277
  22.0 19.1 %collective-permute-start.10 = (bf16[512,512]{1,0:T(8,128)(2,1)S(1)}, bf16[512,512]{1,0:T(8,128)(2,1)S(1)}, u32[]{:S(2)}, u32[]{:S(2)}) collective-permute-start(bf16[512,512]{1,0:T(8,128)(2,1)S(1)} %constant_dynamic-update-slice_fusion.refs_2_), channel_id=1, source_target_pairs={{0,64},{64,0},{1,65},{65,1},{2,66},{66,2},{3,67},{67,3},{4,68},{68... | collective-permute-start | bytes 1572872 | tf_op jit(solution)/shard_map/ppermute | solution.py:277
  41.1 7.0 %collective-permute-start.11 = (bf16[512,512]{1,0:T(8,128)(2,1)S(1)}, bf16[512,512]{1,0:T(8,128)(2,1)S(1)}, u32[]{:S(2)}, u32[]{:S(2)}) collective-permute-start(bf16[512,512]{1,0:T(8,128)(2,1)S(1)} %collective-permute-done.10.refs_0_), channel_id=1, source_target_pairs={{0,2},{2,0},{1,3},{3,1},{4,6},{6,4},{5,7},{7,5},{8,10},{10,8},{9,1... | collective-permute-start | bytes 1572872 | tf_op jit(solution)/shard_map/ppermute | solution.py:277
  54.8 9.7 %collective-permute-start.14 = (bf16[64,1024]{1,0:T(8,128)(2,1)S(1)}, bf16[64,1024]{1,0:T(8,128)(2,1)S(1)}, u32[]{:S(2)}, u32[]{:S(2)}) collective-permute-start(bf16[64,1024]{1,0:T(8,128)(2,1)S(1)} %get-tuple-element.62), channel_id=1, source_target_pairs={{0,16},{16,32},{32,48},{48,0},{1,17},{17,33},{33,49},{49,1},{2,18}... | collective-permute-start | bytes 393224 | tf_op jit(solution)/shard_map/ppermute | solution.py:277
  55.4 9.0 %collective-permute-start.13 = (bf16[64,1024]{1,0:T(8,128)(2,1)S(1)}, bf16[64,1024]{1,0:T(8,128)(2,1)S(1)}, u32[]{:S(2)}, u32[]{:S(2)}) collective-permute-start(bf16[64,1024]{1,0:T(8,128)(2,1)S(1)} %get-tuple-element.61), channel_id=1, source_target_pairs={{0,48},{16,0},{32,16},{48,32},{1,49},{17,1},{33,17},{49,33},{2,50}... | collective-permute-start | bytes 393224 | tf_op jit(solution)/shard_map/ppermute | solution.py:277
  58.1 6.8 %collective-permute-start.12 = (bf16[64,1024]{1,0:T(8,128)(2,1)S(1)}, bf16[64,1024]{1,0:T(8,128)(2,1)S(1)}, u32[]{:S(2)}, u32[]{:S(2)}) collective-permute-start(bf16[64,1024]{1,0:T(8,128)(2,1)S(1)} %get-tuple-element.60), channel_id=1, source_target_pairs={{0,32},{16,48},{32,0},{48,16},{1,33},{17,49},{33,1},{49,17},{2,34}... | collective-permute-start | bytes 393224 | tf_op jit(solution)/shard_map/ppermute | solution.py:277
  64.4 5.6 %copy-start = (bf16[1024,32]{0,1:T(8,128)(2,1)S(1)}, bf16[1024,32]{0,1:T(8,128)(2,1)}, u32[]{:S(2)}) copy-start(bf16[1024,32]{0,1:T(8,128)(2,1)} %param.6) | copy-start | bytes 196612
  64.9 5.0 %collective-permute-start.15 = (f32[32,1024]{1,0:T(8,128)S(1)}, f32[32,1024]{1,0:T(8,128)S(1)}, u32[]{:S(2)}, u32[]{:S(2)}) collective-permute-start(f32[32,1024]{1,0:T(8,128)S(1)} %fusion.2), channel_id=1, source_target_pairs={{0,1},{1,0},{2,3},{3,2},{4,5},{5,4},{6,7},{7,6},{8,9},{9,8},{10,11... | collective-permute-start | bytes 393224 | tf_op jit(solution)/shard_map/ppermute | solution.py:277

commit v16 on v14

--- a/solution.py
+++ b/solution.py
@@ -288,7 +288,7 @@
     own_left, share, entire = second_pack(zl, amp, half, got, kept)
 
     beside = shift(share, "c", 1)
-    near = [shift(share, "y", by) for by in (2, 1, -1)]
+    near = [shift(share, "y", by) for by in (1, 2, -1)]
     entire = shift(entire, "x", 2)
     mined = copy_of(mines, 64, share, 16)
     mined, beside, entire = lax.optimization_barrier((mined, beside, entire))

time: 70.9 us -> 71.5 us (level)
  waiting for transfers between devices: 8.65 us -> 9.85 us
    ppermute x16, waiting for transfers between devices: 8.65 us -> 9.85 us  [shift(): lax.ppermute(value, axis, [(i, (i + by) % size) for i in range(size)])]
where the time goes in v16:
time: 71.5 us; the launch traced here: 71.2 us
  Pallas kernels  36.6 us (51%)
  starting transfers between devices  22.4 us (31%)
  waiting for transfers between devices  9.85 us (14%)
  between operations  1.52 us (2%)
  other arithmetic  0.82 us (1%)
    pallas_call x5, Pallas kernels, add_tiles(): pl.pallas_call(body, grid=(count,), out_shape=sum_shapes + made, in_specs...  34.3 us
    ppermute x16, starting transfers between devices, shift(): lax.ppermute(value, axis, [(i, (i + by) % size) for i in range(size)])  22.4 us
    ppermute x16, waiting for transfers between devices, shift(): lax.ppermute(value, axis, [(i, (i + by) % size) for i in range(size)])  9.85 us
  transfers between devices with their start and end apart: 16, of which 4 were waited for; matrix products, arithmetic and copies ran while one was open for 0% of the time, Pallas kernels for 41%

profile of v16, /device:TPU:0, one launch (start us, length us, event | category | flops | bytes accessed | tf_op | source)
XLA Modules:
  0.0 71.2 jit_solution(12356022716705916866)
XLA Ops:
  0.0 1.0 %first_pack.1 = (bf16[96,512]{1,0:T(8,128)(2,1)S(1)}, bf16[32,512]{1,0:T(8,128)(2,1)S(1)}) custom-call(s32[1]{0:T(128)} %bitcast.zl_ref, bf16[32,1024]{1,0:T(8,128)(2,1)} %bitcast.33, bf16[32,1024]{1,0:T(8,128)(2,1)} %bitcast.32, f32[1,64]{1,0:T(1,128)} %bitcast.34), custom_call_target="tpu_custom_call" | custom-call | tf_op jit(solution)/shard_map/first_pack/pallas_call | solution.py:94
  1.0 2.1 %collective-permute-start = (bf16[96,512]{1,0:T(8,128)(2,1)S(1)}, bf16[96,512]{1,0:T(8,128)(2,1)S(1)}, u32[]{:S(2)}, u32[]{:S(2)}) collective-permute-start(bf16[96,512]{1,0:T(8,128)(2,1)S(1)} %get-tuple-element.34.refs_0_), channel_id=1, source_target_pairs={{0,1},{1,0},{2,3},{3,2},{4,5},{5,4},{6,7},{7,6},{8,9},{9,8},{10,11... | collective-permute-start | bytes 294920 | tf_op jit(solution)/shard_map/ppermute | solution.py:277
  3.1 1.5 %collective-permute-start.1 = (bf16[64,512]{1,0:T(8,128)(2,1)S(1)}, bf16[64,512]{1,0:T(8,128)(2,1)S(1)}, u32[]{:S(2)}, u32[]{:S(2)}) collective-permute-start(bf16[64,512]{1,0:T(8,128)(2,1)S(1)} %copy_of.2.half_ref), channel_id=1, source_target_pairs={{0,16},{16,32},{32,48},{48,0},{1,17},{17,33},{33,49},{49,1},{2,18}... | collective-permute-start | bytes 196616 | tf_op jit(solution)/shard_map/ppermute | solution.py:277
  4.6 1.7 %collective-permute-start.2 = (bf16[64,512]{1,0:T(8,128)(2,1)S(1)}, bf16[64,512]{1,0:T(8,128)(2,1)S(1)}, u32[]{:S(2)}, u32[]{:S(2)}) collective-permute-start(bf16[64,512]{1,0:T(8,128)(2,1)S(1)} %copy_of.2.half_ref), channel_id=1, source_target_pairs={{0,48},{16,0},{32,16},{48,32},{1,49},{17,1},{33,17},{49,33},{2,50}... | collective-permute-start | bytes 196616 | tf_op jit(solution)/shard_map/ppermute | solution.py:277
  7.0 0.1 pad_maximum_fusion.amp_ref
  7.1 0.6 second_pack.1
  7.7 0.1 collective-permute-start.3
  7.8 1.9 %collective-permute-start.4 = (bf16[128,512]{1,0:T(8,128)(2,1)S(1)}, bf16[128,512]{1,0:T(8,128)(2,1)S(1)}, u32[]{:S(2)}, u32[]{:S(2)}) collective-permute-start(bf16[128,512]{1,0:T(8,128)(2,1)S(1)} %get-tuple-element.37), channel_id=1, source_target_pairs={{0,32},{16,48},{32,0},{48,16},{1,33},{17,49},{33,1},{49,17},{2,34}... | collective-permute-start | bytes 393224 | tf_op jit(solution)/shard_map/ppermute | solution.py:277
  9.7 1.6 %collective-permute-start.6 = (bf16[128,512]{1,0:T(8,128)(2,1)S(1)}, bf16[128,512]{1,0:T(8,128)(2,1)S(1)}, u32[]{:S(2)}, u32[]{:S(2)}) collective-permute-start(bf16[128,512]{1,0:T(8,128)(2,1)S(1)} %get-tuple-element.36.token_ref.refs_0_), channel_id=1, source_target_pairs={{0,4},{4,8},{8,12},{12,0},{1,5},{5,9},{9,13},{13,1},{2,6},{6,10},{... | collective-permute-start | bytes 393224 | tf_op jit(solution)/shard_map/ppermute | solution.py:277
  11.3 0.0 collective-permute-done.1.refs_0_
  11.3 2.9 %collective-permute-start.7 = (bf16[128,512]{1,0:T(8,128)(2,1)S(1)}, bf16[128,512]{1,0:T(8,128)(2,1)S(1)}, u32[]{:S(2)}, u32[]{:S(2)}) collective-permute-start(bf16[128,512]{1,0:T(8,128)(2,1)S(1)} %get-tuple-element.36.token_ref.refs_0_), channel_id=1, source_target_pairs={{0,8},{4,12},{8,0},{12,4},{1,9},{5,13},{9,1},{13,5},{2,10},{6,14},... | collective-permute-start | bytes 393224 | tf_op jit(solution)/shard_map/ppermute | solution.py:277
  14.2 0.0 collective-permute-done.2.refs_1_
  14.2 1.3 %collective-permute-start.8 = (bf16[128,512]{1,0:T(8,128)(2,1)S(1)}, bf16[128,512]{1,0:T(8,128)(2,1)S(1)}, u32[]{:S(2)}, u32[]{:S(2)}) collective-permute-start(bf16[128,512]{1,0:T(8,128)(2,1)S(1)} %get-tuple-element.36.token_ref.refs_0_), channel_id=1, source_target_pairs={{0,12},{4,0},{8,4},{12,8},{1,13},{5,1},{9,5},{13,9},{2,14},{6,2},{... | collective-permute-start | bytes 393224 | tf_op jit(solution)/shard_map/ppermute | solution.py:277
  15.6 1.7 %add_tiles.5 = (f32[1,64,1024]{2,1,0:T(8,128)S(1)}, bf16[1024,128]{1,0:T(8,128)(2,1)S(1)}, bf16[64,1024]{1,0:T(8,128)(2,1)S(1)}) custom-call(f32[2]{0:T(128)S(1)} %pad_maximum_fusion.amp_ref, bf16[1,128,1024]{2,1,0:T(8,128)(2,1)S(1)} %get-tuple-element.35.left_ref, bf16[128,512]{1,0:T(8,128)(2,1)S(1)} %get-tuple-element.36.token_ref.refs_0_, ...), custom_call_target="tpu_custom_call" | custom-call | flops 2147483648 | bytes 393216 | tf_op jit(solution)/shard_map/add_tiles/pallas_call | solution.py:256
  17.3 3.2 %collective-permute-done.7 = bf16[128,512]{1,0:T(8,128)(2,1)S(1)} collective-permute-done((bf16[128,512]{1,0:T(8,128)(2,1)S(1)}, bf16[128,512]{1,0:T(8,128)(2,1)S(1)}, u32[]{:S(2)}, u32[]{:S(2)}) %collective-permute-start.7) | collective-permute-done | bytes 131104 | tf_op jit(solution)/shard_map/ppermute | solution.py:277
  20.6 0.1 collective-permute-start.9
  20.7 1.9 %collective-permute-start.5 = (bf16[128,512]{1,0:T(8,128)(2,1)S(1)}, bf16[128,512]{1,0:T(8,128)(2,1)S(1)}, u32[]{:S(2)}, u32[]{:S(2)}) collective-permute-start(bf16[128,512]{1,0:T(8,128)(2,1)S(1)} %copy_of.3), channel_id=1, source_target_pairs={{0,1},{1,0},{2,3},{3,2},{4,5},{5,4},{6,7},{7,6},{8,9},{9,8},{10,11... | collective-permute-start | bytes 393224 | tf_op jit(solution)/shard_map/ppermute | solution.py:277
  22.6 3.6 %collective-permute-start.10 = (bf16[512,512]{1,0:T(8,128)(2,1)S(1)}, bf16[512,512]{1,0:T(8,128)(2,1)S(1)}, u32[]{:S(2)}, u32[]{:S(2)}) collective-permute-start(bf16[512,512]{1,0:T(8,128)(2,1)S(1)} %constant_dynamic-update-slice_fusion.refs_2_), channel_id=1, source_target_pairs={{0,64},{64,0},{1,65},{65,1},{2,66},{66,2},{3,67},{67,3},{4,68},{68... | collective-permute-start | bytes 1572872 | tf_op jit(solution)/shard_map/ppermute | solution.py:277
  26.1 0.5 collective-permute-done.5.refs_2_
  26.6 0.7 ready_rows.1.left_ref
  27.3 12.1 %add_tiles.6 = (f32[3,64,1024]{2,1,0:T(8,128)S(1)}, bf16[3072,128]{1,0:T(8,128)(2,1)S(1)}, bf16[64,3072]{1,0:T(8,128)(2,1)S(1)}) custom-call(f32[2]{0:T(128)S(1)} %pad_maximum_fusion.amp_ref, bf16[3,128,1024]{2,1,0:T(8,128)(2,1)S(1)} %ready_rows.1.left_ref, bf16[1024,128]{1,0:T(8,128)(2,1)S(1)} %get-tuple-element.41.refs_0_, ...), custom_call_target="tpu_custom_call" | custom-call | flops 6442450944 | bytes 1572864 | tf_op jit(solution)/shard_map/add_tiles/pallas_call | solution.py:256
  39.5 1.7 %collective-permute-done.10.refs_0_ = bf16[512,512]{1,0:T(8,128)(2,1)S(1)} collective-permute-done((bf16[512,512]{1,0:T(8,128)(2,1)S(1)}, bf16[512,512]{1,0:T(8,128)(2,1)S(1)}, u32[]{:S(2)}, u32[]{:S(2)}) %collective-permute-start.10) | collective-permute-done | bytes 524320 | tf_op jit(solution)/shard_map/ppermute | solution.py:277
  41.2 0.0 collective-permute-start.11
  41.2 6.6 %add_tiles.7 = (f32[3,64,1024]{2,1,0:T(8,128)S(1)}, bf16[2048,128]{1,0:T(8,128)(2,1)S(1)}, bf16[64,2048]{1,0:T(8,128)(2,1)S(1)}) custom-call(f32[2]{0:T(128)S(1)} %pad_maximum_fusion.amp_ref, bf16[3,128,1024]{2,1,0:T(8,128)(2,1)S(1)} %ready_rows.1.left_ref, bf16[512,512]{1,0:T(8,128)(2,1)S(1)} %collective-permute-done.10.refs_0_, ...), custom_call_target="tpu_custom_call" | custom-call | flops 3221225472 | bytes 786432 | tf_op jit(solution)/shard_map/add_tiles/pallas_call | solution.py:256
  47.8 6.7 %add_tiles.8 = (bf16[64,1024]{1,0:T(8,128)(2,1)S(1)}, bf16[64,1024]{1,0:T(8,128)(2,1)S(1)}, bf16[64,1024]{1,0:T(8,128)(2,1)S(1)}, bf16[2048,128]{1,0:T(8,128)(2,1)S(1)}, bf16[64,2048]{1,0:T(8,128)(2,1)S(1)}) custom-call(f32[2]{0:T(128)S(1)} %pad_maximum_fusion.amp_ref, bf16[3,128,1024]{2,1,0:T(8,128)(2,1)S(1)} %ready_rows.1.left_ref, ...), custom_call_target="tpu_custom_call" | custom-call | flops 3221225472 | bytes 786432 | tf_op jit(solution)/shard_map/add_tiles/pallas_call | solution.py:256
  54.5 0.7 collective-permute-start.14
  55.2 2.6 %collective-permute-start.13 = (bf16[64,1024]{1,0:T(8,128)(2,1)S(1)}, bf16[64,1024]{1,0:T(8,128)(2,1)S(1)}, u32[]{:S(2)}, u32[]{:S(2)}) collective-permute-start(bf16[64,1024]{1,0:T(8,128)(2,1)S(1)} %get-tuple-element.59), channel_id=1, source_target_pairs={{0,48},{16,0},{32,16},{48,32},{1,49},{17,1},{33,17},{49,33},{2,50}... | collective-permute-start | bytes 393224 | tf_op jit(solution)/shard_map/ppermute | solution.py:277
  57.8 0.0 collective-permute-start.12
  57.8 7.2 %add_tiles.9 = f32[1,64,1024]{2,1,0:T(8,128)S(1)} custom-call(f32[2]{0:T(128)S(1)} %pad_maximum_fusion.amp_ref, bf16[1,128,1024]{2,1,0:T(8,128)(2,1)S(1)} %get-tuple-element.35.left_ref, bf16[3072,128]{1,0:T(8,128)(2,1)S(1)} %get-tuple-element.47.refs_0_, bf16[64,3072]{1,0:T(8,128)(2,1)S(1)} %get-tuple-element.48.refs_1_, ...), custom_call_target="tpu_custom_call" | custom-call | flops 3758096384 | bytes 2752512 | tf_op jit(solution)/shard_map/add_tiles/pallas_call | solution.py:256
  65.1 0.4 collective-permute-start.15
  66.1 4.3 %collective-permute-done.15 = f32[32,1024]{1,0:T(8,128)S(1)} collective-permute-done((f32[32,1024]{1,0:T(8,128)S(1)}, f32[32,1024]{1,0:T(8,128)S(1)}, u32[]{:S(2)}, u32[]{:S(2)}) %collective-permute-start.15) | collective-permute-done | bytes 131104 | tf_op jit(solution)/shard_map/ppermute | solution.py:277
  70.5 0.7 %fusion.8 = f32[1024,32]{0,1:T(8,128)} fusion(f32[32,1024]{1,0:T(8,128)S(1)} %collective-permute-done.15, f32[1,64,1024]{2,1,0:T(8,128)S(1)} %add_tiles.9, bf16[1024,32]{0,1:T(8,128)(2,1)S(1)} %copy-done, bf16[64,1024]{1,0:T(8,128)(2,1)S(1)} %collective-permute-done.14, bf16[64,1024]{1,0:T(8,128)(2,1)S(1)} %collective-permute-done.13, ...), kind=kLoop, calls=%fused_computation.10 | loop fusion | flops 327680 | bytes 655364 | tf_op jit(solution)/shard_map/add | solution.py:315
  (19 shorter events, 0.1 us)
Async XLA Ops:
  1.0 6.1 %collective-permute-start = (bf16[96,512]{1,0:T(8,128)(2,1)S(1)}, bf16[96,512]{1,0:T(8,128)(2,1)S(1)}, u32[]{:S(2)}, u32[]{:S(2)}) collective-permute-start(bf16[96,512]{1,0:T(8,128)(2,1)S(1)} %get-tuple-element.34.refs_0_), channel_id=1, source_target_pairs={{0,1},{1,0},{2,3},{3,2},{4,5},{5,4},{6,7},{7,6},{8,9},{9,8},{10,11... | collective-permute-start | bytes 294920 | tf_op jit(solution)/shard_map/ppermute | solution.py:277
  3.1 8.2 %collective-permute-start.1 = (bf16[64,512]{1,0:T(8,128)(2,1)S(1)}, bf16[64,512]{1,0:T(8,128)(2,1)S(1)}, u32[]{:S(2)}, u32[]{:S(2)}) collective-permute-start(bf16[64,512]{1,0:T(8,128)(2,1)S(1)} %copy_of.2.half_ref), channel_id=1, source_target_pairs={{0,16},{16,32},{32,48},{48,0},{1,17},{17,33},{33,49},{49,1},{2,18}... | collective-permute-start | bytes 196616 | tf_op jit(solution)/shard_map/ppermute | solution.py:277
  4.6 9.6 %collective-permute-start.2 = (bf16[64,512]{1,0:T(8,128)(2,1)S(1)}, bf16[64,512]{1,0:T(8,128)(2,1)S(1)}, u32[]{:S(2)}, u32[]{:S(2)}) collective-permute-start(bf16[64,512]{1,0:T(8,128)(2,1)S(1)} %copy_of.2.half_ref), channel_id=1, source_target_pairs={{0,48},{16,0},{32,16},{48,32},{1,49},{17,1},{33,17},{49,33},{2,50}... | collective-permute-start | bytes 196616 | tf_op jit(solution)/shard_map/ppermute | solution.py:277
  7.7 7.9 %collective-permute-start.3 = (bf16[128,512]{1,0:T(8,128)(2,1)S(1)}, bf16[128,512]{1,0:T(8,128)(2,1)S(1)}, u32[]{:S(2)}, u32[]{:S(2)}) collective-permute-start(bf16[128,512]{1,0:T(8,128)(2,1)S(1)} %get-tuple-element.36.token_ref.refs_0_), channel_id=1, source_target_pairs={{0,2},{2,0},{1,3},{3,1},{4,6},{6,4},{5,7},{7,5},{8,10},{10,8},{9,1... | collective-permute-start | bytes 393224 | tf_op jit(solution)/shard_map/ppermute | solution.py:277
  7.8 7.8 %collective-permute-start.4 = (bf16[128,512]{1,0:T(8,128)(2,1)S(1)}, bf16[128,512]{1,0:T(8,128)(2,1)S(1)}, u32[]{:S(2)}, u32[]{:S(2)}) collective-permute-start(bf16[128,512]{1,0:T(8,128)(2,1)S(1)} %get-tuple-element.37), channel_id=1, source_target_pairs={{0,32},{16,48},{32,0},{48,16},{1,33},{17,49},{33,1},{49,17},{2,34}... | collective-permute-start | bytes 393224 | tf_op jit(solution)/shard_map/ppermute | solution.py:277
  9.7 7.6 %collective-permute-start.6 = (bf16[128,512]{1,0:T(8,128)(2,1)S(1)}, bf16[128,512]{1,0:T(8,128)(2,1)S(1)}, u32[]{:S(2)}, u32[]{:S(2)}) collective-permute-start(bf16[128,512]{1,0:T(8,128)(2,1)S(1)} %get-tuple-element.36.token_ref.refs_0_), channel_id=1, source_target_pairs={{0,4},{4,8},{8,12},{12,0},{1,5},{5,9},{9,13},{13,1},{2,6},{6,10},{... | collective-permute-start | bytes 393224 | tf_op jit(solution)/shard_map/ppermute | solution.py:277
  11.3 9.2 %collective-permute-start.7 = (bf16[128,512]{1,0:T(8,128)(2,1)S(1)}, bf16[128,512]{1,0:T(8,128)(2,1)S(1)}, u32[]{:S(2)}, u32[]{:S(2)}) collective-permute-start(bf16[128,512]{1,0:T(8,128)(2,1)S(1)} %get-tuple-element.36.token_ref.refs_0_), channel_id=1, source_target_pairs={{0,8},{4,12},{8,0},{12,4},{1,9},{5,13},{9,1},{13,5},{2,10},{6,14},... | collective-permute-start | bytes 393224 | tf_op jit(solution)/shard_map/ppermute | solution.py:277
  14.2 6.3 %collective-permute-start.8 = (bf16[128,512]{1,0:T(8,128)(2,1)S(1)}, bf16[128,512]{1,0:T(8,128)(2,1)S(1)}, u32[]{:S(2)}, u32[]{:S(2)}) collective-permute-start(bf16[128,512]{1,0:T(8,128)(2,1)S(1)} %get-tuple-element.36.token_ref.refs_0_), channel_id=1, source_target_pairs={{0,12},{4,0},{8,4},{12,8},{1,13},{5,1},{9,5},{13,9},{2,14},{6,2},{... | collective-permute-start | bytes 393224 | tf_op jit(solution)/shard_map/ppermute | solution.py:277
  20.6 6.7 %collective-permute-start.9 = (bf16[512,512]{1,0:T(8,128)(2,1)S(1)}, bf16[512,512]{1,0:T(8,128)(2,1)S(1)}, u32[]{:S(2)}, u32[]{:S(2)}) collective-permute-start(bf16[512,512]{1,0:T(8,128)(2,1)S(1)} %constant_dynamic-update-slice_fusion.refs_2_), channel_id=1, source_target_pairs={{0,2},{2,0},{1,3},{3,1},{4,6},{6,4},{5,7},{7,5},{8,10},{10,8},{9,1... | collective-permute-start | bytes 1572872 | tf_op jit(solution)/shard_map/ppermute | solution.py:277
  20.7 6.0 %collective-permute-start.5 = (bf16[128,512]{1,0:T(8,128)(2,1)S(1)}, bf16[128,512]{1,0:T(8,128)(2,1)S(1)}, u32[]{:S(2)}, u32[]{:S(2)}) collective-permute-start(bf16[128,512]{1,0:T(8,128)(2,1)S(1)} %copy_of.3), channel_id=1, source_target_pairs={{0,1},{1,0},{2,3},{3,2},{4,5},{5,4},{6,7},{7,6},{8,9},{9,8},{10,11... | collective-permute-start | bytes 393224 | tf_op jit(solution)/shard_map/ppermute | solution.py:277
  22.6 18.6 %collective-permute-start.10 = (bf16[512,512]{1,0:T(8,128)(2,1)S(1)}, bf16[512,512]{1,0:T(8,128)(2,1)S(1)}, u32[]{:S(2)}, u32[]{:S(2)}) collective-permute-start(bf16[512,512]{1,0:T(8,128)(2,1)S(1)} %constant_dynamic-update-slice_fusion.refs_2_), channel_id=1, source_target_pairs={{0,64},{64,0},{1,65},{65,1},{2,66},{66,2},{3,67},{67,3},{4,68},{68... | collective-permute-start | bytes 1572872 | tf_op jit(solution)/shard_map/ppermute | solution.py:277
  41.2 6.6 %collective-permute-start.11 = (bf16[512,512]{1,0:T(8,128)(2,1)S(1)}, bf16[512,512]{1,0:T(8,128)(2,1)S(1)}, u32[]{:S(2)}, u32[]{:S(2)}) collective-permute-start(bf16[512,512]{1,0:T(8,128)(2,1)S(1)} %collective-permute-done.10.refs_0_), channel_id=1, source_target_pairs={{0,2},{2,0},{1,3},{3,1},{4,6},{6,4},{5,7},{7,5},{8,10},{10,8},{9,1... | collective-permute-start | bytes 1572872 | tf_op jit(solution)/shard_map/ppermute | solution.py:277
  54.5 10.5 %collective-permute-start.14 = (bf16[64,1024]{1,0:T(8,128)(2,1)S(1)}, bf16[64,1024]{1,0:T(8,128)(2,1)S(1)}, u32[]{:S(2)}, u32[]{:S(2)}) collective-permute-start(bf16[64,1024]{1,0:T(8,128)(2,1)S(1)} %get-tuple-element.60), channel_id=1, source_target_pairs={{0,16},{16,32},{32,48},{48,0},{1,17},{17,33},{33,49},{49,1},{2,18}... | collective-permute-start | bytes 393224 | tf_op jit(solution)/shard_map/ppermute | solution.py:277
  55.2 9.8 %collective-permute-start.13 = (bf16[64,1024]{1,0:T(8,128)(2,1)S(1)}, bf16[64,1024]{1,0:T(8,128)(2,1)S(1)}, u32[]{:S(2)}, u32[]{:S(2)}) collective-permute-start(bf16[64,1024]{1,0:T(8,128)(2,1)S(1)} %get-tuple-element.59), channel_id=1, source_target_pairs={{0,48},{16,0},{32,16},{48,32},{1,49},{17,1},{33,17},{49,33},{2,50}... | collective-permute-start | bytes 393224 | tf_op jit(solution)/shard_map/ppermute | solution.py:277
  57.8 7.2 %collective-permute-start.12 = (bf16[64,1024]{1,0:T(8,128)(2,1)S(1)}, bf16[64,1024]{1,0:T(8,128)(2,1)S(1)}, u32[]{:S(2)}, u32[]{:S(2)}) collective-permute-start(bf16[64,1024]{1,0:T(8,128)(2,1)S(1)} %get-tuple-element.58), channel_id=1, source_target_pairs={{0,32},{16,48},{32,0},{48,16},{1,33},{17,49},{33,1},{49,17},{2,34}... | collective-permute-start | bytes 393224 | tf_op jit(solution)/shard_map/ppermute | solution.py:277
  65.0 5.5 %copy-start = (bf16[1024,32]{0,1:T(8,128)(2,1)S(1)}, bf16[1024,32]{0,1:T(8,128)(2,1)}, u32[]{:S(2)}) copy-start(bf16[1024,32]{0,1:T(8,128)(2,1)} %param.6) | copy-start | bytes 196612
  65.1 5.4 %collective-permute-start.15 = (f32[32,1024]{1,0:T(8,128)S(1)}, f32[32,1024]{1,0:T(8,128)S(1)}, u32[]{:S(2)}, u32[]{:S(2)}) collective-permute-start(f32[32,1024]{1,0:T(8,128)S(1)} %fusion.2), channel_id=1, source_target_pairs={{0,1},{1,0},{2,3},{3,2},{4,5},{5,4},{6,7},{7,6},{8,9},{9,8},{10,11... | collective-permute-start | bytes 393224 | tf_op jit(solution)/shard_map/ppermute | solution.py:277
